TPU v7x, 512 devices: a whole 4x8x8 slice. The times are simulated.
512 devices in a mesh: wide: 64 (over y_hi, z, x), narrow: 8 (over y_lo, core).
Axes of the slice: x: 4, y: 8 (y_hi: 2, y_lo: 4; y = y_hi * 4 + y_lo), z: 8, core: 2. Of those that a mesh axis runs over, the one named last changes fastest.
Arguments:
- hidden_in: bfloat16 [16384, 2048], P('wide', 'narrow'), may hold values from -32 to 32
- attn_gain: bfloat16 [2048], P('narrow'), may hold values from 0.099609375 to 1.8984375
- qkv_weight: bfloat16 [2048, 1920], P('narrow', 'wide'), may hold values from -0.125 to 0.125
- q_gain: bfloat16 [64], replicated, may hold values from 1 to 2
- k_gain: bfloat16 [64], replicated, may hold values from 1 to 2
- out_weight: bfloat16 [1280, 2048], P('wide', 'narrow'), may hold values from -0.3125 to 0.3125
- lengths: int32 [4], replicated, may hold values from 1 to 8192, 16384 in all
- page_table: int32 [256], P('wide'), may hold values from 0 to 3, as said below
Outputs:
- hidden_out: bfloat16 [16384, 2048], P('wide', 'narrow')
- kv_cache: bfloat16 [256, 64, 640], P('wide', 'narrow')
Inputs may be any that keep to these rules, and one draw needn't show every extreme that they name: `lengths`: the 4 prompts sum to 16384 tokens and the longest has exactly 8192. `page_table`: each aligned block of 4 entries holds each slot once.
All inputs are finite; a program needn't handle non-finite values.
Results may differ from a plain program's by a relative error of at most 0.0033.
The roundings to bfloat16 on the way count: a program that leaves them out, or rounds other values in their place, can miss the bound.
Values may be sent and summed in bfloat16 or wider, within the bound.
No kernel may reach another device: no remote copies, remote signals or barrier semaphores. Data moves between devices by JAX's collectives and lax.ppermute only.
A program may use at most 128 MiB of HBM per device.

v0:
```python
import math

import jax
import jax.numpy as jnp
from jax import lax
from jax.sharding import PartitionSpec as P

D = 2048
HEADS = 20
KV_HEADS = 5
HEAD = 64
PAGE = 64
GROUP = 4
Q_DIM = 1280
KV_DIM = 640


rope_base = 10000.0


def token_place(token_ids, lengths):
    prompt_ends = jnp.cumsum(lengths)
    prompt_starts = prompt_ends - lengths
    segment = jnp.sum((token_ids[:, None] >= prompt_ends[None, :]).astype(jnp.int32), axis=1)
    matches = segment[:, None] == jnp.arange(lengths.shape[0], dtype=jnp.int32)[None, :]
    position = token_ids - jnp.sum(jnp.where(matches, prompt_starts[None, :], 0), axis=1)
    return (segment, position)


def rotate(projected_part, head_count, head_gain, position):
    row_count = projected_part.shape[0]
    per_head = projected_part.reshape(row_count, head_count, HEAD)
    per_head = per_head * lax.rsqrt(jnp.mean(per_head * per_head, axis=-1, keepdims=True) + 1e-06)
    per_head = per_head * head_gain.astype(jnp.float32)
    halfway = HEAD // 2
    frequency = jnp.exp(
        jnp.arange(halfway, dtype=jnp.float32) * (-2.0 * math.log(rope_base) / HEAD)
    )
    angles = position.astype(jnp.float32)[:, None] * frequency[None, :]
    cosine_table = jnp.cos(angles)[:, None, :]
    sine_table = jnp.sin(angles)[:, None, :]
    lower_half = per_head[..., :halfway]
    upper_half = per_head[..., halfway:]
    rotated = jnp.concatenate(
        [
            lower_half * cosine_table - upper_half * sine_table,
            upper_half * cosine_table + lower_half * sine_table,
        ],
        axis=-1,
    )
    return rotated.reshape(row_count, head_count * HEAD)


def on_device(hidden_in, attn_gain, qkv_weight, q_gain, k_gain, out_weight, lengths, page_table):
    tokens_dev = hidden_in.shape[0]
    narrow_count = lax.axis_size("narrow")
    narrow_index = lax.axis_index("narrow")
    wide_index = lax.axis_index("wide")
    rows_page = PAGE // narrow_count
    pages_dev = tokens_dev // PAGE
    slice_rows = pages_dev * rows_page
    key_width = KV_DIM // 2
    scale = HEAD ** (-0.5)
    input_values = hidden_in.astype(jnp.float32)
    scaled = (input_values * attn_gain.astype(jnp.float32)[None, :]).astype(jnp.bfloat16)
    square_part = jnp.sum(input_values * input_values, axis=1)
    partial_sums = jnp.dot(
        scaled,
        lax.all_gather(qkv_weight, "wide", axis=1, tiled=True),
        preferred_element_type=jnp.float32,
    )
    first_token = wide_index * tokens_dev
    all_tokens = first_token + jnp.arange(tokens_dev, dtype=jnp.int32)
    own_tokens = (
        first_token
        + jnp.arange(pages_dev, dtype=jnp.int32)[:, None] * PAGE
        + narrow_index * rows_page
        + jnp.arange(rows_page, dtype=jnp.int32)[None, :]
    ).reshape(-1)
    segment_all, position_all = token_place(all_tokens, lengths)
    segment_own, position_own = token_place(own_tokens, lengths)
    summed, squares = lax.psum((partial_sums, square_part), "narrow")
    inverse_norm = lax.rsqrt(squares / D + 1e-06)
    projected = summed * inverse_norm[:, None]
    queries = rotate(projected[:, :Q_DIM], HEADS, q_gain, position_all).astype(jnp.bfloat16)
    own_rows = lax.dynamic_index_in_dim(
        projected[:, Q_DIM:].reshape(pages_dev, narrow_count, rows_page, KV_DIM),
        narrow_index,
        1,
        keepdims=False,
    ).reshape(slice_rows, KV_DIM)
    keys_own = rotate(own_rows[:, :key_width], KV_HEADS, k_gain, position_own).astype(jnp.bfloat16)
    values_own = own_rows[:, key_width:].astype(jnp.bfloat16)
    cache_rows = jnp.concatenate([keys_own, values_own], axis=1).reshape(
        pages_dev, rows_page, KV_DIM
    )
    paged_cache = jnp.zeros_like(cache_rows).at[page_table].set(cache_rows)
    query_groups = queries.reshape(tokens_dev, KV_HEADS, GROUP, HEAD)
    key_block = lax.all_gather(keys_own, "wide", axis=0, tiled=True)
    value_block = lax.all_gather(values_own, "wide", axis=0, tiled=True)
    key_count = key_block.shape[0]
    row_index = jnp.arange(key_count, dtype=jnp.int32)
    shard_index = row_index // slice_rows
    inner_index = row_index % slice_rows
    key_tokens = (
        shard_index * tokens_dev
        + inner_index // rows_page * PAGE
        + narrow_index * rows_page
        + inner_index % rows_page
    )
    key_segment, unused = token_place(key_tokens, lengths)
    visible = (key_segment[None, :] == segment_all[:, None]) & (
        key_tokens[None, :] <= all_tokens[:, None]
    )
    scores = (
        jnp.einsum(
            "tkgd,nkd->tkgn",
            query_groups,
            key_block.reshape(key_count, KV_HEADS, HEAD),
            preferred_element_type=jnp.float32,
        )
        * scale
    )
    weights = jnp.where(visible[:, None, None, :], jnp.exp(scores), 0.0)
    numerator = jnp.einsum(
        "tkgn,nkd->tkgd",
        weights.astype(jnp.bfloat16),
        value_block.reshape(key_count, KV_HEADS, HEAD),
        preferred_element_type=jnp.float32,
    )
    denominator = jnp.sum(weights, axis=-1)
    numerator, denominator = (numerator, denominator)
    numerator, denominator = lax.psum((numerator, denominator), "narrow")
    attended = (numerator / denominator[..., None]).reshape(tokens_dev, Q_DIM).astype(jnp.bfloat16)
    mixed_rows = jnp.dot(
        attended,
        lax.all_gather(out_weight, "wide", axis=0, tiled=True),
        preferred_element_type=jnp.float32,
    )
    hidden_out = (input_values + mixed_rows).astype(jnp.bfloat16)
    return (hidden_out, paged_cache)


def solution(mesh):
    return jax.shard_map(
        on_device,
        mesh=mesh,
        in_specs=(
            P("wide", "narrow"),
            P("narrow"),
            P("narrow", "wide"),
            P(),
            P(),
            P("wide", "narrow"),
            P(),
            P("wide"),
        ),
        out_specs=(P("wide", "narrow"), P("wide", "narrow", None)),
        check_vma=False,
    )
```

profile of v0, /device:TPU:1, one launch (start us, length us, event | category | flops | bytes accessed | tf_op | source)
XLA Modules:
  0.0 859.5 jit_solution(7487213716153726544)
XLA Ops:
  7.2 208.8 %all-gather = bf16[64,30,256]{2,1,0:T(8,128)(2,1)S(1)} all-gather(bf16[1,30,256]{2,1,0:T(8,128)(2,1)} %bitcast.51), channel_id=1, replica_groups=mesh['wide'=64,'narrow'=8] {'wide'}, dimensions={0}, use_global_device_ids=true | all-gather | bytes 998400 | tf_op jit(solution)/shard_map/all_gather | solution.py:69
  216.0 0.3 reshape.393
  216.3 1.8 fusion.11
  218.2 0.6 copy-done.8
  218.9 0.2 reduce-window.8
  219.1 0.1 fusion.10
  219.2 41.6 %psum.29 = f32[256]{0:T(256)S(1)} all-reduce(f32[256]{0:T(256)S(1)} %fusion.10), channel_id=1, replica_groups=mesh['wide'=64,'narrow'=8] {'narrow'}, use_global_device_ids=true, to_apply=%region_2.3 | all-reduce | flops 256 | bytes 2048 | tf_op jit(solution)/shard_map/psum | solution.py:82
  261.0 0.1 multiply_cosine_fusion.1
  261.1 55.8 %all-reduce.3.cloned.1.call-done = f32[256,1920]{1,0:T(8,128)} async-done(((f32[256,1920]{1,0:T(8,128)}), f32[256,1920]{1,0:T(8,128)}) %all-reduce.3.cloned.1.call-update) | async-done | bytes 1966096 | tf_op jit(solution)/shard_map/psum | solution.py:82
  316.9 1.7 broadcast_multiply_fusion
  319.1 0.1 subtract_convert_fusion.1
  319.3 0.7 convert_element_type.68
  320.1 0.5 convert_element_type.69
  320.9 0.2 multiply_cosine_fusion
  321.1 2.3 compare_and_fusion
  323.5 0.7 slice.50
  324.2 0.4 copy.31
  324.6 0.1 multiply_reduce_fusion
  324.8 0.3 multiply_multiply_fusion
  325.1 0.2 subtract_convert_fusion
  325.4 124.1 %all-gather.7.cloned.1.call-done = bf16[2048,320]{1,0:T(8,128)(2,1)} async-done(((bf16[32,320]{1,0:T(8,128)(2,1)}), bf16[2048,320]{1,0:T(8,128)(2,1)}) %all-gather.7.cloned.1.call-update) | async-done | bytes 1310736 | tf_op jit(solution)/shard_map/all_gather | solution.py:99
  449.5 1.7 copy.30
  451.2 15.7 %fusion = (f32[256,5,4]{0,2,1:T(4,128)S(1)}, f32[5,2048,256,4]{2,1,3,0:T(8,128)}) fusion(pred[256,2048]{0,1:T(8,128)(4,1)S(1)} %copy-done.1, bf16[2048,5,64,1]{0,2,3,1:T(8,128)(2,1)S(1)} %bitcast.46, bf16[256,5,4,64]{0,3,2,1:T(8,128)(2,1)S(1)} %bitcast.49), kind=kOutput, calls=%fused_computation.2 | convolution fusion | flops 1373629440 | bytes 44453888 | tf_op jit(solution)/shard_map/tkgd,nkd->tkgn/dot_general | solution.py:116
  466.9 114.4 %all-gather.5.cloned.1.call-done = bf16[2048,320]{1,0:T(8,128)(2,1)} async-done(((bf16[32,320]{1,0:T(8,128)(2,1)}), bf16[2048,320]{1,0:T(8,128)(2,1)}) %all-gather.5.cloned.1.call-update) | async-done | bytes 1310736 | tf_op jit(solution)/shard_map/all_gather | solution.py:100
  581.2 1.7 copy.29
  582.9 17.4 %fusion.5 = f32[256,5,4,64]{0,3,2,1:T(8,128)} fusion(bf16[2048,5,64,1]{0,2,3,1:T(8,128)(2,1)S(1)} %bitcast.47, f32[5,2048,256,4]{2,1,3,0:T(8,128)} %get-tuple-element.11, pred[256,2048]{0,1:T(8,128)(4,1)S(1)} %copy-done.1), kind=kOutput, calls=%fused_computation.7 | convolution fusion | flops 1373634560 | bytes 45088768 | tf_op jit(solution)/shard_map/tkgn,nkd->tkgd/dot_general | solution.py:125
  600.4 193.2 %all-gather.1 = bf16[64,20,256]{2,1,0:T(8,128)(2,1)S(1)} all-gather(bf16[1,20,256]{2,1,0:T(8,128)(2,1)S(1)} %bitcast.52), channel_id=1, replica_groups=mesh['wide'=64,'narrow'=8] {'wide'}, dimensions={0}, use_global_device_ids=true | all-gather | bytes 665600 | tf_op jit(solution)/shard_map/all_gather | solution.py:137
  793.6 0.1 reshape.395
  793.9 0.6 scatter_fusion
  794.6 55.9 %psum.31 = f32[256,5,4]{0,2,1:T(4,128)S(1)} all-reduce(f32[256,5,4]{0,2,1:T(4,128)S(1)} %get-tuple-element.10), channel_id=1, replica_groups=mesh['wide'=64,'narrow'=8] {'narrow'}, use_global_device_ids=true, to_apply=%region_13.14 | all-reduce | flops 5120 | bytes 40960 | tf_op jit(solution)/shard_map/psum | solution.py:133
  850.5 1.5 divide_convert_fusion
  852.0 1.0 fusion.8
  (63 shorter events, 1.6 us)
Async XLA Ops:
  7.2 209.1 %copy-start.7 = (bf16[256]{0:T(256)(128)(2,1)S(1)}, bf16[256]{0:T(256)(128)(2,1)}, u32[]{:S(2)}) copy-start(bf16[256]{0:T(256)(128)(2,1)} %param.9) | copy-start | bytes 1540
  7.2 209.1 %copy-start = (bf16[256,256]{1,0:T(8,128)(2,1)S(1)}, bf16[256,256]{1,0:T(8,128)(2,1)}, u32[]{:S(2)}) copy-start(bf16[256,256]{1,0:T(8,128)(2,1)} %param.8) | copy-start | bytes 393220
  7.2 309.7 %all-reduce.3.cloned.1.call-start = ((), (), s32[]{:S(2)}) async-start(), calls=%async_computation | async-start | bytes 3932160 | tf_op jit(solution)/shard_map/psum | solution.py:82
  218.1 0.7 copy-start.8
  218.1 0.8 copy-start.9
  218.1 231.4 %all-gather.7.cloned.1.call-start = ((), (), s32[]{:S(2)}) async-start(), calls=%async_computation.2 | async-start | bytes 1597440 | tf_op jit(solution)/shard_map/all_gather | solution.py:99
  318.7 1.4 copy-start.10
  320.0 261.2 %all-gather.5.cloned.1.call-start = ((), (), s32[]{:S(2)}) async-start(), calls=%async_computation.1 | async-start | bytes 1597440 | tf_op jit(solution)/shard_map/all_gather | solution.py:100
  324.2 0.6 copy-start.6
  324.7 525.8 %all-reduce.5.cloned.1.call-start = ((), (), s32[]{:S(2)}) async-start(), calls=%async_computation.3 | async-start | bytes 2621440 | tf_op jit(solution)/shard_map/psum | solution.py:133
  325.4 125.8 %copy-start.1 = (pred[256,2048]{0,1:T(8,128)(4,1)S(1)}, pred[256,2048]{0,1:T(8,128)(4,1)}, u32[]{:S(2)}) copy-start(pred[256,2048]{0,1:T(8,128)(4,1)} %compare_and_fusion) | copy-start | bytes 1572868
  582.9 17.5 %copy-start.5 = (bf16[20,256]{1,0:T(8,128)(2,1)S(1)}, bf16[20,256]{1,0:T(8,128)(2,1)}, u32[]{:S(2)}) copy-start(bf16[20,256]{1,0:T(8,128)(2,1)} %param.13) | copy-start | bytes 30724
  600.4 193.4 %copy-start.11 = (s32[4]{0:T(128)S(1)}, s32[4]{0:T(128)}, u32[]{:S(2)}) copy-start(s32[4]{0:T(128)} %param.15) | copy-start | bytes 52
  600.4 193.4 %copy-start.2 = (bf16[32,320]{1,0:T(8,128)(2,1)S(1)}, bf16[32,320]{1,0:T(8,128)(2,1)}, u32[]{:S(2)}) copy-start(bf16[32,320]{1,0:T(8,128)(2,1)} %slice.50) | copy-start | bytes 61444
  600.4 193.4 %copy-start.3 = (bf16[32,320]{1,0:T(8,128)(2,1)S(1)}, bf16[32,320]{1,0:T(8,128)(2,1)}, u32[]{:S(2)}) copy-start(bf16[32,320]{1,0:T(8,128)(2,1)} %convert_element_type.68) | copy-start | bytes 61444
  794.6 58.4 %copy-start.4 = (bf16[4,8,640]{2,1,0:T(8,128)(2,1)}, bf16[4,8,640]{2,1,0:T(8,128)(2,1)S(1)}, u32[]{:S(2)}) copy-start(bf16[4,8,640]{2,1,0:T(8,128)(2,1)S(1)} %scatter_fusion) | copy-start | bytes 122884
Sparse Core Ops, SparseCore 0:
  218.2 98.6 all-reduce.2
  322.8 126.6 all-gather.6
  455.4 125.7 all-gather.4
  600.5 80.4 all-reduce.4
where the time goes:
time: 861 us; the launch traced here: 860 us
  blocking collectives  500 us (58%)
  waiting for transfers between devices  294 us (34%)
  matrix products  35.9 us (4%)
  between operations  14.1 us (2%)
    all_gather x1, blocking collectives, on_device(): lax.all_gather(qkv_weight, 'wide', axis=1, tiled=True)  209 us
    all_gather x1, blocking collectives, on_device(): lax.all_gather(out_weight, 'wide', axis=0, tiled=True)  193 us
    all_gather x1, waiting for transfers between devices, on_device(): key_block = lax.all_gather(keys_own, 'wide', axis=0, tiled=True)  124 us
    all_gather x1, waiting for transfers between devices, on_device(): value_block = lax.all_gather(values_own, 'wide', axis=0, tiled=True)  114 us
    psum x1, blocking collectives, on_device(): numerator, denominator = lax.psum((numerator, denominator), 'narrow')  55.9 us
    psum x1, waiting for transfers between devices, on_device(): summed, squares = lax.psum((partial_sums, square_part), 'narrow')  55.8 us
    psum x1, blocking collectives, on_device(): summed, squares = lax.psum((partial_sums, square_part), 'narrow')  41.6 us
    dot_general x1, matrix products, on_device(): jnp.einsum('tkgn,nkd->tkgd', weights.astype(jnp.bfloat16), value_block.re...  17.4 us
  transfers between devices with their start and end apart: 4, of which 3 were waited for; matrix products, arithmetic and copies ran while one was open for 3% of the time, Pallas kernels for 0%

commit v1 on v0

v1 whole, which is shorter than its diff:
```python
import functools
import math

import jax
import jax.numpy as jnp
from jax import lax
from jax.experimental import pallas as pl
from jax.experimental.pallas import tpu as pltpu
from jax.sharding import Mesh, PartitionSpec as P

D = 2048
HEADS = 20
KV_HEADS = 5
HEAD = 64
GROUP = 4
Q_DIM = 1280
KV_DIM = 640
QKV_DIM = 1920
TOK_DEV = 256
PAGE = 64
PAGES_DEV = 4
ROWS = 32
ROPE_BASE = 10000.0
SUMS = Q_DIM + 128
BF = jnp.bfloat16
F32 = jnp.float32
HIDDEN_BIAS = -1e30
EXP2_SCALE = HEAD ** (-0.5) * math.log2(math.e)

VM = pl.BlockSpec(memory_space=pltpu.VMEM)
SM = pl.BlockSpec(memory_space=pltpu.SMEM)


def call(body, out_shape, in_specs, name, scratch=()):
    many = isinstance(out_shape, tuple)
    return pl.pallas_call(
        body,
        out_shape=out_shape,
        in_specs=in_specs,
        out_specs=(VM,) * len(out_shape) if many else VM,
        scratch_shapes=list(scratch),
        compiler_params=pltpu.CompilerParams(vmem_limit_bytes=48 << 20),
        name=name,
    )


def project_body(flip, place, hidden, gain, weight, out):
    core = place[3] if not flip else 1 - place[3]
    rows = [hidden[p, yl, core].astype(F32) for yl in range(4) for p in range(PAGES_DEV)]
    values = jnp.concatenate(rows, axis=0)
    scaled = (values * gain[...].astype(F32)).astype(BF)
    out[:, :QKV_DIM] = lax.dot_general(
        scaled, weight[...], (((1,), (1,)), ((), ())), preferred_element_type=F32
    )
    squares = jnp.sum(values * values, axis=1, keepdims=True)
    out[:, QKV_DIM:] = jnp.broadcast_to(squares, (128, 128))


def rotate_body(table, parts, cosine, sine, q_gain, k_gain, queries, kv, cache):
    lane = lax.broadcasted_iota(jnp.int32, (ROWS, 128), 1)
    upper_head = lane >= HEAD
    lower_part = (lane % HEAD) < HEAD // 2

    def total(tile):
        at = pl.ds(tile * 128, 128)
        return (parts[0, :, at] + parts[1, :, at]) + (parts[2, :, at] + parts[3, :, at])

    inverse = lax.rsqrt(total(15) / D + 1e-06)
    cos = cosine[...]
    sin = jnp.where(lower_part, -sine[...], sine[...])

    def turned(u, gain):
        square = u * u
        both = jnp.sum(jnp.where(upper_head, 0.0, square), axis=1, keepdims=True)
        other = jnp.sum(jnp.where(upper_head, square, 0.0), axis=1, keepdims=True)
        mean = jnp.where(upper_head, other, both) * (1.0 / HEAD)
        w = u * lax.rsqrt(mean + 1e-06) * gain
        partner = jnp.where(lower_part, pltpu.roll(w, 96, 1), pltpu.roll(w, 32, 1))
        return w * cos + partner * sin

    for tile in range(10):
        u = total(tile) * inverse
        queries[:, tile * 128 : tile * 128 + 128] = turned(u, q_gain[...]).astype(BF)
    for tile in range(10, 15):
        u = total(tile) * inverse
        if tile == 12:
            u = jnp.where(upper_head, u, turned(u, k_gain[...]))
        elif tile < 12:
            u = turned(u, k_gain[...])
        kv[:, (tile - 10) * 128 : (tile - 9) * 128] = u.astype(BF)
    for p in range(PAGES_DEV):
        cache[pl.ds(table[p], 1)] = kv[p * 8 : p * 8 + 8, :].reshape(1, 8, KV_DIM)


def attend_body(flip, place, lengths, q, blocks, far, out, bias, bias_far):
    yh, index, wide, narrow = place[0], place[1], place[2], place[4]
    core = place[3] if not flip else 1 - place[3]
    row = lax.broadcasted_iota(jnp.int32, (128, 1), 0)
    token = (
        wide * TOK_DEV
        + (row % ROWS) // 8 * PAGE
        + row // ROWS * 16
        + core * 8
        + row % 8
    )
    begin = jnp.zeros_like(token)
    end = jnp.int32(0)
    for s in range(3):
        end = end + lengths[s]
        begin = jnp.where(token >= end, end, begin)

    def hide(first_block, lanes, fixed):
        lane = lax.broadcasted_iota(jnp.int32, (1, lanes), 1)
        block = first_block + lane // ROWS
        if fixed:
            source = (1 - yh) * 32 + block
        else:
            source = jnp.where(block <= index, yh, 1 - yh) * 32 + block
        key = source * TOK_DEV + (lane % ROWS) // 8 * PAGE + narrow * 8 + lane % 8
        return jnp.where((key <= token) & (key >= begin), 0.0, HIDDEN_BIAS)

    for chunk in range(4):
        bias[chunk] = hide(chunk * 8, 256, False)
    bias_far[...] = hide(index, ROWS, True)
    half = [q[2 * yl + core] for yl in range(4)]
    half = jnp.concatenate(half, axis=0)
    out[:, Q_DIM:] = jnp.zeros((128, 128), F32)
    for g in range(KV_HEADS):
        heads = [
            half[:, (g * GROUP + h) * HEAD : (g * GROUP + h + 1) * HEAD] for h in range(GROUP)
        ]
        stacked = jnp.concatenate(heads, axis=0)
        denominator = None
        numerator = None
        tail = None
        for chunk in range(5):
            if chunk < 4:
                keys = blocks[chunk * 8 : chunk * 8 + 8, :, g * HEAD : (g + 1) * HEAD]
                keys = keys.reshape(256, HEAD)
                values = blocks[chunk * 8 : chunk * 8 + 8, :, 320 + g * HEAD : 320 + (g + 1) * HEAD]
                values = values.reshape(256, HEAD)
                shade = bias[chunk]
            else:
                keys = far[:, g * HEAD : (g + 1) * HEAD]
                values = far[:, 320 + g * HEAD : 320 + (g + 1) * HEAD]
                shade = bias_far[...]
            scores = lax.dot_general(
                stacked, keys, (((1,), (1,)), ((), ())), preferred_element_type=F32
            )
            wide_scores = scores.reshape(GROUP, 128, keys.shape[0]) * EXP2_SCALE + shade[None]
            weight = jnp.exp2(wide_scores).reshape(GROUP * 128, keys.shape[0])
            product = jnp.dot(weight.astype(BF), values, preferred_element_type=F32)
            numerator = product if numerator is None else numerator + product
            if chunk < 4:
                folded = weight[:, :128] + weight[:, 128:]
                denominator = folded if denominator is None else denominator + folded
            else:
                tail = jnp.sum(weight, axis=1, keepdims=True)
        denominator = jnp.sum(denominator, axis=1, keepdims=True) + tail
        for h in range(GROUP):
            head = g * GROUP + h
            out[:, head * HEAD : (head + 1) * HEAD] = numerator[h * 128 : (h + 1) * 128]
            out[:, Q_DIM + head : Q_DIM + head + 1] = denominator[h * 128 : (h + 1) * 128]


def divide_body(parts, out):
    upper_head = lax.broadcasted_iota(jnp.int32, (ROWS, 128), 1) >= HEAD

    def total(tile):
        at = pl.ds(tile * 128, 128)
        return (parts[0, :, at] + parts[1, :, at]) + (parts[2, :, at] + parts[3, :, at])

    under = total(10)
    for tile in range(10):
        low, high = under[:, 2 * tile : 2 * tile + 1], under[:, 2 * tile + 1 : 2 * tile + 2]
        out[:, tile * 128 : tile * 128 + 128] = (
            total(tile) / jnp.where(upper_head, high, low)
        ).astype(BF)


def mix_body(attended, weight, hidden, out):
    mixed = jnp.dot(attended[...], weight[...], preferred_element_type=F32)
    for n in range(8):
        for p in range(PAGES_DEV):
            at = (n * PAGES_DEV + p) * 8
            out[p, n] = (hidden[p, n].astype(F32) + mixed[at : at + 8]).astype(BF)


def spread(x, axes, count):
    return lax.all_to_all(jnp.broadcast_to(x[None], (count,) + x.shape), axes, 0, 0)


def on_device(hidden_in, attn_gain, qkv_weight, q_gain, k_gain, out_weight, lengths, page_table):
    yh, z, x = lax.axis_index("yh"), lax.axis_index("z"), lax.axis_index("x")
    yl, core = lax.axis_index("yl"), lax.axis_index("c")
    index = z * 4 + x
    wide = yh * 32 + index
    narrow = yl * 2 + core
    place = jnp.stack([yh, index, wide, core, narrow]).astype(jnp.int32)
    swap = [(0, 1), (1, 0)]
    wide_axes = ("yh", "z", "x")

    weight = spread(qkv_weight.T, wide_axes, 64).reshape(QKV_DIM, TOK_DEV)
    hidden5 = hidden_in.reshape(PAGES_DEV, 4, 2, 8, 256)
    gain = attn_gain.reshape(1, 256)
    half_shape = jax.ShapeDtypeStruct((128, 2048), F32)

    def project(flip):
        return call(
            functools.partial(project_body, flip), half_shape, [SM, VM, VM, VM], f"project{flip}"
        )(place, hidden5, gain, weight)

    sent = project(1)
    arrived = lax.ppermute(sent, "c", swap)
    partial = (project(0) + arrived).reshape(4, ROWS, 2048)
    out_part, partial = lax.optimization_barrier((out_weight, partial))
    parts = lax.all_to_all(partial, "yl", 0, 0)

    row = jnp.arange(ROWS, dtype=jnp.int32)
    own = wide * TOK_DEV + row // 8 * PAGE + narrow * 8 + row % 8
    ends = jnp.cumsum(lengths)
    begin = jnp.max(jnp.where(own[:, None] >= ends[None, :], ends[None, :], 0), axis=1)
    position = own - begin
    half = HEAD // 2
    frequency = jnp.exp(jnp.arange(half, dtype=F32) * (-2.0 * math.log(ROPE_BASE) / HEAD))
    angles = position.astype(F32)[:, None] * jnp.tile(frequency, 4)[None, :]
    queries, kv, cache = call(
        rotate_body,
        (
            jax.ShapeDtypeStruct((ROWS, Q_DIM), BF),
            jax.ShapeDtypeStruct((ROWS, KV_DIM), BF),
            jax.ShapeDtypeStruct((PAGES_DEV, 8, KV_DIM), BF),
        ),
        [SM] + [VM] * 5,
        "rotate",
    )(
        page_table,
        parts,
        jnp.cos(angles),
        jnp.sin(angles),
        jnp.tile(q_gain.astype(F32), 2)[None, :],
        jnp.tile(k_gain.astype(F32), 2)[None, :],
    )

    far = lax.ppermute(kv, "yh", swap)
    all_queries = lax.all_gather(queries, ("yl", "c"), axis=0, tiled=False)
    target = jnp.arange(32, dtype=jnp.int32)[:, None, None]
    blocks = lax.all_to_all(jnp.where(target >= index, kv[None], far[None]), ("z", "x"), 0, 0)

    def attend(flip):
        return call(
            functools.partial(attend_body, flip),
            jax.ShapeDtypeStruct((128, SUMS), F32),
            [SM, SM, VM, VM, VM],
            f"attend{flip}",
            [pltpu.VMEM((4, 128, 256), F32), pltpu.VMEM((128, ROWS), F32)],
        )(place, lengths, all_queries, blocks, far)

    sent = attend(1)
    arrived = lax.ppermute(sent, "c", swap)
    sums = (attend(0) + arrived).reshape(4, ROWS, SUMS)
    parts = lax.all_to_all(sums, "yl", 0, 0)
    attended = call(divide_body, jax.ShapeDtypeStruct((ROWS, Q_DIM), BF), [VM], "divide")(parts)
    attended = lax.all_gather(attended, ("yl", "c"), axis=0, tiled=True)
    mixing = spread(out_part, wide_axes, 64).reshape(Q_DIM, 256)
    hidden_out = call(
        mix_body, jax.ShapeDtypeStruct((PAGES_DEV, 8, 8, 256), BF), [VM] * 3, "mix"
    )(attended, mixing, hidden_in.reshape(PAGES_DEV, 8, 8, 256))
    return (hidden_out.reshape(TOK_DEV, 256), cache)


def solution(mesh):
    fine = Mesh(mesh.devices.reshape(2, 8, 4, 4, 2), ("yh", "z", "x", "yl", "c"))
    rows, columns = ("yh", "z", "x"), ("yl", "c")
    return jax.shard_map(
        on_device,
        mesh=fine,
        in_specs=(
            P(rows, columns),
            P(columns),
            P(columns, rows),
            P(),
            P(),
            P(rows, columns),
            P(),
            P(rows),
        ),
        out_specs=(P(rows, columns), P(rows, columns, None)),
        check_vma=False,
    )
```

time: 861 us -> 230 us (0.27)
  blocking collectives: 500 us -> 84.2 us
  waiting for transfers between devices: 294 us -> 74.1 us
  starting transfers between devices: 0.16 us -> 49.6 us
  matrix products: 35.9 us -> 0 us
  Pallas kernels: 0 us -> 14.2 us
  between operations: 14.1 us -> 0.84 us
    all_gather x2, blocking collectives: 402 us -> 46.7 us  [the longest x1 30.2 us: on_device(): all_queries = lax.all_gather(queries, ('yl', 'c'), axis=0, tiled=False)]
    all_gather x2 -> x0, waiting for transfers between devices: 239 us -> none  [the longest x1 124 us: on_device(): key_block = lax.all_gather(keys_own, 'wide', axis=0, tiled=True)]
    psum x2 -> x0, blocking collectives: 97.5 us -> none  [the longest x1 55.9 us: on_device(): numerator, denominator = lax.psum((numerator, denominator), 'narrow')]
    all_to_all x0 -> x4, waiting for transfers between devices: none -> 67 us  [the longest x1 24.6 us: on_device(): parts = lax.all_to_all(partial, 'yl', 0, 0)]
    psum x2 -> x0, waiting for transfers between devices: 55.8 us -> none  [the longest x1 55.8 us: on_device(): summed, squares = lax.psum((partial_sums, square_part), 'narrow')]
    all_to_all x0 -> x4, starting transfers between devices: none -> 38.5 us  [the longest x2 27.1 us: spread(): lax.all_to_all(jnp.broadcast_to(x[None], (count,) + x.shape), axes, 0, 0)]
    all_to_all x0 -> x1, blocking collectives: none -> 37.4 us  [on_device(): lax.all_to_all(jnp.where(target >= index, kv[None], far[None]), ('z', 'x'...]
    dot_general x4 -> x0, matrix products: 35.9 us -> none  [the longest x1 17.4 us: on_device(): jnp.einsum('tkgn,nkd->tkgd', weights.astype(jnp.bfloat16), value_block.re...]
  transfers between devices with their start and end apart: 4 -> 7, of which waited for: 3 -> 5; matrix products, arithmetic and copies ran while one was open for 3% -> 1% of each run, Pallas kernels for 0% -> 4%
where the time goes in v1:
time: 230 us; the launch traced here: 229 us
  blocking collectives  84.2 us (37%)
  waiting for transfers between devices  74.1 us (32%)
  starting transfers between devices  49.6 us (22%)
  Pallas kernels  14.2 us (6%)
  local copies, waits for them, and re-layouts  3.57 us (2%)
  other arithmetic  2.7 us (1%)
    all_to_all x1, blocking collectives, on_device(): lax.all_to_all(jnp.where(target >= index, kv[None], far[None]), ('z', 'x'...  37.4 us
    all_gather x1, blocking collectives, on_device(): all_queries = lax.all_gather(queries, ('yl', 'c'), axis=0, tiled=False)  30.2 us
    all_to_all x2, starting transfers between devices, spread(): lax.all_to_all(jnp.broadcast_to(x[None], (count,) + x.shape), axes, 0, 0)  27.1 us
    all_to_all x1, waiting for transfers between devices, on_device(): parts = lax.all_to_all(partial, 'yl', 0, 0)  24.6 us
    all_to_all x2, waiting for transfers between devices, spread(): lax.all_to_all(jnp.broadcast_to(x[None], (count,) + x.shape), axes, 0, 0)  24.3 us
    all_to_all x1, waiting for transfers between devices, on_device(): parts = lax.all_to_all(sums, 'yl', 0, 0)  18.1 us
    all_gather x1, blocking collectives, on_device(): attended = lax.all_gather(attended, ('yl', 'c'), axis=0, tiled=True)  16.5 us
    pallas_call x2, Pallas kernels, attend(): call(functools.partial(attend_body, flip), jax.ShapeDtypeStruct((128, SUM...  8.72 us
  transfers between devices with their start and end apart: 7, of which 5 were waited for; matrix products, arithmetic and copies ran while one was open for 1% of the time, Pallas kernels for 4%

profile of v1, /device:TPU:1, one launch (start us, length us, event | category | flops | bytes accessed | tf_op | source)
XLA Modules:
  0.0 229.2 jit_solution(8753099834281581287)
XLA Ops:
  0.6 1.8 broadcast_in_dim.38
  2.5 19.7 %all-to-all-start = ((bf16[64,30,256]{2,1,0:T(8,128)(2,1)}), bf16[64,30,256]{2,1,0:T(8,128)(2,1)S(1)}, u32[]{:S(2)}, u32[]{:S(2)}) async-start(bf16[64,30,256]{2,1,0:T(8,128)(2,1)} %broadcast_in_dim.38), calls=%async_computation | async-start | bytes 2097152 | tf_op jit(solution)/shard_map/all_to_all | solution.py:190
  22.3 24.3 %all-to-all-done = bf16[64,30,256]{2,1,0:T(8,128)(2,1)S(1)} async-done(((bf16[64,30,256]{2,1,0:T(8,128)(2,1)}), bf16[64,30,256]{2,1,0:T(8,128)(2,1)S(1)}, u32[]{:S(2)}, u32[]{:S(2)}) %all-to-all-start) | async-done | bytes 983072 | tf_op jit(solution)/shard_map/all_to_all | solution.py:190
  46.7 0.3 reshape.101.weight
  46.9 1.0 project1.1
  48.0 6.1 %collective-permute-start = (f32[128,2048]{1,0:T(8,128)S(1)}, f32[128,2048]{1,0:T(8,128)S(1)}, u32[]{:S(2)}, u32[]{:S(2)}) collective-permute-start(f32[128,2048]{1,0:T(8,128)S(1)} %project1.1), channel_id=1, source_target_pairs={{0,1},{1,0},{2,3},{3,2},{4,5},{5,4},{6,7},{7,6},{8,9},{9,8},{10,11... | collective-permute-start | bytes 3145736 | tf_op jit(solution)/shard_map/ppermute | solution.py:214
  54.1 1.0 project0.1
  55.1 1.3 collective-permute-done
  56.3 1.1 add.75
  57.4 7.9 %all-to-all-start.1 = ((f32[4,32,2048]{2,1,0:T(8,128)}), f32[4,32,2048]{2,1,0:T(8,128)S(1)}, u32[]{:S(2)}, u32[]{:S(2)}) async-start(f32[4,32,2048]{2,1,0:T(8,128)} %bitcast.7), calls=%async_computation.1 | async-start | bytes 2097152 | tf_op jit(solution)/shard_map/all_to_all | solution.py:217
  65.6 0.2 reduce-window.8
  65.8 0.1 select_reduce_fusion
  65.9 0.1 multiply_sine_fusion
  66.1 24.6 %all-to-all-done.1.parts = f32[4,32,2048]{2,1,0:T(8,128)S(1)} async-done(((f32[4,32,2048]{2,1,0:T(8,128)}), f32[4,32,2048]{2,1,0:T(8,128)S(1)}, u32[]{:S(2)}, u32[]{:S(2)}) %all-to-all-start.1) | async-done | bytes 1048608 | tf_op jit(solution)/shard_map/all_to_all | solution.py:217
  90.6 2.3 %rotate.1 = (bf16[32,1280]{1,0:T(8,128)(2,1)S(1)}, bf16[32,640]{1,0:T(8,128)(2,1)S(1)}, bf16[4,8,640]{2,1,0:T(8,128)(2,1)}) custom-call(s32[4]{0:T(128)S(1)} %copy-done.2, f32[4,32,2048]{2,1,0:T(8,128)S(1)} %all-to-all-done.1.parts, f32[32,128]{1,0:T(8,128)S(1)} %get-tuple-element.13.cosine, f32[32,128]{1,0:T(8,128)S(1)} %get-tuple-element.12.sine, ...), custom_call_target="tpu_custom_call" | custom-call | tf_op jit(solution)/shard_map/rotate/pallas_call | solution.py:227
  92.9 2.7 %collective-permute-start.1 = (bf16[32,640]{1,0:T(8,128)(2,1)S(1)}, bf16[32,640]{1,0:T(8,128)(2,1)S(1)}, u32[]{:S(2)}, u32[]{:S(2)}) collective-permute-start(bf16[32,640]{1,0:T(8,128)(2,1)S(1)} %get-tuple-element.9), channel_id=1, source_target_pairs={{0,256},{256,0},{1,257},{257,1},{2,258},{258,2},{3,259},{259,3},{4... | collective-permute-start | bytes 122888 | tf_op jit(solution)/shard_map/ppermute | solution.py:245
  95.6 5.9 %collective-permute-done.1.far = bf16[32,640]{1,0:T(8,128)(2,1)S(1)} collective-permute-done((bf16[32,640]{1,0:T(8,128)(2,1)S(1)}, bf16[32,640]{1,0:T(8,128)(2,1)S(1)}, u32[]{:S(2)}, u32[]{:S(2)}) %collective-permute-start.1) | collective-permute-done | bytes 40992 | tf_op jit(solution)/shard_map/ppermute | solution.py:245
  101.6 0.2 broadcast_select_fusion
  101.8 37.4 %all_to_all.25.blocks = bf16[32,32,640]{2,1,0:T(8,128)(2,1)S(1)} all-to-all(bf16[32,32,640]{2,1,0:T(8,128)(2,1)S(1)} %broadcast_select_fusion), channel_id=1, replica_groups=mesh['yh'=2,'z'=8,'x'=4,'yl'=4,'c'=2] {'z','x'}, dimensions={0} | all-to-all | bytes 2621440 | tf_op jit(solution)/shard_map/all_to_all | solution.py:248
  139.2 1.0 broadcast_in_dim.58
  140.2 7.4 %all-to-all-start.4 = ((bf16[64,20,256]{2,1,0:T(8,128)(2,1)}), bf16[64,20,256]{2,1,0:T(8,128)(2,1)S(1)}, u32[]{:S(2)}, u32[]{:S(2)}) async-start(bf16[64,20,256]{2,1,0:T(8,128)(2,1)} %broadcast_in_dim.58), calls=%async_computation.4 | async-start | bytes 1572864 | tf_op jit(solution)/shard_map/all_to_all | solution.py:190
  147.6 30.2 %all-gather = bf16[256,1280]{1,0:T(8,128)(2,1)S(1)} all-gather(bf16[32,1280]{1,0:T(8,128)(2,1)S(1)} %get-tuple-element.8), channel_id=2, replica_groups=mesh['yh'=2,'z'=8,'x'=4,'yl'=4,'c'=2] {'yl','c'}, dimensions={0}, use_global_device_ids=true | all-gather | bytes 737280 | tf_op jit(solution)/shard_map/all_gather | solution.py:246
  177.8 4.4 %attend1.1 = f32[128,1408]{1,0:T(8,128)S(1)} custom-call(s32[5]{0:T(128)S(1)} %stack.23.place, s32[4]{0:T(128)S(1)} %copy-done.1, bf16[8,32,1280]{2,1,0:T(8,128)(2,1)S(1)} %bitcast.14, bf16[32,32,640]{2,1,0:T(8,128)(2,1)S(1)} %all_to_all.25.blocks, bf16[32,640]{1,0:T(8,128)(2,1)S(1)} %collective-permute-done.1.far), custom_call_target="tpu_custom_call" | custom-call | tf_op jit(solution)/shard_map/attend1/pallas_call | solution.py:251
  182.2 2.2 collective-permute-start.2
  184.5 4.4 %attend0.1 = f32[128,1408]{1,0:T(8,128)S(1)} custom-call(s32[5]{0:T(128)S(1)} %stack.23.place, s32[4]{0:T(128)S(1)} %copy-done.1, bf16[8,32,1280]{2,1,0:T(8,128)(2,1)S(1)} %bitcast.15, bf16[32,32,640]{2,1,0:T(8,128)(2,1)S(1)} %all_to_all.25.blocks, bf16[32,640]{1,0:T(8,128)(2,1)S(1)} %collective-permute-done.1.far), custom_call_target="tpu_custom_call" | custom-call | tf_op jit(solution)/shard_map/attend0/pallas_call | solution.py:251
  188.8 1.0 add.82
  189.8 3.5 %all-to-all-start.3 = ((f32[4,32,1408]{2,1,0:T(8,128)}), f32[4,32,1408]{2,1,0:T(8,128)S(1)}, u32[]{:S(2)}, u32[]{:S(2)}) async-start(f32[4,32,1408]{2,1,0:T(8,128)} %bitcast.11), calls=%async_computation.3 | async-start | bytes 1441792 | tf_op jit(solution)/shard_map/all_to_all | solution.py:262
  193.3 0.1 reshape.106.weight
  193.4 18.1 %all-to-all-done.3.parts = f32[4,32,1408]{2,1,0:T(8,128)S(1)} async-done(((f32[4,32,1408]{2,1,0:T(8,128)}), f32[4,32,1408]{2,1,0:T(8,128)S(1)}, u32[]{:S(2)}, u32[]{:S(2)}) %all-to-all-start.3) | async-done | bytes 720928 | tf_op jit(solution)/shard_map/all_to_all | solution.py:262
  211.5 0.2 divide.1
  211.7 16.5 %all_gather.11.attended = bf16[256,1280]{1,0:T(8,128)(2,1)S(1)} all-gather(bf16[32,1280]{1,0:T(8,128)(2,1)S(1)} %divide.1), channel_id=1, replica_groups=mesh['yh'=2,'z'=8,'x'=4,'yl'=4,'c'=2] {'yl','c'}, dimensions={0}, use_global_device_ids=true | all-gather | bytes 737280 | tf_op jit(solution)/shard_map/all_gather | solution.py:264
  228.2 1.0 mix.1
  (28 shorter events, 0.4 us)
Async XLA Ops:
  2.5 19.8 %copy-start.4 = (bf16[256]{0:T(256)(128)(2,1)S(1)}, bf16[256]{0:T(256)(128)(2,1)}, u32[]{:S(2)}) copy-start(bf16[256]{0:T(256)(128)(2,1)} %param.9) | copy-start | bytes 1540
  2.5 44.2 %all-to-all-start = ((bf16[64,30,256]{2,1,0:T(8,128)(2,1)}), bf16[64,30,256]{2,1,0:T(8,128)(2,1)S(1)}, u32[]{:S(2)}, u32[]{:S(2)}) async-start(bf16[64,30,256]{2,1,0:T(8,128)(2,1)} %broadcast_in_dim.38), calls=%async_computation | async-start | bytes 2097152 | tf_op jit(solution)/shard_map/all_to_all | solution.py:190
  22.2 24.7 %copy-start = (bf16[256,256]{1,0:T(8,128)(2,1)S(1)}, bf16[256,256]{1,0:T(8,128)(2,1)}, u32[]{:S(2)}) copy-start(bf16[256,256]{1,0:T(8,128)(2,1)} %param.8) | copy-start | bytes 393220
  48.0 8.4 %collective-permute-start = (f32[128,2048]{1,0:T(8,128)S(1)}, f32[128,2048]{1,0:T(8,128)S(1)}, u32[]{:S(2)}, u32[]{:S(2)}) collective-permute-start(f32[128,2048]{1,0:T(8,128)S(1)} %project1.1), channel_id=1, source_target_pairs={{0,1},{1,0},{2,3},{3,2},{4,5},{5,4},{6,7},{7,6},{8,9},{9,8},{10,11... | collective-permute-start | bytes 3145736 | tf_op jit(solution)/shard_map/ppermute | solution.py:214
  57.4 8.0 %copy-start.5 = (bf16[64]{0:T(256)(128)(2,1)S(1)}, bf16[64]{0:T(256)(128)(2,1)}, u32[]{:S(2)}) copy-start(bf16[64]{0:T(256)(128)(2,1)} %param.11) | copy-start | bytes 388
  57.4 8.1 %copy-start.6 = (bf16[64]{0:T(256)(128)(2,1)S(1)}, bf16[64]{0:T(256)(128)(2,1)}, u32[]{:S(2)}) copy-start(bf16[64]{0:T(256)(128)(2,1)} %param.12) | copy-start | bytes 388
  57.4 8.2 %copy-start.1 = (s32[4]{0:T(128)S(1)}, s32[4]{0:T(128)}, u32[]{:S(2)}) copy-start(s32[4]{0:T(128)} %lengths.3) | copy-start | bytes 52
  57.4 33.2 %copy-start.2 = (s32[4]{0:T(128)S(1)}, s32[4]{0:T(128)}, u32[]{:S(2)}) copy-start(s32[4]{0:T(128)} %table.1) | copy-start | bytes 52
  57.4 33.2 %all-to-all-start.1 = ((f32[4,32,2048]{2,1,0:T(8,128)}), f32[4,32,2048]{2,1,0:T(8,128)S(1)}, u32[]{:S(2)}, u32[]{:S(2)}) async-start(f32[4,32,2048]{2,1,0:T(8,128)} %bitcast.7), calls=%async_computation.1 | async-start | bytes 2097152 | tf_op jit(solution)/shard_map/all_to_all | solution.py:217
  92.9 8.6 %collective-permute-start.1 = (bf16[32,640]{1,0:T(8,128)(2,1)S(1)}, bf16[32,640]{1,0:T(8,128)(2,1)S(1)}, u32[]{:S(2)}, u32[]{:S(2)}) collective-permute-start(bf16[32,640]{1,0:T(8,128)(2,1)S(1)} %get-tuple-element.9), channel_id=1, source_target_pairs={{0,256},{256,0},{1,257},{257,1},{2,258},{258,2},{3,259},{259,3},{4... | collective-permute-start | bytes 122888 | tf_op jit(solution)/shard_map/ppermute | solution.py:245
  101.8 37.5 %copy-start.3 = (bf16[20,256]{1,0:T(8,128)(2,1)S(1)}, bf16[20,256]{1,0:T(8,128)(2,1)}, u32[]{:S(2)}) copy-start(bf16[20,256]{1,0:T(8,128)(2,1)} %param.13) | copy-start | bytes 30724
  140.2 49.6 %all-to-all-start.4 = ((bf16[64,20,256]{2,1,0:T(8,128)(2,1)}), bf16[64,20,256]{2,1,0:T(8,128)(2,1)S(1)}, u32[]{:S(2)}, u32[]{:S(2)}) async-start(bf16[64,20,256]{2,1,0:T(8,128)(2,1)} %broadcast_in_dim.58), calls=%async_computation.4 | async-start | bytes 1572864 | tf_op jit(solution)/shard_map/all_to_all | solution.py:190
  182.2 6.6 %collective-permute-start.2 = (f32[128,1408]{1,0:T(8,128)S(1)}, f32[128,1408]{1,0:T(8,128)S(1)}, u32[]{:S(2)}, u32[]{:S(2)}) collective-permute-start(f32[128,1408]{1,0:T(8,128)S(1)} %attend1.1), channel_id=1, source_target_pairs={{0,1},{1,0},{2,3},{3,2},{4,5},{5,4},{6,7},{7,6},{8,9},{9,8},{10,11... | collective-permute-start | bytes 2162696 | tf_op jit(solution)/shard_map/ppermute | solution.py:260
  189.8 21.7 %all-to-all-start.3 = ((f32[4,32,1408]{2,1,0:T(8,128)}), f32[4,32,1408]{2,1,0:T(8,128)S(1)}, u32[]{:S(2)}, u32[]{:S(2)}) async-start(f32[4,32,1408]{2,1,0:T(8,128)} %bitcast.11), calls=%async_computation.3 | async-start | bytes 1441792 | tf_op jit(solution)/shard_map/all_to_all | solution.py:262

commit v2 on v1

--- a/solution.py
+++ b/solution.py
@@ -20,6 +20,7 @@
 PAGE = 64
 PAGES_DEV = 4
 ROWS = 32
+PIECE = 30
 ROPE_BASE = 10000.0
 SUMS = Q_DIM + 128
 BF = jnp.bfloat16
@@ -44,16 +45,21 @@
     )
 
 
-def project_body(flip, place, hidden, gain, weight, out):
+def project_body(flip, place, gain, weight, here, one, two, three, out):
     core = place[3] if not flip else 1 - place[3]
-    rows = [hidden[p, yl, core].astype(F32) for yl in range(4) for p in range(PAGES_DEV)]
-    values = jnp.concatenate(rows, axis=0)
-    scaled = (values * gain[...].astype(F32)).astype(BF)
-    out[:, :QKV_DIM] = lax.dot_general(
-        scaled, weight[...], (((1,), (1,)), ((), ())), preferred_element_type=F32
-    )
-    squares = jnp.sum(values * values, axis=1, keepdims=True)
-    out[:, QKV_DIM:] = jnp.broadcast_to(squares, (128, 128))
+    x = place[5]
+    lane = lax.broadcasted_iota(jnp.int32, (128, 128), 1)
+    for step, hidden in enumerate((here, one, two, three)):
+        rows = [hidden[p, yl, core].astype(F32) for yl in range(4) for p in range(PAGES_DEV)]
+        values = jnp.concatenate(rows, axis=0)
+        scaled = (values * gain[...].astype(F32)).astype(BF)
+        product = lax.dot_general(
+            scaled, weight[...], (((1,), (1,)), ((), ())), preferred_element_type=F32
+        )
+        squares = jnp.sum(values * values, axis=1, keepdims=True)
+        owner = lax.rem(x + 4 - step, 4)
+        out[pl.ds(owner, 1), :, :128] = jnp.where(lane == 30, squares, product[:, :128])[None]
+        out[pl.ds(owner, 1), :, 128:] = product[None, :, 128:]
 
 
 def rotate_body(table, parts, cosine, sine, q_gain, k_gain, queries, kv, cache):
@@ -61,11 +67,27 @@
     upper_head = lane >= HEAD
     lower_part = (lane % HEAD) < HEAD // 2
 
-    def total(tile):
+    def summed(x, tile):
         at = pl.ds(tile * 128, 128)
-        return (parts[0, :, at] + parts[1, :, at]) + (parts[2, :, at] + parts[3, :, at])
-
-    inverse = lax.rsqrt(total(15) / D + 1e-06)
+        low, high = parts[4 * x, :, at] + parts[4 * x + 1, :, at], parts[4 * x + 2, :, at]
+        return low + (high + parts[4 * x + 3, :, at])
+
+    tiles = [None] * 15
+    inverse = None
+    for tile in range(4):
+        for x in range(4):
+            source = summed(x, tile)
+            if x == 0 and tile == 0:
+                inverse = lax.rsqrt(source[:, 30:31] / D + 1e-06)
+            for piece in range(4):
+                z, yh = divmod(tile * 4 + piece, 2)
+                start = PIECE * (yh * 32 + z * 4 + x)
+                moved = pltpu.roll(source, (start - piece * 32) % 128, 1)
+                for place_at in range(start // 128, (start + PIECE - 1) // 128 + 1):
+                    first, last = start - place_at * 128, start + PIECE - place_at * 128
+                    inside = (lane >= first) & (lane < last)
+                    old = tiles[place_at]
+                    tiles[place_at] = jnp.where(inside, moved, 0.0 if old is None else old)
     cos = cosine[...]
     sin = jnp.where(lower_part, -sine[...], sine[...])
 
@@ -79,10 +101,10 @@
         return w * cos + partner * sin
 
     for tile in range(10):
-        u = total(tile) * inverse
+        u = tiles[tile] * inverse
         queries[:, tile * 128 : tile * 128 + 128] = turned(u, q_gain[...]).astype(BF)
     for tile in range(10, 15):
-        u = total(tile) * inverse
+        u = tiles[tile] * inverse
         if tile == 12:
             u = jnp.where(upper_head, u, turned(u, k_gain[...]))
         elif tile < 12:
@@ -92,17 +114,11 @@
         cache[pl.ds(table[p], 1)] = kv[p * 8 : p * 8 + 8, :].reshape(1, 8, KV_DIM)
 
 
-def attend_body(flip, place, lengths, q, blocks, far, out, bias, bias_far):
+def attend_body(flip, place, lengths, q0, q1, q2, q3, blocks, far, out, bias, bias_far):
     yh, index, wide, narrow = place[0], place[1], place[2], place[4]
-    core = place[3] if not flip else 1 - place[3]
     row = lax.broadcasted_iota(jnp.int32, (128, 1), 0)
-    token = (
-        wide * TOK_DEV
-        + (row % ROWS) // 8 * PAGE
-        + row // ROWS * 16
-        + core * 8
-        + row % 8
-    )
+    owner = (narrow + 8 - flip - row // ROWS * 2) & 7
+    token = wide * TOK_DEV + (row % ROWS) // 8 * PAGE + owner * 8 + row % 8
     begin = jnp.zeros_like(token)
     end = jnp.int32(0)
     for s in range(3):
@@ -122,9 +138,9 @@
     for chunk in range(4):
         bias[chunk] = hide(chunk * 8, 256, False)
     bias_far[...] = hide(index, ROWS, True)
-    half = [q[2 * yl + core] for yl in range(4)]
-    half = jnp.concatenate(half, axis=0)
-    out[:, Q_DIM:] = jnp.zeros((128, 128), F32)
+    half = jnp.concatenate([q0[...], q1[...], q2[...], q3[...]], axis=0)
+    owners = [((narrow + 8 - flip - 2 * k) & 7) // 2 for k in range(4)]
+    out[:, :, Q_DIM:] = jnp.zeros((4, ROWS, 128), F32)
     for g in range(KV_HEADS):
         heads = [
             half[:, (g * GROUP + h) * HEAD : (g * GROUP + h + 1) * HEAD] for h in range(GROUP)
@@ -159,8 +175,11 @@
         denominator = jnp.sum(denominator, axis=1, keepdims=True) + tail
         for h in range(GROUP):
             head = g * GROUP + h
-            out[:, head * HEAD : (head + 1) * HEAD] = numerator[h * 128 : (h + 1) * 128]
-            out[:, Q_DIM + head : Q_DIM + head + 1] = denominator[h * 128 : (h + 1) * 128]
+            for k in range(4):
+                at = slice(h * 128 + k * ROWS, h * 128 + (k + 1) * ROWS)
+                to = pl.ds(owners[k], 1)
+                out[to, :, head * HEAD : (head + 1) * HEAD] = numerator[at][None]
+                out[to, :, Q_DIM + head : Q_DIM + head + 1] = denominator[at][None]
 
 
 def divide_body(parts, out):
@@ -196,25 +215,39 @@
     index = z * 4 + x
     wide = yh * 32 + index
     narrow = yl * 2 + core
-    place = jnp.stack([yh, index, wide, core, narrow]).astype(jnp.int32)
+    place = jnp.stack([yh, index, wide, core, narrow, x]).astype(jnp.int32)
     swap = [(0, 1), (1, 0)]
-    wide_axes = ("yh", "z", "x")
-
-    weight = spread(qkv_weight.T, wide_axes, 64).reshape(QKV_DIM, TOK_DEV)
-    hidden5 = hidden_in.reshape(PAGES_DEV, 4, 2, 8, 256)
+
+    def both(own):
+        other = lax.ppermute(own, "yh", swap)
+        return jnp.where(yh == 0, jnp.stack([own, other]), jnp.stack([other, own]))
+
+    own = jnp.concatenate(
+        [jnp.pad(qkv_weight.T, ((0, 2), (0, 0))), jnp.pad(out_weight, ((0, 4), (0, 0)))], axis=0
+    )
+    shifts = [[(i, (i + step) % 4) for i in range(4)] for step in range(4)]
+    hidden = [hidden_in] + [lax.ppermute(hidden_in, "x", shifts[step]) for step in range(1, 4)]
+    gathered = spread(both(own), "z", 8)
+    weight = gathered[:, :, :32].reshape(512, TOK_DEV)
+    mixing = gathered[:, :, 32:52]
+    hidden = [h.reshape(PAGES_DEV, 4, 2, 8, 256) for h in hidden]
     gain = attn_gain.reshape(1, 256)
-    half_shape = jax.ShapeDtypeStruct((128, 2048), F32)
+    half_shape = jax.ShapeDtypeStruct((4, 128, 512), F32)
 
     def project(flip):
         return call(
-            functools.partial(project_body, flip), half_shape, [SM, VM, VM, VM], f"project{flip}"
-        )(place, hidden5, gain, weight)
+            functools.partial(project_body, flip), half_shape, [SM] + [VM] * 6, f"project{flip}"
+        )(place, gain, weight, *hidden)
 
     sent = project(1)
     arrived = lax.ppermute(sent, "c", swap)
-    partial = (project(0) + arrived).reshape(4, ROWS, 2048)
-    out_part, partial = lax.optimization_barrier((out_weight, partial))
-    parts = lax.all_to_all(partial, "yl", 0, 0)
+    partial = (project(0) + arrived).reshape(16, ROWS, 512)
+    mixing, partial = lax.optimization_barrier((mixing, partial))
+    parts = lax.all_to_all(partial, ("x", "yl"), 0, 0)
+    ring = [mixing] + [lax.ppermute(mixing, "x", shifts[step]) for step in range(1, 4)]
+    ring = jnp.stack([ring[(3 - k) % 4] for k in range(7)])
+    mixing = lax.dynamic_slice_in_dim(ring, 3 - x, 4, 0)
+    mixing = mixing.transpose(2, 1, 0, 3, 4).reshape(Q_DIM, 256)
 
     row = jnp.arange(ROWS, dtype=jnp.int32)
     own = wide * TOK_DEV + row // 8 * PAGE + narrow * 8 + row % 8
@@ -243,26 +276,29 @@
     )
 
     far = lax.ppermute(kv, "yh", swap)
-    all_queries = lax.all_gather(queries, ("yl", "c"), axis=0, tiled=False)
+    all_queries = [queries] + [
+        lax.ppermute(queries, ("yl", "c"), [(i, (i + step) % 8) for i in range(8)])
+        for step in range(1, 8)
+    ]
     target = jnp.arange(32, dtype=jnp.int32)[:, None, None]
     blocks = lax.all_to_all(jnp.where(target >= index, kv[None], far[None]), ("z", "x"), 0, 0)
+
+    blocks, mixing, all_queries = lax.optimization_barrier((blocks, mixing, all_queries))
 
     def attend(flip):
         return call(
             functools.partial(attend_body, flip),
-            jax.ShapeDtypeStruct((128, SUMS), F32),
-            [SM, SM, VM, VM, VM],
+            jax.ShapeDtypeStruct((4, ROWS, SUMS), F32),
+            [SM, SM] + [VM] * 6,
             f"attend{flip}",
             [pltpu.VMEM((4, 128, 256), F32), pltpu.VMEM((128, ROWS), F32)],
-        )(place, lengths, all_queries, blocks, far)
+        )(place, lengths, *all_queries[flip::2], blocks, far)
 
     sent = attend(1)
     arrived = lax.ppermute(sent, "c", swap)
-    sums = (attend(0) + arrived).reshape(4, ROWS, SUMS)
-    parts = lax.all_to_all(sums, "yl", 0, 0)
+    parts = lax.all_to_all(attend(0) + arrived, "yl", 0, 0)
     attended = call(divide_body, jax.ShapeDtypeStruct((ROWS, Q_DIM), BF), [VM], "divide")(parts)
     attended = lax.all_gather(attended, ("yl", "c"), axis=0, tiled=True)
-    mixing = spread(out_part, wide_axes, 64).reshape(Q_DIM, 256)
     hidden_out = call(
         mix_body, jax.ShapeDtypeStruct((PAGES_DEV, 8, 8, 256), BF), [VM] * 3, "mix"
     )(attended, mixing, hidden_in.reshape(PAGES_DEV, 8, 8, 256))

time: 230 us -> 203 us (0.88)
  blocking collectives: 84.2 us -> 37.3 us
  starting transfers between devices: 49.6 us -> 89.9 us
  waiting for transfers between devices: 74.1 us -> 51.6 us
    ppermute x0 -> x14, starting transfers between devices: none -> 51.1 us  [the longest x7 23 us: on_device(): lax.ppermute(queries, ('yl', 'c'), [(i, (i + step) % 8) for i in range(8)])]
    all_gather x1 -> x0, blocking collectives: 30.2 us -> none  [on_device(): all_queries = lax.all_gather(queries, ('yl', 'c'), axis=0, tiled=False)]
    all_to_all x2 -> x1, waiting for transfers between devices: 24.3 us -> 3.59 us  [spread(): lax.all_to_all(jnp.broadcast_to(x[None], (count,) + x.shape), axes, 0, 0)]
    all_to_all x2 -> x1, starting transfers between devices: 27.1 us -> 10 us  [spread(): lax.all_to_all(jnp.broadcast_to(x[None], (count,) + x.shape), axes, 0, 0)]
    ppermute x0 -> x14, waiting for transfers between devices: none -> 16.7 us  [the longest x3 15.4 us: on_device(): lax.ppermute(mixing, 'x', shifts[step])]
    all_to_all x2, waiting for transfers between devices: 42.6 us -> 26.3 us  [the longest x1 26.3 us: on_device(): parts = lax.all_to_all(partial, ('x', 'yl'), 0, 0)]
    all_to_all x1, blocking collectives: 37.4 us -> 21.3 us  [on_device(): parts = lax.all_to_all(attend(0) + arrived, 'yl', 0, 0)]
    all_to_all x2, starting transfers between devices: 11.4 us -> 14.3 us  [the longest x1 7.23 us: on_device(): lax.all_to_all(jnp.where(target >= index, kv[None], far[None]), ('z', 'x'...]
  transfers between devices with their start and end apart: 7 -> 20, of which waited for: 5 -> 8; matrix products, arithmetic and copies ran while one was open for 1% -> 2% of each run, Pallas kernels for 4% -> 3%
where the time goes in v2:
time: 203 us; the launch traced here: 202 us
  starting transfers between devices  89.9 us (44%)
  waiting for transfers between devices  51.6 us (25%)
  blocking collectives  37.3 us (18%)
  Pallas kernels  14.8 us (7%)
  other arithmetic  3.8 us (2%)
  local copies, waits for them, and re-layouts  3.6 us (2%)
    all_to_all x1, waiting for transfers between devices, on_device(): parts = lax.all_to_all(partial, ('x', 'yl'), 0, 0)  26.3 us
    ppermute x7, starting transfers between devices, on_device(): lax.ppermute(queries, ('yl', 'c'), [(i, (i + step) % 8) for i in range(8)])  23 us
    all_to_all x1, blocking collectives, on_device(): parts = lax.all_to_all(attend(0) + arrived, 'yl', 0, 0)  21.3 us
    all_gather x1, blocking collectives, on_device(): attended = lax.all_gather(attended, ('yl', 'c'), axis=0, tiled=True)  16 us
    ppermute x3, waiting for transfers between devices, on_device(): lax.ppermute(mixing, 'x', shifts[step])  15.4 us
    ppermute x3, starting transfers between devices, on_device(): lax.ppermute(hidden_in, 'x', shifts[step])  10.5 us
    all_to_all x1, starting transfers between devices, spread(): lax.all_to_all(jnp.broadcast_to(x[None], (count,) + x.shape), axes, 0, 0)  10 us
    ppermute x2, starting transfers between devices, on_device(): arrived = lax.ppermute(sent, 'c', swap)  9.59 us
  transfers between devices with their start and end apart: 20, of which 8 were waited for; matrix products, arithmetic and copies ran while one was open for 2% of the time, Pallas kernels for 3%

profile of v2, /device:TPU:1, one launch (start us, length us, event | category | flops | bytes accessed | tf_op | source)
XLA Modules:
  0.0 202.1 jit_solution(17466202858414407639)
XLA Ops:
  1.4 8.3 %collective-permute-start = (bf16[56,256]{1,0:T(8,128)(2,1)S(1)}, bf16[56,256]{1,0:T(8,128)(2,1)S(1)}, u32[]{:S(2)}, u32[]{:S(2)}) collective-permute-start(bf16[56,256]{1,0:T(8,128)(2,1)S(1)} %get-tuple-element.33), channel_id=1, source_target_pairs={{0,256},{256,0},{1,257},{257,1},{2,258},{258,2},{3,259},{259,3},{4... | collective-permute-start | bytes 86024 | tf_op jit(solution)/shard_map/ppermute | solution.py:222
  11.8 10.0 %all-to-all-start = ((bf16[8,2,56,256]{3,2,1,0:T(8,128)(2,1)}), bf16[8,2,56,256]{3,2,1,0:T(8,128)(2,1)S(1)}, u32[]{:S(2)}, u32[]{:S(2)}) async-start(bf16[8,2,56,256]{3,2,1,0:T(8,128)(2,1)} %broadcast_in_dim.48), calls=%async_computation | async-start | bytes 917504 | tf_op jit(solution)/shard_map/all_to_all | solution.py:209
  21.9 3.1 %collective-permute-start.1 = (bf16[256,256]{1,0:T(8,128)(2,1)S(1)}, bf16[256,256]{1,0:T(8,128)(2,1)S(1)}, u32[]{:S(2)}, u32[]{:S(2)}) collective-permute-start(bf16[256,256]{1,0:T(8,128)(2,1)S(1)} %copy-done), channel_id=1, source_target_pairs={{0,8},{8,16},{16,24},{24,0},{1,9},{9,17},{17,25},{25,1},{2,10},{10... | collective-permute-start | bytes 393224 | tf_op jit(solution)/shard_map/ppermute | solution.py:229
  25.0 4.4 %collective-permute-start.2 = (bf16[256,256]{1,0:T(8,128)(2,1)S(1)}, bf16[256,256]{1,0:T(8,128)(2,1)S(1)}, u32[]{:S(2)}, u32[]{:S(2)}) collective-permute-start(bf16[256,256]{1,0:T(8,128)(2,1)S(1)} %copy-done), channel_id=1, source_target_pairs={{0,16},{8,24},{16,0},{24,8},{1,17},{9,25},{17,1},{25,9},{2,18},{10... | collective-permute-start | bytes 393224 | tf_op jit(solution)/shard_map/ppermute | solution.py:229
  29.3 3.1 %collective-permute-start.3 = (bf16[256,256]{1,0:T(8,128)(2,1)S(1)}, bf16[256,256]{1,0:T(8,128)(2,1)S(1)}, u32[]{:S(2)}, u32[]{:S(2)}) collective-permute-start(bf16[256,256]{1,0:T(8,128)(2,1)S(1)} %copy-done), channel_id=1, source_target_pairs={{0,24},{8,0},{16,8},{24,16},{1,25},{9,1},{17,9},{25,17},{2,26},{10... | collective-permute-start | bytes 393224 | tf_op jit(solution)/shard_map/ppermute | solution.py:229
  32.5 3.6 %all-to-all-done = bf16[8,2,56,256]{3,2,1,0:T(8,128)(2,1)S(1)} async-done(((bf16[8,2,56,256]{3,2,1,0:T(8,128)(2,1)}), bf16[8,2,56,256]{3,2,1,0:T(8,128)(2,1)S(1)}, u32[]{:S(2)}, u32[]{:S(2)}) %all-to-all-start) | async-done | bytes 458784 | tf_op jit(solution)/shard_map/all_to_all | solution.py:209
  37.2 4.7 %collective-permute-start.4 = (f32[4,128,512]{2,1,0:T(8,128)S(1)}, f32[4,128,512]{2,1,0:T(8,128)S(1)}, u32[]{:S(2)}, u32[]{:S(2)}) collective-permute-start(f32[4,128,512]{2,1,0:T(8,128)S(1)} %project1.1), channel_id=1, source_target_pairs={{0,1},{1,0},{2,3},{3,2},{4,5},{5,4},{6,7},{7,6},{8,9},{9,8},{10,11... | collective-permute-start | bytes 3145736 | tf_op jit(solution)/shard_map/ppermute | solution.py:243
  45.4 7.1 %all-to-all-start.1 = ((f32[16,32,512]{2,1,0:T(8,128)}), f32[16,32,512]{2,1,0:T(8,128)S(1)}, u32[]{:S(2)}, u32[]{:S(2)}) async-start(f32[16,32,512]{2,1,0:T(8,128)} %bitcast.14), calls=%async_computation.1 | async-start | bytes 2097152 | tf_op jit(solution)/shard_map/all_to_all | solution.py:246
  53.2 26.3 %all-to-all-done.1.parts = f32[16,32,512]{2,1,0:T(8,128)S(1)} async-done(((f32[16,32,512]{2,1,0:T(8,128)}), f32[16,32,512]{2,1,0:T(8,128)S(1)}, u32[]{:S(2)}, u32[]{:S(2)}) %all-to-all-start.1) | async-done | bytes 1048608 | tf_op jit(solution)/shard_map/all_to_all | solution.py:246
  79.5 2.9 %rotate.1 = (bf16[32,1280]{1,0:T(8,128)(2,1)S(1)}, bf16[32,640]{1,0:T(8,128)(2,1)S(1)}, bf16[4,8,640]{2,1,0:T(8,128)(2,1)}) custom-call(s32[4]{0:T(128)S(1)} %copy-done.2, f32[16,32,512]{2,1,0:T(8,128)S(1)} %all-to-all-done.1.parts, f32[32,128]{1,0:T(8,128)S(1)} %get-tuple-element.35.cosine, f32[32,128]{1,0:T(8,128)S(1)} %get-tuple-element.34.sine, ...), custom_call_target="tpu_custom_call" | custom-call | tf_op jit(solution)/shard_map/rotate/pallas_call | solution.py:260
  82.4 4.8 %collective-permute-start.5 = (bf16[32,640]{1,0:T(8,128)(2,1)S(1)}, bf16[32,640]{1,0:T(8,128)(2,1)S(1)}, u32[]{:S(2)}, u32[]{:S(2)}) collective-permute-start(bf16[32,640]{1,0:T(8,128)(2,1)S(1)} %get-tuple-element.18), channel_id=1, source_target_pairs={{0,256},{256,0},{1,257},{257,1},{2,258},{258,2},{3,259},{259,3},{4... | collective-permute-start | bytes 122888 | tf_op jit(solution)/shard_map/ppermute | solution.py:278
  87.2 3.8 %collective-permute-done.5.far = bf16[32,640]{1,0:T(8,128)(2,1)S(1)} collective-permute-done((bf16[32,640]{1,0:T(8,128)(2,1)S(1)}, bf16[32,640]{1,0:T(8,128)(2,1)S(1)}, u32[]{:S(2)}, u32[]{:S(2)}) %collective-permute-start.5) | collective-permute-done | bytes 40992 | tf_op jit(solution)/shard_map/ppermute | solution.py:278
  91.0 1.3 broadcast_select_fusion
  92.3 7.2 %all-to-all-start.2 = ((bf16[32,32,640]{2,1,0:T(8,128)(2,1)}), bf16[32,32,640]{2,1,0:T(8,128)(2,1)S(1)}, u32[]{:S(2)}, u32[]{:S(2)}) async-start(bf16[32,32,640]{2,1,0:T(8,128)(2,1)} %broadcast_select_fusion), calls=%async_computation.2 | async-start | bytes 2621440 | tf_op jit(solution)/shard_map/all_to_all | solution.py:284
  99.5 4.3 %collective-permute-start.6 = (bf16[8,2,20,256]{3,2,1,0:T(8,128)(2,1)S(1)}, bf16[8,2,20,256]{3,2,1,0:T(8,128)(2,1)S(1)}, u32[]{:S(2)}, u32[]{:S(2)}) collective-permute-start(bf16[8,2,20,256]{3,2,1,0:T(8,128)(2,1)S(1)} %slice.8), channel_id=1, source_target_pairs={{0,24},{8,0},{16,8},{24,16},{1,25},{9,1},{17,9},{25,17},{2,26},{10... | collective-permute-start | bytes 491528 | tf_op jit(solution)/shard_map/ppermute | solution.py:247
  103.9 2.5 %collective-permute-start.7 = (bf16[8,2,20,256]{3,2,1,0:T(8,128)(2,1)S(1)}, bf16[8,2,20,256]{3,2,1,0:T(8,128)(2,1)S(1)}, u32[]{:S(2)}, u32[]{:S(2)}) collective-permute-start(bf16[8,2,20,256]{3,2,1,0:T(8,128)(2,1)S(1)} %slice.8), channel_id=1, source_target_pairs={{0,16},{8,24},{16,0},{24,8},{1,17},{9,25},{17,1},{25,9},{2,18},{10... | collective-permute-start | bytes 491528 | tf_op jit(solution)/shard_map/ppermute | solution.py:247
  106.4 2.5 %collective-permute-start.8 = (bf16[8,2,20,256]{3,2,1,0:T(8,128)(2,1)S(1)}, bf16[8,2,20,256]{3,2,1,0:T(8,128)(2,1)S(1)}, u32[]{:S(2)}, u32[]{:S(2)}) collective-permute-start(bf16[8,2,20,256]{3,2,1,0:T(8,128)(2,1)S(1)} %slice.8), channel_id=1, source_target_pairs={{0,8},{8,16},{16,24},{24,0},{1,9},{9,17},{17,25},{25,1},{2,10},{10... | collective-permute-start | bytes 491528 | tf_op jit(solution)/shard_map/ppermute | solution.py:247
  108.9 3.1 %collective-permute-done.6 = bf16[8,2,20,256]{3,2,1,0:T(8,128)(2,1)S(1)} collective-permute-done((bf16[8,2,20,256]{3,2,1,0:T(8,128)(2,1)S(1)}, bf16[8,2,20,256]{3,2,1,0:T(8,128)(2,1)S(1)}, u32[]{:S(2)}, u32[]{:S(2)}) %collective-permute-start.6) | collective-permute-done | bytes 163872 | tf_op jit(solution)/shard_map/ppermute | solution.py:247
  112.0 2.2 %collective-permute-done.7 = bf16[8,2,20,256]{3,2,1,0:T(8,128)(2,1)S(1)} collective-permute-done((bf16[8,2,20,256]{3,2,1,0:T(8,128)(2,1)S(1)}, bf16[8,2,20,256]{3,2,1,0:T(8,128)(2,1)S(1)}, u32[]{:S(2)}, u32[]{:S(2)}) %collective-permute-start.7) | collective-permute-done | bytes 163872 | tf_op jit(solution)/shard_map/ppermute | solution.py:247
  114.1 10.2 %collective-permute-done.8 = bf16[8,2,20,256]{3,2,1,0:T(8,128)(2,1)S(1)} collective-permute-done((bf16[8,2,20,256]{3,2,1,0:T(8,128)(2,1)S(1)}, bf16[8,2,20,256]{3,2,1,0:T(8,128)(2,1)S(1)}, u32[]{:S(2)}, u32[]{:S(2)}) %collective-permute-start.8) | collective-permute-done | bytes 163872 | tf_op jit(solution)/shard_map/ppermute | solution.py:247
  124.4 2.6 %collective-permute-start.10 = (bf16[32,1280]{1,0:T(8,128)(2,1)S(1)}, bf16[32,1280]{1,0:T(8,128)(2,1)S(1)}, u32[]{:S(2)}, u32[]{:S(2)}) collective-permute-start(bf16[32,1280]{1,0:T(8,128)(2,1)S(1)} %get-tuple-element.21.q0), channel_id=1, source_target_pairs={{0,2},{1,3},{2,4},{3,5},{4,6},{5,7},{6,0},{7,1},{8,10},{9,11},{10,... | collective-permute-start | bytes 245768 | tf_op jit(solution)/shard_map/ppermute | solution.py:280
  127.1 6.4 %collective-permute-start.11 = (bf16[32,1280]{1,0:T(8,128)(2,1)S(1)}, bf16[32,1280]{1,0:T(8,128)(2,1)S(1)}, u32[]{:S(2)}, u32[]{:S(2)}) collective-permute-start(bf16[32,1280]{1,0:T(8,128)(2,1)S(1)} %get-tuple-element.21.q0), channel_id=1, source_target_pairs={{0,3},{1,4},{2,5},{3,6},{4,7},{5,0},{6,1},{7,2},{8,11},{9,12},{10,... | collective-permute-start | bytes 245768 | tf_op jit(solution)/shard_map/ppermute | solution.py:280
  133.5 1.9 collective-permute-start.12
  135.4 4.1 %collective-permute-start.13 = (bf16[32,1280]{1,0:T(8,128)(2,1)S(1)}, bf16[32,1280]{1,0:T(8,128)(2,1)S(1)}, u32[]{:S(2)}, u32[]{:S(2)}) collective-permute-start(bf16[32,1280]{1,0:T(8,128)(2,1)S(1)} %get-tuple-element.21.q0), channel_id=1, source_target_pairs={{0,5},{1,6},{2,7},{3,0},{4,1},{5,2},{6,3},{7,4},{8,13},{9,14},{10,... | collective-permute-start | bytes 245768 | tf_op jit(solution)/shard_map/ppermute | solution.py:280
  139.5 2.2 %collective-permute-start.14 = (bf16[32,1280]{1,0:T(8,128)(2,1)S(1)}, bf16[32,1280]{1,0:T(8,128)(2,1)S(1)}, u32[]{:S(2)}, u32[]{:S(2)}) collective-permute-start(bf16[32,1280]{1,0:T(8,128)(2,1)S(1)} %get-tuple-element.21.q0), channel_id=1, source_target_pairs={{0,6},{1,7},{2,0},{3,1},{4,2},{5,3},{6,4},{7,5},{8,14},{9,15},{10,... | collective-permute-start | bytes 245768 | tf_op jit(solution)/shard_map/ppermute | solution.py:280
  141.8 2.6 %collective-permute-start.15 = (bf16[32,1280]{1,0:T(8,128)(2,1)S(1)}, bf16[32,1280]{1,0:T(8,128)(2,1)S(1)}, u32[]{:S(2)}, u32[]{:S(2)}) collective-permute-start(bf16[32,1280]{1,0:T(8,128)(2,1)S(1)} %get-tuple-element.21.q0), channel_id=1, source_target_pairs={{0,7},{1,0},{2,1},{3,2},{4,3},{5,4},{6,5},{7,6},{8,15},{9,8},{10,9... | collective-permute-start | bytes 245768 | tf_op jit(solution)/shard_map/ppermute | solution.py:280
  144.4 3.1 %collective-permute-start.9 = (bf16[32,1280]{1,0:T(8,128)(2,1)S(1)}, bf16[32,1280]{1,0:T(8,128)(2,1)S(1)}, u32[]{:S(2)}, u32[]{:S(2)}) collective-permute-start(bf16[32,1280]{1,0:T(8,128)(2,1)S(1)} %get-tuple-element.21.q0), channel_id=1, source_target_pairs={{0,1},{1,2},{2,3},{3,4},{4,5},{5,6},{6,7},{7,0},{8,9},{9,10},{10,1... | collective-permute-start | bytes 245768 | tf_op jit(solution)/shard_map/ppermute | solution.py:280
  149.9 4.3 %attend1.1 = f32[4,32,1408]{2,1,0:T(8,128)S(1)} custom-call(s32[6]{0:T(128)S(1)} %stack.59.place, s32[4]{0:T(128)S(1)} %copy-done.1, bf16[32,1280]{1,0:T(8,128)(2,1)S(1)} %collective-permute-done.9.q0, bf16[32,1280]{1,0:T(8,128)(2,1)S(1)} %collective-permute-done.11.q1, bf16[32,1280]{1,0:T(8,128)(2,1)S(1)} %collective-permute-done.13.q2, ...), custom_call_target="tpu_custom_call" | custom-call | tf_op jit(solution)/shard_map/attend1/pallas_call | solution.py:289
  154.2 4.9 %collective-permute-start.16 = (f32[4,32,1408]{2,1,0:T(8,128)S(1)}, f32[4,32,1408]{2,1,0:T(8,128)S(1)}, u32[]{:S(2)}, u32[]{:S(2)}) collective-permute-start(f32[4,32,1408]{2,1,0:T(8,128)S(1)} %attend1.1), channel_id=1, source_target_pairs={{0,1},{1,0},{2,3},{3,2},{4,5},{5,4},{6,7},{7,6},{8,9},{9,8},{10,11... | collective-permute-start | bytes 2162696 | tf_op jit(solution)/shard_map/ppermute | solution.py:298
  159.1 4.3 %attend0.1 = f32[4,32,1408]{2,1,0:T(8,128)S(1)} custom-call(s32[6]{0:T(128)S(1)} %stack.59.place, s32[4]{0:T(128)S(1)} %copy-done.1, bf16[32,1280]{1,0:T(8,128)(2,1)S(1)} %get-tuple-element.21.q0, bf16[32,1280]{1,0:T(8,128)(2,1)S(1)} %collective-permute-done.10.q1, bf16[32,1280]{1,0:T(8,128)(2,1)S(1)} %collective-permute-done.12.q2, ...), custom_call_target="tpu_custom_call" | custom-call | tf_op jit(solution)/shard_map/attend0/pallas_call | solution.py:289
  163.6 21.3 %all_to_all.20.parts = f32[4,32,1408]{2,1,0:T(8,128)S(1)} all-to-all(f32[4,32,1408]{2,1,0:T(8,128)S(1)} %add.91), channel_id=1, replica_groups=mesh['yh'=2,'z'=8,'x'=4,'yl'=4,'c'=2] {'yl'}, dimensions={0} | all-to-all | bytes 1441792 | tf_op jit(solution)/shard_map/all_to_all | solution.py:299
  185.0 16.0 %all_gather.3.attended = bf16[256,1280]{1,0:T(8,128)(2,1)S(1)} all-gather(bf16[32,1280]{1,0:T(8,128)(2,1)S(1)} %divide.1), channel_id=1, replica_groups=mesh['yh'=2,'z'=8,'x'=4,'yl'=4,'c'=2] {'yl','c'}, dimensions={0}, use_global_device_ids=true | all-gather | bytes 737280 | tf_op jit(solution)/shard_map/all_gather | solution.py:301
  (62 shorter events, 11.9 us)
Async XLA Ops:
  0.6 21.2 %copy-start = (bf16[256,256]{1,0:T(8,128)(2,1)S(1)}, bf16[256,256]{1,0:T(8,128)(2,1)}, u32[]{:S(2)}) copy-start(bf16[256,256]{1,0:T(8,128)(2,1)} %param.8) | copy-start | bytes 393220
  0.6 31.8 %copy-start.3 = (bf16[256]{0:T(256)(128)(2,1)S(1)}, bf16[256]{0:T(256)(128)(2,1)}, u32[]{:S(2)}) copy-start(bf16[256]{0:T(256)(128)(2,1)} %param.9) | copy-start | bytes 1540
  1.4 9.6 %collective-permute-start = (bf16[56,256]{1,0:T(8,128)(2,1)S(1)}, bf16[56,256]{1,0:T(8,128)(2,1)S(1)}, u32[]{:S(2)}, u32[]{:S(2)}) collective-permute-start(bf16[56,256]{1,0:T(8,128)(2,1)S(1)} %get-tuple-element.33), channel_id=1, source_target_pairs={{0,256},{256,0},{1,257},{257,1},{2,258},{258,2},{3,259},{259,3},{4... | collective-permute-start | bytes 86024 | tf_op jit(solution)/shard_map/ppermute | solution.py:222
  11.8 24.3 %all-to-all-start = ((bf16[8,2,56,256]{3,2,1,0:T(8,128)(2,1)}), bf16[8,2,56,256]{3,2,1,0:T(8,128)(2,1)S(1)}, u32[]{:S(2)}, u32[]{:S(2)}) async-start(bf16[8,2,56,256]{3,2,1,0:T(8,128)(2,1)} %broadcast_in_dim.48), calls=%async_computation | async-start | bytes 917504 | tf_op jit(solution)/shard_map/all_to_all | solution.py:209
  21.9 14.3 %collective-permute-start.1 = (bf16[256,256]{1,0:T(8,128)(2,1)S(1)}, bf16[256,256]{1,0:T(8,128)(2,1)S(1)}, u32[]{:S(2)}, u32[]{:S(2)}) collective-permute-start(bf16[256,256]{1,0:T(8,128)(2,1)S(1)} %copy-done), channel_id=1, source_target_pairs={{0,8},{8,16},{16,24},{24,0},{1,9},{9,17},{17,25},{25,1},{2,10},{10... | collective-permute-start | bytes 393224 | tf_op jit(solution)/shard_map/ppermute | solution.py:229
  25.0 11.2 %collective-permute-start.2 = (bf16[256,256]{1,0:T(8,128)(2,1)S(1)}, bf16[256,256]{1,0:T(8,128)(2,1)S(1)}, u32[]{:S(2)}, u32[]{:S(2)}) collective-permute-start(bf16[256,256]{1,0:T(8,128)(2,1)S(1)} %copy-done), channel_id=1, source_target_pairs={{0,16},{8,24},{16,0},{24,8},{1,17},{9,25},{17,1},{25,9},{2,18},{10... | collective-permute-start | bytes 393224 | tf_op jit(solution)/shard_map/ppermute | solution.py:229
  29.3 6.8 %collective-permute-start.3 = (bf16[256,256]{1,0:T(8,128)(2,1)S(1)}, bf16[256,256]{1,0:T(8,128)(2,1)S(1)}, u32[]{:S(2)}, u32[]{:S(2)}) collective-permute-start(bf16[256,256]{1,0:T(8,128)(2,1)S(1)} %copy-done), channel_id=1, source_target_pairs={{0,24},{8,0},{16,8},{24,16},{1,25},{9,1},{17,9},{25,17},{2,26},{10... | collective-permute-start | bytes 393224 | tf_op jit(solution)/shard_map/ppermute | solution.py:229
  37.2 6.9 %collective-permute-start.4 = (f32[4,128,512]{2,1,0:T(8,128)S(1)}, f32[4,128,512]{2,1,0:T(8,128)S(1)}, u32[]{:S(2)}, u32[]{:S(2)}) collective-permute-start(f32[4,128,512]{2,1,0:T(8,128)S(1)} %project1.1), channel_id=1, source_target_pairs={{0,1},{1,0},{2,3},{3,2},{4,5},{5,4},{6,7},{7,6},{8,9},{9,8},{10,11... | collective-permute-start | bytes 3145736 | tf_op jit(solution)/shard_map/ppermute | solution.py:243
  45.4 7.1 %copy-start.1 = (s32[4]{0:T(128)S(1)}, s32[4]{0:T(128)}, u32[]{:S(2)}) copy-start(s32[4]{0:T(128)} %lengths.3) | copy-start | bytes 52
  45.4 7.4 %copy-start.4 = (bf16[64]{0:T(256)(128)(2,1)S(1)}, bf16[64]{0:T(256)(128)(2,1)}, u32[]{:S(2)}) copy-start(bf16[64]{0:T(256)(128)(2,1)} %param.11) | copy-start | bytes 388
  45.4 7.5 %copy-start.5 = (bf16[64]{0:T(256)(128)(2,1)S(1)}, bf16[64]{0:T(256)(128)(2,1)}, u32[]{:S(2)}) copy-start(bf16[64]{0:T(256)(128)(2,1)} %param.12) | copy-start | bytes 388
  45.4 34.1 %copy-start.2 = (s32[4]{0:T(128)S(1)}, s32[4]{0:T(128)}, u32[]{:S(2)}) copy-start(s32[4]{0:T(128)} %table.1) | copy-start | bytes 52
  45.4 34.1 %all-to-all-start.1 = ((f32[16,32,512]{2,1,0:T(8,128)}), f32[16,32,512]{2,1,0:T(8,128)S(1)}, u32[]{:S(2)}, u32[]{:S(2)}) async-start(f32[16,32,512]{2,1,0:T(8,128)} %bitcast.14), calls=%async_computation.1 | async-start | bytes 2097152 | tf_op jit(solution)/shard_map/all_to_all | solution.py:246
  82.4 8.6 %collective-permute-start.5 = (bf16[32,640]{1,0:T(8,128)(2,1)S(1)}, bf16[32,640]{1,0:T(8,128)(2,1)S(1)}, u32[]{:S(2)}, u32[]{:S(2)}) collective-permute-start(bf16[32,640]{1,0:T(8,128)(2,1)S(1)} %get-tuple-element.18), channel_id=1, source_target_pairs={{0,256},{256,0},{1,257},{257,1},{2,258},{258,2},{3,259},{259,3},{4... | collective-permute-start | bytes 122888 | tf_op jit(solution)/shard_map/ppermute | solution.py:278
  92.3 57.5 %all-to-all-start.2 = ((bf16[32,32,640]{2,1,0:T(8,128)(2,1)}), bf16[32,32,640]{2,1,0:T(8,128)(2,1)S(1)}, u32[]{:S(2)}, u32[]{:S(2)}) async-start(bf16[32,32,640]{2,1,0:T(8,128)(2,1)} %broadcast_select_fusion), calls=%async_computation.2 | async-start | bytes 2621440 | tf_op jit(solution)/shard_map/all_to_all | solution.py:284
  99.5 12.4 %collective-permute-start.6 = (bf16[8,2,20,256]{3,2,1,0:T(8,128)(2,1)S(1)}, bf16[8,2,20,256]{3,2,1,0:T(8,128)(2,1)S(1)}, u32[]{:S(2)}, u32[]{:S(2)}) collective-permute-start(bf16[8,2,20,256]{3,2,1,0:T(8,128)(2,1)S(1)} %slice.8), channel_id=1, source_target_pairs={{0,24},{8,0},{16,8},{24,16},{1,25},{9,1},{17,9},{25,17},{2,26},{10... | collective-permute-start | bytes 491528 | tf_op jit(solution)/shard_map/ppermute | solution.py:247
  103.9 10.2 %collective-permute-start.7 = (bf16[8,2,20,256]{3,2,1,0:T(8,128)(2,1)S(1)}, bf16[8,2,20,256]{3,2,1,0:T(8,128)(2,1)S(1)}, u32[]{:S(2)}, u32[]{:S(2)}) collective-permute-start(bf16[8,2,20,256]{3,2,1,0:T(8,128)(2,1)S(1)} %slice.8), channel_id=1, source_target_pairs={{0,16},{8,24},{16,0},{24,8},{1,17},{9,25},{17,1},{25,9},{2,18},{10... | collective-permute-start | bytes 491528 | tf_op jit(solution)/shard_map/ppermute | solution.py:247
  106.4 18.0 %collective-permute-start.8 = (bf16[8,2,20,256]{3,2,1,0:T(8,128)(2,1)S(1)}, bf16[8,2,20,256]{3,2,1,0:T(8,128)(2,1)S(1)}, u32[]{:S(2)}, u32[]{:S(2)}) collective-permute-start(bf16[8,2,20,256]{3,2,1,0:T(8,128)(2,1)S(1)} %slice.8), channel_id=1, source_target_pairs={{0,8},{8,16},{16,24},{24,0},{1,9},{9,17},{17,25},{25,1},{2,10},{10... | collective-permute-start | bytes 491528 | tf_op jit(solution)/shard_map/ppermute | solution.py:247
  124.4 17.3 %collective-permute-start.10 = (bf16[32,1280]{1,0:T(8,128)(2,1)S(1)}, bf16[32,1280]{1,0:T(8,128)(2,1)S(1)}, u32[]{:S(2)}, u32[]{:S(2)}) collective-permute-start(bf16[32,1280]{1,0:T(8,128)(2,1)S(1)} %get-tuple-element.21.q0), channel_id=1, source_target_pairs={{0,2},{1,3},{2,4},{3,5},{4,6},{5,7},{6,0},{7,1},{8,10},{9,11},{10,... | collective-permute-start | bytes 245768 | tf_op jit(solution)/shard_map/ppermute | solution.py:280
  127.1 17.3 %collective-permute-start.11 = (bf16[32,1280]{1,0:T(8,128)(2,1)S(1)}, bf16[32,1280]{1,0:T(8,128)(2,1)S(1)}, u32[]{:S(2)}, u32[]{:S(2)}) collective-permute-start(bf16[32,1280]{1,0:T(8,128)(2,1)S(1)} %get-tuple-element.21.q0), channel_id=1, source_target_pairs={{0,3},{1,4},{2,5},{3,6},{4,7},{5,0},{6,1},{7,2},{8,11},{9,12},{10,... | collective-permute-start | bytes 245768 | tf_op jit(solution)/shard_map/ppermute | solution.py:280
  133.5 16.3 %collective-permute-start.12 = (bf16[32,1280]{1,0:T(8,128)(2,1)S(1)}, bf16[32,1280]{1,0:T(8,128)(2,1)S(1)}, u32[]{:S(2)}, u32[]{:S(2)}) collective-permute-start(bf16[32,1280]{1,0:T(8,128)(2,1)S(1)} %get-tuple-element.21.q0), channel_id=1, source_target_pairs={{0,4},{1,5},{2,6},{3,7},{4,0},{5,1},{6,2},{7,3},{8,12},{9,13},{10,... | collective-permute-start | bytes 245768 | tf_op jit(solution)/shard_map/ppermute | solution.py:280
  135.4 14.4 %collective-permute-start.13 = (bf16[32,1280]{1,0:T(8,128)(2,1)S(1)}, bf16[32,1280]{1,0:T(8,128)(2,1)S(1)}, u32[]{:S(2)}, u32[]{:S(2)}) collective-permute-start(bf16[32,1280]{1,0:T(8,128)(2,1)S(1)} %get-tuple-element.21.q0), channel_id=1, source_target_pairs={{0,5},{1,6},{2,7},{3,0},{4,1},{5,2},{6,3},{7,4},{8,13},{9,14},{10,... | collective-permute-start | bytes 245768 | tf_op jit(solution)/shard_map/ppermute | solution.py:280
  139.5 10.3 %collective-permute-start.14 = (bf16[32,1280]{1,0:T(8,128)(2,1)S(1)}, bf16[32,1280]{1,0:T(8,128)(2,1)S(1)}, u32[]{:S(2)}, u32[]{:S(2)}) collective-permute-start(bf16[32,1280]{1,0:T(8,128)(2,1)S(1)} %get-tuple-element.21.q0), channel_id=1, source_target_pairs={{0,6},{1,7},{2,0},{3,1},{4,2},{5,3},{6,4},{7,5},{8,14},{9,15},{10,... | collective-permute-start | bytes 245768 | tf_op jit(solution)/shard_map/ppermute | solution.py:280
  141.8 8.1 %collective-permute-start.15 = (bf16[32,1280]{1,0:T(8,128)(2,1)S(1)}, bf16[32,1280]{1,0:T(8,128)(2,1)S(1)}, u32[]{:S(2)}, u32[]{:S(2)}) collective-permute-start(bf16[32,1280]{1,0:T(8,128)(2,1)S(1)} %get-tuple-element.21.q0), channel_id=1, source_target_pairs={{0,7},{1,0},{2,1},{3,2},{4,3},{5,4},{6,5},{7,6},{8,15},{9,8},{10,9... | collective-permute-start | bytes 245768 | tf_op jit(solution)/shard_map/ppermute | solution.py:280
  144.4 5.5 %collective-permute-start.9 = (bf16[32,1280]{1,0:T(8,128)(2,1)S(1)}, bf16[32,1280]{1,0:T(8,128)(2,1)S(1)}, u32[]{:S(2)}, u32[]{:S(2)}) collective-permute-start(bf16[32,1280]{1,0:T(8,128)(2,1)S(1)} %get-tuple-element.21.q0), channel_id=1, source_target_pairs={{0,1},{1,2},{2,3},{3,4},{4,5},{5,6},{6,7},{7,0},{8,9},{9,10},{10,1... | collective-permute-start | bytes 245768 | tf_op jit(solution)/shard_map/ppermute | solution.py:280
  154.2 9.3 %collective-permute-start.16 = (f32[4,32,1408]{2,1,0:T(8,128)S(1)}, f32[4,32,1408]{2,1,0:T(8,128)S(1)}, u32[]{:S(2)}, u32[]{:S(2)}) collective-permute-start(f32[4,32,1408]{2,1,0:T(8,128)S(1)} %attend1.1), channel_id=1, source_target_pairs={{0,1},{1,0},{2,3},{3,2},{4,5},{5,4},{6,7},{7,6},{8,9},{9,8},{10,11... | collective-permute-start | bytes 2162696 | tf_op jit(solution)/shard_map/ppermute | solution.py:298

commit v3 on v2

--- a/solution.py
+++ b/solution.py
@@ -80,7 +80,7 @@
             if x == 0 and tile == 0:
                 inverse = lax.rsqrt(source[:, 30:31] / D + 1e-06)
             for piece in range(4):
-                z, yh = divmod(tile * 4 + piece, 2)
+                yh, z = divmod(tile * 4 + piece, 8)
                 start = PIECE * (yh * 32 + z * 4 + x)
                 moved = pltpu.roll(source, (start - piece * 32) % 128, 1)
                 for place_at in range(start // 128, (start + PIECE - 1) // 128 + 1):
@@ -114,10 +114,11 @@
         cache[pl.ds(table[p], 1)] = kv[p * 8 : p * 8 + 8, :].reshape(1, 8, KV_DIM)
 
 
-def attend_body(flip, place, lengths, q0, q1, q2, q3, blocks, far, out, bias, bias_far):
-    yh, index, wide, narrow = place[0], place[1], place[2], place[4]
+def attend_body(flip, place, lengths, q, blocks, far, out, bias, bias_far):
+    yh, index, wide, narrow, yl = place[0], place[1], place[2], place[4], place[6]
+    core = place[3] if not flip else 1 - place[3]
     row = lax.broadcasted_iota(jnp.int32, (128, 1), 0)
-    owner = (narrow + 8 - flip - row // ROWS * 2) & 7
+    owner = ((yl + 4 - row // ROWS) & 3) * 2 + core
     token = wide * TOK_DEV + (row % ROWS) // 8 * PAGE + owner * 8 + row % 8
     begin = jnp.zeros_like(token)
     end = jnp.int32(0)
@@ -138,8 +139,8 @@
     for chunk in range(4):
         bias[chunk] = hide(chunk * 8, 256, False)
     bias_far[...] = hide(index, ROWS, True)
-    half = jnp.concatenate([q0[...], q1[...], q2[...], q3[...]], axis=0)
-    owners = [((narrow + 8 - flip - 2 * k) & 7) // 2 for k in range(4)]
+    half = q[...].reshape(128, Q_DIM)
+    owners = [(yl + 4 - k) & 3 for k in range(4)]
     out[:, :, Q_DIM:] = jnp.zeros((4, ROWS, 128), F32)
     for g in range(KV_HEADS):
         heads = [
@@ -205,6 +206,15 @@
             out[p, n] = (hidden[p, n].astype(F32) + mixed[at : at + 8]).astype(BF)
 
 
+def order_body(place, blocks, out):
+    x, z = place[5], place[1] // 4
+    for i in range(4):
+        for k in range(8):
+            at = ((z + 8 - k) & 7) * 4 + ((x + 4 - i) & 3)
+            for yh in range(2):
+                out[pl.ds(yh * 32 + at, 1)] = blocks[i, k, yh][None]
+
+
 def spread(x, axes, count):
     return lax.all_to_all(jnp.broadcast_to(x[None], (count,) + x.shape), axes, 0, 0)
 
@@ -215,21 +225,25 @@
     index = z * 4 + x
     wide = yh * 32 + index
     narrow = yl * 2 + core
-    place = jnp.stack([yh, index, wide, core, narrow, x]).astype(jnp.int32)
+    place = jnp.stack([yh, index, wide, core, narrow, x, yl]).astype(jnp.int32)
     swap = [(0, 1), (1, 0)]
 
-    def both(own):
-        other = lax.ppermute(own, "yh", swap)
-        return jnp.where(yh == 0, jnp.stack([own, other]), jnp.stack([other, own]))
-
-    own = jnp.concatenate(
-        [jnp.pad(qkv_weight.T, ((0, 2), (0, 0))), jnp.pad(out_weight, ((0, 4), (0, 0)))], axis=0
-    )
-    shifts = [[(i, (i + step) % 4) for i in range(4)] for step in range(4)]
-    hidden = [hidden_in] + [lax.ppermute(hidden_in, "x", shifts[step]) for step in range(1, 4)]
-    gathered = spread(both(own), "z", 8)
-    weight = gathered[:, :, :32].reshape(512, TOK_DEV)
-    mixing = gathered[:, :, 32:52]
+    def shift(value, axis, count, step):
+        return lax.ppermute(value, axis, [(i, (i + step) % count) for i in range(count)])
+
+    def gather(value, axis, count):
+        step = 1
+        while step < count:
+            value = jnp.concatenate([value, shift(value, axis, count, step)], axis=0)
+            step *= 2
+        return value
+
+    hidden = [hidden_in] + [shift(hidden_in, "x", 4, step) for step in range(1, 4)]
+    columns = jnp.pad(qkv_weight.T, ((0, 2), (0, 0)))
+    weight = spread(columns, ("yh", "z"), 16).reshape(512, TOK_DEV)
+    other = lax.ppermute(out_weight, "yh", swap)
+    weight, other = lax.optimization_barrier((weight, other))
+    mixing = jnp.where(yh == 0, jnp.stack([out_weight, other]), jnp.stack([other, out_weight]))
     hidden = [h.reshape(PAGES_DEV, 4, 2, 8, 256) for h in hidden]
     gain = attn_gain.reshape(1, 256)
     half_shape = jax.ShapeDtypeStruct((4, 128, 512), F32)
@@ -244,10 +258,8 @@
     partial = (project(0) + arrived).reshape(16, ROWS, 512)
     mixing, partial = lax.optimization_barrier((mixing, partial))
     parts = lax.all_to_all(partial, ("x", "yl"), 0, 0)
-    ring = [mixing] + [lax.ppermute(mixing, "x", shifts[step]) for step in range(1, 4)]
-    ring = jnp.stack([ring[(3 - k) % 4] for k in range(7)])
-    mixing = lax.dynamic_slice_in_dim(ring, 3 - x, 4, 0)
-    mixing = mixing.transpose(2, 1, 0, 3, 4).reshape(Q_DIM, 256)
+    mixing = gather(mixing[None], "z", 8)
+    mixing, parts = lax.optimization_barrier((mixing, parts))
 
     row = jnp.arange(ROWS, dtype=jnp.int32)
     own = wide * TOK_DEV + row // 8 * PAGE + narrow * 8 + row % 8
@@ -276,23 +288,24 @@
     )
 
     far = lax.ppermute(kv, "yh", swap)
-    all_queries = [queries] + [
-        lax.ppermute(queries, ("yl", "c"), [(i, (i + step) % 8) for i in range(8)])
-        for step in range(1, 8)
-    ]
+    kept = gather(queries[None], "yl", 4)
+    given = lax.ppermute(kept, "c", swap)
+    mixing = call(order_body, jax.ShapeDtypeStruct((64, 20, 256), BF), [SM, VM], "order")(
+        place, gather(mixing[None], "x", 4)
+    ).reshape(Q_DIM, 256)
     target = jnp.arange(32, dtype=jnp.int32)[:, None, None]
     blocks = lax.all_to_all(jnp.where(target >= index, kv[None], far[None]), ("z", "x"), 0, 0)
 
-    blocks, mixing, all_queries = lax.optimization_barrier((blocks, mixing, all_queries))
+    blocks, mixing, kept, given = lax.optimization_barrier((blocks, mixing, kept, given))
 
     def attend(flip):
         return call(
             functools.partial(attend_body, flip),
             jax.ShapeDtypeStruct((4, ROWS, SUMS), F32),
-            [SM, SM] + [VM] * 6,
+            [SM, SM] + [VM] * 3,
             f"attend{flip}",
             [pltpu.VMEM((4, 128, 256), F32), pltpu.VMEM((128, ROWS), F32)],
-        )(place, lengths, *all_queries[flip::2], blocks, far)
+        )(place, lengths, given if flip else kept, blocks, far)
 
     sent = attend(1)
     arrived = lax.ppermute(sent, "c", swap)

time: 203 us -> 188 us (0.926)
  waiting for transfers between devices: 51.6 us -> 32.4 us
  starting transfers between devices: 89.9 us -> 92.3 us
    all_to_all x1, waiting for transfers between devices: 26.3 us -> 3.5 us  [on_device(): parts = lax.all_to_all(partial, ('x', 'yl'), 0, 0)]
    ppermute x14 -> x12, waiting for transfers between devices: 16.7 us -> 26.3 us  [the longest x10 25.7 us: shift(): lax.ppermute(value, axis, [(i, (i + step) % count) for i in range(count)])]
    all_to_all x1, starting transfers between devices: 10 us -> 16.2 us  [spread(): lax.all_to_all(jnp.broadcast_to(x[None], (count,) + x.shape), axes, 0, 0)]
    all_to_all x1, waiting for transfers between devices: 3.59 us -> 0.01 us  [spread(): lax.all_to_all(jnp.broadcast_to(x[None], (count,) + x.shape), axes, 0, 0)]
    all_to_all x1, starting transfers between devices: 7.09 us -> 3.8 us  [on_device(): parts = lax.all_to_all(partial, ('x', 'yl'), 0, 0)]
    ppermute x14 -> x12, starting transfers between devices: 51.1 us -> 48 us  [the longest x10 33.8 us: shift(): lax.ppermute(value, axis, [(i, (i + step) % count) for i in range(count)])]
    ppermute x1, starting transfers between devices: 4.83 us -> 7.44 us  [on_device(): far = lax.ppermute(kv, 'yh', swap)]
    ppermute x1, waiting for transfers between devices: 3.79 us -> 1.36 us  [on_device(): far = lax.ppermute(kv, 'yh', swap)]
  transfers between devices with their start and end apart: 20 -> 18, of which waited for: 8 -> 10; matrix products, arithmetic and copies ran while one was open for 2% -> 1% of each run, Pallas kernels for 3% -> 3%
where the time goes in v3:
time: 188 us; the launch traced here: 187 us
  starting transfers between devices  92.3 us (49%)
  blocking collectives  39.1 us (21%)
  waiting for transfers between devices  32.4 us (17%)
  Pallas kernels  15.8 us (8%)
  local copies, waits for them, and re-layouts  3.52 us (2%)
  other arithmetic  3.23 us (2%)
    ppermute x10, starting transfers between devices, shift(): lax.ppermute(value, axis, [(i, (i + step) % count) for i in range(count)])  33.8 us
    ppermute x10, waiting for transfers between devices, shift(): lax.ppermute(value, axis, [(i, (i + step) % count) for i in range(count)])  25.7 us
    all_to_all x1, blocking collectives, on_device(): parts = lax.all_to_all(attend(0) + arrived, 'yl', 0, 0)  22.5 us
    all_gather x1, blocking collectives, on_device(): attended = lax.all_gather(attended, ('yl', 'c'), axis=0, tiled=True)  16.6 us
    all_to_all x1, starting transfers between devices, spread(): lax.all_to_all(jnp.broadcast_to(x[None], (count,) + x.shape), axes, 0, 0)  16.2 us
    ppermute x2, starting transfers between devices, on_device(): arrived = lax.ppermute(sent, 'c', swap)  9.24 us
    pallas_call x2, Pallas kernels, attend(): call(functools.partial(attend_body, flip), jax.ShapeDtypeStruct((4, ROWS,...  9.05 us
    all_to_all x1, starting transfers between devices, on_device(): lax.all_to_all(jnp.where(target >= index, kv[None], far[None]), ('z', 'x'...  7.59 us
  transfers between devices with their start and end apart: 18, of which 10 were waited for; matrix products, arithmetic and copies ran while one was open for 1% of the time, Pallas kernels for 3%

profile of v3, /device:TPU:1, one launch (start us, length us, event | category | flops | bytes accessed | tf_op | source)
XLA Modules:
  0.0 187.4 jit_solution(7854991642358681740)
XLA Ops:
  2.1 16.2 %all-to-all-start = ((bf16[16,32,256]{2,1,0:T(8,128)(2,1)}), bf16[16,32,256]{2,1,0:T(8,128)(2,1)S(1)}, u32[]{:S(2)}, u32[]{:S(2)}) async-start(bf16[16,32,256]{2,1,0:T(8,128)(2,1)} %broadcast_in_dim.57), calls=%async_computation | async-start | bytes 524288 | tf_op jit(solution)/shard_map/all_to_all | solution.py:219
  18.3 3.1 %collective-permute-start.1 = (bf16[256,256]{1,0:T(8,128)(2,1)}, bf16[256,256]{1,0:T(8,128)(2,1)S(1)}, u32[]{:S(2)}, u32[]{:S(2)}) collective-permute-start(bf16[256,256]{1,0:T(8,128)(2,1)} %param.8), channel_id=1, source_target_pairs={{0,8},{8,16},{16,24},{24,0},{1,9},{9,17},{17,25},{25,1},{2,10},{10... | collective-permute-start | bytes 393224 | tf_op jit(solution)/shard_map/ppermute | solution.py:232
  21.5 4.4 %collective-permute-start.2 = (bf16[256,256]{1,0:T(8,128)(2,1)}, bf16[256,256]{1,0:T(8,128)(2,1)S(1)}, u32[]{:S(2)}, u32[]{:S(2)}) collective-permute-start(bf16[256,256]{1,0:T(8,128)(2,1)} %param.8), channel_id=1, source_target_pairs={{0,16},{8,24},{16,0},{24,8},{1,17},{9,25},{17,1},{25,9},{2,18},{10... | collective-permute-start | bytes 393224 | tf_op jit(solution)/shard_map/ppermute | solution.py:232
  25.8 3.1 %collective-permute-start.3 = (bf16[256,256]{1,0:T(8,128)(2,1)}, bf16[256,256]{1,0:T(8,128)(2,1)S(1)}, u32[]{:S(2)}, u32[]{:S(2)}) collective-permute-start(bf16[256,256]{1,0:T(8,128)(2,1)} %param.8), channel_id=1, source_target_pairs={{0,24},{8,0},{16,8},{24,16},{1,25},{9,1},{17,9},{25,17},{2,26},{10... | collective-permute-start | bytes 393224 | tf_op jit(solution)/shard_map/ppermute | solution.py:232
  28.9 7.2 %collective-permute-start = (bf16[20,256]{1,0:T(8,128)(2,1)}, bf16[20,256]{1,0:T(8,128)(2,1)S(1)}, u32[]{:S(2)}, u32[]{:S(2)}) collective-permute-start(bf16[20,256]{1,0:T(8,128)(2,1)} %param.13), channel_id=1, source_target_pairs={{0,256},{256,0},{1,257},{257,1},{2,258},{258,2},{3,259},{259,3},{4... | collective-permute-start | bytes 30728 | tf_op jit(solution)/shard_map/ppermute | solution.py:244
  39.4 4.9 %collective-permute-start.4 = (f32[4,128,512]{2,1,0:T(8,128)S(1)}, f32[4,128,512]{2,1,0:T(8,128)S(1)}, u32[]{:S(2)}, u32[]{:S(2)}) collective-permute-start(f32[4,128,512]{2,1,0:T(8,128)S(1)} %project1.1), channel_id=1, source_target_pairs={{0,1},{1,0},{2,3},{3,2},{4,5},{5,4},{6,7},{7,6},{8,9},{9,8},{10,11... | collective-permute-start | bytes 3145736 | tf_op jit(solution)/shard_map/ppermute | solution.py:257
  47.8 3.8 %all-to-all-start.1 = ((f32[16,32,512]{2,1,0:T(8,128)}), f32[16,32,512]{2,1,0:T(8,128)S(1)}, u32[]{:S(2)}, u32[]{:S(2)}) async-start(f32[16,32,512]{2,1,0:T(8,128)} %bitcast.15), calls=%async_computation.1 | async-start | bytes 2097152 | tf_op jit(solution)/shard_map/all_to_all | solution.py:260
  51.9 3.5 %collective-permute-start.5 = (bf16[1,2,20,256]{3,2,1,0:T(8,128)(2,1)S(1)}, bf16[1,2,20,256]{3,2,1,0:T(8,128)(2,1)S(1)}, u32[]{:S(2)}, u32[]{:S(2)}) collective-permute-start(bf16[1,2,20,256]{3,2,1,0:T(8,128)(2,1)S(1)} %bitcast.41), channel_id=1, source_target_pairs={{0,32},{32,64},{64,96},{96,128},{128,160},{160,192},{192,224},{224... | collective-permute-start | bytes 61448 | tf_op jit(solution)/shard_map/ppermute | solution.py:232
  55.4 2.7 %collective-permute-done.5 = bf16[1,2,20,256]{3,2,1,0:T(8,128)(2,1)S(1)} collective-permute-done((bf16[1,2,20,256]{3,2,1,0:T(8,128)(2,1)S(1)}, bf16[1,2,20,256]{3,2,1,0:T(8,128)(2,1)S(1)}, u32[]{:S(2)}, u32[]{:S(2)}) %collective-permute-start.5) | collective-permute-done | bytes 20512 | tf_op jit(solution)/shard_map/ppermute | solution.py:232
  58.1 3.0 %collective-permute-start.6 = (bf16[2,2,20,256]{3,2,1,0:T(8,128)(2,1)S(1)}, bf16[2,2,20,256]{3,2,1,0:T(8,128)(2,1)S(1)}, u32[]{:S(2)}, u32[]{:S(2)}) collective-permute-start(bf16[2,2,20,256]{3,2,1,0:T(8,128)(2,1)S(1)} %pad_maximum_fusion.6), channel_id=1, source_target_pairs={{0,64},{32,96},{64,128},{96,160},{128,192},{160,224},{192,0},{224,... | collective-permute-start | bytes 122888 | tf_op jit(solution)/shard_map/ppermute | solution.py:232
  61.3 4.6 %collective-permute-done.6 = bf16[2,2,20,256]{3,2,1,0:T(8,128)(2,1)S(1)} collective-permute-done((bf16[2,2,20,256]{3,2,1,0:T(8,128)(2,1)S(1)}, bf16[2,2,20,256]{3,2,1,0:T(8,128)(2,1)S(1)}, u32[]{:S(2)}, u32[]{:S(2)}) %collective-permute-start.6) | collective-permute-done | bytes 40992 | tf_op jit(solution)/shard_map/ppermute | solution.py:232
  65.9 7.1 %collective-permute-start.7 = (bf16[4,2,20,256]{3,2,1,0:T(8,128)(2,1)S(1)}, bf16[4,2,20,256]{3,2,1,0:T(8,128)(2,1)S(1)}, u32[]{:S(2)}, u32[]{:S(2)}) collective-permute-start(bf16[4,2,20,256]{3,2,1,0:T(8,128)(2,1)S(1)} %pad_maximum_fusion.5), channel_id=1, source_target_pairs={{0,128},{32,160},{64,192},{96,224},{128,0},{160,32},{192,64},{224,... | collective-permute-start | bytes 245768 | tf_op jit(solution)/shard_map/ppermute | solution.py:232
  73.4 1.9 %collective-permute-done.7 = bf16[4,2,20,256]{3,2,1,0:T(8,128)(2,1)S(1)} collective-permute-done((bf16[4,2,20,256]{3,2,1,0:T(8,128)(2,1)S(1)}, bf16[4,2,20,256]{3,2,1,0:T(8,128)(2,1)S(1)}, u32[]{:S(2)}, u32[]{:S(2)}) %collective-permute-start.7) | collective-permute-done | bytes 81952 | tf_op jit(solution)/shard_map/ppermute | solution.py:232
  75.3 3.5 %all-to-all-done.1.parts = f32[16,32,512]{2,1,0:T(8,128)S(1)} async-done(((f32[16,32,512]{2,1,0:T(8,128)}), f32[16,32,512]{2,1,0:T(8,128)S(1)}, u32[]{:S(2)}, u32[]{:S(2)}) %all-to-all-start.1) | async-done | bytes 1048608 | tf_op jit(solution)/shard_map/all_to_all | solution.py:260
  78.8 2.9 %rotate.1 = (bf16[32,1280]{1,0:T(8,128)(2,1)S(1)}, bf16[32,640]{1,0:T(8,128)(2,1)S(1)}, bf16[4,8,640]{2,1,0:T(8,128)(2,1)}) custom-call(s32[4]{0:T(128)S(1)} %copy-done.3, f32[16,32,512]{2,1,0:T(8,128)S(1)} %all-to-all-done.1.parts, f32[32,128]{1,0:T(8,128)S(1)} %get-tuple-element.29.cosine, f32[32,128]{1,0:T(8,128)S(1)} %get-tuple-element.28.sine, ...), custom_call_target="tpu_custom_call" | custom-call | tf_op jit(solution)/shard_map/rotate/pallas_call | solution.py:272
  81.6 7.4 %collective-permute-start.8 = (bf16[32,640]{1,0:T(8,128)(2,1)S(1)}, bf16[32,640]{1,0:T(8,128)(2,1)S(1)}, u32[]{:S(2)}, u32[]{:S(2)}) collective-permute-start(bf16[32,640]{1,0:T(8,128)(2,1)S(1)} %get-tuple-element.20), channel_id=1, source_target_pairs={{0,256},{256,0},{1,257},{257,1},{2,258},{258,2},{3,259},{259,3},{4... | collective-permute-start | bytes 122888 | tf_op jit(solution)/shard_map/ppermute | solution.py:290
  89.1 1.4 collective-permute-done.8.far
  90.5 1.3 broadcast_select_fusion
  91.7 7.6 %all-to-all-start.2 = ((bf16[32,32,640]{2,1,0:T(8,128)(2,1)}), bf16[32,32,640]{2,1,0:T(8,128)(2,1)S(1)}, u32[]{:S(2)}, u32[]{:S(2)}) async-start(bf16[32,32,640]{2,1,0:T(8,128)(2,1)} %broadcast_select_fusion), calls=%async_computation.2 | async-start | bytes 2621440 | tf_op jit(solution)/shard_map/all_to_all | solution.py:297
  99.3 1.9 %collective-permute-start.11 = (bf16[1,32,1280]{2,1,0:T(8,128)(2,1)S(1)}, bf16[1,32,1280]{2,1,0:T(8,128)(2,1)S(1)}, u32[]{:S(2)}, u32[]{:S(2)}) collective-permute-start(bf16[1,32,1280]{2,1,0:T(8,128)(2,1)S(1)} %bitcast.34), channel_id=1, source_target_pairs={{0,2},{2,4},{4,6},{6,0},{1,3},{3,5},{5,7},{7,1},{8,10},{10,12},{12... | collective-permute-start | bytes 245768 | tf_op jit(solution)/shard_map/ppermute | solution.py:232
  101.2 3.1 %collective-permute-start.9 = (bf16[1,8,2,20,256]{4,3,2,1,0:T(8,128)(2,1)S(1)}, bf16[1,8,2,20,256]{4,3,2,1,0:T(8,128)(2,1)S(1)}, u32[]{:S(2)}, u32[]{:S(2)}) collective-permute-start(bf16[1,8,2,20,256]{4,3,2,1,0:T(8,128)(2,1)S(1)} %bitcast.38), channel_id=1, source_target_pairs={{0,8},{8,16},{16,24},{24,0},{1,9},{9,17},{17,25},{25,1},{2,10},{10... | collective-permute-start | bytes 491528 | tf_op jit(solution)/shard_map/ppermute | solution.py:232
  104.4 1.9 %collective-permute-done.11 = bf16[1,32,1280]{2,1,0:T(8,128)(2,1)S(1)} collective-permute-done((bf16[1,32,1280]{2,1,0:T(8,128)(2,1)S(1)}, bf16[1,32,1280]{2,1,0:T(8,128)(2,1)S(1)}, u32[]{:S(2)}, u32[]{:S(2)}) %collective-permute-start.11) | collective-permute-done | bytes 81952 | tf_op jit(solution)/shard_map/ppermute | solution.py:232
  106.3 2.5 %collective-permute-start.12 = (bf16[2,32,1280]{2,1,0:T(8,128)(2,1)S(1)}, bf16[2,32,1280]{2,1,0:T(8,128)(2,1)S(1)}, u32[]{:S(2)}, u32[]{:S(2)}) collective-permute-start(bf16[2,32,1280]{2,1,0:T(8,128)(2,1)S(1)} %pad_maximum_fusion.4), channel_id=1, source_target_pairs={{0,4},{2,6},{4,0},{6,2},{1,5},{3,7},{5,1},{7,3},{8,12},{10,14},{12... | collective-permute-start | bytes 491528 | tf_op jit(solution)/shard_map/ppermute | solution.py:232
  108.8 4.4 %collective-permute-done.9 = bf16[1,8,2,20,256]{4,3,2,1,0:T(8,128)(2,1)S(1)} collective-permute-done((bf16[1,8,2,20,256]{4,3,2,1,0:T(8,128)(2,1)S(1)}, bf16[1,8,2,20,256]{4,3,2,1,0:T(8,128)(2,1)S(1)}, u32[]{:S(2)}, u32[]{:S(2)}) %collective-permute-start.9) | collective-permute-done | bytes 163872 | tf_op jit(solution)/shard_map/ppermute | solution.py:232
  113.3 1.9 %collective-permute-start.10 = (bf16[2,8,2,20,256]{4,3,2,1,0:T(8,128)(2,1)S(1)}, bf16[2,8,2,20,256]{4,3,2,1,0:T(8,128)(2,1)S(1)}, u32[]{:S(2)}, u32[]{:S(2)}) collective-permute-start(bf16[2,8,2,20,256]{4,3,2,1,0:T(8,128)(2,1)S(1)} %pad_maximum_fusion.1), channel_id=1, source_target_pairs={{0,16},{8,24},{16,0},{24,8},{1,17},{9,25},{17,1},{25,9},{2,18},{10... | collective-permute-start | bytes 983048 | tf_op jit(solution)/shard_map/ppermute | solution.py:232
  115.3 7.1 %collective-permute-start.13 = (bf16[4,32,1280]{2,1,0:T(8,128)(2,1)S(1)}, bf16[4,32,1280]{2,1,0:T(8,128)(2,1)}, u32[]{:S(2)}, u32[]{:S(2)}) collective-permute-start(bf16[4,32,1280]{2,1,0:T(8,128)(2,1)S(1)} %pad_maximum_fusion.2.q), channel_id=1, source_target_pairs={{0,1},{1,0},{2,3},{3,2},{4,5},{5,4},{6,7},{7,6},{8,9},{9,8},{10,11... | collective-permute-start | bytes 983048 | tf_op jit(solution)/shard_map/ppermute | solution.py:292
  122.4 10.2 %collective-permute-done.10 = bf16[2,8,2,20,256]{4,3,2,1,0:T(8,128)(2,1)S(1)} collective-permute-done((bf16[2,8,2,20,256]{4,3,2,1,0:T(8,128)(2,1)S(1)}, bf16[2,8,2,20,256]{4,3,2,1,0:T(8,128)(2,1)S(1)}, u32[]{:S(2)}, u32[]{:S(2)}) %collective-permute-start.10) | collective-permute-done | bytes 327712 | tf_op jit(solution)/shard_map/ppermute | solution.py:232
  133.5 4.7 %attend1.1 = f32[4,32,1408]{2,1,0:T(8,128)S(1)} custom-call(s32[7]{0:T(128)S(1)} %stack.45.place, s32[4]{0:T(128)S(1)} %copy-done.2, bf16[4,32,1280]{2,1,0:T(8,128)(2,1)} %collective-permute-done.13.q, bf16[32,32,640]{2,1,0:T(8,128)(2,1)S(1)} %all-to-all-done.2.blocks, bf16[32,640]{1,0:T(8,128)(2,1)S(1)} %collective-permute-done.8.far), custom_call_target="tpu_custom_call" | custom-call | tf_op jit(solution)/shard_map/attend1/pallas_call | solution.py:302
  138.2 4.4 %collective-permute-start.14 = (f32[4,32,1408]{2,1,0:T(8,128)S(1)}, f32[4,32,1408]{2,1,0:T(8,128)S(1)}, u32[]{:S(2)}, u32[]{:S(2)}) collective-permute-start(f32[4,32,1408]{2,1,0:T(8,128)S(1)} %attend1.1), channel_id=1, source_target_pairs={{0,1},{1,0},{2,3},{3,2},{4,5},{5,4},{6,7},{7,6},{8,9},{9,8},{10,11... | collective-permute-start | bytes 2162696 | tf_op jit(solution)/shard_map/ppermute | solution.py:311
  142.6 4.3 %attend0.1 = f32[4,32,1408]{2,1,0:T(8,128)S(1)} custom-call(s32[7]{0:T(128)S(1)} %stack.45.place, s32[4]{0:T(128)S(1)} %copy-done.2, bf16[4,32,1280]{2,1,0:T(8,128)(2,1)S(1)} %pad_maximum_fusion.2.q, bf16[32,32,640]{2,1,0:T(8,128)(2,1)S(1)} %all-to-all-done.2.blocks, bf16[32,640]{1,0:T(8,128)(2,1)S(1)} %collective-permute-done.8.far), custom_call_target="tpu_custom_call" | custom-call | tf_op jit(solution)/shard_map/attend0/pallas_call | solution.py:302
  147.0 22.5 %all_to_all.20.parts = f32[4,32,1408]{2,1,0:T(8,128)S(1)} all-to-all(f32[4,32,1408]{2,1,0:T(8,128)S(1)} %add.84), channel_id=1, replica_groups=mesh['yh'=2,'z'=8,'x'=4,'yl'=4,'c'=2] {'yl'}, dimensions={0} | all-to-all | bytes 1441792 | tf_op jit(solution)/shard_map/all_to_all | solution.py:312
  169.7 16.6 %all_gather.3.attended = bf16[256,1280]{1,0:T(8,128)(2,1)S(1)} all-gather(bf16[32,1280]{1,0:T(8,128)(2,1)S(1)} %divide.1), channel_id=1, replica_groups=mesh['yh'=2,'z'=8,'x'=4,'yl'=4,'c'=2] {'yl','c'}, dimensions={0}, use_global_device_ids=true | all-gather | bytes 737280 | tf_op jit(solution)/shard_map/all_gather | solution.py:314
  (57 shorter events, 11.2 us)
Async XLA Ops:
  1.4 42.9 %copy-start.1 = (bf16[256,256]{1,0:T(8,128)(2,1)S(1)}, bf16[256,256]{1,0:T(8,128)(2,1)}, u32[]{:S(2)}) copy-start(bf16[256,256]{1,0:T(8,128)(2,1)} %param.8) | copy-start | bytes 393220
  2.1 35.4 %all-to-all-start = ((bf16[16,32,256]{2,1,0:T(8,128)(2,1)}), bf16[16,32,256]{2,1,0:T(8,128)(2,1)S(1)}, u32[]{:S(2)}, u32[]{:S(2)}) async-start(bf16[16,32,256]{2,1,0:T(8,128)(2,1)} %broadcast_in_dim.57), calls=%async_computation | async-start | bytes 524288 | tf_op jit(solution)/shard_map/all_to_all | solution.py:219
  18.3 19.1 %collective-permute-start.1 = (bf16[256,256]{1,0:T(8,128)(2,1)}, bf16[256,256]{1,0:T(8,128)(2,1)S(1)}, u32[]{:S(2)}, u32[]{:S(2)}) collective-permute-start(bf16[256,256]{1,0:T(8,128)(2,1)} %param.8), channel_id=1, source_target_pairs={{0,8},{8,16},{16,24},{24,0},{1,9},{9,17},{17,25},{25,1},{2,10},{10... | collective-permute-start | bytes 393224 | tf_op jit(solution)/shard_map/ppermute | solution.py:232
  21.5 16.0 %collective-permute-start.2 = (bf16[256,256]{1,0:T(8,128)(2,1)}, bf16[256,256]{1,0:T(8,128)(2,1)S(1)}, u32[]{:S(2)}, u32[]{:S(2)}) collective-permute-start(bf16[256,256]{1,0:T(8,128)(2,1)} %param.8), channel_id=1, source_target_pairs={{0,16},{8,24},{16,0},{24,8},{1,17},{9,25},{17,1},{25,9},{2,18},{10... | collective-permute-start | bytes 393224 | tf_op jit(solution)/shard_map/ppermute | solution.py:232
  25.8 11.6 %collective-permute-start.3 = (bf16[256,256]{1,0:T(8,128)(2,1)}, bf16[256,256]{1,0:T(8,128)(2,1)S(1)}, u32[]{:S(2)}, u32[]{:S(2)}) collective-permute-start(bf16[256,256]{1,0:T(8,128)(2,1)} %param.8), channel_id=1, source_target_pairs={{0,24},{8,0},{16,8},{24,16},{1,25},{9,1},{17,9},{25,17},{2,26},{10... | collective-permute-start | bytes 393224 | tf_op jit(solution)/shard_map/ppermute | solution.py:232
  28.9 8.6 %collective-permute-start = (bf16[20,256]{1,0:T(8,128)(2,1)}, bf16[20,256]{1,0:T(8,128)(2,1)S(1)}, u32[]{:S(2)}, u32[]{:S(2)}) collective-permute-start(bf16[20,256]{1,0:T(8,128)(2,1)} %param.13), channel_id=1, source_target_pairs={{0,256},{256,0},{1,257},{257,1},{2,258},{258,2},{3,259},{259,3},{4... | collective-permute-start | bytes 30728 | tf_op jit(solution)/shard_map/ppermute | solution.py:244
  37.5 0.9 copy-start
  39.4 5.9 %copy-start.4 = (bf16[20,256]{1,0:T(8,128)(2,1)S(1)}, bf16[20,256]{1,0:T(8,128)(2,1)}, u32[]{:S(2)}) copy-start(bf16[20,256]{1,0:T(8,128)(2,1)} %param.13) | copy-start | bytes 30724
  39.4 7.1 %collective-permute-start.4 = (f32[4,128,512]{2,1,0:T(8,128)S(1)}, f32[4,128,512]{2,1,0:T(8,128)S(1)}, u32[]{:S(2)}, u32[]{:S(2)}) collective-permute-start(f32[4,128,512]{2,1,0:T(8,128)S(1)} %project1.1), channel_id=1, source_target_pairs={{0,1},{1,0},{2,3},{3,2},{4,5},{5,4},{6,7},{7,6},{8,9},{9,8},{10,11... | collective-permute-start | bytes 3145736 | tf_op jit(solution)/shard_map/ppermute | solution.py:257
  47.8 3.8 %copy-start.2 = (s32[4]{0:T(128)S(1)}, s32[4]{0:T(128)}, u32[]{:S(2)}) copy-start(s32[4]{0:T(128)} %lengths.3) | copy-start | bytes 52
  47.8 25.4 %copy-start.5 = (bf16[64]{0:T(256)(128)(2,1)S(1)}, bf16[64]{0:T(256)(128)(2,1)}, u32[]{:S(2)}) copy-start(bf16[64]{0:T(256)(128)(2,1)} %param.11) | copy-start | bytes 388
  47.8 25.5 %copy-start.6 = (bf16[64]{0:T(256)(128)(2,1)S(1)}, bf16[64]{0:T(256)(128)(2,1)}, u32[]{:S(2)}) copy-start(bf16[64]{0:T(256)(128)(2,1)} %param.12) | copy-start | bytes 388
  47.8 31.0 %copy-start.3 = (s32[4]{0:T(128)S(1)}, s32[4]{0:T(128)}, u32[]{:S(2)}) copy-start(s32[4]{0:T(128)} %table.1) | copy-start | bytes 52
  47.8 31.0 %all-to-all-start.1 = ((f32[16,32,512]{2,1,0:T(8,128)}), f32[16,32,512]{2,1,0:T(8,128)S(1)}, u32[]{:S(2)}, u32[]{:S(2)}) async-start(f32[16,32,512]{2,1,0:T(8,128)} %bitcast.15), calls=%async_computation.1 | async-start | bytes 2097152 | tf_op jit(solution)/shard_map/all_to_all | solution.py:260
  51.9 6.3 %collective-permute-start.5 = (bf16[1,2,20,256]{3,2,1,0:T(8,128)(2,1)S(1)}, bf16[1,2,20,256]{3,2,1,0:T(8,128)(2,1)S(1)}, u32[]{:S(2)}, u32[]{:S(2)}) collective-permute-start(bf16[1,2,20,256]{3,2,1,0:T(8,128)(2,1)S(1)} %bitcast.41), channel_id=1, source_target_pairs={{0,32},{32,64},{64,96},{96,128},{128,160},{160,192},{192,224},{224... | collective-permute-start | bytes 61448 | tf_op jit(solution)/shard_map/ppermute | solution.py:232
  58.1 7.7 %collective-permute-start.6 = (bf16[2,2,20,256]{3,2,1,0:T(8,128)(2,1)S(1)}, bf16[2,2,20,256]{3,2,1,0:T(8,128)(2,1)S(1)}, u32[]{:S(2)}, u32[]{:S(2)}) collective-permute-start(bf16[2,2,20,256]{3,2,1,0:T(8,128)(2,1)S(1)} %pad_maximum_fusion.6), channel_id=1, source_target_pairs={{0,64},{32,96},{64,128},{96,160},{128,192},{160,224},{192,0},{224,... | collective-permute-start | bytes 122888 | tf_op jit(solution)/shard_map/ppermute | solution.py:232
  65.9 9.4 %collective-permute-start.7 = (bf16[4,2,20,256]{3,2,1,0:T(8,128)(2,1)S(1)}, bf16[4,2,20,256]{3,2,1,0:T(8,128)(2,1)S(1)}, u32[]{:S(2)}, u32[]{:S(2)}) collective-permute-start(bf16[4,2,20,256]{3,2,1,0:T(8,128)(2,1)S(1)} %pad_maximum_fusion.5), channel_id=1, source_target_pairs={{0,128},{32,160},{64,192},{96,224},{128,0},{160,32},{192,64},{224,... | collective-permute-start | bytes 245768 | tf_op jit(solution)/shard_map/ppermute | solution.py:232
  81.6 8.8 %collective-permute-start.8 = (bf16[32,640]{1,0:T(8,128)(2,1)S(1)}, bf16[32,640]{1,0:T(8,128)(2,1)S(1)}, u32[]{:S(2)}, u32[]{:S(2)}) collective-permute-start(bf16[32,640]{1,0:T(8,128)(2,1)S(1)} %get-tuple-element.20), channel_id=1, source_target_pairs={{0,256},{256,0},{1,257},{257,1},{2,258},{258,2},{3,259},{259,3},{4... | collective-permute-start | bytes 122888 | tf_op jit(solution)/shard_map/ppermute | solution.py:290
  91.7 41.8 %all-to-all-start.2 = ((bf16[32,32,640]{2,1,0:T(8,128)(2,1)}), bf16[32,32,640]{2,1,0:T(8,128)(2,1)S(1)}, u32[]{:S(2)}, u32[]{:S(2)}) async-start(bf16[32,32,640]{2,1,0:T(8,128)(2,1)} %broadcast_select_fusion), calls=%async_computation.2 | async-start | bytes 2621440 | tf_op jit(solution)/shard_map/all_to_all | solution.py:297
  99.3 7.0 %collective-permute-start.11 = (bf16[1,32,1280]{2,1,0:T(8,128)(2,1)S(1)}, bf16[1,32,1280]{2,1,0:T(8,128)(2,1)S(1)}, u32[]{:S(2)}, u32[]{:S(2)}) collective-permute-start(bf16[1,32,1280]{2,1,0:T(8,128)(2,1)S(1)} %bitcast.34), channel_id=1, source_target_pairs={{0,2},{2,4},{4,6},{6,0},{1,3},{3,5},{5,7},{7,1},{8,10},{10,12},{12... | collective-permute-start | bytes 245768 | tf_op jit(solution)/shard_map/ppermute | solution.py:232
  101.2 12.0 %collective-permute-start.9 = (bf16[1,8,2,20,256]{4,3,2,1,0:T(8,128)(2,1)S(1)}, bf16[1,8,2,20,256]{4,3,2,1,0:T(8,128)(2,1)S(1)}, u32[]{:S(2)}, u32[]{:S(2)}) collective-permute-start(bf16[1,8,2,20,256]{4,3,2,1,0:T(8,128)(2,1)S(1)} %bitcast.38), channel_id=1, source_target_pairs={{0,8},{8,16},{16,24},{24,0},{1,9},{9,17},{17,25},{25,1},{2,10},{10... | collective-permute-start | bytes 491528 | tf_op jit(solution)/shard_map/ppermute | solution.py:232
  106.3 8.9 %collective-permute-start.12 = (bf16[2,32,1280]{2,1,0:T(8,128)(2,1)S(1)}, bf16[2,32,1280]{2,1,0:T(8,128)(2,1)S(1)}, u32[]{:S(2)}, u32[]{:S(2)}) collective-permute-start(bf16[2,32,1280]{2,1,0:T(8,128)(2,1)S(1)} %pad_maximum_fusion.4), channel_id=1, source_target_pairs={{0,4},{2,6},{4,0},{6,2},{1,5},{3,7},{5,1},{7,3},{8,12},{10,14},{12... | collective-permute-start | bytes 491528 | tf_op jit(solution)/shard_map/ppermute | solution.py:232
  113.3 19.3 %collective-permute-start.10 = (bf16[2,8,2,20,256]{4,3,2,1,0:T(8,128)(2,1)S(1)}, bf16[2,8,2,20,256]{4,3,2,1,0:T(8,128)(2,1)S(1)}, u32[]{:S(2)}, u32[]{:S(2)}) collective-permute-start(bf16[2,8,2,20,256]{4,3,2,1,0:T(8,128)(2,1)S(1)} %pad_maximum_fusion.1), channel_id=1, source_target_pairs={{0,16},{8,24},{16,0},{24,8},{1,17},{9,25},{17,1},{25,9},{2,18},{10... | collective-permute-start | bytes 983048 | tf_op jit(solution)/shard_map/ppermute | solution.py:232
  115.3 18.2 %collective-permute-start.13 = (bf16[4,32,1280]{2,1,0:T(8,128)(2,1)S(1)}, bf16[4,32,1280]{2,1,0:T(8,128)(2,1)}, u32[]{:S(2)}, u32[]{:S(2)}) collective-permute-start(bf16[4,32,1280]{2,1,0:T(8,128)(2,1)S(1)} %pad_maximum_fusion.2.q), channel_id=1, source_target_pairs={{0,1},{1,0},{2,3},{3,2},{4,5},{5,4},{6,7},{7,6},{8,9},{9,8},{10,11... | collective-permute-start | bytes 983048 | tf_op jit(solution)/shard_map/ppermute | solution.py:292
  138.2 8.7 %collective-permute-start.14 = (f32[4,32,1408]{2,1,0:T(8,128)S(1)}, f32[4,32,1408]{2,1,0:T(8,128)S(1)}, u32[]{:S(2)}, u32[]{:S(2)}) collective-permute-start(f32[4,32,1408]{2,1,0:T(8,128)S(1)} %attend1.1), channel_id=1, source_target_pairs={{0,1},{1,0},{2,3},{3,2},{4,5},{5,4},{6,7},{7,6},{8,9},{9,8},{10,11... | collective-permute-start | bytes 2162696 | tf_op jit(solution)/shard_map/ppermute | solution.py:311

commit v4 on v3

--- a/solution.py
+++ b/solution.py
@@ -45,12 +45,12 @@
     )
 
 
-def project_body(flip, place, gain, weight, here, one, two, three, out):
+def project_body(flip, place, gain, weight, hidden, out):
     core = place[3] if not flip else 1 - place[3]
     x = place[5]
     lane = lax.broadcasted_iota(jnp.int32, (128, 128), 1)
-    for step, hidden in enumerate((here, one, two, three)):
-        rows = [hidden[p, yl, core].astype(F32) for yl in range(4) for p in range(PAGES_DEV)]
+    for step in range(4):
+        rows = [hidden[step, p, yl, core].astype(F32) for yl in range(4) for p in range(PAGES_DEV)]
         values = jnp.concatenate(rows, axis=0)
         scaled = (values * gain[...].astype(F32)).astype(BF)
         product = lax.dot_general(
@@ -231,34 +231,35 @@
     def shift(value, axis, count, step):
         return lax.ppermute(value, axis, [(i, (i + step) % count) for i in range(count)])
 
-    def gather(value, axis, count):
+    def gather(value, axis, size, count):
         step = 1
         while step < count:
-            value = jnp.concatenate([value, shift(value, axis, count, step)], axis=0)
+            value = jnp.concatenate([value, shift(value, axis, size, step)], axis=0)
             step *= 2
         return value
 
-    hidden = [hidden_in] + [shift(hidden_in, "x", 4, step) for step in range(1, 4)]
+    hidden = gather(hidden_in[None], "x", 4, 2)
     columns = jnp.pad(qkv_weight.T, ((0, 2), (0, 0)))
+    other = lax.ppermute(out_weight, "yh", swap)
+    hidden, columns, other = lax.optimization_barrier((hidden, columns, other))
+    mixing = jnp.where(yh == 0, jnp.stack([out_weight, other]), jnp.stack([other, out_weight]))
     weight = spread(columns, ("yh", "z"), 16).reshape(512, TOK_DEV)
-    other = lax.ppermute(out_weight, "yh", swap)
-    weight, other = lax.optimization_barrier((weight, other))
-    mixing = jnp.where(yh == 0, jnp.stack([out_weight, other]), jnp.stack([other, out_weight]))
-    hidden = [h.reshape(PAGES_DEV, 4, 2, 8, 256) for h in hidden]
+    hidden = jnp.concatenate([hidden, shift(hidden, "x", 4, 2)], axis=0)
+    hidden = hidden.reshape(4, PAGES_DEV, 4, 2, 8, 256)
     gain = attn_gain.reshape(1, 256)
     half_shape = jax.ShapeDtypeStruct((4, 128, 512), F32)
 
     def project(flip):
         return call(
-            functools.partial(project_body, flip), half_shape, [SM] + [VM] * 6, f"project{flip}"
-        )(place, gain, weight, *hidden)
+            functools.partial(project_body, flip), half_shape, [SM] + [VM] * 3, f"project{flip}"
+        )(place, gain, weight, hidden)
 
     sent = project(1)
     arrived = lax.ppermute(sent, "c", swap)
     partial = (project(0) + arrived).reshape(16, ROWS, 512)
     mixing, partial = lax.optimization_barrier((mixing, partial))
     parts = lax.all_to_all(partial, ("x", "yl"), 0, 0)
-    mixing = gather(mixing[None], "z", 8)
+    mixing = gather(mixing[None], "z", 8, 4)
     mixing, parts = lax.optimization_barrier((mixing, parts))
 
     row = jnp.arange(ROWS, dtype=jnp.int32)
@@ -288,11 +289,9 @@
     )
 
     far = lax.ppermute(kv, "yh", swap)
-    kept = gather(queries[None], "yl", 4)
+    kept = gather(queries[None], "yl", 4, 4)
     given = lax.ppermute(kept, "c", swap)
-    mixing = call(order_body, jax.ShapeDtypeStruct((64, 20, 256), BF), [SM, VM], "order")(
-        place, gather(mixing[None], "x", 4)
-    ).reshape(Q_DIM, 256)
+    mixing = jnp.concatenate([mixing, shift(mixing, "z", 8, 4)], axis=0)
     target = jnp.arange(32, dtype=jnp.int32)[:, None, None]
     blocks = lax.all_to_all(jnp.where(target >= index, kv[None], far[None]), ("z", "x"), 0, 0)
 
@@ -310,6 +309,9 @@
     sent = attend(1)
     arrived = lax.ppermute(sent, "c", swap)
     parts = lax.all_to_all(attend(0) + arrived, "yl", 0, 0)
+    mixing = call(order_body, jax.ShapeDtypeStruct((64, 20, 256), BF), [SM, VM], "order")(
+        place, gather(mixing[None], "x", 4, 4)
+    ).reshape(Q_DIM, 256)
     attended = call(divide_body, jax.ShapeDtypeStruct((ROWS, Q_DIM), BF), [VM], "divide")(parts)
     attended = lax.all_gather(attended, ("yl", "c"), axis=0, tiled=True)
     hidden_out = call(

time: 188 us -> 198 us (1.053)
  waiting for transfers between devices: 32.4 us -> 69 us
  blocking collectives: 39.1 us -> 16.7 us
  starting transfers between devices: 92.3 us -> 87.5 us
    all_to_all x1 -> x0, blocking collectives: 22.5 us -> none  [on_device(): parts = lax.all_to_all(attend(0) + arrived, 'yl', 0, 0)]
    ppermute x10 -> x9, waiting for transfers between devices: 25.7 us -> 47 us  [shift(): lax.ppermute(value, axis, [(i, (i + step) % count) for i in range(count)])]
    all_to_all x1, waiting for transfers between devices: 3.5 us -> 13.4 us  [on_device(): parts = lax.all_to_all(partial, ('x', 'yl'), 0, 0)]
    ppermute x1, starting transfers between devices: 7.44 us -> 3.74 us  [on_device(): far = lax.ppermute(kv, 'yh', swap)]
    ppermute x1, waiting for transfers between devices: 1.36 us -> 4.88 us  [on_device(): far = lax.ppermute(kv, 'yh', swap)]
    all_to_all x0 -> x1, starting transfers between devices: none -> 3.49 us  [on_device(): parts = lax.all_to_all(attend(0) + arrived, 'yl', 0, 0)]
    all_to_all x1, starting transfers between devices: 7.59 us -> 4.12 us  [on_device(): lax.all_to_all(jnp.where(target >= index, kv[None], far[None]), ('z', 'x'...]
    all_to_all x1, waiting for transfers between devices: 0.01 us -> 2.44 us  [spread(): lax.all_to_all(jnp.broadcast_to(x[None], (count,) + x.shape), axes, 0, 0)]
  transfers between devices with their start and end apart: 18 -> 18, of which waited for: 10 -> 12; matrix products, arithmetic and copies ran while one was open for 1% -> 1% of each run, Pallas kernels for 3% -> 3%
where the time goes in v4:
time: 198 us; the launch traced here: 197 us
  starting transfers between devices  87.5 us (44%)
  waiting for transfers between devices  69 us (35%)
  blocking collectives  16.7 us (8%)
  Pallas kernels  15.4 us (8%)
  other arithmetic  5.1 us (3%)
    ppermute x9, waiting for transfers between devices, shift(): lax.ppermute(value, axis, [(i, (i + step) % count) for i in range(count)])  47 us
    ppermute x9, starting transfers between devices, shift(): lax.ppermute(value, axis, [(i, (i + step) % count) for i in range(count)])  32.2 us
    all_gather x1, blocking collectives, on_device(): attended = lax.all_gather(attended, ('yl', 'c'), axis=0, tiled=True)  16.7 us
    all_to_all x1, starting transfers between devices, spread(): lax.all_to_all(jnp.broadcast_to(x[None], (count,) + x.shape), axes, 0, 0)  14.8 us
    all_to_all x1, waiting for transfers between devices, on_device(): parts = lax.all_to_all(partial, ('x', 'yl'), 0, 0)  13.4 us
    ppermute x2, starting transfers between devices, on_device(): arrived = lax.ppermute(sent, 'c', swap)  9.63 us
    pallas_call x2, Pallas kernels, attend(): call(functools.partial(attend_body, flip), jax.ShapeDtypeStruct((4, ROWS,...  8.69 us
    ppermute x1, starting transfers between devices, on_device(): other = lax.ppermute(out_weight, 'yh', swap)  7.46 us
  transfers between devices with their start and end apart: 18, of which 12 were waited for; matrix products, arithmetic and copies ran while one was open for 1% of the time, Pallas kernels for 3%

profile of v4, /device:TPU:1, one launch (start us, length us, event | category | flops | bytes accessed | tf_op | source)
XLA Modules:
  0.0 196.7 jit_solution(17907557803334129703)
XLA Ops:
  0.6 4.0 %collective-permute-start = (bf16[1,256,256]{2,1,0:T(8,128)(2,1)}, bf16[1,256,256]{2,1,0:T(8,128)(2,1)S(1)}, u32[]{:S(2)}, u32[]{:S(2)}) collective-permute-start(bf16[1,256,256]{2,1,0:T(8,128)(2,1)} %bitcast.25), channel_id=1, source_target_pairs={{0,8},{8,16},{16,24},{24,0},{1,9},{9,17},{17,25},{25,1},{2,10},{10... | collective-permute-start | bytes 393224 | tf_op jit(solution)/shard_map/ppermute | solution.py:232
  4.6 7.5 %collective-permute-start.1 = (bf16[20,256]{1,0:T(8,128)(2,1)}, bf16[20,256]{1,0:T(8,128)(2,1)S(1)}, u32[]{:S(2)}, u32[]{:S(2)}) collective-permute-start(bf16[20,256]{1,0:T(8,128)(2,1)} %param.13), channel_id=1, source_target_pairs={{0,256},{256,0},{1,257},{257,1},{2,258},{258,2},{3,259},{259,3},{4... | collective-permute-start | bytes 30728 | tf_op jit(solution)/shard_map/ppermute | solution.py:243
  14.5 14.8 %all-to-all-start = ((bf16[16,32,256]{2,1,0:T(8,128)(2,1)}), bf16[16,32,256]{2,1,0:T(8,128)(2,1)S(1)}, u32[]{:S(2)}, u32[]{:S(2)}) async-start(bf16[16,32,256]{2,1,0:T(8,128)(2,1)} %broadcast_in_dim.61), calls=%async_computation | async-start | bytes 524288 | tf_op jit(solution)/shard_map/all_to_all | solution.py:219
  29.3 4.4 %collective-permute-start.2 = (bf16[2,256,256]{2,1,0:T(8,128)(2,1)S(1)}, bf16[2,256,256]{2,1,0:T(8,128)(2,1)S(1)}, u32[]{:S(2)}, u32[]{:S(2)}) collective-permute-start(bf16[2,256,256]{2,1,0:T(8,128)(2,1)S(1)} %pad_maximum_fusion.4), channel_id=1, source_target_pairs={{0,16},{8,24},{16,0},{24,8},{1,17},{9,25},{17,1},{25,9},{2,18},{10... | collective-permute-start | bytes 786440 | tf_op jit(solution)/shard_map/ppermute | solution.py:232
  33.8 4.4 %collective-permute-done.2 = bf16[2,256,256]{2,1,0:T(8,128)(2,1)S(1)} collective-permute-done((bf16[2,256,256]{2,1,0:T(8,128)(2,1)S(1)}, bf16[2,256,256]{2,1,0:T(8,128)(2,1)S(1)}, u32[]{:S(2)}, u32[]{:S(2)}) %collective-permute-start.2) | collective-permute-done | bytes 262176 | tf_op jit(solution)/shard_map/ppermute | solution.py:232
  38.3 2.4 %all-to-all-done = bf16[16,32,256]{2,1,0:T(8,128)(2,1)S(1)} async-done(((bf16[16,32,256]{2,1,0:T(8,128)(2,1)}), bf16[16,32,256]{2,1,0:T(8,128)(2,1)S(1)}, u32[]{:S(2)}, u32[]{:S(2)}) %all-to-all-start) | async-done | bytes 262176 | tf_op jit(solution)/shard_map/all_to_all | solution.py:219
  41.7 5.4 %collective-permute-start.3 = (f32[4,128,512]{2,1,0:T(8,128)S(1)}, f32[4,128,512]{2,1,0:T(8,128)S(1)}, u32[]{:S(2)}, u32[]{:S(2)}) collective-permute-start(f32[4,128,512]{2,1,0:T(8,128)S(1)} %project1.1), channel_id=1, source_target_pairs={{0,1},{1,0},{2,3},{3,2},{4,5},{5,4},{6,7},{7,6},{8,9},{9,8},{10,11... | collective-permute-start | bytes 3145736 | tf_op jit(solution)/shard_map/ppermute | solution.py:258
  50.7 5.3 %all-to-all-start.1 = ((f32[16,32,512]{2,1,0:T(8,128)}), f32[16,32,512]{2,1,0:T(8,128)S(1)}, u32[]{:S(2)}, u32[]{:S(2)}) async-start(f32[16,32,512]{2,1,0:T(8,128)} %bitcast.13), calls=%async_computation.1 | async-start | bytes 2097152 | tf_op jit(solution)/shard_map/all_to_all | solution.py:261
  56.3 3.2 %collective-permute-start.4 = (bf16[1,2,20,256]{3,2,1,0:T(8,128)(2,1)S(1)}, bf16[1,2,20,256]{3,2,1,0:T(8,128)(2,1)S(1)}, u32[]{:S(2)}, u32[]{:S(2)}) collective-permute-start(bf16[1,2,20,256]{3,2,1,0:T(8,128)(2,1)S(1)} %bitcast.35), channel_id=1, source_target_pairs={{0,32},{32,64},{64,96},{96,128},{128,160},{160,192},{192,224},{224... | collective-permute-start | bytes 61448 | tf_op jit(solution)/shard_map/ppermute | solution.py:232
  59.6 2.8 %collective-permute-done.4 = bf16[1,2,20,256]{3,2,1,0:T(8,128)(2,1)S(1)} collective-permute-done((bf16[1,2,20,256]{3,2,1,0:T(8,128)(2,1)S(1)}, bf16[1,2,20,256]{3,2,1,0:T(8,128)(2,1)S(1)}, u32[]{:S(2)}, u32[]{:S(2)}) %collective-permute-start.4) | collective-permute-done | bytes 20512 | tf_op jit(solution)/shard_map/ppermute | solution.py:232
  62.4 2.1 %collective-permute-start.5 = (bf16[2,2,20,256]{3,2,1,0:T(8,128)(2,1)S(1)}, bf16[2,2,20,256]{3,2,1,0:T(8,128)(2,1)S(1)}, u32[]{:S(2)}, u32[]{:S(2)}) collective-permute-start(bf16[2,2,20,256]{3,2,1,0:T(8,128)(2,1)S(1)} %pad_maximum_fusion.8), channel_id=1, source_target_pairs={{0,64},{32,96},{64,128},{96,160},{128,192},{160,224},{192,0},{224,... | collective-permute-start | bytes 122888 | tf_op jit(solution)/shard_map/ppermute | solution.py:232
  64.8 4.8 %collective-permute-done.5 = bf16[2,2,20,256]{3,2,1,0:T(8,128)(2,1)S(1)} collective-permute-done((bf16[2,2,20,256]{3,2,1,0:T(8,128)(2,1)S(1)}, bf16[2,2,20,256]{3,2,1,0:T(8,128)(2,1)S(1)}, u32[]{:S(2)}, u32[]{:S(2)}) %collective-permute-start.5) | collective-permute-done | bytes 40992 | tf_op jit(solution)/shard_map/ppermute | solution.py:232
  69.6 13.4 %all-to-all-done.1.parts = f32[16,32,512]{2,1,0:T(8,128)S(1)} async-done(((f32[16,32,512]{2,1,0:T(8,128)}), f32[16,32,512]{2,1,0:T(8,128)S(1)}, u32[]{:S(2)}, u32[]{:S(2)}) %all-to-all-start.1) | async-done | bytes 1048608 | tf_op jit(solution)/shard_map/all_to_all | solution.py:261
  83.0 2.9 %rotate.1 = (bf16[32,1280]{1,0:T(8,128)(2,1)S(1)}, bf16[32,640]{1,0:T(8,128)(2,1)S(1)}, bf16[4,8,640]{2,1,0:T(8,128)(2,1)}) custom-call(s32[4]{0:T(128)S(1)} %copy-done.2, f32[16,32,512]{2,1,0:T(8,128)S(1)} %all-to-all-done.1.parts, f32[32,128]{1,0:T(8,128)S(1)} %get-tuple-element.31.cosine, f32[32,128]{1,0:T(8,128)S(1)} %get-tuple-element.30.sine, ...), custom_call_target="tpu_custom_call" | custom-call | tf_op jit(solution)/shard_map/rotate/pallas_call | solution.py:273
  85.9 3.7 %collective-permute-start.6 = (bf16[32,640]{1,0:T(8,128)(2,1)S(1)}, bf16[32,640]{1,0:T(8,128)(2,1)S(1)}, u32[]{:S(2)}, u32[]{:S(2)}) collective-permute-start(bf16[32,640]{1,0:T(8,128)(2,1)S(1)} %get-tuple-element.22), channel_id=1, source_target_pairs={{0,256},{256,0},{1,257},{257,1},{2,258},{258,2},{3,259},{259,3},{4... | collective-permute-start | bytes 122888 | tf_op jit(solution)/shard_map/ppermute | solution.py:291
  89.6 4.9 %collective-permute-done.6.far = bf16[32,640]{1,0:T(8,128)(2,1)S(1)} collective-permute-done((bf16[32,640]{1,0:T(8,128)(2,1)S(1)}, bf16[32,640]{1,0:T(8,128)(2,1)S(1)}, u32[]{:S(2)}, u32[]{:S(2)}) %collective-permute-start.6) | collective-permute-done | bytes 40992 | tf_op jit(solution)/shard_map/ppermute | solution.py:291
  95.8 4.1 %all-to-all-start.2 = ((bf16[32,32,640]{2,1,0:T(8,128)(2,1)}), bf16[32,32,640]{2,1,0:T(8,128)(2,1)S(1)}, u32[]{:S(2)}, u32[]{:S(2)}) async-start(bf16[32,32,640]{2,1,0:T(8,128)(2,1)} %broadcast_select_fusion), calls=%async_computation.2 | async-start | bytes 2621440 | tf_op jit(solution)/shard_map/all_to_all | solution.py:296
  99.9 1.9 collective-permute-start.8
  101.8 5.1 %collective-permute-done.8 = bf16[1,32,1280]{2,1,0:T(8,128)(2,1)S(1)} collective-permute-done((bf16[1,32,1280]{2,1,0:T(8,128)(2,1)S(1)}, bf16[1,32,1280]{2,1,0:T(8,128)(2,1)S(1)}, u32[]{:S(2)}, u32[]{:S(2)}) %collective-permute-start.8) | collective-permute-done | bytes 81952 | tf_op jit(solution)/shard_map/ppermute | solution.py:232
  108.8 6.0 %collective-permute-done.9 = bf16[2,32,1280]{2,1,0:T(8,128)(2,1)S(1)} collective-permute-done((bf16[2,32,1280]{2,1,0:T(8,128)(2,1)S(1)}, bf16[2,32,1280]{2,1,0:T(8,128)(2,1)S(1)}, u32[]{:S(2)}, u32[]{:S(2)}) %collective-permute-start.9) | collective-permute-done | bytes 163872 | tf_op jit(solution)/shard_map/ppermute | solution.py:232
  114.8 6.8 %collective-permute-start.10 = (bf16[4,32,1280]{2,1,0:T(8,128)(2,1)S(1)}, bf16[4,32,1280]{2,1,0:T(8,128)(2,1)S(1)}, u32[]{:S(2)}, u32[]{:S(2)}) collective-permute-start(bf16[4,32,1280]{2,1,0:T(8,128)(2,1)S(1)} %pad_maximum_fusion.3.q), channel_id=1, source_target_pairs={{0,1},{1,0},{2,3},{3,2},{4,5},{5,4},{6,7},{7,6},{8,9},{9,8},{10,11... | collective-permute-start | bytes 983048 | tf_op jit(solution)/shard_map/ppermute | solution.py:293
  121.6 7.5 %collective-permute-start.7 = (bf16[4,2,20,256]{3,2,1,0:T(8,128)(2,1)S(1)}, bf16[4,2,20,256]{3,2,1,0:T(8,128)(2,1)S(1)}, u32[]{:S(2)}, u32[]{:S(2)}) collective-permute-start(bf16[4,2,20,256]{3,2,1,0:T(8,128)(2,1)S(1)} %pad_maximum_fusion.7), channel_id=1, source_target_pairs={{0,128},{32,160},{64,192},{96,224},{128,0},{160,32},{192,64},{224,... | collective-permute-start | bytes 245768 | tf_op jit(solution)/shard_map/ppermute | solution.py:232
  129.1 7.9 %collective-permute-done.7 = bf16[4,2,20,256]{3,2,1,0:T(8,128)(2,1)S(1)} collective-permute-done((bf16[4,2,20,256]{3,2,1,0:T(8,128)(2,1)S(1)}, bf16[4,2,20,256]{3,2,1,0:T(8,128)(2,1)S(1)}, u32[]{:S(2)}, u32[]{:S(2)}) %collective-permute-start.7) | collective-permute-done | bytes 81952 | tf_op jit(solution)/shard_map/ppermute | solution.py:232
  137.0 4.4 %attend1.1 = f32[4,32,1408]{2,1,0:T(8,128)S(1)} custom-call(s32[7]{0:T(128)S(1)} %stack.45.place, s32[4]{0:T(128)S(1)} %copy-done.1, bf16[4,32,1280]{2,1,0:T(8,128)(2,1)S(1)} %collective-permute-done.10.q, bf16[32,32,640]{2,1,0:T(8,128)(2,1)S(1)} %all-to-all-done.2.blocks, bf16[32,640]{1,0:T(8,128)(2,1)S(1)} %collective-permute-done.6.far), custom_call_target="tpu_custom_call" | custom-call | tf_op jit(solution)/shard_map/attend1/pallas_call | solution.py:301
  141.4 4.2 %collective-permute-start.11 = (f32[4,32,1408]{2,1,0:T(8,128)S(1)}, f32[4,32,1408]{2,1,0:T(8,128)S(1)}, u32[]{:S(2)}, u32[]{:S(2)}) collective-permute-start(f32[4,32,1408]{2,1,0:T(8,128)S(1)} %attend1.1), channel_id=1, source_target_pairs={{0,1},{1,0},{2,3},{3,2},{4,5},{5,4},{6,7},{7,6},{8,9},{9,8},{10,11... | collective-permute-start | bytes 2162696 | tf_op jit(solution)/shard_map/ppermute | solution.py:310
  145.6 4.3 %attend0.1 = f32[4,32,1408]{2,1,0:T(8,128)S(1)} custom-call(s32[7]{0:T(128)S(1)} %stack.45.place, s32[4]{0:T(128)S(1)} %copy-done.1, bf16[4,32,1280]{2,1,0:T(8,128)(2,1)S(1)} %pad_maximum_fusion.3.q, bf16[32,32,640]{2,1,0:T(8,128)(2,1)S(1)} %all-to-all-done.2.blocks, bf16[32,640]{1,0:T(8,128)(2,1)S(1)} %collective-permute-done.6.far), custom_call_target="tpu_custom_call" | custom-call | tf_op jit(solution)/shard_map/attend0/pallas_call | solution.py:301
  150.9 3.5 %all-to-all-start.3 = ((f32[4,32,1408]{2,1,0:T(8,128)}), f32[4,32,1408]{2,1,0:T(8,128)S(1)}, u32[]{:S(2)}, u32[]{:S(2)}) async-start(f32[4,32,1408]{2,1,0:T(8,128)} %add.84), calls=%async_computation.3 | async-start | bytes 1441792 | tf_op jit(solution)/shard_map/all_to_all | solution.py:311
  154.4 3.9 %collective-permute-start.12 = (bf16[1,8,2,20,256]{4,3,2,1,0:T(8,128)(2,1)S(1)}, bf16[1,8,2,20,256]{4,3,2,1,0:T(8,128)(2,1)S(1)}, u32[]{:S(2)}, u32[]{:S(2)}) collective-permute-start(bf16[1,8,2,20,256]{4,3,2,1,0:T(8,128)(2,1)S(1)} %bitcast.32), channel_id=1, source_target_pairs={{0,8},{8,16},{16,24},{24,0},{1,9},{9,17},{17,25},{25,1},{2,10},{10... | collective-permute-start | bytes 491528 | tf_op jit(solution)/shard_map/ppermute | solution.py:232
  158.3 6.3 %collective-permute-done.12 = bf16[1,8,2,20,256]{4,3,2,1,0:T(8,128)(2,1)S(1)} collective-permute-done((bf16[1,8,2,20,256]{4,3,2,1,0:T(8,128)(2,1)S(1)}, bf16[1,8,2,20,256]{4,3,2,1,0:T(8,128)(2,1)S(1)}, u32[]{:S(2)}, u32[]{:S(2)}) %collective-permute-start.12) | collective-permute-done | bytes 163872 | tf_op jit(solution)/shard_map/ppermute | solution.py:232
  164.6 3.3 %collective-permute-start.13 = (bf16[2,8,2,20,256]{4,3,2,1,0:T(8,128)(2,1)S(1)}, bf16[2,8,2,20,256]{4,3,2,1,0:T(8,128)(2,1)S(1)}, u32[]{:S(2)}, u32[]{:S(2)}) collective-permute-start(bf16[2,8,2,20,256]{4,3,2,1,0:T(8,128)(2,1)S(1)} %pad_maximum_fusion.2), channel_id=1, source_target_pairs={{0,16},{8,24},{16,0},{24,8},{1,17},{9,25},{17,1},{25,9},{2,18},{10... | collective-permute-start | bytes 983048 | tf_op jit(solution)/shard_map/ppermute | solution.py:232
  167.9 9.9 %collective-permute-done.13 = bf16[2,8,2,20,256]{4,3,2,1,0:T(8,128)(2,1)S(1)} collective-permute-done((bf16[2,8,2,20,256]{4,3,2,1,0:T(8,128)(2,1)S(1)}, bf16[2,8,2,20,256]{4,3,2,1,0:T(8,128)(2,1)S(1)}, u32[]{:S(2)}, u32[]{:S(2)}) %collective-permute-start.13) | collective-permute-done | bytes 327712 | tf_op jit(solution)/shard_map/ppermute | solution.py:232
  178.9 16.7 %all_gather.3.attended = bf16[256,1280]{1,0:T(8,128)(2,1)S(1)} all-gather(bf16[32,1280]{1,0:T(8,128)(2,1)S(1)} %divide.1), channel_id=1, replica_groups=mesh['yh'=2,'z'=8,'x'=4,'yl'=4,'c'=2] {'yl','c'}, dimensions={0}, use_global_device_ids=true | all-gather | bytes 737280 | tf_op jit(solution)/shard_map/all_gather | solution.py:316
  (58 shorter events, 14.1 us)
Async XLA Ops:
  0.6 33.0 %copy-start.4 = (bf16[256]{0:T(256)(128)(2,1)S(1)}, bf16[256]{0:T(256)(128)(2,1)}, u32[]{:S(2)}) copy-start(bf16[256]{0:T(256)(128)(2,1)} %param.9) | copy-start | bytes 1540
  0.6 12.2 %collective-permute-start = (bf16[1,256,256]{2,1,0:T(8,128)(2,1)}, bf16[1,256,256]{2,1,0:T(8,128)(2,1)S(1)}, u32[]{:S(2)}, u32[]{:S(2)}) collective-permute-start(bf16[1,256,256]{2,1,0:T(8,128)(2,1)} %bitcast.25), channel_id=1, source_target_pairs={{0,8},{8,16},{16,24},{24,0},{1,9},{9,17},{17,25},{25,1},{2,10},{10... | collective-permute-start | bytes 393224 | tf_op jit(solution)/shard_map/ppermute | solution.py:232
  4.6 9.1 %collective-permute-start.1 = (bf16[20,256]{1,0:T(8,128)(2,1)}, bf16[20,256]{1,0:T(8,128)(2,1)S(1)}, u32[]{:S(2)}, u32[]{:S(2)}) collective-permute-start(bf16[20,256]{1,0:T(8,128)(2,1)} %param.13), channel_id=1, source_target_pairs={{0,256},{256,0},{1,257},{257,1},{2,258},{258,2},{3,259},{259,3},{4... | collective-permute-start | bytes 30728 | tf_op jit(solution)/shard_map/ppermute | solution.py:243
  14.5 26.2 %all-to-all-start = ((bf16[16,32,256]{2,1,0:T(8,128)(2,1)}), bf16[16,32,256]{2,1,0:T(8,128)(2,1)S(1)}, u32[]{:S(2)}, u32[]{:S(2)}) async-start(bf16[16,32,256]{2,1,0:T(8,128)(2,1)} %broadcast_in_dim.61), calls=%async_computation | async-start | bytes 524288 | tf_op jit(solution)/shard_map/all_to_all | solution.py:219
  29.3 8.9 %collective-permute-start.2 = (bf16[2,256,256]{2,1,0:T(8,128)(2,1)S(1)}, bf16[2,256,256]{2,1,0:T(8,128)(2,1)S(1)}, u32[]{:S(2)}, u32[]{:S(2)}) collective-permute-start(bf16[2,256,256]{2,1,0:T(8,128)(2,1)S(1)} %pad_maximum_fusion.4), channel_id=1, source_target_pairs={{0,16},{8,24},{16,0},{24,8},{1,17},{9,25},{17,1},{25,9},{2,18},{10... | collective-permute-start | bytes 786440 | tf_op jit(solution)/shard_map/ppermute | solution.py:232
  33.8 13.4 %copy-start.3 = (bf16[20,256]{1,0:T(8,128)(2,1)S(1)}, bf16[20,256]{1,0:T(8,128)(2,1)}, u32[]{:S(2)}) copy-start(bf16[20,256]{1,0:T(8,128)(2,1)} %param.13) | copy-start | bytes 30724
  41.7 7.7 %collective-permute-start.3 = (f32[4,128,512]{2,1,0:T(8,128)S(1)}, f32[4,128,512]{2,1,0:T(8,128)S(1)}, u32[]{:S(2)}, u32[]{:S(2)}) collective-permute-start(f32[4,128,512]{2,1,0:T(8,128)S(1)} %project1.1), channel_id=1, source_target_pairs={{0,1},{1,0},{2,3},{3,2},{4,5},{5,4},{6,7},{7,6},{8,9},{9,8},{10,11... | collective-permute-start | bytes 3145736 | tf_op jit(solution)/shard_map/ppermute | solution.py:258
  50.7 5.3 %copy-start.1 = (s32[4]{0:T(128)S(1)}, s32[4]{0:T(128)}, u32[]{:S(2)}) copy-start(s32[4]{0:T(128)} %lengths.3) | copy-start | bytes 52
  50.7 14.0 %copy-start.5 = (bf16[64]{0:T(256)(128)(2,1)S(1)}, bf16[64]{0:T(256)(128)(2,1)}, u32[]{:S(2)}) copy-start(bf16[64]{0:T(256)(128)(2,1)} %param.11) | copy-start | bytes 388
  50.7 14.1 %copy-start.6 = (bf16[64]{0:T(256)(128)(2,1)S(1)}, bf16[64]{0:T(256)(128)(2,1)}, u32[]{:S(2)}) copy-start(bf16[64]{0:T(256)(128)(2,1)} %param.12) | copy-start | bytes 388
  50.7 32.3 %copy-start.2 = (s32[4]{0:T(128)S(1)}, s32[4]{0:T(128)}, u32[]{:S(2)}) copy-start(s32[4]{0:T(128)} %table.1) | copy-start | bytes 52
  50.7 32.3 %all-to-all-start.1 = ((f32[16,32,512]{2,1,0:T(8,128)}), f32[16,32,512]{2,1,0:T(8,128)S(1)}, u32[]{:S(2)}, u32[]{:S(2)}) async-start(f32[16,32,512]{2,1,0:T(8,128)} %bitcast.13), calls=%async_computation.1 | async-start | bytes 2097152 | tf_op jit(solution)/shard_map/all_to_all | solution.py:261
  56.3 6.1 %collective-permute-start.4 = (bf16[1,2,20,256]{3,2,1,0:T(8,128)(2,1)S(1)}, bf16[1,2,20,256]{3,2,1,0:T(8,128)(2,1)S(1)}, u32[]{:S(2)}, u32[]{:S(2)}) collective-permute-start(bf16[1,2,20,256]{3,2,1,0:T(8,128)(2,1)S(1)} %bitcast.35), channel_id=1, source_target_pairs={{0,32},{32,64},{64,96},{96,128},{128,160},{160,192},{192,224},{224... | collective-permute-start | bytes 61448 | tf_op jit(solution)/shard_map/ppermute | solution.py:232
  62.4 7.2 %collective-permute-start.5 = (bf16[2,2,20,256]{3,2,1,0:T(8,128)(2,1)S(1)}, bf16[2,2,20,256]{3,2,1,0:T(8,128)(2,1)S(1)}, u32[]{:S(2)}, u32[]{:S(2)}) collective-permute-start(bf16[2,2,20,256]{3,2,1,0:T(8,128)(2,1)S(1)} %pad_maximum_fusion.8), channel_id=1, source_target_pairs={{0,64},{32,96},{64,128},{96,160},{128,192},{160,224},{192,0},{224,... | collective-permute-start | bytes 122888 | tf_op jit(solution)/shard_map/ppermute | solution.py:232
  85.9 8.6 %collective-permute-start.6 = (bf16[32,640]{1,0:T(8,128)(2,1)S(1)}, bf16[32,640]{1,0:T(8,128)(2,1)S(1)}, u32[]{:S(2)}, u32[]{:S(2)}) collective-permute-start(bf16[32,640]{1,0:T(8,128)(2,1)S(1)} %get-tuple-element.22), channel_id=1, source_target_pairs={{0,256},{256,0},{1,257},{257,1},{2,258},{258,2},{3,259},{259,3},{4... | collective-permute-start | bytes 122888 | tf_op jit(solution)/shard_map/ppermute | solution.py:291
  95.8 41.2 %all-to-all-start.2 = ((bf16[32,32,640]{2,1,0:T(8,128)(2,1)}), bf16[32,32,640]{2,1,0:T(8,128)(2,1)S(1)}, u32[]{:S(2)}, u32[]{:S(2)}) async-start(bf16[32,32,640]{2,1,0:T(8,128)(2,1)} %broadcast_select_fusion), calls=%async_computation.2 | async-start | bytes 2621440 | tf_op jit(solution)/shard_map/all_to_all | solution.py:296
  99.9 7.0 %collective-permute-start.8 = (bf16[1,32,1280]{2,1,0:T(8,128)(2,1)S(1)}, bf16[1,32,1280]{2,1,0:T(8,128)(2,1)S(1)}, u32[]{:S(2)}, u32[]{:S(2)}) collective-permute-start(bf16[1,32,1280]{2,1,0:T(8,128)(2,1)S(1)} %bitcast.28), channel_id=1, source_target_pairs={{0,2},{2,4},{4,6},{6,0},{1,3},{3,5},{5,7},{7,1},{8,10},{10,12},{12... | collective-permute-start | bytes 245768 | tf_op jit(solution)/shard_map/ppermute | solution.py:232
  106.9 7.9 %collective-permute-start.9 = (bf16[2,32,1280]{2,1,0:T(8,128)(2,1)S(1)}, bf16[2,32,1280]{2,1,0:T(8,128)(2,1)S(1)}, u32[]{:S(2)}, u32[]{:S(2)}) collective-permute-start(bf16[2,32,1280]{2,1,0:T(8,128)(2,1)S(1)} %pad_maximum_fusion.6), channel_id=1, source_target_pairs={{0,4},{2,6},{4,0},{6,2},{1,5},{3,7},{5,1},{7,3},{8,12},{10,14},{12... | collective-permute-start | bytes 491528 | tf_op jit(solution)/shard_map/ppermute | solution.py:232
  114.8 22.2 %collective-permute-start.10 = (bf16[4,32,1280]{2,1,0:T(8,128)(2,1)S(1)}, bf16[4,32,1280]{2,1,0:T(8,128)(2,1)S(1)}, u32[]{:S(2)}, u32[]{:S(2)}) collective-permute-start(bf16[4,32,1280]{2,1,0:T(8,128)(2,1)S(1)} %pad_maximum_fusion.3.q), channel_id=1, source_target_pairs={{0,1},{1,0},{2,3},{3,2},{4,5},{5,4},{6,7},{7,6},{8,9},{9,8},{10,11... | collective-permute-start | bytes 983048 | tf_op jit(solution)/shard_map/ppermute | solution.py:293
  121.6 15.4 %collective-permute-start.7 = (bf16[4,2,20,256]{3,2,1,0:T(8,128)(2,1)S(1)}, bf16[4,2,20,256]{3,2,1,0:T(8,128)(2,1)S(1)}, u32[]{:S(2)}, u32[]{:S(2)}) collective-permute-start(bf16[4,2,20,256]{3,2,1,0:T(8,128)(2,1)S(1)} %pad_maximum_fusion.7), channel_id=1, source_target_pairs={{0,128},{32,160},{64,192},{96,224},{128,0},{160,32},{192,64},{224,... | collective-permute-start | bytes 245768 | tf_op jit(solution)/shard_map/ppermute | solution.py:232
  141.4 8.5 %collective-permute-start.11 = (f32[4,32,1408]{2,1,0:T(8,128)S(1)}, f32[4,32,1408]{2,1,0:T(8,128)S(1)}, u32[]{:S(2)}, u32[]{:S(2)}) collective-permute-start(f32[4,32,1408]{2,1,0:T(8,128)S(1)} %attend1.1), channel_id=1, source_target_pairs={{0,1},{1,0},{2,3},{3,2},{4,5},{5,4},{6,7},{7,6},{8,9},{9,8},{10,11... | collective-permute-start | bytes 2162696 | tf_op jit(solution)/shard_map/ppermute | solution.py:310
  150.9 27.8 %all-to-all-start.3 = ((f32[4,32,1408]{2,1,0:T(8,128)}), f32[4,32,1408]{2,1,0:T(8,128)S(1)}, u32[]{:S(2)}, u32[]{:S(2)}) async-start(f32[4,32,1408]{2,1,0:T(8,128)} %add.84), calls=%async_computation.3 | async-start | bytes 1441792 | tf_op jit(solution)/shard_map/all_to_all | solution.py:311
  154.4 10.2 %collective-permute-start.12 = (bf16[1,8,2,20,256]{4,3,2,1,0:T(8,128)(2,1)S(1)}, bf16[1,8,2,20,256]{4,3,2,1,0:T(8,128)(2,1)S(1)}, u32[]{:S(2)}, u32[]{:S(2)}) collective-permute-start(bf16[1,8,2,20,256]{4,3,2,1,0:T(8,128)(2,1)S(1)} %bitcast.32), channel_id=1, source_target_pairs={{0,8},{8,16},{16,24},{24,0},{1,9},{9,17},{17,25},{25,1},{2,10},{10... | collective-permute-start | bytes 491528 | tf_op jit(solution)/shard_map/ppermute | solution.py:232
  164.6 13.2 %collective-permute-start.13 = (bf16[2,8,2,20,256]{4,3,2,1,0:T(8,128)(2,1)S(1)}, bf16[2,8,2,20,256]{4,3,2,1,0:T(8,128)(2,1)S(1)}, u32[]{:S(2)}, u32[]{:S(2)}) collective-permute-start(bf16[2,8,2,20,256]{4,3,2,1,0:T(8,128)(2,1)S(1)} %pad_maximum_fusion.2), channel_id=1, source_target_pairs={{0,16},{8,24},{16,0},{24,8},{1,17},{9,25},{17,1},{25,9},{2,18},{10... | collective-permute-start | bytes 983048 | tf_op jit(solution)/shard_map/ppermute | solution.py:232
  178.6 17.1 %copy-start = (bf16[256,256]{1,0:T(8,128)(2,1)S(1)}, bf16[256,256]{1,0:T(8,128)(2,1)}, u32[]{:S(2)}) copy-start(bf16[256,256]{1,0:T(8,128)(2,1)} %param.8) | copy-start | bytes 393220

commit v5 on v3

--- a/solution.py
+++ b/solution.py
@@ -62,54 +62,60 @@
         out[pl.ds(owner, 1), :, 128:] = product[None, :, 128:]
 
 
-def rotate_body(table, parts, cosine, sine, q_gain, k_gain, queries, kv, cache):
+def pieces_in_order(parts, first_tile, count):
     lane = lax.broadcasted_iota(jnp.int32, (ROWS, 128), 1)
-    upper_head = lane >= HEAD
-    lower_part = (lane % HEAD) < HEAD // 2
 
     def summed(x, tile):
         at = pl.ds(tile * 128, 128)
         low, high = parts[4 * x, :, at] + parts[4 * x + 1, :, at], parts[4 * x + 2, :, at]
         return low + (high + parts[4 * x + 3, :, at])
 
-    tiles = [None] * 15
-    inverse = None
+    inverse = lax.rsqrt(summed(0, 0)[:, 30:31] / D + 1e-06)
+    tiles = [None] * count
     for tile in range(4):
         for x in range(4):
-            source = summed(x, tile)
-            if x == 0 and tile == 0:
-                inverse = lax.rsqrt(source[:, 30:31] / D + 1e-06)
+            source = None
             for piece in range(4):
                 yh, z = divmod(tile * 4 + piece, 8)
-                start = PIECE * (yh * 32 + z * 4 + x)
+                start = PIECE * (yh * 32 + z * 4 + x) - 128 * first_tile
+                touched = range(start // 128, (start + PIECE - 1) // 128 + 1)
+                touched = [t for t in touched if 0 <= t < count]
+                if not touched:
+                    continue
+                source = summed(x, tile) if source is None else source
                 moved = pltpu.roll(source, (start - piece * 32) % 128, 1)
-                for place_at in range(start // 128, (start + PIECE - 1) // 128 + 1):
-                    first, last = start - place_at * 128, start + PIECE - place_at * 128
-                    inside = (lane >= first) & (lane < last)
-                    old = tiles[place_at]
-                    tiles[place_at] = jnp.where(inside, moved, 0.0 if old is None else old)
-    cos = cosine[...]
-    sin = jnp.where(lower_part, -sine[...], sine[...])
-
-    def turned(u, gain):
-        square = u * u
-        both = jnp.sum(jnp.where(upper_head, 0.0, square), axis=1, keepdims=True)
-        other = jnp.sum(jnp.where(upper_head, square, 0.0), axis=1, keepdims=True)
-        mean = jnp.where(upper_head, other, both) * (1.0 / HEAD)
-        w = u * lax.rsqrt(mean + 1e-06) * gain
-        partner = jnp.where(lower_part, pltpu.roll(w, 96, 1), pltpu.roll(w, 32, 1))
-        return w * cos + partner * sin
-
-    for tile in range(10):
-        u = tiles[tile] * inverse
-        queries[:, tile * 128 : tile * 128 + 128] = turned(u, q_gain[...]).astype(BF)
-    for tile in range(10, 15):
-        u = tiles[tile] * inverse
-        if tile == 12:
-            u = jnp.where(upper_head, u, turned(u, k_gain[...]))
-        elif tile < 12:
-            u = turned(u, k_gain[...])
-        kv[:, (tile - 10) * 128 : (tile - 9) * 128] = u.astype(BF)
+                for t in touched:
+                    inside = (lane >= start - t * 128) & (lane < start + PIECE - t * 128)
+                    tiles[t] = jnp.where(inside, moved, 0.0 if tiles[t] is None else tiles[t])
+    return [u * inverse for u in tiles]
+
+
+def turn(u, cosine, sine, gain):
+    lane = lax.broadcasted_iota(jnp.int32, (ROWS, 128), 1)
+    upper_head = lane >= HEAD
+    lower_part = (lane % HEAD) < HEAD // 2
+    square = u * u
+    both = jnp.sum(jnp.where(upper_head, 0.0, square), axis=1, keepdims=True)
+    other = jnp.sum(jnp.where(upper_head, square, 0.0), axis=1, keepdims=True)
+    mean = jnp.where(upper_head, other, both) * (1.0 / HEAD)
+    w = u * lax.rsqrt(mean + 1e-06) * gain[...]
+    partner = jnp.where(lower_part, pltpu.roll(w, 96, 1), pltpu.roll(w, 32, 1))
+    return w * cosine[...] + partner * jnp.where(lower_part, -sine[...], sine[...])
+
+
+def rotate_queries_body(parts, cosine, sine, gain, queries):
+    for tile, u in enumerate(pieces_in_order(parts, 0, 10)):
+        queries[:, tile * 128 : tile * 128 + 128] = turn(u, cosine, sine, gain).astype(BF)
+
+
+def rotate_keys_body(table, parts, cosine, sine, gain, kv, cache):
+    upper_head = lax.broadcasted_iota(jnp.int32, (ROWS, 128), 1) >= HEAD
+    for tile, u in enumerate(pieces_in_order(parts, 10, 5)):
+        if tile == 2:
+            u = jnp.where(upper_head, u, turn(u, cosine, sine, gain))
+        elif tile < 2:
+            u = turn(u, cosine, sine, gain)
+        kv[:, tile * 128 : tile * 128 + 128] = u.astype(BF)
     for p in range(PAGES_DEV):
         cache[pl.ds(table[p], 1)] = kv[p * 8 : p * 8 + 8, :].reshape(1, 8, KV_DIM)
 
@@ -212,7 +218,7 @@
         for k in range(8):
             at = ((z + 8 - k) & 7) * 4 + ((x + 4 - i) & 3)
             for yh in range(2):
-                out[pl.ds(yh * 32 + at, 1)] = blocks[i, k, yh][None]
+                out[pl.ds(yh * 32 + at, 1)] = blocks[i, yh, k][None]
 
 
 def spread(x, axes, count):
@@ -231,19 +237,16 @@
     def shift(value, axis, count, step):
         return lax.ppermute(value, axis, [(i, (i + step) % count) for i in range(count)])
 
-    def gather(value, axis, count):
+    def gather(value, axis, size, count):
         step = 1
         while step < count:
-            value = jnp.concatenate([value, shift(value, axis, count, step)], axis=0)
+            value = jnp.concatenate([value, shift(value, axis, size, step)], axis=0)
             step *= 2
         return value
 
-    hidden = [hidden_in] + [shift(hidden_in, "x", 4, step) for step in range(1, 4)]
     columns = jnp.pad(qkv_weight.T, ((0, 2), (0, 0)))
     weight = spread(columns, ("yh", "z"), 16).reshape(512, TOK_DEV)
-    other = lax.ppermute(out_weight, "yh", swap)
-    weight, other = lax.optimization_barrier((weight, other))
-    mixing = jnp.where(yh == 0, jnp.stack([out_weight, other]), jnp.stack([other, out_weight]))
+    hidden = [hidden_in] + [shift(hidden_in, "x", 4, step) for step in range(1, 4)]
     hidden = [h.reshape(PAGES_DEV, 4, 2, 8, 256) for h in hidden]
     gain = attn_gain.reshape(1, 256)
     half_shape = jax.ShapeDtypeStruct((4, 128, 512), F32)
@@ -256,9 +259,9 @@
     sent = project(1)
     arrived = lax.ppermute(sent, "c", swap)
     partial = (project(0) + arrived).reshape(16, ROWS, 512)
-    mixing, partial = lax.optimization_barrier((mixing, partial))
+    mixing, partial = lax.optimization_barrier((out_weight[None], partial))
     parts = lax.all_to_all(partial, ("x", "yl"), 0, 0)
-    mixing = gather(mixing[None], "z", 8)
+    mixing = gather(mixing, "z", 8, 8)
     mixing, parts = lax.optimization_barrier((mixing, parts))
 
     row = jnp.arange(ROWS, dtype=jnp.int32)
@@ -269,30 +272,26 @@
     half = HEAD // 2
     frequency = jnp.exp(jnp.arange(half, dtype=F32) * (-2.0 * math.log(ROPE_BASE) / HEAD))
     angles = position.astype(F32)[:, None] * jnp.tile(frequency, 4)[None, :]
-    queries, kv, cache = call(
-        rotate_body,
+    tables = (jnp.cos(angles), jnp.sin(angles))
+    gains = [jnp.tile(g.astype(F32), 2)[None, :] for g in (q_gain, k_gain)]
+    kv, cache = call(
+        rotate_keys_body,
         (
-            jax.ShapeDtypeStruct((ROWS, Q_DIM), BF),
             jax.ShapeDtypeStruct((ROWS, KV_DIM), BF),
             jax.ShapeDtypeStruct((PAGES_DEV, 8, KV_DIM), BF),
         ),
-        [SM] + [VM] * 5,
-        "rotate",
-    )(
-        page_table,
-        parts,
-        jnp.cos(angles),
-        jnp.sin(angles),
-        jnp.tile(q_gain.astype(F32), 2)[None, :],
-        jnp.tile(k_gain.astype(F32), 2)[None, :],
-    )
-
+        [SM] + [VM] * 4,
+        "rotate_keys",
+    )(page_table, parts, *tables, gains[1])
     far = lax.ppermute(kv, "yh", swap)
-    kept = gather(queries[None], "yl", 4)
+    queries = call(
+        rotate_queries_body, jax.ShapeDtypeStruct((ROWS, Q_DIM), BF), [VM] * 4, "rotate_queries"
+    )(parts, *tables, gains[0])
+    far, queries = lax.optimization_barrier((far, queries))
+    kept = gather(queries[None], "yl", 4, 4)
     given = lax.ppermute(kept, "c", swap)
-    mixing = call(order_body, jax.ShapeDtypeStruct((64, 20, 256), BF), [SM, VM], "order")(
-        place, gather(mixing[None], "x", 4)
-    ).reshape(Q_DIM, 256)
+    other = lax.ppermute(mixing, "yh", swap)
+    mixing = jnp.where(yh == 0, jnp.stack([mixing, other]), jnp.stack([other, mixing]))
     target = jnp.arange(32, dtype=jnp.int32)[:, None, None]
     blocks = lax.all_to_all(jnp.where(target >= index, kv[None], far[None]), ("z", "x"), 0, 0)
 
@@ -310,8 +309,15 @@
     sent = attend(1)
     arrived = lax.ppermute(sent, "c", swap)
     parts = lax.all_to_all(attend(0) + arrived, "yl", 0, 0)
+    mixing = gather(mixing[None], "x", 4, 2)
+    mixing, parts = lax.optimization_barrier((mixing, parts))
+    mixing = jnp.concatenate([mixing, shift(mixing, "x", 4, 2)], axis=0)
     attended = call(divide_body, jax.ShapeDtypeStruct((ROWS, Q_DIM), BF), [VM], "divide")(parts)
     attended = lax.all_gather(attended, ("yl", "c"), axis=0, tiled=True)
+    attended, mixing = lax.optimization_barrier((attended, mixing))
+    mixing = call(order_body, jax.ShapeDtypeStruct((64, 20, 256), BF), [SM, VM], "order")(
+        place, mixing
+    ).reshape(Q_DIM, 256)
     hidden_out = call(
         mix_body, jax.ShapeDtypeStruct((PAGES_DEV, 8, 8, 256), BF), [VM] * 3, "mix"
     )(attended, mixing, hidden_in.reshape(PAGES_DEV, 8, 8, 256))

time: 188 us -> 186 us (0.989)
  blocking collectives: 39.1 us -> 16.3 us
  waiting for transfers between devices: 32.4 us -> 45.8 us
  starting transfers between devices: 92.3 us -> 98.5 us
    all_to_all x1 -> x0, blocking collectives: 22.5 us -> none  [on_device(): parts = lax.all_to_all(attend(0) + arrived, 'yl', 0, 0)]
    all_to_all x0 -> x1, waiting for transfers between devices: none -> 8.99 us  [on_device(): parts = lax.all_to_all(attend(0) + arrived, 'yl', 0, 0)]
    all_to_all x0 -> x1, starting transfers between devices: none -> 3.49 us  [on_device(): parts = lax.all_to_all(attend(0) + arrived, 'yl', 0, 0)]
    ppermute x1, waiting for transfers between devices: 0.62 us -> 3.21 us  [on_device(): other = lax.ppermute(mixing, 'yh', swap)]
    ppermute x10, starting transfers between devices: 33.8 us -> 35.7 us  [shift(): lax.ppermute(value, axis, [(i, (i + step) % count) for i in range(count)])]
  transfers between devices with their start and end apart: 18 -> 19, of which waited for: 10 -> 12; matrix products, arithmetic and copies ran while one was open for 1% -> 1% of each run, Pallas kernels for 3% -> 4%
where the time goes in v5:
time: 186 us; the launch traced here: 185 us
  starting transfers between devices  98.5 us (53%)
  waiting for transfers between devices  45.8 us (25%)
  blocking collectives  16.3 us (9%)
  Pallas kernels  15.3 us (8%)
  other arithmetic  4.16 us (2%)
  local copies, waits for them, and re-layouts  3.65 us (2%)
    ppermute x10, starting transfers between devices, shift(): lax.ppermute(value, axis, [(i, (i + step) % count) for i in range(count)])  35.7 us
    ppermute x10, waiting for transfers between devices, shift(): lax.ppermute(value, axis, [(i, (i + step) % count) for i in range(count)])  27.3 us
    all_gather x1, blocking collectives, on_device(): attended = lax.all_gather(attended, ('yl', 'c'), axis=0, tiled=True)  16.3 us
    all_to_all x1, starting transfers between devices, spread(): lax.all_to_all(jnp.broadcast_to(x[None], (count,) + x.shape), axes, 0, 0)  16.2 us
    ppermute x2, starting transfers between devices, on_device(): arrived = lax.ppermute(sent, 'c', swap)  9.56 us
    all_to_all x1, waiting for transfers between devices, on_device(): parts = lax.all_to_all(attend(0) + arrived, 'yl', 0, 0)  8.99 us
    pallas_call x2, Pallas kernels, attend(): call(functools.partial(attend_body, flip), jax.ShapeDtypeStruct((4, ROWS,...  8.69 us
    all_to_all x1, starting transfers between devices, on_device(): lax.all_to_all(jnp.where(target >= index, kv[None], far[None]), ('z', 'x'...  7.5 us
  transfers between devices with their start and end apart: 19, of which 12 were waited for; matrix products, arithmetic and copies ran while one was open for 1% of the time, Pallas kernels for 4%

profile of v5, /device:TPU:1, one launch (start us, length us, event | category | flops | bytes accessed | tf_op | source)
XLA Modules:
  0.0 184.7 jit_solution(2555674089750234319)
XLA Ops:
  2.1 16.2 %all-to-all-start = ((bf16[16,32,256]{2,1,0:T(8,128)(2,1)}), bf16[16,32,256]{2,1,0:T(8,128)(2,1)S(1)}, u32[]{:S(2)}, u32[]{:S(2)}) async-start(bf16[16,32,256]{2,1,0:T(8,128)(2,1)} %broadcast_in_dim.58), calls=%async_computation | async-start | bytes 524288 | tf_op jit(solution)/shard_map/all_to_all | solution.py:225
  18.3 3.1 %collective-permute-start = (bf16[256,256]{1,0:T(8,128)(2,1)}, bf16[256,256]{1,0:T(8,128)(2,1)S(1)}, u32[]{:S(2)}, u32[]{:S(2)}) collective-permute-start(bf16[256,256]{1,0:T(8,128)(2,1)} %param.8), channel_id=1, source_target_pairs={{0,8},{8,16},{16,24},{24,0},{1,9},{9,17},{17,25},{25,1},{2,10},{10... | collective-permute-start | bytes 393224 | tf_op jit(solution)/shard_map/ppermute | solution.py:238
  21.5 4.4 %collective-permute-start.1 = (bf16[256,256]{1,0:T(8,128)(2,1)}, bf16[256,256]{1,0:T(8,128)(2,1)S(1)}, u32[]{:S(2)}, u32[]{:S(2)}) collective-permute-start(bf16[256,256]{1,0:T(8,128)(2,1)} %param.8), channel_id=1, source_target_pairs={{0,16},{8,24},{16,0},{24,8},{1,17},{9,25},{17,1},{25,9},{2,18},{10... | collective-permute-start | bytes 393224 | tf_op jit(solution)/shard_map/ppermute | solution.py:238
  25.8 3.1 %collective-permute-start.2 = (bf16[256,256]{1,0:T(8,128)(2,1)}, bf16[256,256]{1,0:T(8,128)(2,1)S(1)}, u32[]{:S(2)}, u32[]{:S(2)}) collective-permute-start(bf16[256,256]{1,0:T(8,128)(2,1)} %param.8), channel_id=1, source_target_pairs={{0,24},{8,0},{16,8},{24,16},{1,25},{9,1},{17,9},{25,17},{2,26},{10... | collective-permute-start | bytes 393224 | tf_op jit(solution)/shard_map/ppermute | solution.py:238
  29.7 2.1 %collective-permute-done.2 = bf16[256,256]{1,0:T(8,128)(2,1)S(1)} collective-permute-done((bf16[256,256]{1,0:T(8,128)(2,1)}, bf16[256,256]{1,0:T(8,128)(2,1)S(1)}, u32[]{:S(2)}, u32[]{:S(2)}) %collective-permute-start.2) | collective-permute-done | bytes 131104 | tf_op jit(solution)/shard_map/ppermute | solution.py:238
  33.7 4.6 %collective-permute-start.3 = (f32[4,128,512]{2,1,0:T(8,128)S(1)}, f32[4,128,512]{2,1,0:T(8,128)S(1)}, u32[]{:S(2)}, u32[]{:S(2)}) collective-permute-start(f32[4,128,512]{2,1,0:T(8,128)S(1)} %project1.1), channel_id=1, source_target_pairs={{0,1},{1,0},{2,3},{3,2},{4,5},{5,4},{6,7},{7,6},{8,9},{9,8},{10,11... | collective-permute-start | bytes 3145736 | tf_op jit(solution)/shard_map/ppermute | solution.py:260
  41.8 4.5 %all-to-all-start.1 = ((f32[16,32,512]{2,1,0:T(8,128)}), f32[16,32,512]{2,1,0:T(8,128)S(1)}, u32[]{:S(2)}, u32[]{:S(2)}) async-start(f32[16,32,512]{2,1,0:T(8,128)} %bitcast.14), calls=%async_computation.1 | async-start | bytes 2097152 | tf_op jit(solution)/shard_map/all_to_all | solution.py:263
  46.6 3.3 %collective-permute-start.4 = (bf16[1,20,256]{2,1,0:T(8,128)(2,1)S(1)}, bf16[1,20,256]{2,1,0:T(8,128)(2,1)S(1)}, u32[]{:S(2)}, u32[]{:S(2)}) collective-permute-start(bf16[1,20,256]{2,1,0:T(8,128)(2,1)S(1)} %bitcast.42), channel_id=1, source_target_pairs={{0,32},{32,64},{64,96},{96,128},{128,160},{160,192},{192,224},{224... | collective-permute-start | bytes 30728 | tf_op jit(solution)/shard_map/ppermute | solution.py:238
  49.9 2.7 %collective-permute-done.4 = bf16[1,20,256]{2,1,0:T(8,128)(2,1)S(1)} collective-permute-done((bf16[1,20,256]{2,1,0:T(8,128)(2,1)S(1)}, bf16[1,20,256]{2,1,0:T(8,128)(2,1)S(1)}, u32[]{:S(2)}, u32[]{:S(2)}) %collective-permute-start.4) | collective-permute-done | bytes 10272 | tf_op jit(solution)/shard_map/ppermute | solution.py:238
  52.6 2.6 %collective-permute-start.5 = (bf16[2,20,256]{2,1,0:T(8,128)(2,1)S(1)}, bf16[2,20,256]{2,1,0:T(8,128)(2,1)S(1)}, u32[]{:S(2)}, u32[]{:S(2)}) collective-permute-start(bf16[2,20,256]{2,1,0:T(8,128)(2,1)S(1)} %pad_maximum_fusion.6), channel_id=1, source_target_pairs={{0,64},{32,96},{64,128},{96,160},{128,192},{160,224},{192,0},{224,... | collective-permute-start | bytes 61448 | tf_op jit(solution)/shard_map/ppermute | solution.py:238
  55.3 4.2 %collective-permute-done.5 = bf16[2,20,256]{2,1,0:T(8,128)(2,1)S(1)} collective-permute-done((bf16[2,20,256]{2,1,0:T(8,128)(2,1)S(1)}, bf16[2,20,256]{2,1,0:T(8,128)(2,1)S(1)}, u32[]{:S(2)}, u32[]{:S(2)}) %collective-permute-start.5) | collective-permute-done | bytes 20512 | tf_op jit(solution)/shard_map/ppermute | solution.py:238
  59.5 7.3 %collective-permute-start.6 = (bf16[4,20,256]{2,1,0:T(8,128)(2,1)S(1)}, bf16[4,20,256]{2,1,0:T(8,128)(2,1)S(1)}, u32[]{:S(2)}, u32[]{:S(2)}) collective-permute-start(bf16[4,20,256]{2,1,0:T(8,128)(2,1)S(1)} %pad_maximum_fusion.5), channel_id=1, source_target_pairs={{0,128},{32,160},{64,192},{96,224},{128,0},{160,32},{192,64},{224,... | collective-permute-start | bytes 122888 | tf_op jit(solution)/shard_map/ppermute | solution.py:238
  68.4 5.0 %all-to-all-done.1.parts = f32[16,32,512]{2,1,0:T(8,128)S(1)} async-done(((f32[16,32,512]{2,1,0:T(8,128)}), f32[16,32,512]{2,1,0:T(8,128)S(1)}, u32[]{:S(2)}, u32[]{:S(2)}) %all-to-all-start.1) | async-done | bytes 1048608 | tf_op jit(solution)/shard_map/all_to_all | solution.py:263
  73.4 1.5 rotate_keys.1
  74.9 7.1 %collective-permute-start.7 = (bf16[32,640]{1,0:T(8,128)(2,1)S(1)}, bf16[32,640]{1,0:T(8,128)(2,1)S(1)}, u32[]{:S(2)}, u32[]{:S(2)}) collective-permute-start(bf16[32,640]{1,0:T(8,128)(2,1)S(1)} %get-tuple-element.21), channel_id=1, source_target_pairs={{0,256},{256,0},{1,257},{257,1},{2,258},{258,2},{3,259},{259,3},{4... | collective-permute-start | bytes 122888 | tf_op jit(solution)/shard_map/ppermute | solution.py:286
  84.8 7.5 %all-to-all-start.2 = ((bf16[32,32,640]{2,1,0:T(8,128)(2,1)}), bf16[32,32,640]{2,1,0:T(8,128)(2,1)S(1)}, u32[]{:S(2)}, u32[]{:S(2)}) async-start(bf16[32,32,640]{2,1,0:T(8,128)(2,1)} %broadcast_select_fusion), calls=%async_computation.2 | async-start | bytes 2621440 | tf_op jit(solution)/shard_map/all_to_all | solution.py:296
  92.3 1.9 %collective-permute-start.9 = (bf16[1,32,1280]{2,1,0:T(8,128)(2,1)S(1)}, bf16[1,32,1280]{2,1,0:T(8,128)(2,1)S(1)}, u32[]{:S(2)}, u32[]{:S(2)}) collective-permute-start(bf16[1,32,1280]{2,1,0:T(8,128)(2,1)S(1)} %bitcast.28), channel_id=1, source_target_pairs={{0,2},{2,4},{4,6},{6,0},{1,3},{3,5},{5,7},{7,1},{8,10},{10,12},{12... | collective-permute-start | bytes 245768 | tf_op jit(solution)/shard_map/ppermute | solution.py:238
  94.2 5.1 %collective-permute-done.9 = bf16[1,32,1280]{2,1,0:T(8,128)(2,1)S(1)} collective-permute-done((bf16[1,32,1280]{2,1,0:T(8,128)(2,1)S(1)}, bf16[1,32,1280]{2,1,0:T(8,128)(2,1)S(1)}, u32[]{:S(2)}, u32[]{:S(2)}) %collective-permute-start.9) | collective-permute-done | bytes 81952 | tf_op jit(solution)/shard_map/ppermute | solution.py:238
  99.3 1.9 %collective-permute-start.10 = (bf16[2,32,1280]{2,1,0:T(8,128)(2,1)S(1)}, bf16[2,32,1280]{2,1,0:T(8,128)(2,1)S(1)}, u32[]{:S(2)}, u32[]{:S(2)}) collective-permute-start(bf16[2,32,1280]{2,1,0:T(8,128)(2,1)S(1)} %pad_maximum_fusion.3), channel_id=1, source_target_pairs={{0,4},{2,6},{4,0},{6,2},{1,5},{3,7},{5,1},{7,3},{8,12},{10,14},{12... | collective-permute-start | bytes 491528 | tf_op jit(solution)/shard_map/ppermute | solution.py:238
  101.2 5.4 %collective-permute-done.10 = bf16[2,32,1280]{2,1,0:T(8,128)(2,1)S(1)} collective-permute-done((bf16[2,32,1280]{2,1,0:T(8,128)(2,1)S(1)}, bf16[2,32,1280]{2,1,0:T(8,128)(2,1)S(1)}, u32[]{:S(2)}, u32[]{:S(2)}) %collective-permute-start.10) | collective-permute-done | bytes 163872 | tf_op jit(solution)/shard_map/ppermute | solution.py:238
  106.6 7.4 %collective-permute-start.11 = (bf16[4,32,1280]{2,1,0:T(8,128)(2,1)S(1)}, bf16[4,32,1280]{2,1,0:T(8,128)(2,1)S(1)}, u32[]{:S(2)}, u32[]{:S(2)}) collective-permute-start(bf16[4,32,1280]{2,1,0:T(8,128)(2,1)S(1)} %pad_maximum_fusion.2.q), channel_id=1, source_target_pairs={{0,1},{1,0},{2,3},{3,2},{4,5},{5,4},{6,7},{7,6},{8,9},{9,8},{10,11... | collective-permute-start | bytes 983048 | tf_op jit(solution)/shard_map/ppermute | solution.py:292
  114.0 7.0 %collective-permute-start.8 = (bf16[8,20,256]{2,1,0:T(8,128)(2,1)S(1)}, bf16[8,20,256]{2,1,0:T(8,128)(2,1)S(1)}, u32[]{:S(2)}, u32[]{:S(2)}) collective-permute-start(bf16[8,20,256]{2,1,0:T(8,128)(2,1)S(1)} %pad_maximum_fusion.4), channel_id=1, source_target_pairs={{0,256},{256,0},{1,257},{257,1},{2,258},{258,2},{3,259},{259,3},{4... | collective-permute-start | bytes 245768 | tf_op jit(solution)/shard_map/ppermute | solution.py:293
  121.0 3.2 %collective-permute-done.8 = bf16[8,20,256]{2,1,0:T(8,128)(2,1)S(1)} collective-permute-done((bf16[8,20,256]{2,1,0:T(8,128)(2,1)S(1)}, bf16[8,20,256]{2,1,0:T(8,128)(2,1)S(1)}, u32[]{:S(2)}, u32[]{:S(2)}) %collective-permute-start.8) | collective-permute-done | bytes 81952 | tf_op jit(solution)/shard_map/ppermute | solution.py:293
  124.3 4.4 %attend1.1 = f32[4,32,1408]{2,1,0:T(8,128)S(1)} custom-call(s32[7]{0:T(128)S(1)} %stack.45.place, s32[4]{0:T(128)S(1)} %copy-done.2, bf16[4,32,1280]{2,1,0:T(8,128)(2,1)S(1)} %collective-permute-done.11.q, bf16[32,32,640]{2,1,0:T(8,128)(2,1)S(1)} %all-to-all-done.2.blocks, bf16[32,640]{1,0:T(8,128)(2,1)S(1)} %collective-permute-done.7.far), custom_call_target="tpu_custom_call" | custom-call | tf_op jit(solution)/shard_map/attend1/pallas_call | solution.py:301
  128.6 5.0 %collective-permute-start.13 = (f32[4,32,1408]{2,1,0:T(8,128)S(1)}, f32[4,32,1408]{2,1,0:T(8,128)S(1)}, u32[]{:S(2)}, u32[]{:S(2)}) collective-permute-start(f32[4,32,1408]{2,1,0:T(8,128)S(1)} %attend1.1), channel_id=1, source_target_pairs={{0,1},{1,0},{2,3},{3,2},{4,5},{5,4},{6,7},{7,6},{8,9},{9,8},{10,11... | collective-permute-start | bytes 2162696 | tf_op jit(solution)/shard_map/ppermute | solution.py:310
  133.6 4.3 %attend0.1 = f32[4,32,1408]{2,1,0:T(8,128)S(1)} custom-call(s32[7]{0:T(128)S(1)} %stack.45.place, s32[4]{0:T(128)S(1)} %copy-done.2, bf16[4,32,1280]{2,1,0:T(8,128)(2,1)S(1)} %pad_maximum_fusion.2.q, bf16[32,32,640]{2,1,0:T(8,128)(2,1)S(1)} %all-to-all-done.2.blocks, bf16[32,640]{1,0:T(8,128)(2,1)S(1)} %collective-permute-done.7.far), custom_call_target="tpu_custom_call" | custom-call | tf_op jit(solution)/shard_map/attend0/pallas_call | solution.py:301
  138.9 3.5 %all-to-all-start.3 = ((f32[4,32,1408]{2,1,0:T(8,128)}), f32[4,32,1408]{2,1,0:T(8,128)S(1)}, u32[]{:S(2)}, u32[]{:S(2)}) async-start(f32[4,32,1408]{2,1,0:T(8,128)} %add.84), calls=%async_computation.3 | async-start | bytes 1441792 | tf_op jit(solution)/shard_map/all_to_all | solution.py:311
  142.4 2.9 %collective-permute-start.12 = (bf16[1,2,8,20,256]{4,3,2,1,0:T(8,128)(2,1)S(1)}, bf16[1,2,8,20,256]{4,3,2,1,0:T(8,128)(2,1)S(1)}, u32[]{:S(2)}, u32[]{:S(2)}) collective-permute-start(bf16[1,2,8,20,256]{4,3,2,1,0:T(8,128)(2,1)S(1)} %bitcast.38), channel_id=1, source_target_pairs={{0,8},{8,16},{16,24},{24,0},{1,9},{9,17},{17,25},{25,1},{2,10},{10... | collective-permute-start | bytes 491528 | tf_op jit(solution)/shard_map/ppermute | solution.py:238
  145.4 6.6 %collective-permute-done.12 = bf16[1,2,8,20,256]{4,3,2,1,0:T(8,128)(2,1)S(1)} collective-permute-done((bf16[1,2,8,20,256]{4,3,2,1,0:T(8,128)(2,1)S(1)}, bf16[1,2,8,20,256]{4,3,2,1,0:T(8,128)(2,1)S(1)}, u32[]{:S(2)}, u32[]{:S(2)}) %collective-permute-start.12) | collective-permute-done | bytes 163872 | tf_op jit(solution)/shard_map/ppermute | solution.py:238
  152.1 9.0 %all-to-all-done.3.parts = f32[4,32,1408]{2,1,0:T(8,128)S(1)} async-done(((f32[4,32,1408]{2,1,0:T(8,128)}), f32[4,32,1408]{2,1,0:T(8,128)S(1)}, u32[]{:S(2)}, u32[]{:S(2)}) %all-to-all-start.3) | async-done | bytes 720928 | tf_op jit(solution)/shard_map/all_to_all | solution.py:311
  161.1 5.1 %collective-permute-start.14 = (bf16[2,2,8,20,256]{4,3,2,1,0:T(8,128)(2,1)S(1)}, bf16[2,2,8,20,256]{4,3,2,1,0:T(8,128)(2,1)S(1)}, u32[]{:S(2)}, u32[]{:S(2)}) collective-permute-start(bf16[2,2,8,20,256]{4,3,2,1,0:T(8,128)(2,1)S(1)} %pad_maximum_fusion.1), channel_id=1, source_target_pairs={{0,16},{8,24},{16,0},{24,8},{1,17},{9,25},{17,1},{25,9},{2,18},{10... | collective-permute-start | bytes 983048 | tf_op jit(solution)/shard_map/ppermute | solution.py:238
  166.4 16.3 %all_gather.3.attended = bf16[256,1280]{1,0:T(8,128)(2,1)S(1)} all-gather(bf16[32,1280]{1,0:T(8,128)(2,1)S(1)} %divide.1), channel_id=1, replica_groups=mesh['yh'=2,'z'=8,'x'=4,'yl'=4,'c'=2] {'yl','c'}, dimensions={0}, use_global_device_ids=true | all-gather | bytes 737280 | tf_op jit(solution)/shard_map/all_gather | solution.py:316
  (59 shorter events, 15.5 us)
Async XLA Ops:
  2.1 29.7 %all-to-all-start = ((bf16[16,32,256]{2,1,0:T(8,128)(2,1)}), bf16[16,32,256]{2,1,0:T(8,128)(2,1)S(1)}, u32[]{:S(2)}, u32[]{:S(2)}) async-start(bf16[16,32,256]{2,1,0:T(8,128)(2,1)} %broadcast_in_dim.58), calls=%async_computation | async-start | bytes 524288 | tf_op jit(solution)/shard_map/all_to_all | solution.py:225
  18.3 11.3 %collective-permute-start = (bf16[256,256]{1,0:T(8,128)(2,1)}, bf16[256,256]{1,0:T(8,128)(2,1)S(1)}, u32[]{:S(2)}, u32[]{:S(2)}) collective-permute-start(bf16[256,256]{1,0:T(8,128)(2,1)} %param.8), channel_id=1, source_target_pairs={{0,8},{8,16},{16,24},{24,0},{1,9},{9,17},{17,25},{25,1},{2,10},{10... | collective-permute-start | bytes 393224 | tf_op jit(solution)/shard_map/ppermute | solution.py:238
  21.5 8.2 %collective-permute-start.1 = (bf16[256,256]{1,0:T(8,128)(2,1)}, bf16[256,256]{1,0:T(8,128)(2,1)S(1)}, u32[]{:S(2)}, u32[]{:S(2)}) collective-permute-start(bf16[256,256]{1,0:T(8,128)(2,1)} %param.8), channel_id=1, source_target_pairs={{0,16},{8,24},{16,0},{24,8},{1,17},{9,25},{17,1},{25,9},{2,18},{10... | collective-permute-start | bytes 393224 | tf_op jit(solution)/shard_map/ppermute | solution.py:238
  25.8 5.9 %collective-permute-start.2 = (bf16[256,256]{1,0:T(8,128)(2,1)}, bf16[256,256]{1,0:T(8,128)(2,1)S(1)}, u32[]{:S(2)}, u32[]{:S(2)}) collective-permute-start(bf16[256,256]{1,0:T(8,128)(2,1)} %param.8), channel_id=1, source_target_pairs={{0,24},{8,0},{16,8},{24,16},{1,25},{9,1},{17,9},{25,17},{2,26},{10... | collective-permute-start | bytes 393224 | tf_op jit(solution)/shard_map/ppermute | solution.py:238
  31.8 0.9 copy-start
  33.7 6.8 %collective-permute-start.3 = (f32[4,128,512]{2,1,0:T(8,128)S(1)}, f32[4,128,512]{2,1,0:T(8,128)S(1)}, u32[]{:S(2)}, u32[]{:S(2)}) collective-permute-start(f32[4,128,512]{2,1,0:T(8,128)S(1)} %project1.1), channel_id=1, source_target_pairs={{0,1},{1,0},{2,3},{3,2},{4,5},{5,4},{6,7},{7,6},{8,9},{9,8},{10,11... | collective-permute-start | bytes 3145736 | tf_op jit(solution)/shard_map/ppermute | solution.py:260
  41.8 4.6 %copy-start.2 = (s32[4]{0:T(128)S(1)}, s32[4]{0:T(128)}, u32[]{:S(2)}) copy-start(s32[4]{0:T(128)} %lengths.3) | copy-start | bytes 52
  41.8 4.8 %copy-start.4 = (bf16[20,256]{1,0:T(8,128)(2,1)S(1)}, bf16[20,256]{1,0:T(8,128)(2,1)}, u32[]{:S(2)}) copy-start(bf16[20,256]{1,0:T(8,128)(2,1)} %param.13) | copy-start | bytes 30724
  41.8 25.3 %copy-start.5 = (bf16[64]{0:T(256)(128)(2,1)S(1)}, bf16[64]{0:T(256)(128)(2,1)}, u32[]{:S(2)}) copy-start(bf16[64]{0:T(256)(128)(2,1)} %param.12) | copy-start | bytes 388
  41.8 31.6 %copy-start.3 = (s32[4]{0:T(128)S(1)}, s32[4]{0:T(128)}, u32[]{:S(2)}) copy-start(s32[4]{0:T(128)} %table.1) | copy-start | bytes 52
  41.8 40.3 %copy-start.6 = (bf16[64]{0:T(256)(128)(2,1)S(1)}, bf16[64]{0:T(256)(128)(2,1)}, u32[]{:S(2)}) copy-start(bf16[64]{0:T(256)(128)(2,1)} %param.11) | copy-start | bytes 388
  41.8 31.6 %all-to-all-start.1 = ((f32[16,32,512]{2,1,0:T(8,128)}), f32[16,32,512]{2,1,0:T(8,128)S(1)}, u32[]{:S(2)}, u32[]{:S(2)}) async-start(f32[16,32,512]{2,1,0:T(8,128)} %bitcast.14), calls=%async_computation.1 | async-start | bytes 2097152 | tf_op jit(solution)/shard_map/all_to_all | solution.py:263
  46.6 5.9 %collective-permute-start.4 = (bf16[1,20,256]{2,1,0:T(8,128)(2,1)S(1)}, bf16[1,20,256]{2,1,0:T(8,128)(2,1)S(1)}, u32[]{:S(2)}, u32[]{:S(2)}) collective-permute-start(bf16[1,20,256]{2,1,0:T(8,128)(2,1)S(1)} %bitcast.42), channel_id=1, source_target_pairs={{0,32},{32,64},{64,96},{96,128},{128,160},{160,192},{192,224},{224... | collective-permute-start | bytes 30728 | tf_op jit(solution)/shard_map/ppermute | solution.py:238
  52.6 7.0 %collective-permute-start.5 = (bf16[2,20,256]{2,1,0:T(8,128)(2,1)S(1)}, bf16[2,20,256]{2,1,0:T(8,128)(2,1)S(1)}, u32[]{:S(2)}, u32[]{:S(2)}) collective-permute-start(bf16[2,20,256]{2,1,0:T(8,128)(2,1)S(1)} %pad_maximum_fusion.6), channel_id=1, source_target_pairs={{0,64},{32,96},{64,128},{96,160},{128,192},{160,224},{192,0},{224,... | collective-permute-start | bytes 61448 | tf_op jit(solution)/shard_map/ppermute | solution.py:238
  59.5 8.8 %collective-permute-start.6 = (bf16[4,20,256]{2,1,0:T(8,128)(2,1)S(1)}, bf16[4,20,256]{2,1,0:T(8,128)(2,1)S(1)}, u32[]{:S(2)}, u32[]{:S(2)}) collective-permute-start(bf16[4,20,256]{2,1,0:T(8,128)(2,1)S(1)} %pad_maximum_fusion.5), channel_id=1, source_target_pairs={{0,128},{32,160},{64,192},{96,224},{128,0},{160,32},{192,64},{224,... | collective-permute-start | bytes 122888 | tf_op jit(solution)/shard_map/ppermute | solution.py:238
  74.9 8.6 %collective-permute-start.7 = (bf16[32,640]{1,0:T(8,128)(2,1)S(1)}, bf16[32,640]{1,0:T(8,128)(2,1)S(1)}, u32[]{:S(2)}, u32[]{:S(2)}) collective-permute-start(bf16[32,640]{1,0:T(8,128)(2,1)S(1)} %get-tuple-element.21), channel_id=1, source_target_pairs={{0,256},{256,0},{1,257},{257,1},{2,258},{258,2},{3,259},{259,3},{4... | collective-permute-start | bytes 122888 | tf_op jit(solution)/shard_map/ppermute | solution.py:286
  84.8 39.5 %all-to-all-start.2 = ((bf16[32,32,640]{2,1,0:T(8,128)(2,1)}), bf16[32,32,640]{2,1,0:T(8,128)(2,1)S(1)}, u32[]{:S(2)}, u32[]{:S(2)}) async-start(bf16[32,32,640]{2,1,0:T(8,128)(2,1)} %broadcast_select_fusion), calls=%async_computation.2 | async-start | bytes 2621440 | tf_op jit(solution)/shard_map/all_to_all | solution.py:296
  92.3 7.0 %collective-permute-start.9 = (bf16[1,32,1280]{2,1,0:T(8,128)(2,1)S(1)}, bf16[1,32,1280]{2,1,0:T(8,128)(2,1)S(1)}, u32[]{:S(2)}, u32[]{:S(2)}) collective-permute-start(bf16[1,32,1280]{2,1,0:T(8,128)(2,1)S(1)} %bitcast.28), channel_id=1, source_target_pairs={{0,2},{2,4},{4,6},{6,0},{1,3},{3,5},{5,7},{7,1},{8,10},{10,12},{12... | collective-permute-start | bytes 245768 | tf_op jit(solution)/shard_map/ppermute | solution.py:238
  99.3 7.3 %collective-permute-start.10 = (bf16[2,32,1280]{2,1,0:T(8,128)(2,1)S(1)}, bf16[2,32,1280]{2,1,0:T(8,128)(2,1)S(1)}, u32[]{:S(2)}, u32[]{:S(2)}) collective-permute-start(bf16[2,32,1280]{2,1,0:T(8,128)(2,1)S(1)} %pad_maximum_fusion.3), channel_id=1, source_target_pairs={{0,4},{2,6},{4,0},{6,2},{1,5},{3,7},{5,1},{7,3},{8,12},{10,14},{12... | collective-permute-start | bytes 491528 | tf_op jit(solution)/shard_map/ppermute | solution.py:238
  106.6 17.6 %collective-permute-start.11 = (bf16[4,32,1280]{2,1,0:T(8,128)(2,1)S(1)}, bf16[4,32,1280]{2,1,0:T(8,128)(2,1)S(1)}, u32[]{:S(2)}, u32[]{:S(2)}) collective-permute-start(bf16[4,32,1280]{2,1,0:T(8,128)(2,1)S(1)} %pad_maximum_fusion.2.q), channel_id=1, source_target_pairs={{0,1},{1,0},{2,3},{3,2},{4,5},{5,4},{6,7},{7,6},{8,9},{9,8},{10,11... | collective-permute-start | bytes 983048 | tf_op jit(solution)/shard_map/ppermute | solution.py:292
  114.0 10.2 %collective-permute-start.8 = (bf16[8,20,256]{2,1,0:T(8,128)(2,1)S(1)}, bf16[8,20,256]{2,1,0:T(8,128)(2,1)S(1)}, u32[]{:S(2)}, u32[]{:S(2)}) collective-permute-start(bf16[8,20,256]{2,1,0:T(8,128)(2,1)S(1)} %pad_maximum_fusion.4), channel_id=1, source_target_pairs={{0,256},{256,0},{1,257},{257,1},{2,258},{258,2},{3,259},{259,3},{4... | collective-permute-start | bytes 245768 | tf_op jit(solution)/shard_map/ppermute | solution.py:293
  128.6 9.3 %collective-permute-start.13 = (f32[4,32,1408]{2,1,0:T(8,128)S(1)}, f32[4,32,1408]{2,1,0:T(8,128)S(1)}, u32[]{:S(2)}, u32[]{:S(2)}) collective-permute-start(f32[4,32,1408]{2,1,0:T(8,128)S(1)} %attend1.1), channel_id=1, source_target_pairs={{0,1},{1,0},{2,3},{3,2},{4,5},{5,4},{6,7},{7,6},{8,9},{9,8},{10,11... | collective-permute-start | bytes 2162696 | tf_op jit(solution)/shard_map/ppermute | solution.py:310
  138.9 22.1 %all-to-all-start.3 = ((f32[4,32,1408]{2,1,0:T(8,128)}), f32[4,32,1408]{2,1,0:T(8,128)S(1)}, u32[]{:S(2)}, u32[]{:S(2)}) async-start(f32[4,32,1408]{2,1,0:T(8,128)} %add.84), calls=%async_computation.3 | async-start | bytes 1441792 | tf_op jit(solution)/shard_map/all_to_all | solution.py:311
  142.4 9.6 %collective-permute-start.12 = (bf16[1,2,8,20,256]{4,3,2,1,0:T(8,128)(2,1)S(1)}, bf16[1,2,8,20,256]{4,3,2,1,0:T(8,128)(2,1)S(1)}, u32[]{:S(2)}, u32[]{:S(2)}) collective-permute-start(bf16[1,2,8,20,256]{4,3,2,1,0:T(8,128)(2,1)S(1)} %bitcast.38), channel_id=1, source_target_pairs={{0,8},{8,16},{16,24},{24,0},{1,9},{9,17},{17,25},{25,1},{2,10},{10... | collective-permute-start | bytes 491528 | tf_op jit(solution)/shard_map/ppermute | solution.py:238
  161.1 21.6 %collective-permute-start.14 = (bf16[2,2,8,20,256]{4,3,2,1,0:T(8,128)(2,1)S(1)}, bf16[2,2,8,20,256]{4,3,2,1,0:T(8,128)(2,1)S(1)}, u32[]{:S(2)}, u32[]{:S(2)}) collective-permute-start(bf16[2,2,8,20,256]{4,3,2,1,0:T(8,128)(2,1)S(1)} %pad_maximum_fusion.1), channel_id=1, source_target_pairs={{0,16},{8,24},{16,0},{24,8},{1,17},{9,25},{17,1},{25,9},{2,18},{10... | collective-permute-start | bytes 983048 | tf_op jit(solution)/shard_map/ppermute | solution.py:238
  182.8 0.9 copy-start.1

commit v6 on v5

--- a/solution.py
+++ b/solution.py
@@ -186,7 +186,21 @@
                 at = slice(h * 128 + k * ROWS, h * 128 + (k + 1) * ROWS)
                 to = pl.ds(owners[k], 1)
                 out[to, :, head * HEAD : (head + 1) * HEAD] = numerator[at][None]
-                out[to, :, Q_DIM + head : Q_DIM + head + 1] = denominator[at][None]
+                for lane in (Q_DIM + head, Q_DIM + HEAD + head):
+                    out[to, :, lane : lane + 1] = denominator[at][None]
+
+
+def pack_body(here, there, out):
+    lane = lax.broadcasted_iota(jnp.int32, (ROWS, 128), 1)
+    for k in range(4):
+        for tile in range(11):
+            at = pl.ds(tile * 128, 128)
+            total = here[k, :, at] + there[k, :, at]
+            low = total.astype(BF)
+            if tile == 10:
+                rest = total - low.astype(F32)
+                low = jnp.where(lane < HEAD, low.astype(F32), rest).astype(BF)
+            out[k, :, at] = low
 
 
 def divide_body(parts, out):
@@ -194,9 +208,11 @@
 
     def total(tile):
         at = pl.ds(tile * 128, 128)
-        return (parts[0, :, at] + parts[1, :, at]) + (parts[2, :, at] + parts[3, :, at])
+        four = [parts[k, :, at].astype(F32) for k in range(4)]
+        return (four[0] + four[1]) + (four[2] + four[3])
 
     under = total(10)
+    under = under + pltpu.roll(under, HEAD, 1)
     for tile in range(10):
         low, high = under[:, 2 * tile : 2 * tile + 1], under[:, 2 * tile + 1 : 2 * tile + 2]
         out[:, tile * 128 : tile * 128 + 128] = (
@@ -288,10 +304,14 @@
         rotate_queries_body, jax.ShapeDtypeStruct((ROWS, Q_DIM), BF), [VM] * 4, "rotate_queries"
     )(parts, *tables, gains[0])
     far, queries = lax.optimization_barrier((far, queries))
-    kept = gather(queries[None], "yl", 4, 4)
+    kept = gather(queries[None], "yl", 4, 2)
+    other = lax.ppermute(mixing, "yh", swap)
+    kept, other = lax.optimization_barrier((kept, other))
+    mixing = jnp.where(yh == 0, jnp.stack([mixing, other]), jnp.stack([other, mixing]))
+    kept = jnp.concatenate([kept, shift(kept, "yl", 4, 2)], axis=0)
+    mixing = gather(mixing[None], "x", 4, 2)
+    kept, mixing = lax.optimization_barrier((kept, mixing))
     given = lax.ppermute(kept, "c", swap)
-    other = lax.ppermute(mixing, "yh", swap)
-    mixing = jnp.where(yh == 0, jnp.stack([mixing, other]), jnp.stack([other, mixing]))
     target = jnp.arange(32, dtype=jnp.int32)[:, None, None]
     blocks = lax.all_to_all(jnp.where(target >= index, kv[None], far[None]), ("z", "x"), 0, 0)
 
@@ -308,16 +328,17 @@
 
     sent = attend(1)
     arrived = lax.ppermute(sent, "c", swap)
-    parts = lax.all_to_all(attend(0) + arrived, "yl", 0, 0)
-    mixing = gather(mixing[None], "x", 4, 2)
-    mixing, parts = lax.optimization_barrier((mixing, parts))
+    packed = call(pack_body, jax.ShapeDtypeStruct((4, ROWS, SUMS), BF), [VM, VM], "pack")(
+        attend(0), arrived
+    )
+    mixing, packed = lax.optimization_barrier((mixing, packed))
+    parts = lax.all_to_all(packed, "yl", 0, 0)
     mixing = jnp.concatenate([mixing, shift(mixing, "x", 4, 2)], axis=0)
-    attended = call(divide_body, jax.ShapeDtypeStruct((ROWS, Q_DIM), BF), [VM], "divide")(parts)
-    attended = lax.all_gather(attended, ("yl", "c"), axis=0, tiled=True)
-    attended, mixing = lax.optimization_barrier((attended, mixing))
     mixing = call(order_body, jax.ShapeDtypeStruct((64, 20, 256), BF), [SM, VM], "order")(
         place, mixing
     ).reshape(Q_DIM, 256)
+    attended = call(divide_body, jax.ShapeDtypeStruct((ROWS, Q_DIM), BF), [VM], "divide")(parts)
+    attended = lax.all_gather(attended, ("yl", "c"), axis=0, tiled=True)
     hidden_out = call(
         mix_body, jax.ShapeDtypeStruct((PAGES_DEV, 8, 8, 256), BF), [VM] * 3, "mix"
     )(attended, mixing, hidden_in.reshape(PAGES_DEV, 8, 8, 256))

time: 186 us -> 177 us (0.952)
  waiting for transfers between devices: 45.8 us -> 34.2 us
    all_to_all x1, waiting for transfers between devices: 8.99 us -> 0.01 us  [on_device(): parts = lax.all_to_all(packed, 'yl', 0, 0)]
    ppermute x10, waiting for transfers between devices: 27.3 us -> 24.1 us  [shift(): lax.ppermute(value, axis, [(i, (i + step) % count) for i in range(count)])]
    ppermute x10, starting transfers between devices: 35.7 us -> 38.6 us  [shift(): lax.ppermute(value, axis, [(i, (i + step) % count) for i in range(count)])]
    ppermute x2, starting transfers between devices: 9.56 us -> 7.5 us  [on_device(): arrived = lax.ppermute(sent, 'c', swap)]
where the time goes in v6:
time: 177 us; the launch traced here: 174 us
  starting transfers between devices  100 us (56%)
  waiting for transfers between devices  34.2 us (19%)
  blocking collectives  16.3 us (9%)
  Pallas kernels  16.2 us (9%)
  local copies, waits for them, and re-layouts  3.52 us (2%)
  other arithmetic  3.19 us (2%)
    ppermute x10, starting transfers between devices, shift(): lax.ppermute(value, axis, [(i, (i + step) % count) for i in range(count)])  38.6 us
    ppermute x10, waiting for transfers between devices, shift(): lax.ppermute(value, axis, [(i, (i + step) % count) for i in range(count)])  24.1 us
    all_gather x1, blocking collectives, on_device(): attended = lax.all_gather(attended, ('yl', 'c'), axis=0, tiled=True)  16.3 us
    all_to_all x1, starting transfers between devices, spread(): lax.all_to_all(jnp.broadcast_to(x[None], (count,) + x.shape), axes, 0, 0)  16.2 us
    pallas_call x2, Pallas kernels, attend(): call(functools.partial(attend_body, flip), jax.ShapeDtypeStruct((4, ROWS,...  8.68 us
    ppermute x1, starting transfers between devices, on_device(): given = lax.ppermute(kept, 'c', swap)  7.75 us
    ppermute x2, starting transfers between devices, on_device(): arrived = lax.ppermute(sent, 'c', swap)  7.5 us
    all_to_all x1, starting transfers between devices, on_device(): lax.all_to_all(jnp.where(target >= index, kv[None], far[None]), ('z', 'x'...  7.5 us
  transfers between devices with their start and end apart: 19, of which 12 were waited for; matrix products, arithmetic and copies ran while one was open for 1% of the time, Pallas kernels for 4%

profile of v6, /device:TPU:1, one launch (start us, length us, event | category | flops | bytes accessed | tf_op | source)
XLA Modules:
  0.0 174.4 jit_solution(2368682946357278779)
XLA Ops:
  2.1 16.2 %all-to-all-start = ((bf16[16,32,256]{2,1,0:T(8,128)(2,1)}), bf16[16,32,256]{2,1,0:T(8,128)(2,1)S(1)}, u32[]{:S(2)}, u32[]{:S(2)}) async-start(bf16[16,32,256]{2,1,0:T(8,128)(2,1)} %broadcast_in_dim.56), calls=%async_computation | async-start | bytes 524288 | tf_op jit(solution)/shard_map/all_to_all | solution.py:241
  18.3 3.1 %collective-permute-start = (bf16[256,256]{1,0:T(8,128)(2,1)}, bf16[256,256]{1,0:T(8,128)(2,1)S(1)}, u32[]{:S(2)}, u32[]{:S(2)}) collective-permute-start(bf16[256,256]{1,0:T(8,128)(2,1)} %param.8), channel_id=1, source_target_pairs={{0,8},{8,16},{16,24},{24,0},{1,9},{9,17},{17,25},{25,1},{2,10},{10... | collective-permute-start | bytes 393224 | tf_op jit(solution)/shard_map/ppermute | solution.py:254
  21.5 4.4 %collective-permute-start.1 = (bf16[256,256]{1,0:T(8,128)(2,1)}, bf16[256,256]{1,0:T(8,128)(2,1)S(1)}, u32[]{:S(2)}, u32[]{:S(2)}) collective-permute-start(bf16[256,256]{1,0:T(8,128)(2,1)} %param.8), channel_id=1, source_target_pairs={{0,16},{8,24},{16,0},{24,8},{1,17},{9,25},{17,1},{25,9},{2,18},{10... | collective-permute-start | bytes 393224 | tf_op jit(solution)/shard_map/ppermute | solution.py:254
  25.8 3.1 %collective-permute-start.2 = (bf16[256,256]{1,0:T(8,128)(2,1)}, bf16[256,256]{1,0:T(8,128)(2,1)S(1)}, u32[]{:S(2)}, u32[]{:S(2)}) collective-permute-start(bf16[256,256]{1,0:T(8,128)(2,1)} %param.8), channel_id=1, source_target_pairs={{0,24},{8,0},{16,8},{24,16},{1,25},{9,1},{17,9},{25,17},{2,26},{10... | collective-permute-start | bytes 393224 | tf_op jit(solution)/shard_map/ppermute | solution.py:254
  29.7 2.1 %collective-permute-done.2 = bf16[256,256]{1,0:T(8,128)(2,1)S(1)} collective-permute-done((bf16[256,256]{1,0:T(8,128)(2,1)}, bf16[256,256]{1,0:T(8,128)(2,1)S(1)}, u32[]{:S(2)}, u32[]{:S(2)}) %collective-permute-start.2) | collective-permute-done | bytes 131104 | tf_op jit(solution)/shard_map/ppermute | solution.py:254
  33.7 4.6 %collective-permute-start.3 = (f32[4,128,512]{2,1,0:T(8,128)S(1)}, f32[4,128,512]{2,1,0:T(8,128)S(1)}, u32[]{:S(2)}, u32[]{:S(2)}) collective-permute-start(f32[4,128,512]{2,1,0:T(8,128)S(1)} %project1.1), channel_id=1, source_target_pairs={{0,1},{1,0},{2,3},{3,2},{4,5},{5,4},{6,7},{7,6},{8,9},{9,8},{10,11... | collective-permute-start | bytes 3145736 | tf_op jit(solution)/shard_map/ppermute | solution.py:276
  41.8 4.5 %all-to-all-start.1 = ((f32[16,32,512]{2,1,0:T(8,128)}), f32[16,32,512]{2,1,0:T(8,128)S(1)}, u32[]{:S(2)}, u32[]{:S(2)}) async-start(f32[16,32,512]{2,1,0:T(8,128)} %bitcast.14), calls=%async_computation.1 | async-start | bytes 2097152 | tf_op jit(solution)/shard_map/all_to_all | solution.py:279
  46.6 3.3 %collective-permute-start.4 = (bf16[1,20,256]{2,1,0:T(8,128)(2,1)S(1)}, bf16[1,20,256]{2,1,0:T(8,128)(2,1)S(1)}, u32[]{:S(2)}, u32[]{:S(2)}) collective-permute-start(bf16[1,20,256]{2,1,0:T(8,128)(2,1)S(1)} %bitcast.38), channel_id=1, source_target_pairs={{0,32},{32,64},{64,96},{96,128},{128,160},{160,192},{192,224},{224... | collective-permute-start | bytes 30728 | tf_op jit(solution)/shard_map/ppermute | solution.py:254
  49.9 2.7 %collective-permute-done.4 = bf16[1,20,256]{2,1,0:T(8,128)(2,1)S(1)} collective-permute-done((bf16[1,20,256]{2,1,0:T(8,128)(2,1)S(1)}, bf16[1,20,256]{2,1,0:T(8,128)(2,1)S(1)}, u32[]{:S(2)}, u32[]{:S(2)}) %collective-permute-start.4) | collective-permute-done | bytes 10272 | tf_op jit(solution)/shard_map/ppermute | solution.py:254
  52.6 2.6 %collective-permute-start.5 = (bf16[2,20,256]{2,1,0:T(8,128)(2,1)S(1)}, bf16[2,20,256]{2,1,0:T(8,128)(2,1)S(1)}, u32[]{:S(2)}, u32[]{:S(2)}) collective-permute-start(bf16[2,20,256]{2,1,0:T(8,128)(2,1)S(1)} %pad_maximum_fusion.6), channel_id=1, source_target_pairs={{0,64},{32,96},{64,128},{96,160},{128,192},{160,224},{192,0},{224,... | collective-permute-start | bytes 61448 | tf_op jit(solution)/shard_map/ppermute | solution.py:254
  55.3 4.2 %collective-permute-done.5 = bf16[2,20,256]{2,1,0:T(8,128)(2,1)S(1)} collective-permute-done((bf16[2,20,256]{2,1,0:T(8,128)(2,1)S(1)}, bf16[2,20,256]{2,1,0:T(8,128)(2,1)S(1)}, u32[]{:S(2)}, u32[]{:S(2)}) %collective-permute-start.5) | collective-permute-done | bytes 20512 | tf_op jit(solution)/shard_map/ppermute | solution.py:254
  59.5 7.3 %collective-permute-start.6 = (bf16[4,20,256]{2,1,0:T(8,128)(2,1)S(1)}, bf16[4,20,256]{2,1,0:T(8,128)(2,1)S(1)}, u32[]{:S(2)}, u32[]{:S(2)}) collective-permute-start(bf16[4,20,256]{2,1,0:T(8,128)(2,1)S(1)} %pad_maximum_fusion.5), channel_id=1, source_target_pairs={{0,128},{32,160},{64,192},{96,224},{128,0},{160,32},{192,64},{224,... | collective-permute-start | bytes 122888 | tf_op jit(solution)/shard_map/ppermute | solution.py:254
  68.4 5.0 %all-to-all-done.1.parts = f32[16,32,512]{2,1,0:T(8,128)S(1)} async-done(((f32[16,32,512]{2,1,0:T(8,128)}), f32[16,32,512]{2,1,0:T(8,128)S(1)}, u32[]{:S(2)}, u32[]{:S(2)}) %all-to-all-start.1) | async-done | bytes 1048608 | tf_op jit(solution)/shard_map/all_to_all | solution.py:279
  73.4 1.5 rotate_keys.1
  74.9 7.1 %collective-permute-start.7 = (bf16[32,640]{1,0:T(8,128)(2,1)S(1)}, bf16[32,640]{1,0:T(8,128)(2,1)S(1)}, u32[]{:S(2)}, u32[]{:S(2)}) collective-permute-start(bf16[32,640]{1,0:T(8,128)(2,1)S(1)} %get-tuple-element.23), channel_id=1, source_target_pairs={{0,256},{256,0},{1,257},{257,1},{2,258},{258,2},{3,259},{259,3},{4... | collective-permute-start | bytes 122888 | tf_op jit(solution)/shard_map/ppermute | solution.py:302
  83.5 1.3 broadcast_select_fusion
  84.8 7.5 %all-to-all-start.2 = ((bf16[32,32,640]{2,1,0:T(8,128)(2,1)}), bf16[32,32,640]{2,1,0:T(8,128)(2,1)S(1)}, u32[]{:S(2)}, u32[]{:S(2)}) async-start(bf16[32,32,640]{2,1,0:T(8,128)(2,1)} %broadcast_select_fusion), calls=%async_computation.2 | async-start | bytes 2621440 | tf_op jit(solution)/shard_map/all_to_all | solution.py:316
  92.3 1.9 %collective-permute-start.8 = (bf16[1,32,1280]{2,1,0:T(8,128)(2,1)S(1)}, bf16[1,32,1280]{2,1,0:T(8,128)(2,1)S(1)}, u32[]{:S(2)}, u32[]{:S(2)}) collective-permute-start(bf16[1,32,1280]{2,1,0:T(8,128)(2,1)S(1)} %bitcast.33), channel_id=1, source_target_pairs={{0,2},{2,4},{4,6},{6,0},{1,3},{3,5},{5,7},{7,1},{8,10},{10,12},{12... | collective-permute-start | bytes 245768 | tf_op jit(solution)/shard_map/ppermute | solution.py:254
  94.2 7.0 %collective-permute-start.9 = (bf16[8,20,256]{2,1,0:T(8,128)(2,1)S(1)}, bf16[8,20,256]{2,1,0:T(8,128)(2,1)S(1)}, u32[]{:S(2)}, u32[]{:S(2)}) collective-permute-start(bf16[8,20,256]{2,1,0:T(8,128)(2,1)S(1)} %pad_maximum_fusion.4), channel_id=1, source_target_pairs={{0,256},{256,0},{1,257},{257,1},{2,258},{258,2},{3,259},{259,3},{4... | collective-permute-start | bytes 245768 | tf_op jit(solution)/shard_map/ppermute | solution.py:308
  101.3 2.5 %collective-permute-done.9 = bf16[8,20,256]{2,1,0:T(8,128)(2,1)S(1)} collective-permute-done((bf16[8,20,256]{2,1,0:T(8,128)(2,1)S(1)}, bf16[8,20,256]{2,1,0:T(8,128)(2,1)S(1)}, u32[]{:S(2)}, u32[]{:S(2)}) %collective-permute-start.9) | collective-permute-done | bytes 81952 | tf_op jit(solution)/shard_map/ppermute | solution.py:308
  103.8 3.1 %collective-permute-start.11 = (bf16[1,2,8,20,256]{4,3,2,1,0:T(8,128)(2,1)S(1)}, bf16[1,2,8,20,256]{4,3,2,1,0:T(8,128)(2,1)S(1)}, u32[]{:S(2)}, u32[]{:S(2)}) collective-permute-start(bf16[1,2,8,20,256]{4,3,2,1,0:T(8,128)(2,1)S(1)} %maximum_select_fusion), channel_id=1, source_target_pairs={{0,8},{8,16},{16,24},{24,0},{1,9},{9,17},{17,25},{25,1},{2,10},{10... | collective-permute-start | bytes 491528 | tf_op jit(solution)/shard_map/ppermute | solution.py:254
  107.0 5.2 %collective-permute-start.10 = (bf16[2,32,1280]{2,1,0:T(8,128)(2,1)S(1)}, bf16[2,32,1280]{2,1,0:T(8,128)(2,1)S(1)}, u32[]{:S(2)}, u32[]{:S(2)}) collective-permute-start(bf16[2,32,1280]{2,1,0:T(8,128)(2,1)S(1)} %pad_maximum_fusion.3), channel_id=1, source_target_pairs={{0,4},{2,6},{4,0},{6,2},{1,5},{3,7},{5,1},{7,3},{8,12},{10,14},{12... | collective-permute-start | bytes 491528 | tf_op jit(solution)/shard_map/ppermute | solution.py:254
  112.2 2.6 %collective-permute-done.11 = bf16[1,2,8,20,256]{4,3,2,1,0:T(8,128)(2,1)S(1)} collective-permute-done((bf16[1,2,8,20,256]{4,3,2,1,0:T(8,128)(2,1)S(1)}, bf16[1,2,8,20,256]{4,3,2,1,0:T(8,128)(2,1)S(1)}, u32[]{:S(2)}, u32[]{:S(2)}) %collective-permute-start.11) | collective-permute-done | bytes 163872 | tf_op jit(solution)/shard_map/ppermute | solution.py:254
  114.8 2.1 %collective-permute-done.10 = bf16[2,32,1280]{2,1,0:T(8,128)(2,1)S(1)} collective-permute-done((bf16[2,32,1280]{2,1,0:T(8,128)(2,1)S(1)}, bf16[2,32,1280]{2,1,0:T(8,128)(2,1)S(1)}, u32[]{:S(2)}, u32[]{:S(2)}) %collective-permute-start.10) | collective-permute-done | bytes 163872 | tf_op jit(solution)/shard_map/ppermute | solution.py:254
  117.0 7.7 %collective-permute-start.12 = (bf16[4,32,1280]{2,1,0:T(8,128)(2,1)S(1)}, bf16[4,32,1280]{2,1,0:T(8,128)(2,1)S(1)}, u32[]{:S(2)}, u32[]{:S(2)}) collective-permute-start(bf16[4,32,1280]{2,1,0:T(8,128)(2,1)S(1)} %pad_maximum_fusion.2.q), channel_id=1, source_target_pairs={{0,1},{1,0},{2,3},{3,2},{4,5},{5,4},{6,7},{7,6},{8,9},{9,8},{10,11... | collective-permute-start | bytes 983048 | tf_op jit(solution)/shard_map/ppermute | solution.py:314
  126.0 4.4 %attend1.1 = f32[4,32,1408]{2,1,0:T(8,128)S(1)} custom-call(s32[7]{0:T(128)S(1)} %stack.45.place, s32[4]{0:T(128)S(1)} %copy-done.2, bf16[4,32,1280]{2,1,0:T(8,128)(2,1)S(1)} %collective-permute-done.12.q, bf16[32,32,640]{2,1,0:T(8,128)(2,1)S(1)} %all-to-all-done.2.blocks, bf16[32,640]{1,0:T(8,128)(2,1)S(1)} %collective-permute-done.7.far), custom_call_target="tpu_custom_call" | custom-call | tf_op jit(solution)/shard_map/attend1/pallas_call | solution.py:321
  130.3 2.9 %collective-permute-start.13 = (f32[4,32,1408]{2,1,0:T(8,128)S(1)}, f32[4,32,1408]{2,1,0:T(8,128)S(1)}, u32[]{:S(2)}, u32[]{:S(2)}) collective-permute-start(f32[4,32,1408]{2,1,0:T(8,128)S(1)} %attend1.1), channel_id=1, source_target_pairs={{0,1},{1,0},{2,3},{3,2},{4,5},{5,4},{6,7},{7,6},{8,9},{9,8},{10,11... | collective-permute-start | bytes 2162696 | tf_op jit(solution)/shard_map/ppermute | solution.py:330
  133.3 4.3 %attend0.1.here = f32[4,32,1408]{2,1,0:T(8,128)S(1)} custom-call(s32[7]{0:T(128)S(1)} %stack.45.place, s32[4]{0:T(128)S(1)} %copy-done.2, bf16[4,32,1280]{2,1,0:T(8,128)(2,1)S(1)} %pad_maximum_fusion.2.q, bf16[32,32,640]{2,1,0:T(8,128)(2,1)S(1)} %all-to-all-done.2.blocks, bf16[32,640]{1,0:T(8,128)(2,1)S(1)} %collective-permute-done.7.far), custom_call_target="tpu_custom_call" | custom-call | tf_op jit(solution)/shard_map/attend0/pallas_call | solution.py:321
  138.4 3.7 %all-to-all-start.3 = ((bf16[4,32,1408]{2,1,0:T(8,128)(2,1)}), bf16[4,32,1408]{2,1,0:T(8,128)(2,1)S(1)}, u32[]{:S(2)}, u32[]{:S(2)}) async-start(bf16[4,32,1408]{2,1,0:T(8,128)(2,1)} %pack.1), calls=%async_computation.3 | async-start | bytes 720896 | tf_op jit(solution)/shard_map/all_to_all | solution.py:335
  142.1 4.6 %collective-permute-start.14 = (bf16[2,2,8,20,256]{4,3,2,1,0:T(8,128)(2,1)S(1)}, bf16[2,2,8,20,256]{4,3,2,1,0:T(8,128)(2,1)S(1)}, u32[]{:S(2)}, u32[]{:S(2)}) collective-permute-start(bf16[2,2,8,20,256]{4,3,2,1,0:T(8,128)(2,1)S(1)} %pad_maximum_fusion.1), channel_id=1, source_target_pairs={{0,16},{8,24},{16,0},{24,8},{1,17},{9,25},{17,1},{25,9},{2,18},{10... | collective-permute-start | bytes 983048 | tf_op jit(solution)/shard_map/ppermute | solution.py:254
  146.7 9.2 %collective-permute-done.14 = bf16[2,2,8,20,256]{4,3,2,1,0:T(8,128)(2,1)S(1)} collective-permute-done((bf16[2,2,8,20,256]{4,3,2,1,0:T(8,128)(2,1)S(1)}, bf16[2,2,8,20,256]{4,3,2,1,0:T(8,128)(2,1)S(1)}, u32[]{:S(2)}, u32[]{:S(2)}) %collective-permute-start.14) | collective-permute-done | bytes 327712 | tf_op jit(solution)/shard_map/ppermute | solution.py:254
  157.1 16.3 %all_gather.3.attended = bf16[256,1280]{1,0:T(8,128)(2,1)S(1)} all-gather(bf16[32,1280]{1,0:T(8,128)(2,1)S(1)} %divide.1), channel_id=1, replica_groups=mesh['yh'=2,'z'=8,'x'=4,'yl'=4,'c'=2] {'yl','c'}, dimensions={0}, use_global_device_ids=true | all-gather | bytes 737280 | tf_op jit(solution)/shard_map/all_gather | solution.py:341
  (59 shorter events, 15.3 us)
Async XLA Ops:
  2.1 29.7 %all-to-all-start = ((bf16[16,32,256]{2,1,0:T(8,128)(2,1)}), bf16[16,32,256]{2,1,0:T(8,128)(2,1)S(1)}, u32[]{:S(2)}, u32[]{:S(2)}) async-start(bf16[16,32,256]{2,1,0:T(8,128)(2,1)} %broadcast_in_dim.56), calls=%async_computation | async-start | bytes 524288 | tf_op jit(solution)/shard_map/all_to_all | solution.py:241
  18.3 11.3 %collective-permute-start = (bf16[256,256]{1,0:T(8,128)(2,1)}, bf16[256,256]{1,0:T(8,128)(2,1)S(1)}, u32[]{:S(2)}, u32[]{:S(2)}) collective-permute-start(bf16[256,256]{1,0:T(8,128)(2,1)} %param.8), channel_id=1, source_target_pairs={{0,8},{8,16},{16,24},{24,0},{1,9},{9,17},{17,25},{25,1},{2,10},{10... | collective-permute-start | bytes 393224 | tf_op jit(solution)/shard_map/ppermute | solution.py:254
  21.5 8.2 %collective-permute-start.1 = (bf16[256,256]{1,0:T(8,128)(2,1)}, bf16[256,256]{1,0:T(8,128)(2,1)S(1)}, u32[]{:S(2)}, u32[]{:S(2)}) collective-permute-start(bf16[256,256]{1,0:T(8,128)(2,1)} %param.8), channel_id=1, source_target_pairs={{0,16},{8,24},{16,0},{24,8},{1,17},{9,25},{17,1},{25,9},{2,18},{10... | collective-permute-start | bytes 393224 | tf_op jit(solution)/shard_map/ppermute | solution.py:254
  25.8 5.9 %collective-permute-start.2 = (bf16[256,256]{1,0:T(8,128)(2,1)}, bf16[256,256]{1,0:T(8,128)(2,1)S(1)}, u32[]{:S(2)}, u32[]{:S(2)}) collective-permute-start(bf16[256,256]{1,0:T(8,128)(2,1)} %param.8), channel_id=1, source_target_pairs={{0,24},{8,0},{16,8},{24,16},{1,25},{9,1},{17,9},{25,17},{2,26},{10... | collective-permute-start | bytes 393224 | tf_op jit(solution)/shard_map/ppermute | solution.py:254
  31.8 0.9 copy-start
  33.7 6.8 %collective-permute-start.3 = (f32[4,128,512]{2,1,0:T(8,128)S(1)}, f32[4,128,512]{2,1,0:T(8,128)S(1)}, u32[]{:S(2)}, u32[]{:S(2)}) collective-permute-start(f32[4,128,512]{2,1,0:T(8,128)S(1)} %project1.1), channel_id=1, source_target_pairs={{0,1},{1,0},{2,3},{3,2},{4,5},{5,4},{6,7},{7,6},{8,9},{9,8},{10,11... | collective-permute-start | bytes 3145736 | tf_op jit(solution)/shard_map/ppermute | solution.py:276
  41.8 4.6 %copy-start.2 = (s32[4]{0:T(128)S(1)}, s32[4]{0:T(128)}, u32[]{:S(2)}) copy-start(s32[4]{0:T(128)} %lengths.3) | copy-start | bytes 52
  41.8 4.8 %copy-start.4 = (bf16[20,256]{1,0:T(8,128)(2,1)S(1)}, bf16[20,256]{1,0:T(8,128)(2,1)}, u32[]{:S(2)}) copy-start(bf16[20,256]{1,0:T(8,128)(2,1)} %param.13) | copy-start | bytes 30724
  41.8 25.3 %copy-start.5 = (bf16[64]{0:T(256)(128)(2,1)S(1)}, bf16[64]{0:T(256)(128)(2,1)}, u32[]{:S(2)}) copy-start(bf16[64]{0:T(256)(128)(2,1)} %param.12) | copy-start | bytes 388
  41.8 31.6 %copy-start.3 = (s32[4]{0:T(128)S(1)}, s32[4]{0:T(128)}, u32[]{:S(2)}) copy-start(s32[4]{0:T(128)} %table.1) | copy-start | bytes 52
  41.8 40.3 %copy-start.6 = (bf16[64]{0:T(256)(128)(2,1)S(1)}, bf16[64]{0:T(256)(128)(2,1)}, u32[]{:S(2)}) copy-start(bf16[64]{0:T(256)(128)(2,1)} %param.11) | copy-start | bytes 388
  41.8 31.6 %all-to-all-start.1 = ((f32[16,32,512]{2,1,0:T(8,128)}), f32[16,32,512]{2,1,0:T(8,128)S(1)}, u32[]{:S(2)}, u32[]{:S(2)}) async-start(f32[16,32,512]{2,1,0:T(8,128)} %bitcast.14), calls=%async_computation.1 | async-start | bytes 2097152 | tf_op jit(solution)/shard_map/all_to_all | solution.py:279
  46.6 5.9 %collective-permute-start.4 = (bf16[1,20,256]{2,1,0:T(8,128)(2,1)S(1)}, bf16[1,20,256]{2,1,0:T(8,128)(2,1)S(1)}, u32[]{:S(2)}, u32[]{:S(2)}) collective-permute-start(bf16[1,20,256]{2,1,0:T(8,128)(2,1)S(1)} %bitcast.38), channel_id=1, source_target_pairs={{0,32},{32,64},{64,96},{96,128},{128,160},{160,192},{192,224},{224... | collective-permute-start | bytes 30728 | tf_op jit(solution)/shard_map/ppermute | solution.py:254
  52.6 7.0 %collective-permute-start.5 = (bf16[2,20,256]{2,1,0:T(8,128)(2,1)S(1)}, bf16[2,20,256]{2,1,0:T(8,128)(2,1)S(1)}, u32[]{:S(2)}, u32[]{:S(2)}) collective-permute-start(bf16[2,20,256]{2,1,0:T(8,128)(2,1)S(1)} %pad_maximum_fusion.6), channel_id=1, source_target_pairs={{0,64},{32,96},{64,128},{96,160},{128,192},{160,224},{192,0},{224,... | collective-permute-start | bytes 61448 | tf_op jit(solution)/shard_map/ppermute | solution.py:254
  59.5 8.8 %collective-permute-start.6 = (bf16[4,20,256]{2,1,0:T(8,128)(2,1)S(1)}, bf16[4,20,256]{2,1,0:T(8,128)(2,1)S(1)}, u32[]{:S(2)}, u32[]{:S(2)}) collective-permute-start(bf16[4,20,256]{2,1,0:T(8,128)(2,1)S(1)} %pad_maximum_fusion.5), channel_id=1, source_target_pairs={{0,128},{32,160},{64,192},{96,224},{128,0},{160,32},{192,64},{224,... | collective-permute-start | bytes 122888 | tf_op jit(solution)/shard_map/ppermute | solution.py:254
  74.9 8.6 %collective-permute-start.7 = (bf16[32,640]{1,0:T(8,128)(2,1)S(1)}, bf16[32,640]{1,0:T(8,128)(2,1)S(1)}, u32[]{:S(2)}, u32[]{:S(2)}) collective-permute-start(bf16[32,640]{1,0:T(8,128)(2,1)S(1)} %get-tuple-element.23), channel_id=1, source_target_pairs={{0,256},{256,0},{1,257},{257,1},{2,258},{258,2},{3,259},{259,3},{4... | collective-permute-start | bytes 122888 | tf_op jit(solution)/shard_map/ppermute | solution.py:302
  84.8 41.2 %all-to-all-start.2 = ((bf16[32,32,640]{2,1,0:T(8,128)(2,1)}), bf16[32,32,640]{2,1,0:T(8,128)(2,1)S(1)}, u32[]{:S(2)}, u32[]{:S(2)}) async-start(bf16[32,32,640]{2,1,0:T(8,128)(2,1)} %broadcast_select_fusion), calls=%async_computation.2 | async-start | bytes 2621440 | tf_op jit(solution)/shard_map/all_to_all | solution.py:316
  92.3 8.9 %collective-permute-start.8 = (bf16[1,32,1280]{2,1,0:T(8,128)(2,1)S(1)}, bf16[1,32,1280]{2,1,0:T(8,128)(2,1)S(1)}, u32[]{:S(2)}, u32[]{:S(2)}) collective-permute-start(bf16[1,32,1280]{2,1,0:T(8,128)(2,1)S(1)} %bitcast.33), channel_id=1, source_target_pairs={{0,2},{2,4},{4,6},{6,0},{1,3},{3,5},{5,7},{7,1},{8,10},{10,12},{12... | collective-permute-start | bytes 245768 | tf_op jit(solution)/shard_map/ppermute | solution.py:254
  94.2 9.6 %collective-permute-start.9 = (bf16[8,20,256]{2,1,0:T(8,128)(2,1)S(1)}, bf16[8,20,256]{2,1,0:T(8,128)(2,1)S(1)}, u32[]{:S(2)}, u32[]{:S(2)}) collective-permute-start(bf16[8,20,256]{2,1,0:T(8,128)(2,1)S(1)} %pad_maximum_fusion.4), channel_id=1, source_target_pairs={{0,256},{256,0},{1,257},{257,1},{2,258},{258,2},{3,259},{259,3},{4... | collective-permute-start | bytes 245768 | tf_op jit(solution)/shard_map/ppermute | solution.py:308
  103.8 10.9 %collective-permute-start.11 = (bf16[1,2,8,20,256]{4,3,2,1,0:T(8,128)(2,1)S(1)}, bf16[1,2,8,20,256]{4,3,2,1,0:T(8,128)(2,1)S(1)}, u32[]{:S(2)}, u32[]{:S(2)}) collective-permute-start(bf16[1,2,8,20,256]{4,3,2,1,0:T(8,128)(2,1)S(1)} %maximum_select_fusion), channel_id=1, source_target_pairs={{0,8},{8,16},{16,24},{24,0},{1,9},{9,17},{17,25},{25,1},{2,10},{10... | collective-permute-start | bytes 491528 | tf_op jit(solution)/shard_map/ppermute | solution.py:254
  107.0 10.0 %collective-permute-start.10 = (bf16[2,32,1280]{2,1,0:T(8,128)(2,1)S(1)}, bf16[2,32,1280]{2,1,0:T(8,128)(2,1)S(1)}, u32[]{:S(2)}, u32[]{:S(2)}) collective-permute-start(bf16[2,32,1280]{2,1,0:T(8,128)(2,1)S(1)} %pad_maximum_fusion.3), channel_id=1, source_target_pairs={{0,4},{2,6},{4,0},{6,2},{1,5},{3,7},{5,1},{7,3},{8,12},{10,14},{12... | collective-permute-start | bytes 491528 | tf_op jit(solution)/shard_map/ppermute | solution.py:254
  117.0 9.0 %collective-permute-start.12 = (bf16[4,32,1280]{2,1,0:T(8,128)(2,1)S(1)}, bf16[4,32,1280]{2,1,0:T(8,128)(2,1)S(1)}, u32[]{:S(2)}, u32[]{:S(2)}) collective-permute-start(bf16[4,32,1280]{2,1,0:T(8,128)(2,1)S(1)} %pad_maximum_fusion.2.q), channel_id=1, source_target_pairs={{0,1},{1,0},{2,3},{3,2},{4,5},{5,4},{6,7},{7,6},{8,9},{9,8},{10,11... | collective-permute-start | bytes 983048 | tf_op jit(solution)/shard_map/ppermute | solution.py:314
  130.3 7.3 %collective-permute-start.13 = (f32[4,32,1408]{2,1,0:T(8,128)S(1)}, f32[4,32,1408]{2,1,0:T(8,128)S(1)}, u32[]{:S(2)}, u32[]{:S(2)}) collective-permute-start(f32[4,32,1408]{2,1,0:T(8,128)S(1)} %attend1.1), channel_id=1, source_target_pairs={{0,1},{1,0},{2,3},{3,2},{4,5},{5,4},{6,7},{7,6},{8,9},{9,8},{10,11... | collective-permute-start | bytes 2162696 | tf_op jit(solution)/shard_map/ppermute | solution.py:330
  138.4 18.4 %all-to-all-start.3 = ((bf16[4,32,1408]{2,1,0:T(8,128)(2,1)}), bf16[4,32,1408]{2,1,0:T(8,128)(2,1)S(1)}, u32[]{:S(2)}, u32[]{:S(2)}) async-start(bf16[4,32,1408]{2,1,0:T(8,128)(2,1)} %pack.1), calls=%async_computation.3 | async-start | bytes 720896 | tf_op jit(solution)/shard_map/all_to_all | solution.py:335
  142.1 13.8 %collective-permute-start.14 = (bf16[2,2,8,20,256]{4,3,2,1,0:T(8,128)(2,1)S(1)}, bf16[2,2,8,20,256]{4,3,2,1,0:T(8,128)(2,1)S(1)}, u32[]{:S(2)}, u32[]{:S(2)}) collective-permute-start(bf16[2,2,8,20,256]{4,3,2,1,0:T(8,128)(2,1)S(1)} %pad_maximum_fusion.1), channel_id=1, source_target_pairs={{0,16},{8,24},{16,0},{24,8},{1,17},{9,25},{17,1},{25,9},{2,18},{10... | collective-permute-start | bytes 983048 | tf_op jit(solution)/shard_map/ppermute | solution.py:254
  156.7 16.7 %copy-start.1 = (bf16[256,256]{1,0:T(8,128)(2,1)S(1)}, bf16[256,256]{1,0:T(8,128)(2,1)}, u32[]{:S(2)}) copy-start(bf16[256,256]{1,0:T(8,128)(2,1)} %param.8) | copy-start | bytes 393220

commit v7 on v6

--- a/solution.py
+++ b/solution.py
@@ -48,13 +48,14 @@
 def project_body(flip, place, gain, weight, here, one, two, three, out):
     core = place[3] if not flip else 1 - place[3]
     x = place[5]
+    columns = weight[:, :32, :].reshape(512, 256)
     lane = lax.broadcasted_iota(jnp.int32, (128, 128), 1)
     for step, hidden in enumerate((here, one, two, three)):
         rows = [hidden[p, yl, core].astype(F32) for yl in range(4) for p in range(PAGES_DEV)]
         values = jnp.concatenate(rows, axis=0)
         scaled = (values * gain[...].astype(F32)).astype(BF)
         product = lax.dot_general(
-            scaled, weight[...], (((1,), (1,)), ((), ())), preferred_element_type=F32
+            scaled, columns, (((1,), (1,)), ((), ())), preferred_element_type=F32
         )
         squares = jnp.sum(values * values, axis=1, keepdims=True)
         owner = lax.rem(x + 4 - step, 4)
@@ -229,12 +230,10 @@
 
 
 def order_body(place, blocks, out):
-    x, z = place[5], place[1] // 4
     for i in range(4):
-        for k in range(8):
-            at = ((z + 8 - k) & 7) * 4 + ((x + 4 - i) & 3)
-            for yh in range(2):
-                out[pl.ds(yh * 32 + at, 1)] = blocks[i, yh, k][None]
+        x = (place[5] + 4 - i) & 3
+        for k in range(16):
+            out[pl.ds(k * 4 + x, 1)] = blocks[i, k, :20][None]
 
 
 def spread(x, axes, count):
@@ -260,8 +259,8 @@
             step *= 2
         return value
 
-    columns = jnp.pad(qkv_weight.T, ((0, 2), (0, 0)))
-    weight = spread(columns, ("yh", "z"), 16).reshape(512, TOK_DEV)
+    own = [jnp.pad(qkv_weight.T, ((0, 2), (0, 0))), jnp.pad(out_weight, ((0, 4), (0, 0)))]
+    weight = spread(jnp.concatenate(own, axis=0), ("yh", "z"), 16)
     hidden = [hidden_in] + [shift(hidden_in, "x", 4, step) for step in range(1, 4)]
     hidden = [h.reshape(PAGES_DEV, 4, 2, 8, 256) for h in hidden]
     gain = attn_gain.reshape(1, 256)
@@ -275,9 +274,9 @@
     sent = project(1)
     arrived = lax.ppermute(sent, "c", swap)
     partial = (project(0) + arrived).reshape(16, ROWS, 512)
-    mixing, partial = lax.optimization_barrier((out_weight[None], partial))
+    mixing, partial = lax.optimization_barrier((weight[None, :, 32:], partial))
     parts = lax.all_to_all(partial, ("x", "yl"), 0, 0)
-    mixing = gather(mixing, "z", 8, 8)
+    mixing = gather(mixing, "x", 4, 2)
     mixing, parts = lax.optimization_barrier((mixing, parts))
 
     row = jnp.arange(ROWS, dtype=jnp.int32)
@@ -304,13 +303,8 @@
         rotate_queries_body, jax.ShapeDtypeStruct((ROWS, Q_DIM), BF), [VM] * 4, "rotate_queries"
     )(parts, *tables, gains[0])
     far, queries = lax.optimization_barrier((far, queries))
-    kept = gather(queries[None], "yl", 4, 2)
-    other = lax.ppermute(mixing, "yh", swap)
-    kept, other = lax.optimization_barrier((kept, other))
-    mixing = jnp.where(yh == 0, jnp.stack([mixing, other]), jnp.stack([other, mixing]))
-    kept = jnp.concatenate([kept, shift(kept, "yl", 4, 2)], axis=0)
-    mixing = gather(mixing[None], "x", 4, 2)
-    kept, mixing = lax.optimization_barrier((kept, mixing))
+    kept = gather(queries[None], "yl", 4, 4)
+    mixing = jnp.concatenate([mixing, shift(mixing, "x", 4, 2)], axis=0)
     given = lax.ppermute(kept, "c", swap)
     target = jnp.arange(32, dtype=jnp.int32)[:, None, None]
     blocks = lax.all_to_all(jnp.where(target >= index, kv[None], far[None]), ("z", "x"), 0, 0)
@@ -333,7 +327,6 @@
     )
     mixing, packed = lax.optimization_barrier((mixing, packed))
     parts = lax.all_to_all(packed, "yl", 0, 0)
-    mixing = jnp.concatenate([mixing, shift(mixing, "x", 4, 2)], axis=0)
     mixing = call(order_body, jax.ShapeDtypeStruct((64, 20, 256), BF), [SM, VM], "order")(
         place, mixing
     ).reshape(Q_DIM, 256)

time: 177 us -> 172 us (0.972); the launches traced: 174 us -> 172 us
  starting transfers between devices: 100 us -> 75 us
  waiting for transfers between devices: 34.2 us -> 56.5 us
  other arithmetic: 3.19 us -> 5.59 us
  local copies, waits for them, and re-layouts: 3.52 us -> 1.32 us
    ppermute x10 -> x7, starting transfers between devices: 38.6 us -> 22.3 us  [shift(): lax.ppermute(value, axis, [(i, (i + step) % count) for i in range(count)])]
    all_to_all x1, waiting for transfers between devices: 0.01 us -> 10.1 us  [on_device(): parts = lax.all_to_all(packed, 'yl', 0, 0)]
    ppermute x1 -> x0, starting transfers between devices: 7 us -> none  [on_device(): other = lax.ppermute(mixing, 'yh', swap)]
    ppermute x10 -> x7, waiting for transfers between devices: 24.1 us -> 29.4 us  [shift(): lax.ppermute(value, axis, [(i, (i + step) % count) for i in range(count)])]
    ppermute x1, starting transfers between devices: 7.14 us -> 2.61 us  [on_device(): far = lax.ppermute(kv, 'yh', swap)]
    ppermute x1, waiting for transfers between devices: 0.13 us -> 4.67 us  [on_device(): far = lax.ppermute(kv, 'yh', swap)]
    ppermute x2, starting transfers between devices: 7.5 us -> 11.1 us  [on_device(): arrived = lax.ppermute(sent, 'c', swap)]
    all_to_all x1, waiting for transfers between devices: 4.98 us -> 8.57 us  [on_device(): parts = lax.all_to_all(partial, ('x', 'yl'), 0, 0)]
  transfers between devices with their start and end apart: 19 -> 15, of which waited for: 12 -> 12; matrix products, arithmetic and copies ran while one was open for 1% -> 2% of each run, Pallas kernels for 4% -> 4%
where the time goes in v7:
time: 172 us
  starting transfers between devices  75 us (44%)
  waiting for transfers between devices  56.5 us (33%)
  blocking collectives  16.2 us (9%)
  Pallas kernels  16.1 us (9%)
  other arithmetic  5.59 us (3%)
    ppermute x7, waiting for transfers between devices, shift(): lax.ppermute(value, axis, [(i, (i + step) % count) for i in range(count)])  29.4 us
    ppermute x7, starting transfers between devices, shift(): lax.ppermute(value, axis, [(i, (i + step) % count) for i in range(count)])  22.3 us
    all_to_all x1, starting transfers between devices, spread(): lax.all_to_all(jnp.broadcast_to(x[None], (count,) + x.shape), axes, 0, 0)  16.2 us
    all_gather x1, blocking collectives, on_device(): attended = lax.all_gather(attended, ('yl', 'c'), axis=0, tiled=True)  16.2 us
    ppermute x2, starting transfers between devices, on_device(): arrived = lax.ppermute(sent, 'c', swap)  11.1 us
    all_to_all x1, waiting for transfers between devices, on_device(): parts = lax.all_to_all(packed, 'yl', 0, 0)  10.1 us
    pallas_call x2, Pallas kernels, attend(): call(functools.partial(attend_body, flip), jax.ShapeDtypeStruct((4, ROWS,...  8.62 us
    all_to_all x1, waiting for transfers between devices, on_device(): parts = lax.all_to_all(partial, ('x', 'yl'), 0, 0)  8.57 us
  transfers between devices with their start and end apart: 15, of which 12 were waited for; matrix products, arithmetic and copies ran while one was open for 2% of the time, Pallas kernels for 4%

profile of v7, /device:TPU:1, one launch (start us, length us, event | category | flops | bytes accessed | tf_op | source)
XLA Modules:
  0.0 171.6 jit_solution(14746361026697505990)
XLA Ops:
  2.2 16.2 %all-to-all-start = ((bf16[16,56,256]{2,1,0:T(8,128)(2,1)}), bf16[16,56,256]{2,1,0:T(8,128)(2,1)S(1)}, u32[]{:S(2)}, u32[]{:S(2)}) async-start(bf16[16,56,256]{2,1,0:T(8,128)(2,1)} %broadcast_in_dim.54), calls=%async_computation | async-start | bytes 917504 | tf_op jit(solution)/shard_map/all_to_all | solution.py:240
  18.5 3.1 %collective-permute-start = (bf16[256,256]{1,0:T(8,128)(2,1)S(1)}, bf16[256,256]{1,0:T(8,128)(2,1)S(1)}, u32[]{:S(2)}, u32[]{:S(2)}) collective-permute-start(bf16[256,256]{1,0:T(8,128)(2,1)S(1)} %copy-done), channel_id=1, source_target_pairs={{0,8},{8,16},{16,24},{24,0},{1,9},{9,17},{17,25},{25,1},{2,10},{10... | collective-permute-start | bytes 393224 | tf_op jit(solution)/shard_map/ppermute | solution.py:253
  21.6 4.4 %collective-permute-start.1 = (bf16[256,256]{1,0:T(8,128)(2,1)S(1)}, bf16[256,256]{1,0:T(8,128)(2,1)S(1)}, u32[]{:S(2)}, u32[]{:S(2)}) collective-permute-start(bf16[256,256]{1,0:T(8,128)(2,1)S(1)} %copy-done), channel_id=1, source_target_pairs={{0,16},{8,24},{16,0},{24,8},{1,17},{9,25},{17,1},{25,9},{2,18},{10... | collective-permute-start | bytes 393224 | tf_op jit(solution)/shard_map/ppermute | solution.py:253
  26.0 3.1 %collective-permute-start.2 = (bf16[256,256]{1,0:T(8,128)(2,1)S(1)}, bf16[256,256]{1,0:T(8,128)(2,1)S(1)}, u32[]{:S(2)}, u32[]{:S(2)}) collective-permute-start(bf16[256,256]{1,0:T(8,128)(2,1)S(1)} %copy-done), channel_id=1, source_target_pairs={{0,24},{8,0},{16,8},{24,16},{1,25},{9,1},{17,9},{25,17},{2,26},{10... | collective-permute-start | bytes 393224 | tf_op jit(solution)/shard_map/ppermute | solution.py:253
  29.5 2.5 %collective-permute-done.2 = bf16[256,256]{1,0:T(8,128)(2,1)S(1)} collective-permute-done((bf16[256,256]{1,0:T(8,128)(2,1)S(1)}, bf16[256,256]{1,0:T(8,128)(2,1)S(1)}, u32[]{:S(2)}, u32[]{:S(2)}) %collective-permute-start.2) | collective-permute-done | bytes 131104 | tf_op jit(solution)/shard_map/ppermute | solution.py:253
  32.0 1.4 all-to-all-done.weight
  34.4 4.4 %collective-permute-start.3 = (f32[4,128,512]{2,1,0:T(8,128)S(1)}, f32[4,128,512]{2,1,0:T(8,128)S(1)}, u32[]{:S(2)}, u32[]{:S(2)}) collective-permute-start(f32[4,128,512]{2,1,0:T(8,128)S(1)} %project1.1), channel_id=1, source_target_pairs={{0,1},{1,0},{2,3},{3,2},{4,5},{5,4},{6,7},{7,6},{8,9},{9,8},{10,11... | collective-permute-start | bytes 3145736 | tf_op jit(solution)/shard_map/ppermute | solution.py:275
  39.9 1.2 collective-permute-done.3
  41.1 1.2 add.76
  42.3 7.5 %all-to-all-start.1 = ((f32[16,32,512]{2,1,0:T(8,128)}), f32[16,32,512]{2,1,0:T(8,128)S(1)}, u32[]{:S(2)}, u32[]{:S(2)}) async-start(f32[16,32,512]{2,1,0:T(8,128)} %bitcast.13), calls=%async_computation.1 | async-start | bytes 2097152 | tf_op jit(solution)/shard_map/all_to_all | solution.py:278
  50.3 3.3 %collective-permute-start.4 = (bf16[1,16,24,256]{3,2,1,0:T(8,128)(2,1)S(1)}, bf16[1,16,24,256]{3,2,1,0:T(8,128)(2,1)S(1)}, u32[]{:S(2)}, u32[]{:S(2)}) collective-permute-start(bf16[1,16,24,256]{3,2,1,0:T(8,128)(2,1)S(1)} %slice_bitcast_fusion), channel_id=1, source_target_pairs={{0,8},{8,16},{16,24},{24,0},{1,9},{9,17},{17,25},{25,1},{2,10},{10... | collective-permute-start | bytes 589832 | tf_op jit(solution)/shard_map/ppermute | solution.py:253
  53.8 13.8 %collective-permute-done.4 = bf16[1,16,24,256]{3,2,1,0:T(8,128)(2,1)S(1)} collective-permute-done((bf16[1,16,24,256]{3,2,1,0:T(8,128)(2,1)S(1)}, bf16[1,16,24,256]{3,2,1,0:T(8,128)(2,1)S(1)}, u32[]{:S(2)}, u32[]{:S(2)}) %collective-permute-start.4) | collective-permute-done | bytes 196640 | tf_op jit(solution)/shard_map/ppermute | solution.py:253
  68.3 8.6 %all-to-all-done.1.parts = f32[16,32,512]{2,1,0:T(8,128)S(1)} async-done(((f32[16,32,512]{2,1,0:T(8,128)}), f32[16,32,512]{2,1,0:T(8,128)S(1)}, u32[]{:S(2)}, u32[]{:S(2)}) %all-to-all-start.1) | async-done | bytes 1048608 | tf_op jit(solution)/shard_map/all_to_all | solution.py:278
  76.9 1.5 rotate_keys.1
  78.4 2.6 %collective-permute-start.5 = (bf16[32,640]{1,0:T(8,128)(2,1)S(1)}, bf16[32,640]{1,0:T(8,128)(2,1)S(1)}, u32[]{:S(2)}, u32[]{:S(2)}) collective-permute-start(bf16[32,640]{1,0:T(8,128)(2,1)S(1)} %get-tuple-element.19), channel_id=1, source_target_pairs={{0,256},{256,0},{1,257},{257,1},{2,258},{258,2},{3,259},{259,3},{4... | collective-permute-start | bytes 122888 | tf_op jit(solution)/shard_map/ppermute | solution.py:301
  81.1 1.2 rotate_queries.1
  82.4 4.7 %collective-permute-done.5.far = bf16[32,640]{1,0:T(8,128)(2,1)S(1)} collective-permute-done((bf16[32,640]{1,0:T(8,128)(2,1)S(1)}, bf16[32,640]{1,0:T(8,128)(2,1)S(1)}, u32[]{:S(2)}, u32[]{:S(2)}) %collective-permute-start.5) | collective-permute-done | bytes 40992 | tf_op jit(solution)/shard_map/ppermute | solution.py:301
  87.0 1.3 broadcast_select_fusion
  88.3 4.7 %all-to-all-start.2 = ((bf16[32,32,640]{2,1,0:T(8,128)(2,1)}), bf16[32,32,640]{2,1,0:T(8,128)(2,1)S(1)}, u32[]{:S(2)}, u32[]{:S(2)}) async-start(bf16[32,32,640]{2,1,0:T(8,128)(2,1)} %broadcast_select_fusion), calls=%async_computation.2 | async-start | bytes 2621440 | tf_op jit(solution)/shard_map/all_to_all | solution.py:310
  93.0 1.9 %collective-permute-start.7 = (bf16[1,32,1280]{2,1,0:T(8,128)(2,1)S(1)}, bf16[1,32,1280]{2,1,0:T(8,128)(2,1)S(1)}, u32[]{:S(2)}, u32[]{:S(2)}) collective-permute-start(bf16[1,32,1280]{2,1,0:T(8,128)(2,1)S(1)} %bitcast.23), channel_id=1, source_target_pairs={{0,2},{2,4},{4,6},{6,0},{1,3},{3,5},{5,7},{7,1},{8,10},{10,12},{12... | collective-permute-start | bytes 245768 | tf_op jit(solution)/shard_map/ppermute | solution.py:253
  95.0 5.1 %collective-permute-done.7 = bf16[1,32,1280]{2,1,0:T(8,128)(2,1)S(1)} collective-permute-done((bf16[1,32,1280]{2,1,0:T(8,128)(2,1)S(1)}, bf16[1,32,1280]{2,1,0:T(8,128)(2,1)S(1)}, u32[]{:S(2)}, u32[]{:S(2)}) %collective-permute-start.7) | collective-permute-done | bytes 81952 | tf_op jit(solution)/shard_map/ppermute | solution.py:253
  100.1 1.9 %collective-permute-start.8 = (bf16[2,32,1280]{2,1,0:T(8,128)(2,1)S(1)}, bf16[2,32,1280]{2,1,0:T(8,128)(2,1)S(1)}, u32[]{:S(2)}, u32[]{:S(2)}) collective-permute-start(bf16[2,32,1280]{2,1,0:T(8,128)(2,1)S(1)} %pad_maximum_fusion.3), channel_id=1, source_target_pairs={{0,4},{2,6},{4,0},{6,2},{1,5},{3,7},{5,1},{7,3},{8,12},{10,14},{12... | collective-permute-start | bytes 491528 | tf_op jit(solution)/shard_map/ppermute | solution.py:253
  102.0 4.6 %collective-permute-start.6 = (bf16[2,16,24,256]{3,2,1,0:T(8,128)(2,1)}, bf16[2,16,24,256]{3,2,1,0:T(8,128)(2,1)S(1)}, u32[]{:S(2)}, u32[]{:S(2)}) collective-permute-start(bf16[2,16,24,256]{3,2,1,0:T(8,128)(2,1)} %pad_maximum_fusion.1), channel_id=1, source_target_pairs={{0,16},{8,24},{16,0},{24,8},{1,17},{9,25},{17,1},{25,9},{2,18},{10... | collective-permute-start | bytes 1179656 | tf_op jit(solution)/shard_map/ppermute | solution.py:253
  106.6 1.2 collective-permute-done.8
  107.9 6.3 %collective-permute-start.9 = (bf16[4,32,1280]{2,1,0:T(8,128)(2,1)S(1)}, bf16[4,32,1280]{2,1,0:T(8,128)(2,1)S(1)}, u32[]{:S(2)}, u32[]{:S(2)}) collective-permute-start(bf16[4,32,1280]{2,1,0:T(8,128)(2,1)S(1)} %pad_maximum_fusion.2.q), channel_id=1, source_target_pairs={{0,1},{1,0},{2,3},{3,2},{4,5},{5,4},{6,7},{7,6},{8,9},{9,8},{10,11... | collective-permute-start | bytes 983048 | tf_op jit(solution)/shard_map/ppermute | solution.py:308
  114.2 6.6 %collective-permute-done.6 = bf16[2,16,24,256]{3,2,1,0:T(8,128)(2,1)S(1)} collective-permute-done((bf16[2,16,24,256]{3,2,1,0:T(8,128)(2,1)}, bf16[2,16,24,256]{3,2,1,0:T(8,128)(2,1)S(1)}, u32[]{:S(2)}, u32[]{:S(2)}) %collective-permute-start.6) | collective-permute-done | bytes 393248 | tf_op jit(solution)/shard_map/ppermute | solution.py:253
  123.0 4.3 %attend1.1 = f32[4,32,1408]{2,1,0:T(8,128)S(1)} custom-call(s32[7]{0:T(128)S(1)} %stack.31.place, s32[4]{0:T(128)S(1)} %copy-done.1, bf16[4,32,1280]{2,1,0:T(8,128)(2,1)S(1)} %collective-permute-done.9.q, bf16[32,32,640]{2,1,0:T(8,128)(2,1)S(1)} %all-to-all-done.2.blocks, bf16[32,640]{1,0:T(8,128)(2,1)S(1)} %collective-permute-done.5.far), custom_call_target="tpu_custom_call" | custom-call | tf_op jit(solution)/shard_map/attend1/pallas_call | solution.py:315
  127.3 6.7 %collective-permute-start.10 = (f32[4,32,1408]{2,1,0:T(8,128)S(1)}, f32[4,32,1408]{2,1,0:T(8,128)S(1)}, u32[]{:S(2)}, u32[]{:S(2)}) collective-permute-start(f32[4,32,1408]{2,1,0:T(8,128)S(1)} %attend1.1), channel_id=1, source_target_pairs={{0,1},{1,0},{2,3},{3,2},{4,5},{5,4},{6,7},{7,6},{8,9},{9,8},{10,11... | collective-permute-start | bytes 2162696 | tf_op jit(solution)/shard_map/ppermute | solution.py:324
  134.0 4.3 %attend0.1.here = f32[4,32,1408]{2,1,0:T(8,128)S(1)} custom-call(s32[7]{0:T(128)S(1)} %stack.31.place, s32[4]{0:T(128)S(1)} %copy-done.1, bf16[4,32,1280]{2,1,0:T(8,128)(2,1)S(1)} %pad_maximum_fusion.2.q, bf16[32,32,640]{2,1,0:T(8,128)(2,1)S(1)} %all-to-all-done.2.blocks, bf16[32,640]{1,0:T(8,128)(2,1)S(1)} %collective-permute-done.5.far), custom_call_target="tpu_custom_call" | custom-call | tf_op jit(solution)/shard_map/attend0/pallas_call | solution.py:315
  139.1 4.2 %all-to-all-start.3 = ((bf16[4,32,1408]{2,1,0:T(8,128)(2,1)}), bf16[4,32,1408]{2,1,0:T(8,128)(2,1)S(1)}, u32[]{:S(2)}, u32[]{:S(2)}) async-start(bf16[4,32,1408]{2,1,0:T(8,128)(2,1)} %pack.1), calls=%async_computation.3 | async-start | bytes 720896 | tf_op jit(solution)/shard_map/all_to_all | solution.py:329
  144.1 10.1 %all-to-all-done.3.parts = bf16[4,32,1408]{2,1,0:T(8,128)(2,1)S(1)} async-done(((bf16[4,32,1408]{2,1,0:T(8,128)(2,1)}), bf16[4,32,1408]{2,1,0:T(8,128)(2,1)S(1)}, u32[]{:S(2)}, u32[]{:S(2)}) %all-to-all-start.3) | async-done | bytes 360480 | tf_op jit(solution)/shard_map/all_to_all | solution.py:329
  154.4 16.2 %all_gather.3.attended = bf16[256,1280]{1,0:T(8,128)(2,1)S(1)} all-gather(bf16[32,1280]{1,0:T(8,128)(2,1)S(1)} %divide.1), channel_id=1, replica_groups=mesh['yh'=2,'z'=8,'x'=4,'yl'=4,'c'=2] {'yl','c'}, dimensions={0}, use_global_device_ids=true | all-gather | bytes 737280 | tf_op jit(solution)/shard_map/all_gather | solution.py:334
  (46 shorter events, 10.6 us)
Async XLA Ops:
  0.6 17.8 %copy-start = (bf16[256,256]{1,0:T(8,128)(2,1)S(1)}, bf16[256,256]{1,0:T(8,128)(2,1)}, u32[]{:S(2)}) copy-start(bf16[256,256]{1,0:T(8,128)(2,1)} %param.8) | copy-start | bytes 393220
  0.6 28.4 %copy-start.3 = (bf16[256]{0:T(256)(128)(2,1)S(1)}, bf16[256]{0:T(256)(128)(2,1)}, u32[]{:S(2)}) copy-start(bf16[256]{0:T(256)(128)(2,1)} %param.9) | copy-start | bytes 1540
  2.2 31.2 %all-to-all-start = ((bf16[16,56,256]{2,1,0:T(8,128)(2,1)}), bf16[16,56,256]{2,1,0:T(8,128)(2,1)S(1)}, u32[]{:S(2)}, u32[]{:S(2)}) async-start(bf16[16,56,256]{2,1,0:T(8,128)(2,1)} %broadcast_in_dim.54), calls=%async_computation | async-start | bytes 917504 | tf_op jit(solution)/shard_map/all_to_all | solution.py:240
  18.5 10.7 %collective-permute-start = (bf16[256,256]{1,0:T(8,128)(2,1)S(1)}, bf16[256,256]{1,0:T(8,128)(2,1)S(1)}, u32[]{:S(2)}, u32[]{:S(2)}) collective-permute-start(bf16[256,256]{1,0:T(8,128)(2,1)S(1)} %copy-done), channel_id=1, source_target_pairs={{0,8},{8,16},{16,24},{24,0},{1,9},{9,17},{17,25},{25,1},{2,10},{10... | collective-permute-start | bytes 393224 | tf_op jit(solution)/shard_map/ppermute | solution.py:253
  21.6 7.9 %collective-permute-start.1 = (bf16[256,256]{1,0:T(8,128)(2,1)S(1)}, bf16[256,256]{1,0:T(8,128)(2,1)S(1)}, u32[]{:S(2)}, u32[]{:S(2)}) collective-permute-start(bf16[256,256]{1,0:T(8,128)(2,1)S(1)} %copy-done), channel_id=1, source_target_pairs={{0,16},{8,24},{16,0},{24,8},{1,17},{9,25},{17,1},{25,9},{2,18},{10... | collective-permute-start | bytes 393224 | tf_op jit(solution)/shard_map/ppermute | solution.py:253
  26.0 6.0 %collective-permute-start.2 = (bf16[256,256]{1,0:T(8,128)(2,1)S(1)}, bf16[256,256]{1,0:T(8,128)(2,1)S(1)}, u32[]{:S(2)}, u32[]{:S(2)}) collective-permute-start(bf16[256,256]{1,0:T(8,128)(2,1)S(1)} %copy-done), channel_id=1, source_target_pairs={{0,24},{8,0},{16,8},{24,16},{1,25},{9,1},{17,9},{25,17},{2,26},{10... | collective-permute-start | bytes 393224 | tf_op jit(solution)/shard_map/ppermute | solution.py:253
  34.4 6.7 %collective-permute-start.3 = (f32[4,128,512]{2,1,0:T(8,128)S(1)}, f32[4,128,512]{2,1,0:T(8,128)S(1)}, u32[]{:S(2)}, u32[]{:S(2)}) collective-permute-start(f32[4,128,512]{2,1,0:T(8,128)S(1)} %project1.1), channel_id=1, source_target_pairs={{0,1},{1,0},{2,3},{3,2},{4,5},{5,4},{6,7},{7,6},{8,9},{9,8},{10,11... | collective-permute-start | bytes 3145736 | tf_op jit(solution)/shard_map/ppermute | solution.py:275
  42.3 7.6 %copy-start.4 = (bf16[64]{0:T(256)(128)(2,1)S(1)}, bf16[64]{0:T(256)(128)(2,1)}, u32[]{:S(2)}) copy-start(bf16[64]{0:T(256)(128)(2,1)} %param.12) | copy-start | bytes 388
  42.3 7.7 %copy-start.1 = (s32[4]{0:T(128)S(1)}, s32[4]{0:T(128)}, u32[]{:S(2)}) copy-start(s32[4]{0:T(128)} %lengths.3) | copy-start | bytes 52
  42.3 34.5 %copy-start.2 = (s32[4]{0:T(128)S(1)}, s32[4]{0:T(128)}, u32[]{:S(2)}) copy-start(s32[4]{0:T(128)} %table.1) | copy-start | bytes 52
  42.3 34.5 %all-to-all-start.1 = ((f32[16,32,512]{2,1,0:T(8,128)}), f32[16,32,512]{2,1,0:T(8,128)S(1)}, u32[]{:S(2)}, u32[]{:S(2)}) async-start(f32[16,32,512]{2,1,0:T(8,128)} %bitcast.13), calls=%async_computation.1 | async-start | bytes 2097152 | tf_op jit(solution)/shard_map/all_to_all | solution.py:278
  49.8 31.2 %copy-start.5 = (bf16[64]{0:T(256)(128)(2,1)S(1)}, bf16[64]{0:T(256)(128)(2,1)}, u32[]{:S(2)}) copy-start(bf16[64]{0:T(256)(128)(2,1)} %param.11) | copy-start | bytes 388
  50.3 17.2 %collective-permute-start.4 = (bf16[1,16,24,256]{3,2,1,0:T(8,128)(2,1)S(1)}, bf16[1,16,24,256]{3,2,1,0:T(8,128)(2,1)S(1)}, u32[]{:S(2)}, u32[]{:S(2)}) collective-permute-start(bf16[1,16,24,256]{3,2,1,0:T(8,128)(2,1)S(1)} %slice_bitcast_fusion), channel_id=1, source_target_pairs={{0,8},{8,16},{16,24},{24,0},{1,9},{9,17},{17,25},{25,1},{2,10},{10... | collective-permute-start | bytes 589832 | tf_op jit(solution)/shard_map/ppermute | solution.py:253
  78.4 8.6 %collective-permute-start.5 = (bf16[32,640]{1,0:T(8,128)(2,1)S(1)}, bf16[32,640]{1,0:T(8,128)(2,1)S(1)}, u32[]{:S(2)}, u32[]{:S(2)}) collective-permute-start(bf16[32,640]{1,0:T(8,128)(2,1)S(1)} %get-tuple-element.19), channel_id=1, source_target_pairs={{0,256},{256,0},{1,257},{257,1},{2,258},{258,2},{3,259},{259,3},{4... | collective-permute-start | bytes 122888 | tf_op jit(solution)/shard_map/ppermute | solution.py:301
  88.3 34.6 %all-to-all-start.2 = ((bf16[32,32,640]{2,1,0:T(8,128)(2,1)}), bf16[32,32,640]{2,1,0:T(8,128)(2,1)S(1)}, u32[]{:S(2)}, u32[]{:S(2)}) async-start(bf16[32,32,640]{2,1,0:T(8,128)(2,1)} %broadcast_select_fusion), calls=%async_computation.2 | async-start | bytes 2621440 | tf_op jit(solution)/shard_map/all_to_all | solution.py:310
  93.0 7.0 %collective-permute-start.7 = (bf16[1,32,1280]{2,1,0:T(8,128)(2,1)S(1)}, bf16[1,32,1280]{2,1,0:T(8,128)(2,1)S(1)}, u32[]{:S(2)}, u32[]{:S(2)}) collective-permute-start(bf16[1,32,1280]{2,1,0:T(8,128)(2,1)S(1)} %bitcast.23), channel_id=1, source_target_pairs={{0,2},{2,4},{4,6},{6,0},{1,3},{3,5},{5,7},{7,1},{8,10},{10,12},{12... | collective-permute-start | bytes 245768 | tf_op jit(solution)/shard_map/ppermute | solution.py:253
  100.1 7.8 %collective-permute-start.8 = (bf16[2,32,1280]{2,1,0:T(8,128)(2,1)S(1)}, bf16[2,32,1280]{2,1,0:T(8,128)(2,1)S(1)}, u32[]{:S(2)}, u32[]{:S(2)}) collective-permute-start(bf16[2,32,1280]{2,1,0:T(8,128)(2,1)S(1)} %pad_maximum_fusion.3), channel_id=1, source_target_pairs={{0,4},{2,6},{4,0},{6,2},{1,5},{3,7},{5,1},{7,3},{8,12},{10,14},{12... | collective-permute-start | bytes 491528 | tf_op jit(solution)/shard_map/ppermute | solution.py:253
  102.0 18.8 %collective-permute-start.6 = (bf16[2,16,24,256]{3,2,1,0:T(8,128)(2,1)}, bf16[2,16,24,256]{3,2,1,0:T(8,128)(2,1)S(1)}, u32[]{:S(2)}, u32[]{:S(2)}) collective-permute-start(bf16[2,16,24,256]{3,2,1,0:T(8,128)(2,1)} %pad_maximum_fusion.1), channel_id=1, source_target_pairs={{0,16},{8,24},{16,0},{24,8},{1,17},{9,25},{17,1},{25,9},{2,18},{10... | collective-permute-start | bytes 1179656 | tf_op jit(solution)/shard_map/ppermute | solution.py:253
  107.9 13.9 %collective-permute-start.9 = (bf16[4,32,1280]{2,1,0:T(8,128)(2,1)S(1)}, bf16[4,32,1280]{2,1,0:T(8,128)(2,1)S(1)}, u32[]{:S(2)}, u32[]{:S(2)}) collective-permute-start(bf16[4,32,1280]{2,1,0:T(8,128)(2,1)S(1)} %pad_maximum_fusion.2.q), channel_id=1, source_target_pairs={{0,1},{1,0},{2,3},{3,2},{4,5},{5,4},{6,7},{7,6},{8,9},{9,8},{10,11... | collective-permute-start | bytes 983048 | tf_op jit(solution)/shard_map/ppermute | solution.py:308
  127.3 11.0 %collective-permute-start.10 = (f32[4,32,1408]{2,1,0:T(8,128)S(1)}, f32[4,32,1408]{2,1,0:T(8,128)S(1)}, u32[]{:S(2)}, u32[]{:S(2)}) collective-permute-start(f32[4,32,1408]{2,1,0:T(8,128)S(1)} %attend1.1), channel_id=1, source_target_pairs={{0,1},{1,0},{2,3},{3,2},{4,5},{5,4},{6,7},{7,6},{8,9},{9,8},{10,11... | collective-permute-start | bytes 2162696 | tf_op jit(solution)/shard_map/ppermute | solution.py:324
  139.1 15.0 %all-to-all-start.3 = ((bf16[4,32,1408]{2,1,0:T(8,128)(2,1)}), bf16[4,32,1408]{2,1,0:T(8,128)(2,1)S(1)}, u32[]{:S(2)}, u32[]{:S(2)}) async-start(bf16[4,32,1408]{2,1,0:T(8,128)(2,1)} %pack.1), calls=%async_computation.3 | async-start | bytes 720896 | tf_op jit(solution)/shard_map/all_to_all | solution.py:329

commit v8 on v7

--- a/solution.py
+++ b/solution.py
@@ -63,15 +63,36 @@
         out[pl.ds(owner, 1), :, 128:] = product[None, :, 128:]
 
 
+def round_body(here, there, out):
+    lane = lax.broadcasted_iota(jnp.int32, (128, 128), 1)
+    for k in range(4):
+        for tile in range(4):
+            at = pl.ds(tile * 128, 128)
+            total = here[k, :, at] + there[k, :, at]
+            low = total.astype(BF)
+            if tile == 0:
+                rest = pltpu.roll(total - low.astype(F32), 1, 1)
+                low = jnp.where(lane == 31, rest, low.astype(F32)).astype(BF)
+            if tile >= 2:
+                rest = (total - low.astype(F32)).astype(BF)
+                out[k, :, pl.ds((7 - tile) * 128, 128)] = rest
+            out[k, :, at] = low
+
+
 def pieces_in_order(parts, first_tile, count):
     lane = lax.broadcasted_iota(jnp.int32, (ROWS, 128), 1)
 
     def summed(x, tile):
-        at = pl.ds(tile * 128, 128)
-        low, high = parts[4 * x, :, at] + parts[4 * x + 1, :, at], parts[4 * x + 2, :, at]
-        return low + (high + parts[4 * x + 3, :, at])
-
-    inverse = lax.rsqrt(summed(0, 0)[:, 30:31] / D + 1e-06)
+        def part(k):
+            value = parts[4 * x + k, :, pl.ds(tile * 128, 128)].astype(F32)
+            if tile < 2:
+                return value
+            return value + parts[4 * x + k, :, pl.ds((7 - tile) * 128, 128)].astype(F32)
+
+        return (part(0) + part(1)) + (part(2) + part(3))
+
+    squares = summed(0, 0)
+    inverse = lax.rsqrt((squares[:, 30:31] + squares[:, 31:32]) / D + 1e-06)
     tiles = [None] * count
     for tile in range(4):
         for x in range(4):
@@ -273,7 +294,9 @@
 
     sent = project(1)
     arrived = lax.ppermute(sent, "c", swap)
-    partial = (project(0) + arrived).reshape(16, ROWS, 512)
+    partial = call(round_body, jax.ShapeDtypeStruct((4, 128, 768), BF), [VM, VM], "round")(
+        project(0), arrived
+    ).reshape(16, ROWS, 768)
     mixing, partial = lax.optimization_barrier((weight[None, :, 32:], partial))
     parts = lax.all_to_all(partial, ("x", "yl"), 0, 0)
     mixing = gather(mixing, "x", 4, 2)

time: 172 us -> 166 us (0.965)
  waiting for transfers between devices: 56.5 us -> 52.2 us
  other arithmetic: 5.59 us -> 2.65 us
    all_to_all x1, waiting for transfers between devices: 8.57 us -> 5.91 us  [on_device(): parts = lax.all_to_all(partial, ('x', 'yl'), 0, 0)]
    ppermute x7, waiting for transfers between devices: 29.4 us -> 26.8 us  [shift(): lax.ppermute(value, axis, [(i, (i + step) % count) for i in range(count)])]
  transfers between devices with their start and end apart: 15 -> 15, of which waited for: 12 -> 12; matrix products, arithmetic and copies ran while one was open for 2% -> 1% of each run, Pallas kernels for 4% -> 4%
where the time goes in v8:
time: 166 us
  starting transfers between devices  75.1 us (45%)
  waiting for transfers between devices  52.2 us (31%)
  Pallas kernels  17.2 us (10%)
  blocking collectives  16.2 us (10%)
  other arithmetic  2.65 us (2%)
    ppermute x7, waiting for transfers between devices, shift(): lax.ppermute(value, axis, [(i, (i + step) % count) for i in range(count)])  26.8 us
    ppermute x7, starting transfers between devices, shift(): lax.ppermute(value, axis, [(i, (i + step) % count) for i in range(count)])  22.3 us
    all_to_all x1, starting transfers between devices, spread(): lax.all_to_all(jnp.broadcast_to(x[None], (count,) + x.shape), axes, 0, 0)  16.2 us
    all_gather x1, blocking collectives, on_device(): attended = lax.all_gather(attended, ('yl', 'c'), axis=0, tiled=True)  16.2 us
    ppermute x2, starting transfers between devices, on_device(): arrived = lax.ppermute(sent, 'c', swap)  11.1 us
    all_to_all x1, waiting for transfers between devices, on_device(): parts = lax.all_to_all(packed, 'yl', 0, 0)  10.1 us
    pallas_call x2, Pallas kernels, attend(): call(functools.partial(attend_body, flip), jax.ShapeDtypeStruct((4, ROWS,...  8.62 us
    all_to_all x1, starting transfers between devices, on_device(): parts = lax.all_to_all(partial, ('x', 'yl'), 0, 0)  7.5 us
  transfers between devices with their start and end apart: 15, of which 12 were waited for; matrix products, arithmetic and copies ran while one was open for 1% of the time, Pallas kernels for 4%

profile of v8, /device:TPU:1, one launch (start us, length us, event | category | flops | bytes accessed | tf_op | source)
XLA Modules:
  0.0 165.6 jit_solution(16083802838355675130)
XLA Ops:
  2.2 16.2 %all-to-all-start = ((bf16[16,56,256]{2,1,0:T(8,128)(2,1)}), bf16[16,56,256]{2,1,0:T(8,128)(2,1)S(1)}, u32[]{:S(2)}, u32[]{:S(2)}) async-start(bf16[16,56,256]{2,1,0:T(8,128)(2,1)} %broadcast_in_dim.54), calls=%async_computation | async-start | bytes 917504 | tf_op jit(solution)/shard_map/all_to_all | solution.py:261
  18.5 3.1 %collective-permute-start = (bf16[256,256]{1,0:T(8,128)(2,1)S(1)}, bf16[256,256]{1,0:T(8,128)(2,1)S(1)}, u32[]{:S(2)}, u32[]{:S(2)}) collective-permute-start(bf16[256,256]{1,0:T(8,128)(2,1)S(1)} %copy-done), channel_id=1, source_target_pairs={{0,8},{8,16},{16,24},{24,0},{1,9},{9,17},{17,25},{25,1},{2,10},{10... | collective-permute-start | bytes 393224 | tf_op jit(solution)/shard_map/ppermute | solution.py:274
  21.6 4.4 %collective-permute-start.1 = (bf16[256,256]{1,0:T(8,128)(2,1)S(1)}, bf16[256,256]{1,0:T(8,128)(2,1)S(1)}, u32[]{:S(2)}, u32[]{:S(2)}) collective-permute-start(bf16[256,256]{1,0:T(8,128)(2,1)S(1)} %copy-done), channel_id=1, source_target_pairs={{0,16},{8,24},{16,0},{24,8},{1,17},{9,25},{17,1},{25,9},{2,18},{10... | collective-permute-start | bytes 393224 | tf_op jit(solution)/shard_map/ppermute | solution.py:274
  26.0 3.1 %collective-permute-start.2 = (bf16[256,256]{1,0:T(8,128)(2,1)S(1)}, bf16[256,256]{1,0:T(8,128)(2,1)S(1)}, u32[]{:S(2)}, u32[]{:S(2)}) collective-permute-start(bf16[256,256]{1,0:T(8,128)(2,1)S(1)} %copy-done), channel_id=1, source_target_pairs={{0,24},{8,0},{16,8},{24,16},{1,25},{9,1},{17,9},{25,17},{2,26},{10... | collective-permute-start | bytes 393224 | tf_op jit(solution)/shard_map/ppermute | solution.py:274
  29.5 2.5 %collective-permute-done.2 = bf16[256,256]{1,0:T(8,128)(2,1)S(1)} collective-permute-done((bf16[256,256]{1,0:T(8,128)(2,1)S(1)}, bf16[256,256]{1,0:T(8,128)(2,1)S(1)}, u32[]{:S(2)}, u32[]{:S(2)}) %collective-permute-start.2) | collective-permute-done | bytes 131104 | tf_op jit(solution)/shard_map/ppermute | solution.py:274
  32.0 1.4 all-to-all-done.weight
  34.4 4.4 %collective-permute-start.3 = (f32[4,128,512]{2,1,0:T(8,128)S(1)}, f32[4,128,512]{2,1,0:T(8,128)S(1)}, u32[]{:S(2)}, u32[]{:S(2)}) collective-permute-start(f32[4,128,512]{2,1,0:T(8,128)S(1)} %project1.1), channel_id=1, source_target_pairs={{0,1},{1,0},{2,3},{3,2},{4,5},{5,4},{6,7},{7,6},{8,9},{9,8},{10,11... | collective-permute-start | bytes 3145736 | tf_op jit(solution)/shard_map/ppermute | solution.py:296
  39.9 1.2 collective-permute-done.3.there
  41.1 1.1 round.1
  42.3 7.5 %all-to-all-start.1 = ((bf16[16,32,768]{2,1,0:T(8,128)(2,1)}), bf16[16,32,768]{2,1,0:T(8,128)(2,1)S(1)}, u32[]{:S(2)}, u32[]{:S(2)}) async-start(bf16[16,32,768]{2,1,0:T(8,128)(2,1)} %bitcast.13), calls=%async_computation.1 | async-start | bytes 1572864 | tf_op jit(solution)/shard_map/all_to_all | solution.py:301
  50.3 3.3 %collective-permute-start.4 = (bf16[1,16,24,256]{3,2,1,0:T(8,128)(2,1)S(1)}, bf16[1,16,24,256]{3,2,1,0:T(8,128)(2,1)S(1)}, u32[]{:S(2)}, u32[]{:S(2)}) collective-permute-start(bf16[1,16,24,256]{3,2,1,0:T(8,128)(2,1)S(1)} %slice_bitcast_fusion), channel_id=1, source_target_pairs={{0,8},{8,16},{16,24},{24,0},{1,9},{9,17},{17,25},{25,1},{2,10},{10... | collective-permute-start | bytes 589832 | tf_op jit(solution)/shard_map/ppermute | solution.py:274
  53.7 11.6 %collective-permute-done.4 = bf16[1,16,24,256]{3,2,1,0:T(8,128)(2,1)S(1)} collective-permute-done((bf16[1,16,24,256]{3,2,1,0:T(8,128)(2,1)S(1)}, bf16[1,16,24,256]{3,2,1,0:T(8,128)(2,1)S(1)}, u32[]{:S(2)}, u32[]{:S(2)}) %collective-permute-start.4) | collective-permute-done | bytes 196640 | tf_op jit(solution)/shard_map/ppermute | solution.py:274
  65.3 5.9 %all-to-all-done.1.parts = bf16[16,32,768]{2,1,0:T(8,128)(2,1)S(1)} async-done(((bf16[16,32,768]{2,1,0:T(8,128)(2,1)}), bf16[16,32,768]{2,1,0:T(8,128)(2,1)S(1)}, u32[]{:S(2)}, u32[]{:S(2)}) %all-to-all-start.1) | async-done | bytes 786464 | tf_op jit(solution)/shard_map/all_to_all | solution.py:301
  71.2 1.5 rotate_keys.1
  72.7 2.6 %collective-permute-start.5 = (bf16[32,640]{1,0:T(8,128)(2,1)S(1)}, bf16[32,640]{1,0:T(8,128)(2,1)S(1)}, u32[]{:S(2)}, u32[]{:S(2)}) collective-permute-start(bf16[32,640]{1,0:T(8,128)(2,1)S(1)} %get-tuple-element.19), channel_id=1, source_target_pairs={{0,256},{256,0},{1,257},{257,1},{2,258},{258,2},{3,259},{259,3},{4... | collective-permute-start | bytes 122888 | tf_op jit(solution)/shard_map/ppermute | solution.py:324
  75.5 1.2 rotate_queries.1
  76.7 4.7 %collective-permute-done.5.far = bf16[32,640]{1,0:T(8,128)(2,1)S(1)} collective-permute-done((bf16[32,640]{1,0:T(8,128)(2,1)S(1)}, bf16[32,640]{1,0:T(8,128)(2,1)S(1)}, u32[]{:S(2)}, u32[]{:S(2)}) %collective-permute-start.5) | collective-permute-done | bytes 40992 | tf_op jit(solution)/shard_map/ppermute | solution.py:324
  81.4 1.3 broadcast_select_fusion
  82.7 5.0 %all-to-all-start.2 = ((bf16[32,32,640]{2,1,0:T(8,128)(2,1)}), bf16[32,32,640]{2,1,0:T(8,128)(2,1)S(1)}, u32[]{:S(2)}, u32[]{:S(2)}) async-start(bf16[32,32,640]{2,1,0:T(8,128)(2,1)} %broadcast_select_fusion), calls=%async_computation.2 | async-start | bytes 2621440 | tf_op jit(solution)/shard_map/all_to_all | solution.py:333
  87.6 1.9 %collective-permute-start.7 = (bf16[1,32,1280]{2,1,0:T(8,128)(2,1)S(1)}, bf16[1,32,1280]{2,1,0:T(8,128)(2,1)S(1)}, u32[]{:S(2)}, u32[]{:S(2)}) collective-permute-start(bf16[1,32,1280]{2,1,0:T(8,128)(2,1)S(1)} %bitcast.23), channel_id=1, source_target_pairs={{0,2},{2,4},{4,6},{6,0},{1,3},{3,5},{5,7},{7,1},{8,10},{10,12},{12... | collective-permute-start | bytes 245768 | tf_op jit(solution)/shard_map/ppermute | solution.py:274
  89.6 5.1 %collective-permute-done.7 = bf16[1,32,1280]{2,1,0:T(8,128)(2,1)S(1)} collective-permute-done((bf16[1,32,1280]{2,1,0:T(8,128)(2,1)S(1)}, bf16[1,32,1280]{2,1,0:T(8,128)(2,1)S(1)}, u32[]{:S(2)}, u32[]{:S(2)}) %collective-permute-start.7) | collective-permute-done | bytes 81952 | tf_op jit(solution)/shard_map/ppermute | solution.py:274
  94.6 1.9 %collective-permute-start.8 = (bf16[2,32,1280]{2,1,0:T(8,128)(2,1)S(1)}, bf16[2,32,1280]{2,1,0:T(8,128)(2,1)S(1)}, u32[]{:S(2)}, u32[]{:S(2)}) collective-permute-start(bf16[2,32,1280]{2,1,0:T(8,128)(2,1)S(1)} %pad_maximum_fusion.3), channel_id=1, source_target_pairs={{0,4},{2,6},{4,0},{6,2},{1,5},{3,7},{5,1},{7,3},{8,12},{10,14},{12... | collective-permute-start | bytes 491528 | tf_op jit(solution)/shard_map/ppermute | solution.py:274
  96.6 4.6 %collective-permute-start.6 = (bf16[2,16,24,256]{3,2,1,0:T(8,128)(2,1)S(1)}, bf16[2,16,24,256]{3,2,1,0:T(8,128)(2,1)S(1)}, u32[]{:S(2)}, u32[]{:S(2)}) collective-permute-start(bf16[2,16,24,256]{3,2,1,0:T(8,128)(2,1)S(1)} %pad_maximum_fusion.1), channel_id=1, source_target_pairs={{0,16},{8,24},{16,0},{24,8},{1,17},{9,25},{17,1},{25,9},{2,18},{10... | collective-permute-start | bytes 1179656 | tf_op jit(solution)/shard_map/ppermute | solution.py:274
  101.9 6.8 %collective-permute-start.9 = (bf16[4,32,1280]{2,1,0:T(8,128)(2,1)S(1)}, bf16[4,32,1280]{2,1,0:T(8,128)(2,1)S(1)}, u32[]{:S(2)}, u32[]{:S(2)}) collective-permute-start(bf16[4,32,1280]{2,1,0:T(8,128)(2,1)S(1)} %pad_maximum_fusion.2.q), channel_id=1, source_target_pairs={{0,1},{1,0},{2,3},{3,2},{4,5},{5,4},{6,7},{7,6},{8,9},{9,8},{10,11... | collective-permute-start | bytes 983048 | tf_op jit(solution)/shard_map/ppermute | solution.py:331
  108.7 6.7 %collective-permute-done.6 = bf16[2,16,24,256]{3,2,1,0:T(8,128)(2,1)S(1)} collective-permute-done((bf16[2,16,24,256]{3,2,1,0:T(8,128)(2,1)S(1)}, bf16[2,16,24,256]{3,2,1,0:T(8,128)(2,1)S(1)}, u32[]{:S(2)}, u32[]{:S(2)}) %collective-permute-start.6) | collective-permute-done | bytes 393248 | tf_op jit(solution)/shard_map/ppermute | solution.py:274
  115.5 2.1 %all-to-all-done.2.blocks = bf16[32,32,640]{2,1,0:T(8,128)(2,1)S(1)} async-done(((bf16[32,32,640]{2,1,0:T(8,128)(2,1)}), bf16[32,32,640]{2,1,0:T(8,128)(2,1)S(1)}, u32[]{:S(2)}, u32[]{:S(2)}) %all-to-all-start.2) | async-done | bytes 1310752 | tf_op jit(solution)/shard_map/all_to_all | solution.py:333
  117.6 4.3 %attend1.1 = f32[4,32,1408]{2,1,0:T(8,128)S(1)} custom-call(s32[7]{0:T(128)S(1)} %stack.31.place, s32[4]{0:T(128)S(1)} %copy-done.1, bf16[4,32,1280]{2,1,0:T(8,128)(2,1)S(1)} %collective-permute-done.9.q, bf16[32,32,640]{2,1,0:T(8,128)(2,1)S(1)} %all-to-all-done.2.blocks, bf16[32,640]{1,0:T(8,128)(2,1)S(1)} %collective-permute-done.5.far), custom_call_target="tpu_custom_call" | custom-call | tf_op jit(solution)/shard_map/attend1/pallas_call | solution.py:338
  121.9 6.6 %collective-permute-start.10 = (f32[4,32,1408]{2,1,0:T(8,128)S(1)}, f32[4,32,1408]{2,1,0:T(8,128)S(1)}, u32[]{:S(2)}, u32[]{:S(2)}) collective-permute-start(f32[4,32,1408]{2,1,0:T(8,128)S(1)} %attend1.1), channel_id=1, source_target_pairs={{0,1},{1,0},{2,3},{3,2},{4,5},{5,4},{6,7},{7,6},{8,9},{9,8},{10,11... | collective-permute-start | bytes 2162696 | tf_op jit(solution)/shard_map/ppermute | solution.py:347
  128.6 4.3 %attend0.1.here = f32[4,32,1408]{2,1,0:T(8,128)S(1)} custom-call(s32[7]{0:T(128)S(1)} %stack.31.place, s32[4]{0:T(128)S(1)} %copy-done.1, bf16[4,32,1280]{2,1,0:T(8,128)(2,1)S(1)} %pad_maximum_fusion.2.q, bf16[32,32,640]{2,1,0:T(8,128)(2,1)S(1)} %all-to-all-done.2.blocks, bf16[32,640]{1,0:T(8,128)(2,1)S(1)} %collective-permute-done.5.far), custom_call_target="tpu_custom_call" | custom-call | tf_op jit(solution)/shard_map/attend0/pallas_call | solution.py:338
  133.7 3.6 %all-to-all-start.3 = ((bf16[4,32,1408]{2,1,0:T(8,128)(2,1)}), bf16[4,32,1408]{2,1,0:T(8,128)(2,1)S(1)}, u32[]{:S(2)}, u32[]{:S(2)}) async-start(bf16[4,32,1408]{2,1,0:T(8,128)(2,1)} %pack.1), calls=%async_computation.3 | async-start | bytes 720896 | tf_op jit(solution)/shard_map/all_to_all | solution.py:352
  138.1 10.1 %all-to-all-done.3.parts = bf16[4,32,1408]{2,1,0:T(8,128)(2,1)S(1)} async-done(((bf16[4,32,1408]{2,1,0:T(8,128)(2,1)}), bf16[4,32,1408]{2,1,0:T(8,128)(2,1)S(1)}, u32[]{:S(2)}, u32[]{:S(2)}) %all-to-all-start.3) | async-done | bytes 360480 | tf_op jit(solution)/shard_map/all_to_all | solution.py:352
  148.4 16.2 %all_gather.3.attended = bf16[256,1280]{1,0:T(8,128)(2,1)S(1)} all-gather(bf16[32,1280]{1,0:T(8,128)(2,1)S(1)} %divide.1), channel_id=1, replica_groups=mesh['yh'=2,'z'=8,'x'=4,'yl'=4,'c'=2] {'yl','c'}, dimensions={0}, use_global_device_ids=true | all-gather | bytes 737280 | tf_op jit(solution)/shard_map/all_gather | solution.py:357
  (46 shorter events, 8.4 us)
Async XLA Ops:
  0.6 17.8 %copy-start = (bf16[256,256]{1,0:T(8,128)(2,1)S(1)}, bf16[256,256]{1,0:T(8,128)(2,1)}, u32[]{:S(2)}) copy-start(bf16[256,256]{1,0:T(8,128)(2,1)} %param.8) | copy-start | bytes 393220
  0.6 28.4 %copy-start.3 = (bf16[256]{0:T(256)(128)(2,1)S(1)}, bf16[256]{0:T(256)(128)(2,1)}, u32[]{:S(2)}) copy-start(bf16[256]{0:T(256)(128)(2,1)} %param.9) | copy-start | bytes 1540
  2.2 31.2 %all-to-all-start = ((bf16[16,56,256]{2,1,0:T(8,128)(2,1)}), bf16[16,56,256]{2,1,0:T(8,128)(2,1)S(1)}, u32[]{:S(2)}, u32[]{:S(2)}) async-start(bf16[16,56,256]{2,1,0:T(8,128)(2,1)} %broadcast_in_dim.54), calls=%async_computation | async-start | bytes 917504 | tf_op jit(solution)/shard_map/all_to_all | solution.py:261
  18.5 10.7 %collective-permute-start = (bf16[256,256]{1,0:T(8,128)(2,1)S(1)}, bf16[256,256]{1,0:T(8,128)(2,1)S(1)}, u32[]{:S(2)}, u32[]{:S(2)}) collective-permute-start(bf16[256,256]{1,0:T(8,128)(2,1)S(1)} %copy-done), channel_id=1, source_target_pairs={{0,8},{8,16},{16,24},{24,0},{1,9},{9,17},{17,25},{25,1},{2,10},{10... | collective-permute-start | bytes 393224 | tf_op jit(solution)/shard_map/ppermute | solution.py:274
  21.6 7.9 %collective-permute-start.1 = (bf16[256,256]{1,0:T(8,128)(2,1)S(1)}, bf16[256,256]{1,0:T(8,128)(2,1)S(1)}, u32[]{:S(2)}, u32[]{:S(2)}) collective-permute-start(bf16[256,256]{1,0:T(8,128)(2,1)S(1)} %copy-done), channel_id=1, source_target_pairs={{0,16},{8,24},{16,0},{24,8},{1,17},{9,25},{17,1},{25,9},{2,18},{10... | collective-permute-start | bytes 393224 | tf_op jit(solution)/shard_map/ppermute | solution.py:274
  26.0 6.0 %collective-permute-start.2 = (bf16[256,256]{1,0:T(8,128)(2,1)S(1)}, bf16[256,256]{1,0:T(8,128)(2,1)S(1)}, u32[]{:S(2)}, u32[]{:S(2)}) collective-permute-start(bf16[256,256]{1,0:T(8,128)(2,1)S(1)} %copy-done), channel_id=1, source_target_pairs={{0,24},{8,0},{16,8},{24,16},{1,25},{9,1},{17,9},{25,17},{2,26},{10... | collective-permute-start | bytes 393224 | tf_op jit(solution)/shard_map/ppermute | solution.py:274
  34.4 6.7 %collective-permute-start.3 = (f32[4,128,512]{2,1,0:T(8,128)S(1)}, f32[4,128,512]{2,1,0:T(8,128)S(1)}, u32[]{:S(2)}, u32[]{:S(2)}) collective-permute-start(f32[4,128,512]{2,1,0:T(8,128)S(1)} %project1.1), channel_id=1, source_target_pairs={{0,1},{1,0},{2,3},{3,2},{4,5},{5,4},{6,7},{7,6},{8,9},{9,8},{10,11... | collective-permute-start | bytes 3145736 | tf_op jit(solution)/shard_map/ppermute | solution.py:296
  42.3 7.6 %copy-start.4 = (bf16[64]{0:T(256)(128)(2,1)S(1)}, bf16[64]{0:T(256)(128)(2,1)}, u32[]{:S(2)}) copy-start(bf16[64]{0:T(256)(128)(2,1)} %param.12) | copy-start | bytes 388
  42.3 7.7 %copy-start.1 = (s32[4]{0:T(128)S(1)}, s32[4]{0:T(128)}, u32[]{:S(2)}) copy-start(s32[4]{0:T(128)} %lengths.3) | copy-start | bytes 52
  42.3 28.9 %copy-start.2 = (s32[4]{0:T(128)S(1)}, s32[4]{0:T(128)}, u32[]{:S(2)}) copy-start(s32[4]{0:T(128)} %table.1) | copy-start | bytes 52
  42.3 33.1 %copy-start.5 = (bf16[64]{0:T(256)(128)(2,1)S(1)}, bf16[64]{0:T(256)(128)(2,1)}, u32[]{:S(2)}) copy-start(bf16[64]{0:T(256)(128)(2,1)} %param.11) | copy-start | bytes 388
  42.3 28.9 %all-to-all-start.1 = ((bf16[16,32,768]{2,1,0:T(8,128)(2,1)}), bf16[16,32,768]{2,1,0:T(8,128)(2,1)S(1)}, u32[]{:S(2)}, u32[]{:S(2)}) async-start(bf16[16,32,768]{2,1,0:T(8,128)(2,1)} %bitcast.13), calls=%async_computation.1 | async-start | bytes 1572864 | tf_op jit(solution)/shard_map/all_to_all | solution.py:301
  50.3 15.0 %collective-permute-start.4 = (bf16[1,16,24,256]{3,2,1,0:T(8,128)(2,1)S(1)}, bf16[1,16,24,256]{3,2,1,0:T(8,128)(2,1)S(1)}, u32[]{:S(2)}, u32[]{:S(2)}) collective-permute-start(bf16[1,16,24,256]{3,2,1,0:T(8,128)(2,1)S(1)} %slice_bitcast_fusion), channel_id=1, source_target_pairs={{0,8},{8,16},{16,24},{24,0},{1,9},{9,17},{17,25},{25,1},{2,10},{10... | collective-permute-start | bytes 589832 | tf_op jit(solution)/shard_map/ppermute | solution.py:274
  72.7 8.6 %collective-permute-start.5 = (bf16[32,640]{1,0:T(8,128)(2,1)S(1)}, bf16[32,640]{1,0:T(8,128)(2,1)S(1)}, u32[]{:S(2)}, u32[]{:S(2)}) collective-permute-start(bf16[32,640]{1,0:T(8,128)(2,1)S(1)} %get-tuple-element.19), channel_id=1, source_target_pairs={{0,256},{256,0},{1,257},{257,1},{2,258},{258,2},{3,259},{259,3},{4... | collective-permute-start | bytes 122888 | tf_op jit(solution)/shard_map/ppermute | solution.py:324
  82.7 35.0 %all-to-all-start.2 = ((bf16[32,32,640]{2,1,0:T(8,128)(2,1)}), bf16[32,32,640]{2,1,0:T(8,128)(2,1)S(1)}, u32[]{:S(2)}, u32[]{:S(2)}) async-start(bf16[32,32,640]{2,1,0:T(8,128)(2,1)} %broadcast_select_fusion), calls=%async_computation.2 | async-start | bytes 2621440 | tf_op jit(solution)/shard_map/all_to_all | solution.py:333
  87.6 7.0 %collective-permute-start.7 = (bf16[1,32,1280]{2,1,0:T(8,128)(2,1)S(1)}, bf16[1,32,1280]{2,1,0:T(8,128)(2,1)S(1)}, u32[]{:S(2)}, u32[]{:S(2)}) collective-permute-start(bf16[1,32,1280]{2,1,0:T(8,128)(2,1)S(1)} %bitcast.23), channel_id=1, source_target_pairs={{0,2},{2,4},{4,6},{6,0},{1,3},{3,5},{5,7},{7,1},{8,10},{10,12},{12... | collective-permute-start | bytes 245768 | tf_op jit(solution)/shard_map/ppermute | solution.py:274
  94.6 7.3 %collective-permute-start.8 = (bf16[2,32,1280]{2,1,0:T(8,128)(2,1)S(1)}, bf16[2,32,1280]{2,1,0:T(8,128)(2,1)S(1)}, u32[]{:S(2)}, u32[]{:S(2)}) collective-permute-start(bf16[2,32,1280]{2,1,0:T(8,128)(2,1)S(1)} %pad_maximum_fusion.3), channel_id=1, source_target_pairs={{0,4},{2,6},{4,0},{6,2},{1,5},{3,7},{5,1},{7,3},{8,12},{10,14},{12... | collective-permute-start | bytes 491528 | tf_op jit(solution)/shard_map/ppermute | solution.py:274
  96.6 18.9 %collective-permute-start.6 = (bf16[2,16,24,256]{3,2,1,0:T(8,128)(2,1)S(1)}, bf16[2,16,24,256]{3,2,1,0:T(8,128)(2,1)S(1)}, u32[]{:S(2)}, u32[]{:S(2)}) collective-permute-start(bf16[2,16,24,256]{3,2,1,0:T(8,128)(2,1)S(1)} %pad_maximum_fusion.1), channel_id=1, source_target_pairs={{0,16},{8,24},{16,0},{24,8},{1,17},{9,25},{17,1},{25,9},{2,18},{10... | collective-permute-start | bytes 1179656 | tf_op jit(solution)/shard_map/ppermute | solution.py:274
  101.9 13.6 %collective-permute-start.9 = (bf16[4,32,1280]{2,1,0:T(8,128)(2,1)S(1)}, bf16[4,32,1280]{2,1,0:T(8,128)(2,1)S(1)}, u32[]{:S(2)}, u32[]{:S(2)}) collective-permute-start(bf16[4,32,1280]{2,1,0:T(8,128)(2,1)S(1)} %pad_maximum_fusion.2.q), channel_id=1, source_target_pairs={{0,1},{1,0},{2,3},{3,2},{4,5},{5,4},{6,7},{7,6},{8,9},{9,8},{10,11... | collective-permute-start | bytes 983048 | tf_op jit(solution)/shard_map/ppermute | solution.py:331
  121.9 11.0 %collective-permute-start.10 = (f32[4,32,1408]{2,1,0:T(8,128)S(1)}, f32[4,32,1408]{2,1,0:T(8,128)S(1)}, u32[]{:S(2)}, u32[]{:S(2)}) collective-permute-start(f32[4,32,1408]{2,1,0:T(8,128)S(1)} %attend1.1), channel_id=1, source_target_pairs={{0,1},{1,0},{2,3},{3,2},{4,5},{5,4},{6,7},{7,6},{8,9},{9,8},{10,11... | collective-permute-start | bytes 2162696 | tf_op jit(solution)/shard_map/ppermute | solution.py:347
  133.7 14.4 %all-to-all-start.3 = ((bf16[4,32,1408]{2,1,0:T(8,128)(2,1)}), bf16[4,32,1408]{2,1,0:T(8,128)(2,1)S(1)}, u32[]{:S(2)}, u32[]{:S(2)}) async-start(bf16[4,32,1408]{2,1,0:T(8,128)(2,1)} %pack.1), calls=%async_computation.3 | async-start | bytes 720896 | tf_op jit(solution)/shard_map/all_to_all | solution.py:352

commit v9 on v8

--- a/solution.py
+++ b/solution.py
@@ -250,11 +250,11 @@
             out[p, n] = (hidden[p, n].astype(F32) + mixed[at : at + 8]).astype(BF)
 
 
-def order_body(place, blocks, out):
-    for i in range(4):
+def order_body(place, own, one, two, three, out):
+    for i, blocks in enumerate((own, one, two, three)):
         x = (place[5] + 4 - i) & 3
         for k in range(16):
-            out[pl.ds(k * 4 + x, 1)] = blocks[i, k, :20][None]
+            out[pl.ds(k * 4 + x, 1)] = blocks[k, :20][None]
 
 
 def spread(x, axes, count):
@@ -297,10 +297,10 @@
     partial = call(round_body, jax.ShapeDtypeStruct((4, 128, 768), BF), [VM, VM], "round")(
         project(0), arrived
     ).reshape(16, ROWS, 768)
-    mixing, partial = lax.optimization_barrier((weight[None, :, 32:], partial))
+    mixing, partial = lax.optimization_barrier((weight[:, 32:], partial))
     parts = lax.all_to_all(partial, ("x", "yl"), 0, 0)
-    mixing = gather(mixing, "x", 4, 2)
-    mixing, parts = lax.optimization_barrier((mixing, parts))
+    after = shift(mixing, "x", 4, 1)
+    mixing, after, parts = lax.optimization_barrier((mixing, after, parts))
 
     row = jnp.arange(ROWS, dtype=jnp.int32)
     own = wide * TOK_DEV + row // 8 * PAGE + narrow * 8 + row % 8
@@ -327,12 +327,12 @@
     )(parts, *tables, gains[0])
     far, queries = lax.optimization_barrier((far, queries))
     kept = gather(queries[None], "yl", 4, 4)
-    mixing = jnp.concatenate([mixing, shift(mixing, "x", 4, 2)], axis=0)
+    before = shift(mixing, "x", 4, 3)
     given = lax.ppermute(kept, "c", swap)
     target = jnp.arange(32, dtype=jnp.int32)[:, None, None]
     blocks = lax.all_to_all(jnp.where(target >= index, kv[None], far[None]), ("z", "x"), 0, 0)
 
-    blocks, mixing, kept, given = lax.optimization_barrier((blocks, mixing, kept, given))
+    blocks, before, kept, given = lax.optimization_barrier((blocks, before, kept, given))
 
     def attend(flip):
         return call(
@@ -350,8 +350,8 @@
     )
     mixing, packed = lax.optimization_barrier((mixing, packed))
     parts = lax.all_to_all(packed, "yl", 0, 0)
-    mixing = call(order_body, jax.ShapeDtypeStruct((64, 20, 256), BF), [SM, VM], "order")(
-        place, mixing
+    mixing = call(order_body, jax.ShapeDtypeStruct((64, 20, 256), BF), [SM] + [VM] * 4, "order")(
+        place, mixing, after, shift(mixing, "x", 4, 2), before
     ).reshape(Q_DIM, 256)
     attended = call(divide_body, jax.ShapeDtypeStruct((ROWS, Q_DIM), BF), [VM], "divide")(parts)
     attended = lax.all_gather(attended, ("yl", "c"), axis=0, tiled=True)

time: 166 us -> 166 us (level)
  starting transfers between devices: 75.1 us -> 77.5 us
  waiting for transfers between devices: 52.2 us -> 49.9 us
    all_to_all x1, waiting for transfers between devices: 10.1 us -> 0.15 us  [on_device(): parts = lax.all_to_all(packed, 'yl', 0, 0)]
    ppermute x7 -> x8, waiting for transfers between devices: 26.8 us -> 36.5 us  [shift(): lax.ppermute(value, axis, [(i, (i + step) % count) for i in range(count)])]
    ppermute x7 -> x8, starting transfers between devices: 22.3 us -> 27.3 us  [shift(): lax.ppermute(value, axis, [(i, (i + step) % count) for i in range(count)])]
    ppermute x2, starting transfers between devices: 11.1 us -> 8.47 us  [on_device(): arrived = lax.ppermute(sent, 'c', swap)]
    all_to_all x1, waiting for transfers between devices: 2.08 us -> 0.01 us  [on_device(): lax.all_to_all(jnp.where(target >= index, kv[None], far[None]), ('z', 'x'...]
  transfers between devices with their start and end apart: 15 -> 16, of which waited for: 12 -> 12; matrix products, arithmetic and copies ran while one was open for 1% -> 1% of each run, Pallas kernels for 4% -> 4%
where the time goes in v9:
time: 166 us
  starting transfers between devices  77.5 us (47%)
  waiting for transfers between devices  49.9 us (30%)
  Pallas kernels  17.3 us (10%)
  blocking collectives  16 us (10%)
  other arithmetic  2.54 us (2%)
    ppermute x8, waiting for transfers between devices, shift(): lax.ppermute(value, axis, [(i, (i + step) % count) for i in range(count)])  36.5 us
    ppermute x8, starting transfers between devices, shift(): lax.ppermute(value, axis, [(i, (i + step) % count) for i in range(count)])  27.3 us
    all_to_all x1, starting transfers between devices, spread(): lax.all_to_all(jnp.broadcast_to(x[None], (count,) + x.shape), axes, 0, 0)  16.2 us
    all_gather x1, blocking collectives, on_device(): attended = lax.all_gather(attended, ('yl', 'c'), axis=0, tiled=True)  16 us
    pallas_call x2, Pallas kernels, attend(): call(functools.partial(attend_body, flip), jax.ShapeDtypeStruct((4, ROWS,...  8.69 us
    ppermute x2, starting transfers between devices, on_device(): arrived = lax.ppermute(sent, 'c', swap)  8.47 us
    all_to_all x1, starting transfers between devices, on_device(): parts = lax.all_to_all(partial, ('x', 'yl'), 0, 0)  7.5 us
    ppermute x1, starting transfers between devices, on_device(): given = lax.ppermute(kept, 'c', swap)  6.79 us
  transfers between devices with their start and end apart: 16, of which 12 were waited for; matrix products, arithmetic and copies ran while one was open for 1% of the time, Pallas kernels for 4%

profile of v9, /device:TPU:1, one launch (start us, length us, event | category | flops | bytes accessed | tf_op | source)
XLA Modules:
  0.0 165.5 jit_solution(13101130559174370709)
XLA Ops:
  2.2 16.2 %all-to-all-start = ((bf16[16,56,256]{2,1,0:T(8,128)(2,1)}), bf16[16,56,256]{2,1,0:T(8,128)(2,1)S(1)}, u32[]{:S(2)}, u32[]{:S(2)}) async-start(bf16[16,56,256]{2,1,0:T(8,128)(2,1)} %broadcast_in_dim.50), calls=%async_computation | async-start | bytes 917504 | tf_op jit(solution)/shard_map/all_to_all | solution.py:261
  18.5 3.1 %collective-permute-start = (bf16[256,256]{1,0:T(8,128)(2,1)S(1)}, bf16[256,256]{1,0:T(8,128)(2,1)S(1)}, u32[]{:S(2)}, u32[]{:S(2)}) collective-permute-start(bf16[256,256]{1,0:T(8,128)(2,1)S(1)} %copy-done), channel_id=1, source_target_pairs={{0,8},{8,16},{16,24},{24,0},{1,9},{9,17},{17,25},{25,1},{2,10},{10... | collective-permute-start | bytes 393224 | tf_op jit(solution)/shard_map/ppermute | solution.py:274
  21.6 4.4 %collective-permute-start.1 = (bf16[256,256]{1,0:T(8,128)(2,1)S(1)}, bf16[256,256]{1,0:T(8,128)(2,1)S(1)}, u32[]{:S(2)}, u32[]{:S(2)}) collective-permute-start(bf16[256,256]{1,0:T(8,128)(2,1)S(1)} %copy-done), channel_id=1, source_target_pairs={{0,16},{8,24},{16,0},{24,8},{1,17},{9,25},{17,1},{25,9},{2,18},{10... | collective-permute-start | bytes 393224 | tf_op jit(solution)/shard_map/ppermute | solution.py:274
  26.0 3.1 %collective-permute-start.2 = (bf16[256,256]{1,0:T(8,128)(2,1)S(1)}, bf16[256,256]{1,0:T(8,128)(2,1)S(1)}, u32[]{:S(2)}, u32[]{:S(2)}) collective-permute-start(bf16[256,256]{1,0:T(8,128)(2,1)S(1)} %copy-done), channel_id=1, source_target_pairs={{0,24},{8,0},{16,8},{24,16},{1,25},{9,1},{17,9},{25,17},{2,26},{10... | collective-permute-start | bytes 393224 | tf_op jit(solution)/shard_map/ppermute | solution.py:274
  29.5 2.5 %collective-permute-done.2 = bf16[256,256]{1,0:T(8,128)(2,1)S(1)} collective-permute-done((bf16[256,256]{1,0:T(8,128)(2,1)S(1)}, bf16[256,256]{1,0:T(8,128)(2,1)S(1)}, u32[]{:S(2)}, u32[]{:S(2)}) %collective-permute-start.2) | collective-permute-done | bytes 131104 | tf_op jit(solution)/shard_map/ppermute | solution.py:274
  32.0 1.4 all-to-all-done.weight
  34.4 4.4 %collective-permute-start.3 = (f32[4,128,512]{2,1,0:T(8,128)S(1)}, f32[4,128,512]{2,1,0:T(8,128)S(1)}, u32[]{:S(2)}, u32[]{:S(2)}) collective-permute-start(f32[4,128,512]{2,1,0:T(8,128)S(1)} %project1.1), channel_id=1, source_target_pairs={{0,1},{1,0},{2,3},{3,2},{4,5},{5,4},{6,7},{7,6},{8,9},{9,8},{10,11... | collective-permute-start | bytes 3145736 | tf_op jit(solution)/shard_map/ppermute | solution.py:296
  39.9 1.2 collective-permute-done.3.there
  42.3 7.5 %all-to-all-start.1 = ((bf16[16,32,768]{2,1,0:T(8,128)(2,1)}), bf16[16,32,768]{2,1,0:T(8,128)(2,1)S(1)}, u32[]{:S(2)}, u32[]{:S(2)}) async-start(bf16[16,32,768]{2,1,0:T(8,128)(2,1)} %bitcast.12), calls=%async_computation.1 | async-start | bytes 1572864 | tf_op jit(solution)/shard_map/all_to_all | solution.py:301
  50.3 3.3 %collective-permute-start.4 = (bf16[16,24,256]{2,1,0:T(8,128)(2,1)S(1)}, bf16[16,24,256]{2,1,0:T(8,128)(2,1)S(1)}, u32[]{:S(2)}, u32[]{:S(2)}) collective-permute-start(bf16[16,24,256]{2,1,0:T(8,128)(2,1)S(1)} %slice.4.own), channel_id=1, source_target_pairs={{0,8},{8,16},{16,24},{24,0},{1,9},{9,17},{17,25},{25,1},{2,10},{10... | collective-permute-start | bytes 589832 | tf_op jit(solution)/shard_map/ppermute | solution.py:274
  53.7 11.6 %collective-permute-done.4.one = bf16[16,24,256]{2,1,0:T(8,128)(2,1)S(1)} collective-permute-done((bf16[16,24,256]{2,1,0:T(8,128)(2,1)S(1)}, bf16[16,24,256]{2,1,0:T(8,128)(2,1)S(1)}, u32[]{:S(2)}, u32[]{:S(2)}) %collective-permute-start.4) | collective-permute-done | bytes 196640 | tf_op jit(solution)/shard_map/ppermute | solution.py:274
  65.3 5.9 %all-to-all-done.1.parts = bf16[16,32,768]{2,1,0:T(8,128)(2,1)S(1)} async-done(((bf16[16,32,768]{2,1,0:T(8,128)(2,1)}), bf16[16,32,768]{2,1,0:T(8,128)(2,1)S(1)}, u32[]{:S(2)}, u32[]{:S(2)}) %all-to-all-start.1) | async-done | bytes 786464 | tf_op jit(solution)/shard_map/all_to_all | solution.py:301
  71.2 1.5 rotate_keys.1
  72.8 2.6 %collective-permute-start.5 = (bf16[32,640]{1,0:T(8,128)(2,1)S(1)}, bf16[32,640]{1,0:T(8,128)(2,1)S(1)}, u32[]{:S(2)}, u32[]{:S(2)}) collective-permute-start(bf16[32,640]{1,0:T(8,128)(2,1)S(1)} %get-tuple-element.21), channel_id=1, source_target_pairs={{0,256},{256,0},{1,257},{257,1},{2,258},{258,2},{3,259},{259,3},{4... | collective-permute-start | bytes 122888 | tf_op jit(solution)/shard_map/ppermute | solution.py:324
  75.5 1.2 rotate_queries.1
  76.7 4.7 %collective-permute-done.5.far = bf16[32,640]{1,0:T(8,128)(2,1)S(1)} collective-permute-done((bf16[32,640]{1,0:T(8,128)(2,1)S(1)}, bf16[32,640]{1,0:T(8,128)(2,1)S(1)}, u32[]{:S(2)}, u32[]{:S(2)}) %collective-permute-start.5) | collective-permute-done | bytes 40992 | tf_op jit(solution)/shard_map/ppermute | solution.py:324
  81.4 1.3 broadcast_select_fusion
  82.7 5.0 %all-to-all-start.2 = ((bf16[32,32,640]{2,1,0:T(8,128)(2,1)}), bf16[32,32,640]{2,1,0:T(8,128)(2,1)S(1)}, u32[]{:S(2)}, u32[]{:S(2)}) async-start(bf16[32,32,640]{2,1,0:T(8,128)(2,1)} %broadcast_select_fusion), calls=%async_computation.2 | async-start | bytes 2621440 | tf_op jit(solution)/shard_map/all_to_all | solution.py:333
  87.7 1.9 %collective-permute-start.7 = (bf16[1,32,1280]{2,1,0:T(8,128)(2,1)S(1)}, bf16[1,32,1280]{2,1,0:T(8,128)(2,1)S(1)}, u32[]{:S(2)}, u32[]{:S(2)}) collective-permute-start(bf16[1,32,1280]{2,1,0:T(8,128)(2,1)S(1)} %bitcast.21), channel_id=1, source_target_pairs={{0,2},{2,4},{4,6},{6,0},{1,3},{3,5},{5,7},{7,1},{8,10},{10,12},{12... | collective-permute-start | bytes 245768 | tf_op jit(solution)/shard_map/ppermute | solution.py:274
  89.6 5.1 %collective-permute-done.7 = bf16[1,32,1280]{2,1,0:T(8,128)(2,1)S(1)} collective-permute-done((bf16[1,32,1280]{2,1,0:T(8,128)(2,1)S(1)}, bf16[1,32,1280]{2,1,0:T(8,128)(2,1)S(1)}, u32[]{:S(2)}, u32[]{:S(2)}) %collective-permute-start.7) | collective-permute-done | bytes 81952 | tf_op jit(solution)/shard_map/ppermute | solution.py:274
  94.7 1.9 %collective-permute-start.8 = (bf16[2,32,1280]{2,1,0:T(8,128)(2,1)S(1)}, bf16[2,32,1280]{2,1,0:T(8,128)(2,1)S(1)}, u32[]{:S(2)}, u32[]{:S(2)}) collective-permute-start(bf16[2,32,1280]{2,1,0:T(8,128)(2,1)S(1)} %pad_maximum_fusion.1), channel_id=1, source_target_pairs={{0,4},{2,6},{4,0},{6,2},{1,5},{3,7},{5,1},{7,3},{8,12},{10,14},{12... | collective-permute-start | bytes 491528 | tf_op jit(solution)/shard_map/ppermute | solution.py:274
  96.6 5.3 %collective-permute-done.8 = bf16[2,32,1280]{2,1,0:T(8,128)(2,1)S(1)} collective-permute-done((bf16[2,32,1280]{2,1,0:T(8,128)(2,1)S(1)}, bf16[2,32,1280]{2,1,0:T(8,128)(2,1)S(1)}, u32[]{:S(2)}, u32[]{:S(2)}) %collective-permute-start.8) | collective-permute-done | bytes 163872 | tf_op jit(solution)/shard_map/ppermute | solution.py:274
  102.0 6.8 %collective-permute-start.9 = (bf16[4,32,1280]{2,1,0:T(8,128)(2,1)S(1)}, bf16[4,32,1280]{2,1,0:T(8,128)(2,1)S(1)}, u32[]{:S(2)}, u32[]{:S(2)}) collective-permute-start(bf16[4,32,1280]{2,1,0:T(8,128)(2,1)S(1)} %pad_maximum_fusion.q), channel_id=1, source_target_pairs={{0,1},{1,0},{2,3},{3,2},{4,5},{5,4},{6,7},{7,6},{8,9},{9,8},{10,11... | collective-permute-start | bytes 983048 | tf_op jit(solution)/shard_map/ppermute | solution.py:331
  108.8 4.6 %collective-permute-start.6 = (bf16[16,24,256]{2,1,0:T(8,128)(2,1)S(1)}, bf16[16,24,256]{2,1,0:T(8,128)(2,1)S(1)}, u32[]{:S(2)}, u32[]{:S(2)}) collective-permute-start(bf16[16,24,256]{2,1,0:T(8,128)(2,1)S(1)} %slice.4.own), channel_id=1, source_target_pairs={{0,24},{8,0},{16,8},{24,16},{1,25},{9,1},{17,9},{25,17},{2,26},{10... | collective-permute-start | bytes 589832 | tf_op jit(solution)/shard_map/ppermute | solution.py:274
  113.4 6.8 %collective-permute-done.6.three = bf16[16,24,256]{2,1,0:T(8,128)(2,1)S(1)} collective-permute-done((bf16[16,24,256]{2,1,0:T(8,128)(2,1)S(1)}, bf16[16,24,256]{2,1,0:T(8,128)(2,1)S(1)}, u32[]{:S(2)}, u32[]{:S(2)}) %collective-permute-start.6) | collective-permute-done | bytes 196640 | tf_op jit(solution)/shard_map/ppermute | solution.py:274
  120.2 4.3 %attend1.1 = f32[4,32,1408]{2,1,0:T(8,128)S(1)} custom-call(s32[7]{0:T(128)S(1)} %stack.31.place, s32[4]{0:T(128)S(1)} %copy-done.1, bf16[4,32,1280]{2,1,0:T(8,128)(2,1)S(1)} %collective-permute-done.9.q, bf16[32,32,640]{2,1,0:T(8,128)(2,1)S(1)} %all-to-all-done.2.blocks, bf16[32,640]{1,0:T(8,128)(2,1)S(1)} %collective-permute-done.5.far), custom_call_target="tpu_custom_call" | custom-call | tf_op jit(solution)/shard_map/attend1/pallas_call | solution.py:338
  124.5 4.0 %collective-permute-start.10 = (f32[4,32,1408]{2,1,0:T(8,128)S(1)}, f32[4,32,1408]{2,1,0:T(8,128)S(1)}, u32[]{:S(2)}, u32[]{:S(2)}) collective-permute-start(f32[4,32,1408]{2,1,0:T(8,128)S(1)} %attend1.1), channel_id=1, source_target_pairs={{0,1},{1,0},{2,3},{3,2},{4,5},{5,4},{6,7},{7,6},{8,9},{9,8},{10,11... | collective-permute-start | bytes 2162696 | tf_op jit(solution)/shard_map/ppermute | solution.py:347
  128.6 4.4 %attend0.1.here = f32[4,32,1408]{2,1,0:T(8,128)S(1)} custom-call(s32[7]{0:T(128)S(1)} %stack.31.place, s32[4]{0:T(128)S(1)} %copy-done.1, bf16[4,32,1280]{2,1,0:T(8,128)(2,1)S(1)} %pad_maximum_fusion.q, bf16[32,32,640]{2,1,0:T(8,128)(2,1)S(1)} %all-to-all-done.2.blocks, bf16[32,640]{1,0:T(8,128)(2,1)S(1)} %collective-permute-done.5.far), custom_call_target="tpu_custom_call" | custom-call | tf_op jit(solution)/shard_map/attend0/pallas_call | solution.py:338
  133.8 3.6 %all-to-all-start.3 = ((bf16[4,32,1408]{2,1,0:T(8,128)(2,1)}), bf16[4,32,1408]{2,1,0:T(8,128)(2,1)S(1)}, u32[]{:S(2)}, u32[]{:S(2)}) async-start(bf16[4,32,1408]{2,1,0:T(8,128)(2,1)} %pack.1), calls=%async_computation.3 | async-start | bytes 720896 | tf_op jit(solution)/shard_map/all_to_all | solution.py:352
  137.4 5.0 %collective-permute-start.11 = (bf16[16,24,256]{2,1,0:T(8,128)(2,1)S(1)}, bf16[16,24,256]{2,1,0:T(8,128)(2,1)S(1)}, u32[]{:S(2)}, u32[]{:S(2)}) collective-permute-start(bf16[16,24,256]{2,1,0:T(8,128)(2,1)S(1)} %slice.4.own), channel_id=1, source_target_pairs={{0,16},{8,24},{16,0},{24,8},{1,17},{9,25},{17,1},{25,9},{2,18},{10... | collective-permute-start | bytes 589832 | tf_op jit(solution)/shard_map/ppermute | solution.py:274
  142.4 4.9 %collective-permute-done.11.two = bf16[16,24,256]{2,1,0:T(8,128)(2,1)S(1)} collective-permute-done((bf16[16,24,256]{2,1,0:T(8,128)(2,1)S(1)}, bf16[16,24,256]{2,1,0:T(8,128)(2,1)S(1)}, u32[]{:S(2)}, u32[]{:S(2)}) %collective-permute-start.11) | collective-permute-done | bytes 196640 | tf_op jit(solution)/shard_map/ppermute | solution.py:274
  148.5 16.0 %all_gather.3.attended = bf16[256,1280]{1,0:T(8,128)(2,1)S(1)} all-gather(bf16[32,1280]{1,0:T(8,128)(2,1)S(1)} %divide.1), channel_id=1, replica_groups=mesh['yh'=2,'z'=8,'x'=4,'yl'=4,'c'=2] {'yl','c'}, dimensions={0}, use_global_device_ids=true | all-gather | bytes 737280 | tf_op jit(solution)/shard_map/all_gather | solution.py:357
  (46 shorter events, 9.0 us)
Async XLA Ops:
  0.6 17.8 %copy-start = (bf16[256,256]{1,0:T(8,128)(2,1)S(1)}, bf16[256,256]{1,0:T(8,128)(2,1)}, u32[]{:S(2)}) copy-start(bf16[256,256]{1,0:T(8,128)(2,1)} %param.8) | copy-start | bytes 393220
  0.6 28.4 %copy-start.3 = (bf16[256]{0:T(256)(128)(2,1)S(1)}, bf16[256]{0:T(256)(128)(2,1)}, u32[]{:S(2)}) copy-start(bf16[256]{0:T(256)(128)(2,1)} %param.9) | copy-start | bytes 1540
  2.2 31.2 %all-to-all-start = ((bf16[16,56,256]{2,1,0:T(8,128)(2,1)}), bf16[16,56,256]{2,1,0:T(8,128)(2,1)S(1)}, u32[]{:S(2)}, u32[]{:S(2)}) async-start(bf16[16,56,256]{2,1,0:T(8,128)(2,1)} %broadcast_in_dim.50), calls=%async_computation | async-start | bytes 917504 | tf_op jit(solution)/shard_map/all_to_all | solution.py:261
  18.5 10.7 %collective-permute-start = (bf16[256,256]{1,0:T(8,128)(2,1)S(1)}, bf16[256,256]{1,0:T(8,128)(2,1)S(1)}, u32[]{:S(2)}, u32[]{:S(2)}) collective-permute-start(bf16[256,256]{1,0:T(8,128)(2,1)S(1)} %copy-done), channel_id=1, source_target_pairs={{0,8},{8,16},{16,24},{24,0},{1,9},{9,17},{17,25},{25,1},{2,10},{10... | collective-permute-start | bytes 393224 | tf_op jit(solution)/shard_map/ppermute | solution.py:274
  21.6 7.9 %collective-permute-start.1 = (bf16[256,256]{1,0:T(8,128)(2,1)S(1)}, bf16[256,256]{1,0:T(8,128)(2,1)S(1)}, u32[]{:S(2)}, u32[]{:S(2)}) collective-permute-start(bf16[256,256]{1,0:T(8,128)(2,1)S(1)} %copy-done), channel_id=1, source_target_pairs={{0,16},{8,24},{16,0},{24,8},{1,17},{9,25},{17,1},{25,9},{2,18},{10... | collective-permute-start | bytes 393224 | tf_op jit(solution)/shard_map/ppermute | solution.py:274
  26.0 6.0 %collective-permute-start.2 = (bf16[256,256]{1,0:T(8,128)(2,1)S(1)}, bf16[256,256]{1,0:T(8,128)(2,1)S(1)}, u32[]{:S(2)}, u32[]{:S(2)}) collective-permute-start(bf16[256,256]{1,0:T(8,128)(2,1)S(1)} %copy-done), channel_id=1, source_target_pairs={{0,24},{8,0},{16,8},{24,16},{1,25},{9,1},{17,9},{25,17},{2,26},{10... | collective-permute-start | bytes 393224 | tf_op jit(solution)/shard_map/ppermute | solution.py:274
  34.4 6.7 %collective-permute-start.3 = (f32[4,128,512]{2,1,0:T(8,128)S(1)}, f32[4,128,512]{2,1,0:T(8,128)S(1)}, u32[]{:S(2)}, u32[]{:S(2)}) collective-permute-start(f32[4,128,512]{2,1,0:T(8,128)S(1)} %project1.1), channel_id=1, source_target_pairs={{0,1},{1,0},{2,3},{3,2},{4,5},{5,4},{6,7},{7,6},{8,9},{9,8},{10,11... | collective-permute-start | bytes 3145736 | tf_op jit(solution)/shard_map/ppermute | solution.py:296
  42.3 7.6 %copy-start.4 = (bf16[64]{0:T(256)(128)(2,1)S(1)}, bf16[64]{0:T(256)(128)(2,1)}, u32[]{:S(2)}) copy-start(bf16[64]{0:T(256)(128)(2,1)} %param.12) | copy-start | bytes 388
  42.3 7.7 %copy-start.1 = (s32[4]{0:T(128)S(1)}, s32[4]{0:T(128)}, u32[]{:S(2)}) copy-start(s32[4]{0:T(128)} %lengths.3) | copy-start | bytes 52
  42.3 28.9 %copy-start.2 = (s32[4]{0:T(128)S(1)}, s32[4]{0:T(128)}, u32[]{:S(2)}) copy-start(s32[4]{0:T(128)} %table.1) | copy-start | bytes 52
  42.3 33.1 %copy-start.5 = (bf16[64]{0:T(256)(128)(2,1)S(1)}, bf16[64]{0:T(256)(128)(2,1)}, u32[]{:S(2)}) copy-start(bf16[64]{0:T(256)(128)(2,1)} %param.11) | copy-start | bytes 388
  42.3 28.9 %all-to-all-start.1 = ((bf16[16,32,768]{2,1,0:T(8,128)(2,1)}), bf16[16,32,768]{2,1,0:T(8,128)(2,1)S(1)}, u32[]{:S(2)}, u32[]{:S(2)}) async-start(bf16[16,32,768]{2,1,0:T(8,128)(2,1)} %bitcast.12), calls=%async_computation.1 | async-start | bytes 1572864 | tf_op jit(solution)/shard_map/all_to_all | solution.py:301
  50.3 15.0 %collective-permute-start.4 = (bf16[16,24,256]{2,1,0:T(8,128)(2,1)S(1)}, bf16[16,24,256]{2,1,0:T(8,128)(2,1)S(1)}, u32[]{:S(2)}, u32[]{:S(2)}) collective-permute-start(bf16[16,24,256]{2,1,0:T(8,128)(2,1)S(1)} %slice.4.own), channel_id=1, source_target_pairs={{0,8},{8,16},{16,24},{24,0},{1,9},{9,17},{17,25},{25,1},{2,10},{10... | collective-permute-start | bytes 589832 | tf_op jit(solution)/shard_map/ppermute | solution.py:274
  72.8 8.6 %collective-permute-start.5 = (bf16[32,640]{1,0:T(8,128)(2,1)S(1)}, bf16[32,640]{1,0:T(8,128)(2,1)S(1)}, u32[]{:S(2)}, u32[]{:S(2)}) collective-permute-start(bf16[32,640]{1,0:T(8,128)(2,1)S(1)} %get-tuple-element.21), channel_id=1, source_target_pairs={{0,256},{256,0},{1,257},{257,1},{2,258},{258,2},{3,259},{259,3},{4... | collective-permute-start | bytes 122888 | tf_op jit(solution)/shard_map/ppermute | solution.py:324
  82.7 37.5 %all-to-all-start.2 = ((bf16[32,32,640]{2,1,0:T(8,128)(2,1)}), bf16[32,32,640]{2,1,0:T(8,128)(2,1)S(1)}, u32[]{:S(2)}, u32[]{:S(2)}) async-start(bf16[32,32,640]{2,1,0:T(8,128)(2,1)} %broadcast_select_fusion), calls=%async_computation.2 | async-start | bytes 2621440 | tf_op jit(solution)/shard_map/all_to_all | solution.py:333
  87.7 7.0 %collective-permute-start.7 = (bf16[1,32,1280]{2,1,0:T(8,128)(2,1)S(1)}, bf16[1,32,1280]{2,1,0:T(8,128)(2,1)S(1)}, u32[]{:S(2)}, u32[]{:S(2)}) collective-permute-start(bf16[1,32,1280]{2,1,0:T(8,128)(2,1)S(1)} %bitcast.21), channel_id=1, source_target_pairs={{0,2},{2,4},{4,6},{6,0},{1,3},{3,5},{5,7},{7,1},{8,10},{10,12},{12... | collective-permute-start | bytes 245768 | tf_op jit(solution)/shard_map/ppermute | solution.py:274
  94.7 7.3 %collective-permute-start.8 = (bf16[2,32,1280]{2,1,0:T(8,128)(2,1)S(1)}, bf16[2,32,1280]{2,1,0:T(8,128)(2,1)S(1)}, u32[]{:S(2)}, u32[]{:S(2)}) collective-permute-start(bf16[2,32,1280]{2,1,0:T(8,128)(2,1)S(1)} %pad_maximum_fusion.1), channel_id=1, source_target_pairs={{0,4},{2,6},{4,0},{6,2},{1,5},{3,7},{5,1},{7,3},{8,12},{10,14},{12... | collective-permute-start | bytes 491528 | tf_op jit(solution)/shard_map/ppermute | solution.py:274
  102.0 18.3 %collective-permute-start.9 = (bf16[4,32,1280]{2,1,0:T(8,128)(2,1)S(1)}, bf16[4,32,1280]{2,1,0:T(8,128)(2,1)S(1)}, u32[]{:S(2)}, u32[]{:S(2)}) collective-permute-start(bf16[4,32,1280]{2,1,0:T(8,128)(2,1)S(1)} %pad_maximum_fusion.q), channel_id=1, source_target_pairs={{0,1},{1,0},{2,3},{3,2},{4,5},{5,4},{6,7},{7,6},{8,9},{9,8},{10,11... | collective-permute-start | bytes 983048 | tf_op jit(solution)/shard_map/ppermute | solution.py:331
  108.8 11.5 %collective-permute-start.6 = (bf16[16,24,256]{2,1,0:T(8,128)(2,1)S(1)}, bf16[16,24,256]{2,1,0:T(8,128)(2,1)S(1)}, u32[]{:S(2)}, u32[]{:S(2)}) collective-permute-start(bf16[16,24,256]{2,1,0:T(8,128)(2,1)S(1)} %slice.4.own), channel_id=1, source_target_pairs={{0,24},{8,0},{16,8},{24,16},{1,25},{9,1},{17,9},{25,17},{2,26},{10... | collective-permute-start | bytes 589832 | tf_op jit(solution)/shard_map/ppermute | solution.py:274
  124.5 8.4 %collective-permute-start.10 = (f32[4,32,1408]{2,1,0:T(8,128)S(1)}, f32[4,32,1408]{2,1,0:T(8,128)S(1)}, u32[]{:S(2)}, u32[]{:S(2)}) collective-permute-start(f32[4,32,1408]{2,1,0:T(8,128)S(1)} %attend1.1), channel_id=1, source_target_pairs={{0,1},{1,0},{2,3},{3,2},{4,5},{5,4},{6,7},{7,6},{8,9},{9,8},{10,11... | collective-permute-start | bytes 2162696 | tf_op jit(solution)/shard_map/ppermute | solution.py:347
  133.8 14.5 %all-to-all-start.3 = ((bf16[4,32,1408]{2,1,0:T(8,128)(2,1)}), bf16[4,32,1408]{2,1,0:T(8,128)(2,1)S(1)}, u32[]{:S(2)}, u32[]{:S(2)}) async-start(bf16[4,32,1408]{2,1,0:T(8,128)(2,1)} %pack.1), calls=%async_computation.3 | async-start | bytes 720896 | tf_op jit(solution)/shard_map/all_to_all | solution.py:352
  137.4 9.9 %collective-permute-start.11 = (bf16[16,24,256]{2,1,0:T(8,128)(2,1)S(1)}, bf16[16,24,256]{2,1,0:T(8,128)(2,1)S(1)}, u32[]{:S(2)}, u32[]{:S(2)}) collective-permute-start(bf16[16,24,256]{2,1,0:T(8,128)(2,1)S(1)} %slice.4.own), channel_id=1, source_target_pairs={{0,16},{8,24},{16,0},{24,8},{1,17},{9,25},{17,1},{25,9},{2,18},{10... | collective-permute-start | bytes 589832 | tf_op jit(solution)/shard_map/ppermute | solution.py:274

commit v10 on v9

--- a/solution.py
+++ b/solution.py
@@ -299,8 +299,8 @@
     ).reshape(16, ROWS, 768)
     mixing, partial = lax.optimization_barrier((weight[:, 32:], partial))
     parts = lax.all_to_all(partial, ("x", "yl"), 0, 0)
-    after = shift(mixing, "x", 4, 1)
-    mixing, after, parts = lax.optimization_barrier((mixing, after, parts))
+    after, across = shift(mixing, "x", 4, 1), shift(mixing, "x", 4, 2)
+    mixing, after, across, parts = lax.optimization_barrier((mixing, after, across, parts))
 
     row = jnp.arange(ROWS, dtype=jnp.int32)
     own = wide * TOK_DEV + row // 8 * PAGE + narrow * 8 + row % 8
@@ -351,7 +351,7 @@
     mixing, packed = lax.optimization_barrier((mixing, packed))
     parts = lax.all_to_all(packed, "yl", 0, 0)
     mixing = call(order_body, jax.ShapeDtypeStruct((64, 20, 256), BF), [SM] + [VM] * 4, "order")(
-        place, mixing, after, shift(mixing, "x", 4, 2), before
+        place, mixing, after, across, before
     ).reshape(Q_DIM, 256)
     attended = call(divide_body, jax.ShapeDtypeStruct((ROWS, Q_DIM), BF), [VM], "divide")(parts)
     attended = lax.all_gather(attended, ("yl", "c"), axis=0, tiled=True)

time: 166 us -> 167 us (level)
    all_to_all x1, waiting for transfers between devices: 0.15 us -> 10.1 us  [on_device(): parts = lax.all_to_all(packed, 'yl', 0, 0)]
    ppermute x8, waiting for transfers between devices: 36.5 us -> 31.3 us  [shift(): lax.ppermute(value, axis, [(i, (i + step) % count) for i in range(count)])]
    all_to_all x1, waiting for transfers between devices: 5.95 us -> 1.91 us  [on_device(): parts = lax.all_to_all(partial, ('x', 'yl'), 0, 0)]
where the time goes in v10:
time: 167 us; the launch traced here: 166 us
  starting transfers between devices  76.3 us (46%)
  waiting for transfers between devices  51.1 us (31%)
  Pallas kernels  17.3 us (10%)
  blocking collectives  16.2 us (10%)
  other arithmetic  2.54 us (2%)
    ppermute x8, waiting for transfers between devices, shift(): lax.ppermute(value, axis, [(i, (i + step) % count) for i in range(count)])  31.3 us
    ppermute x8, starting transfers between devices, shift(): lax.ppermute(value, axis, [(i, (i + step) % count) for i in range(count)])  26.6 us
    all_to_all x1, starting transfers between devices, spread(): lax.all_to_all(jnp.broadcast_to(x[None], (count,) + x.shape), axes, 0, 0)  16.2 us
    all_gather x1, blocking collectives, on_device(): attended = lax.all_gather(attended, ('yl', 'c'), axis=0, tiled=True)  16.2 us
    all_to_all x1, waiting for transfers between devices, on_device(): parts = lax.all_to_all(packed, 'yl', 0, 0)  10.1 us
    pallas_call x2, Pallas kernels, attend(): call(functools.partial(attend_body, flip), jax.ShapeDtypeStruct((4, ROWS,...  8.69 us
    ppermute x2, starting transfers between devices, on_device(): arrived = lax.ppermute(sent, 'c', swap)  8.48 us
    all_to_all x1, starting transfers between devices, on_device(): parts = lax.all_to_all(partial, ('x', 'yl'), 0, 0)  7.5 us
  transfers between devices with their start and end apart: 16, of which 12 were waited for; matrix products, arithmetic and copies ran while one was open for 1% of the time, Pallas kernels for 4%

profile of v10, /device:TPU:1, one launch (start us, length us, event | category | flops | bytes accessed | tf_op | source)
XLA Modules:
  0.0 165.7 jit_solution(16984859840003906931)
XLA Ops:
  2.2 16.2 %all-to-all-start = ((bf16[16,56,256]{2,1,0:T(8,128)(2,1)}), bf16[16,56,256]{2,1,0:T(8,128)(2,1)S(1)}, u32[]{:S(2)}, u32[]{:S(2)}) async-start(bf16[16,56,256]{2,1,0:T(8,128)(2,1)} %broadcast_in_dim.50), calls=%async_computation | async-start | bytes 917504 | tf_op jit(solution)/shard_map/all_to_all | solution.py:261
  18.5 3.1 %collective-permute-start = (bf16[256,256]{1,0:T(8,128)(2,1)S(1)}, bf16[256,256]{1,0:T(8,128)(2,1)S(1)}, u32[]{:S(2)}, u32[]{:S(2)}) collective-permute-start(bf16[256,256]{1,0:T(8,128)(2,1)S(1)} %copy-done), channel_id=1, source_target_pairs={{0,8},{8,16},{16,24},{24,0},{1,9},{9,17},{17,25},{25,1},{2,10},{10... | collective-permute-start | bytes 393224 | tf_op jit(solution)/shard_map/ppermute | solution.py:274
  21.6 4.4 %collective-permute-start.1 = (bf16[256,256]{1,0:T(8,128)(2,1)S(1)}, bf16[256,256]{1,0:T(8,128)(2,1)S(1)}, u32[]{:S(2)}, u32[]{:S(2)}) collective-permute-start(bf16[256,256]{1,0:T(8,128)(2,1)S(1)} %copy-done), channel_id=1, source_target_pairs={{0,16},{8,24},{16,0},{24,8},{1,17},{9,25},{17,1},{25,9},{2,18},{10... | collective-permute-start | bytes 393224 | tf_op jit(solution)/shard_map/ppermute | solution.py:274
  26.0 3.1 %collective-permute-start.2 = (bf16[256,256]{1,0:T(8,128)(2,1)S(1)}, bf16[256,256]{1,0:T(8,128)(2,1)S(1)}, u32[]{:S(2)}, u32[]{:S(2)}) collective-permute-start(bf16[256,256]{1,0:T(8,128)(2,1)S(1)} %copy-done), channel_id=1, source_target_pairs={{0,24},{8,0},{16,8},{24,16},{1,25},{9,1},{17,9},{25,17},{2,26},{10... | collective-permute-start | bytes 393224 | tf_op jit(solution)/shard_map/ppermute | solution.py:274
  29.5 2.5 %collective-permute-done.2 = bf16[256,256]{1,0:T(8,128)(2,1)S(1)} collective-permute-done((bf16[256,256]{1,0:T(8,128)(2,1)S(1)}, bf16[256,256]{1,0:T(8,128)(2,1)S(1)}, u32[]{:S(2)}, u32[]{:S(2)}) %collective-permute-start.2) | collective-permute-done | bytes 131104 | tf_op jit(solution)/shard_map/ppermute | solution.py:274
  32.0 1.4 all-to-all-done.weight
  34.4 4.4 %collective-permute-start.3 = (f32[4,128,512]{2,1,0:T(8,128)S(1)}, f32[4,128,512]{2,1,0:T(8,128)S(1)}, u32[]{:S(2)}, u32[]{:S(2)}) collective-permute-start(f32[4,128,512]{2,1,0:T(8,128)S(1)} %project1.1), channel_id=1, source_target_pairs={{0,1},{1,0},{2,3},{3,2},{4,5},{5,4},{6,7},{7,6},{8,9},{9,8},{10,11... | collective-permute-start | bytes 3145736 | tf_op jit(solution)/shard_map/ppermute | solution.py:296
  42.3 7.5 %all-to-all-start.1 = ((bf16[16,32,768]{2,1,0:T(8,128)(2,1)}), bf16[16,32,768]{2,1,0:T(8,128)(2,1)S(1)}, u32[]{:S(2)}, u32[]{:S(2)}) async-start(bf16[16,32,768]{2,1,0:T(8,128)(2,1)} %bitcast.12), calls=%async_computation.1 | async-start | bytes 1572864 | tf_op jit(solution)/shard_map/all_to_all | solution.py:301
  50.3 3.3 %collective-permute-start.4 = (bf16[16,24,256]{2,1,0:T(8,128)(2,1)S(1)}, bf16[16,24,256]{2,1,0:T(8,128)(2,1)S(1)}, u32[]{:S(2)}, u32[]{:S(2)}) collective-permute-start(bf16[16,24,256]{2,1,0:T(8,128)(2,1)S(1)} %slice.4.own), channel_id=1, source_target_pairs={{0,8},{8,16},{16,24},{24,0},{1,9},{9,17},{17,25},{25,1},{2,10},{10... | collective-permute-start | bytes 589832 | tf_op jit(solution)/shard_map/ppermute | solution.py:274
  53.6 4.3 %collective-permute-start.5 = (bf16[16,24,256]{2,1,0:T(8,128)(2,1)S(1)}, bf16[16,24,256]{2,1,0:T(8,128)(2,1)S(1)}, u32[]{:S(2)}, u32[]{:S(2)}) collective-permute-start(bf16[16,24,256]{2,1,0:T(8,128)(2,1)S(1)} %slice.4.own), channel_id=1, source_target_pairs={{0,16},{8,24},{16,0},{24,8},{1,17},{9,25},{17,1},{25,9},{2,18},{10... | collective-permute-start | bytes 589832 | tf_op jit(solution)/shard_map/ppermute | solution.py:274
  58.0 7.4 %collective-permute-done.4.one = bf16[16,24,256]{2,1,0:T(8,128)(2,1)S(1)} collective-permute-done((bf16[16,24,256]{2,1,0:T(8,128)(2,1)S(1)}, bf16[16,24,256]{2,1,0:T(8,128)(2,1)S(1)}, u32[]{:S(2)}, u32[]{:S(2)}) %collective-permute-start.4) | collective-permute-done | bytes 196640 | tf_op jit(solution)/shard_map/ppermute | solution.py:274
  65.5 3.9 %collective-permute-done.5.two = bf16[16,24,256]{2,1,0:T(8,128)(2,1)S(1)} collective-permute-done((bf16[16,24,256]{2,1,0:T(8,128)(2,1)S(1)}, bf16[16,24,256]{2,1,0:T(8,128)(2,1)S(1)}, u32[]{:S(2)}, u32[]{:S(2)}) %collective-permute-start.5) | collective-permute-done | bytes 196640 | tf_op jit(solution)/shard_map/ppermute | solution.py:274
  69.3 1.9 %all-to-all-done.1.parts = bf16[16,32,768]{2,1,0:T(8,128)(2,1)S(1)} async-done(((bf16[16,32,768]{2,1,0:T(8,128)(2,1)}), bf16[16,32,768]{2,1,0:T(8,128)(2,1)S(1)}, u32[]{:S(2)}, u32[]{:S(2)}) %all-to-all-start.1) | async-done | bytes 786464 | tf_op jit(solution)/shard_map/all_to_all | solution.py:301
  71.2 1.5 rotate_keys.1
  72.8 2.6 %collective-permute-start.6 = (bf16[32,640]{1,0:T(8,128)(2,1)S(1)}, bf16[32,640]{1,0:T(8,128)(2,1)S(1)}, u32[]{:S(2)}, u32[]{:S(2)}) collective-permute-start(bf16[32,640]{1,0:T(8,128)(2,1)S(1)} %get-tuple-element.22), channel_id=1, source_target_pairs={{0,256},{256,0},{1,257},{257,1},{2,258},{258,2},{3,259},{259,3},{4... | collective-permute-start | bytes 122888 | tf_op jit(solution)/shard_map/ppermute | solution.py:324
  75.5 1.2 rotate_queries.1
  76.7 5.1 %collective-permute-done.6.far = bf16[32,640]{1,0:T(8,128)(2,1)S(1)} collective-permute-done((bf16[32,640]{1,0:T(8,128)(2,1)S(1)}, bf16[32,640]{1,0:T(8,128)(2,1)S(1)}, u32[]{:S(2)}, u32[]{:S(2)}) %collective-permute-start.6) | collective-permute-done | bytes 40992 | tf_op jit(solution)/shard_map/ppermute | solution.py:324
  81.9 1.3 broadcast_select_fusion
  83.1 4.6 %all-to-all-start.2 = ((bf16[32,32,640]{2,1,0:T(8,128)(2,1)}), bf16[32,32,640]{2,1,0:T(8,128)(2,1)S(1)}, u32[]{:S(2)}, u32[]{:S(2)}) async-start(bf16[32,32,640]{2,1,0:T(8,128)(2,1)} %broadcast_select_fusion), calls=%async_computation.2 | async-start | bytes 2621440 | tf_op jit(solution)/shard_map/all_to_all | solution.py:333
  87.7 1.9 %collective-permute-start.8 = (bf16[1,32,1280]{2,1,0:T(8,128)(2,1)S(1)}, bf16[1,32,1280]{2,1,0:T(8,128)(2,1)S(1)}, u32[]{:S(2)}, u32[]{:S(2)}) collective-permute-start(bf16[1,32,1280]{2,1,0:T(8,128)(2,1)S(1)} %bitcast.21), channel_id=1, source_target_pairs={{0,2},{2,4},{4,6},{6,0},{1,3},{3,5},{5,7},{7,1},{8,10},{10,12},{12... | collective-permute-start | bytes 245768 | tf_op jit(solution)/shard_map/ppermute | solution.py:274
  89.6 5.1 %collective-permute-done.8 = bf16[1,32,1280]{2,1,0:T(8,128)(2,1)S(1)} collective-permute-done((bf16[1,32,1280]{2,1,0:T(8,128)(2,1)S(1)}, bf16[1,32,1280]{2,1,0:T(8,128)(2,1)S(1)}, u32[]{:S(2)}, u32[]{:S(2)}) %collective-permute-start.8) | collective-permute-done | bytes 81952 | tf_op jit(solution)/shard_map/ppermute | solution.py:274
  94.7 1.9 %collective-permute-start.9 = (bf16[2,32,1280]{2,1,0:T(8,128)(2,1)S(1)}, bf16[2,32,1280]{2,1,0:T(8,128)(2,1)S(1)}, u32[]{:S(2)}, u32[]{:S(2)}) collective-permute-start(bf16[2,32,1280]{2,1,0:T(8,128)(2,1)S(1)} %pad_maximum_fusion.1), channel_id=1, source_target_pairs={{0,4},{2,6},{4,0},{6,2},{1,5},{3,7},{5,1},{7,3},{8,12},{10,14},{12... | collective-permute-start | bytes 491528 | tf_op jit(solution)/shard_map/ppermute | solution.py:274
  96.7 5.3 %collective-permute-done.9 = bf16[2,32,1280]{2,1,0:T(8,128)(2,1)S(1)} collective-permute-done((bf16[2,32,1280]{2,1,0:T(8,128)(2,1)S(1)}, bf16[2,32,1280]{2,1,0:T(8,128)(2,1)S(1)}, u32[]{:S(2)}, u32[]{:S(2)}) %collective-permute-start.9) | collective-permute-done | bytes 163872 | tf_op jit(solution)/shard_map/ppermute | solution.py:274
  102.0 6.8 %collective-permute-start.10 = (bf16[4,32,1280]{2,1,0:T(8,128)(2,1)S(1)}, bf16[4,32,1280]{2,1,0:T(8,128)(2,1)S(1)}, u32[]{:S(2)}, u32[]{:S(2)}) collective-permute-start(bf16[4,32,1280]{2,1,0:T(8,128)(2,1)S(1)} %pad_maximum_fusion.q), channel_id=1, source_target_pairs={{0,1},{1,0},{2,3},{3,2},{4,5},{5,4},{6,7},{7,6},{8,9},{9,8},{10,11... | collective-permute-start | bytes 983048 | tf_op jit(solution)/shard_map/ppermute | solution.py:331
  108.8 4.6 %collective-permute-start.7 = (bf16[16,24,256]{2,1,0:T(8,128)(2,1)S(1)}, bf16[16,24,256]{2,1,0:T(8,128)(2,1)S(1)}, u32[]{:S(2)}, u32[]{:S(2)}) collective-permute-start(bf16[16,24,256]{2,1,0:T(8,128)(2,1)S(1)} %slice.4.own), channel_id=1, source_target_pairs={{0,24},{8,0},{16,8},{24,16},{1,25},{9,1},{17,9},{25,17},{2,26},{10... | collective-permute-start | bytes 589832 | tf_op jit(solution)/shard_map/ppermute | solution.py:274
  113.4 6.8 %collective-permute-done.7.three = bf16[16,24,256]{2,1,0:T(8,128)(2,1)S(1)} collective-permute-done((bf16[16,24,256]{2,1,0:T(8,128)(2,1)S(1)}, bf16[16,24,256]{2,1,0:T(8,128)(2,1)S(1)}, u32[]{:S(2)}, u32[]{:S(2)}) %collective-permute-start.7) | collective-permute-done | bytes 196640 | tf_op jit(solution)/shard_map/ppermute | solution.py:274
  120.3 4.3 %attend1.1 = f32[4,32,1408]{2,1,0:T(8,128)S(1)} custom-call(s32[7]{0:T(128)S(1)} %stack.31.place, s32[4]{0:T(128)S(1)} %copy-done.1, bf16[4,32,1280]{2,1,0:T(8,128)(2,1)S(1)} %collective-permute-done.10.q, bf16[32,32,640]{2,1,0:T(8,128)(2,1)S(1)} %all-to-all-done.2.blocks, bf16[32,640]{1,0:T(8,128)(2,1)S(1)} %collective-permute-done.6.far), custom_call_target="tpu_custom_call" | custom-call | tf_op jit(solution)/shard_map/attend1/pallas_call | solution.py:338
  124.6 4.1 %collective-permute-start.11 = (f32[4,32,1408]{2,1,0:T(8,128)S(1)}, f32[4,32,1408]{2,1,0:T(8,128)S(1)}, u32[]{:S(2)}, u32[]{:S(2)}) collective-permute-start(f32[4,32,1408]{2,1,0:T(8,128)S(1)} %attend1.1), channel_id=1, source_target_pairs={{0,1},{1,0},{2,3},{3,2},{4,5},{5,4},{6,7},{7,6},{8,9},{9,8},{10,11... | collective-permute-start | bytes 2162696 | tf_op jit(solution)/shard_map/ppermute | solution.py:347
  128.6 4.4 %attend0.1.here = f32[4,32,1408]{2,1,0:T(8,128)S(1)} custom-call(s32[7]{0:T(128)S(1)} %stack.31.place, s32[4]{0:T(128)S(1)} %copy-done.1, bf16[4,32,1280]{2,1,0:T(8,128)(2,1)S(1)} %pad_maximum_fusion.q, bf16[32,32,640]{2,1,0:T(8,128)(2,1)S(1)} %all-to-all-done.2.blocks, bf16[32,640]{1,0:T(8,128)(2,1)S(1)} %collective-permute-done.6.far), custom_call_target="tpu_custom_call" | custom-call | tf_op jit(solution)/shard_map/attend0/pallas_call | solution.py:338
  133.9 3.6 %all-to-all-start.3 = ((bf16[4,32,1408]{2,1,0:T(8,128)(2,1)}), bf16[4,32,1408]{2,1,0:T(8,128)(2,1)S(1)}, u32[]{:S(2)}, u32[]{:S(2)}) async-start(bf16[4,32,1408]{2,1,0:T(8,128)(2,1)} %pack.1), calls=%async_computation.3 | async-start | bytes 720896 | tf_op jit(solution)/shard_map/all_to_all | solution.py:352
  138.2 10.1 %all-to-all-done.3.parts = bf16[4,32,1408]{2,1,0:T(8,128)(2,1)S(1)} async-done(((bf16[4,32,1408]{2,1,0:T(8,128)(2,1)}), bf16[4,32,1408]{2,1,0:T(8,128)(2,1)S(1)}, u32[]{:S(2)}, u32[]{:S(2)}) %all-to-all-start.3) | async-done | bytes 360480 | tf_op jit(solution)/shard_map/all_to_all | solution.py:352
  148.5 16.2 %all_gather.3.attended = bf16[256,1280]{1,0:T(8,128)(2,1)S(1)} all-gather(bf16[32,1280]{1,0:T(8,128)(2,1)S(1)} %divide.1), channel_id=1, replica_groups=mesh['yh'=2,'z'=8,'x'=4,'yl'=4,'c'=2] {'yl','c'}, dimensions={0}, use_global_device_ids=true | all-gather | bytes 737280 | tf_op jit(solution)/shard_map/all_gather | solution.py:357
  (46 shorter events, 10.0 us)
Async XLA Ops:
  0.6 17.8 %copy-start = (bf16[256,256]{1,0:T(8,128)(2,1)S(1)}, bf16[256,256]{1,0:T(8,128)(2,1)}, u32[]{:S(2)}) copy-start(bf16[256,256]{1,0:T(8,128)(2,1)} %param.8) | copy-start | bytes 393220
  0.6 28.4 %copy-start.3 = (bf16[256]{0:T(256)(128)(2,1)S(1)}, bf16[256]{0:T(256)(128)(2,1)}, u32[]{:S(2)}) copy-start(bf16[256]{0:T(256)(128)(2,1)} %param.9) | copy-start | bytes 1540
  2.2 31.2 %all-to-all-start = ((bf16[16,56,256]{2,1,0:T(8,128)(2,1)}), bf16[16,56,256]{2,1,0:T(8,128)(2,1)S(1)}, u32[]{:S(2)}, u32[]{:S(2)}) async-start(bf16[16,56,256]{2,1,0:T(8,128)(2,1)} %broadcast_in_dim.50), calls=%async_computation | async-start | bytes 917504 | tf_op jit(solution)/shard_map/all_to_all | solution.py:261
  18.5 10.7 %collective-permute-start = (bf16[256,256]{1,0:T(8,128)(2,1)S(1)}, bf16[256,256]{1,0:T(8,128)(2,1)S(1)}, u32[]{:S(2)}, u32[]{:S(2)}) collective-permute-start(bf16[256,256]{1,0:T(8,128)(2,1)S(1)} %copy-done), channel_id=1, source_target_pairs={{0,8},{8,16},{16,24},{24,0},{1,9},{9,17},{17,25},{25,1},{2,10},{10... | collective-permute-start | bytes 393224 | tf_op jit(solution)/shard_map/ppermute | solution.py:274
  21.6 7.9 %collective-permute-start.1 = (bf16[256,256]{1,0:T(8,128)(2,1)S(1)}, bf16[256,256]{1,0:T(8,128)(2,1)S(1)}, u32[]{:S(2)}, u32[]{:S(2)}) collective-permute-start(bf16[256,256]{1,0:T(8,128)(2,1)S(1)} %copy-done), channel_id=1, source_target_pairs={{0,16},{8,24},{16,0},{24,8},{1,17},{9,25},{17,1},{25,9},{2,18},{10... | collective-permute-start | bytes 393224 | tf_op jit(solution)/shard_map/ppermute | solution.py:274
  26.0 6.0 %collective-permute-start.2 = (bf16[256,256]{1,0:T(8,128)(2,1)S(1)}, bf16[256,256]{1,0:T(8,128)(2,1)S(1)}, u32[]{:S(2)}, u32[]{:S(2)}) collective-permute-start(bf16[256,256]{1,0:T(8,128)(2,1)S(1)} %copy-done), channel_id=1, source_target_pairs={{0,24},{8,0},{16,8},{24,16},{1,25},{9,1},{17,9},{25,17},{2,26},{10... | collective-permute-start | bytes 393224 | tf_op jit(solution)/shard_map/ppermute | solution.py:274
  34.4 6.7 %collective-permute-start.3 = (f32[4,128,512]{2,1,0:T(8,128)S(1)}, f32[4,128,512]{2,1,0:T(8,128)S(1)}, u32[]{:S(2)}, u32[]{:S(2)}) collective-permute-start(f32[4,128,512]{2,1,0:T(8,128)S(1)} %project1.1), channel_id=1, source_target_pairs={{0,1},{1,0},{2,3},{3,2},{4,5},{5,4},{6,7},{7,6},{8,9},{9,8},{10,11... | collective-permute-start | bytes 3145736 | tf_op jit(solution)/shard_map/ppermute | solution.py:296
  42.3 7.6 %copy-start.4 = (bf16[64]{0:T(256)(128)(2,1)S(1)}, bf16[64]{0:T(256)(128)(2,1)}, u32[]{:S(2)}) copy-start(bf16[64]{0:T(256)(128)(2,1)} %param.12) | copy-start | bytes 388
  42.3 7.7 %copy-start.1 = (s32[4]{0:T(128)S(1)}, s32[4]{0:T(128)}, u32[]{:S(2)}) copy-start(s32[4]{0:T(128)} %lengths.3) | copy-start | bytes 52
  42.3 28.9 %copy-start.2 = (s32[4]{0:T(128)S(1)}, s32[4]{0:T(128)}, u32[]{:S(2)}) copy-start(s32[4]{0:T(128)} %table.1) | copy-start | bytes 52
  42.3 33.1 %copy-start.5 = (bf16[64]{0:T(256)(128)(2,1)S(1)}, bf16[64]{0:T(256)(128)(2,1)}, u32[]{:S(2)}) copy-start(bf16[64]{0:T(256)(128)(2,1)} %param.11) | copy-start | bytes 388
  42.3 28.9 %all-to-all-start.1 = ((bf16[16,32,768]{2,1,0:T(8,128)(2,1)}), bf16[16,32,768]{2,1,0:T(8,128)(2,1)S(1)}, u32[]{:S(2)}, u32[]{:S(2)}) async-start(bf16[16,32,768]{2,1,0:T(8,128)(2,1)} %bitcast.12), calls=%async_computation.1 | async-start | bytes 1572864 | tf_op jit(solution)/shard_map/all_to_all | solution.py:301
  50.3 15.2 %collective-permute-start.4 = (bf16[16,24,256]{2,1,0:T(8,128)(2,1)S(1)}, bf16[16,24,256]{2,1,0:T(8,128)(2,1)S(1)}, u32[]{:S(2)}, u32[]{:S(2)}) collective-permute-start(bf16[16,24,256]{2,1,0:T(8,128)(2,1)S(1)} %slice.4.own), channel_id=1, source_target_pairs={{0,8},{8,16},{16,24},{24,0},{1,9},{9,17},{17,25},{25,1},{2,10},{10... | collective-permute-start | bytes 589832 | tf_op jit(solution)/shard_map/ppermute | solution.py:274
  53.6 15.7 %collective-permute-start.5 = (bf16[16,24,256]{2,1,0:T(8,128)(2,1)S(1)}, bf16[16,24,256]{2,1,0:T(8,128)(2,1)S(1)}, u32[]{:S(2)}, u32[]{:S(2)}) collective-permute-start(bf16[16,24,256]{2,1,0:T(8,128)(2,1)S(1)} %slice.4.own), channel_id=1, source_target_pairs={{0,16},{8,24},{16,0},{24,8},{1,17},{9,25},{17,1},{25,9},{2,18},{10... | collective-permute-start | bytes 589832 | tf_op jit(solution)/shard_map/ppermute | solution.py:274
  72.8 9.1 %collective-permute-start.6 = (bf16[32,640]{1,0:T(8,128)(2,1)S(1)}, bf16[32,640]{1,0:T(8,128)(2,1)S(1)}, u32[]{:S(2)}, u32[]{:S(2)}) collective-permute-start(bf16[32,640]{1,0:T(8,128)(2,1)S(1)} %get-tuple-element.22), channel_id=1, source_target_pairs={{0,256},{256,0},{1,257},{257,1},{2,258},{258,2},{3,259},{259,3},{4... | collective-permute-start | bytes 122888 | tf_op jit(solution)/shard_map/ppermute | solution.py:324
  83.1 37.1 %all-to-all-start.2 = ((bf16[32,32,640]{2,1,0:T(8,128)(2,1)}), bf16[32,32,640]{2,1,0:T(8,128)(2,1)S(1)}, u32[]{:S(2)}, u32[]{:S(2)}) async-start(bf16[32,32,640]{2,1,0:T(8,128)(2,1)} %broadcast_select_fusion), calls=%async_computation.2 | async-start | bytes 2621440 | tf_op jit(solution)/shard_map/all_to_all | solution.py:333
  87.7 7.0 %collective-permute-start.8 = (bf16[1,32,1280]{2,1,0:T(8,128)(2,1)S(1)}, bf16[1,32,1280]{2,1,0:T(8,128)(2,1)S(1)}, u32[]{:S(2)}, u32[]{:S(2)}) collective-permute-start(bf16[1,32,1280]{2,1,0:T(8,128)(2,1)S(1)} %bitcast.21), channel_id=1, source_target_pairs={{0,2},{2,4},{4,6},{6,0},{1,3},{3,5},{5,7},{7,1},{8,10},{10,12},{12... | collective-permute-start | bytes 245768 | tf_op jit(solution)/shard_map/ppermute | solution.py:274
  94.7 7.3 %collective-permute-start.9 = (bf16[2,32,1280]{2,1,0:T(8,128)(2,1)S(1)}, bf16[2,32,1280]{2,1,0:T(8,128)(2,1)S(1)}, u32[]{:S(2)}, u32[]{:S(2)}) collective-permute-start(bf16[2,32,1280]{2,1,0:T(8,128)(2,1)S(1)} %pad_maximum_fusion.1), channel_id=1, source_target_pairs={{0,4},{2,6},{4,0},{6,2},{1,5},{3,7},{5,1},{7,3},{8,12},{10,14},{12... | collective-permute-start | bytes 491528 | tf_op jit(solution)/shard_map/ppermute | solution.py:274
  102.0 18.3 %collective-permute-start.10 = (bf16[4,32,1280]{2,1,0:T(8,128)(2,1)S(1)}, bf16[4,32,1280]{2,1,0:T(8,128)(2,1)S(1)}, u32[]{:S(2)}, u32[]{:S(2)}) collective-permute-start(bf16[4,32,1280]{2,1,0:T(8,128)(2,1)S(1)} %pad_maximum_fusion.q), channel_id=1, source_target_pairs={{0,1},{1,0},{2,3},{3,2},{4,5},{5,4},{6,7},{7,6},{8,9},{9,8},{10,11... | collective-permute-start | bytes 983048 | tf_op jit(solution)/shard_map/ppermute | solution.py:331
  108.8 11.5 %collective-permute-start.7 = (bf16[16,24,256]{2,1,0:T(8,128)(2,1)S(1)}, bf16[16,24,256]{2,1,0:T(8,128)(2,1)S(1)}, u32[]{:S(2)}, u32[]{:S(2)}) collective-permute-start(bf16[16,24,256]{2,1,0:T(8,128)(2,1)S(1)} %slice.4.own), channel_id=1, source_target_pairs={{0,24},{8,0},{16,8},{24,16},{1,25},{9,1},{17,9},{25,17},{2,26},{10... | collective-permute-start | bytes 589832 | tf_op jit(solution)/shard_map/ppermute | solution.py:274
  124.6 8.5 %collective-permute-start.11 = (f32[4,32,1408]{2,1,0:T(8,128)S(1)}, f32[4,32,1408]{2,1,0:T(8,128)S(1)}, u32[]{:S(2)}, u32[]{:S(2)}) collective-permute-start(f32[4,32,1408]{2,1,0:T(8,128)S(1)} %attend1.1), channel_id=1, source_target_pairs={{0,1},{1,0},{2,3},{3,2},{4,5},{5,4},{6,7},{7,6},{8,9},{9,8},{10,11... | collective-permute-start | bytes 2162696 | tf_op jit(solution)/shard_map/ppermute | solution.py:347
  133.9 14.4 %all-to-all-start.3 = ((bf16[4,32,1408]{2,1,0:T(8,128)(2,1)}), bf16[4,32,1408]{2,1,0:T(8,128)(2,1)S(1)}, u32[]{:S(2)}, u32[]{:S(2)}) async-start(bf16[4,32,1408]{2,1,0:T(8,128)(2,1)} %pack.1), calls=%async_computation.3 | async-start | bytes 720896 | tf_op jit(solution)/shard_map/all_to_all | solution.py:352

commit v11 on v10

--- a/solution.py
+++ b/solution.py
@@ -142,7 +142,7 @@
         cache[pl.ds(table[p], 1)] = kv[p * 8 : p * 8 + 8, :].reshape(1, 8, KV_DIM)
 
 
-def attend_body(flip, place, lengths, q, blocks, far, out, bias, bias_far):
+def attend_body(flip, place, lengths, q, blocks, far, out, bias, bias_far, tops, unders):
     yh, index, wide, narrow, yl = place[0], place[1], place[2], place[4], place[6]
     core = place[3] if not flip else 1 - place[3]
     row = lax.broadcasted_iota(jnp.int32, (128, 1), 0)
@@ -164,44 +164,32 @@
         key = source * TOK_DEV + (lane % ROWS) // 8 * PAGE + narrow * 8 + lane % 8
         return jnp.where((key <= token) & (key >= begin), 0.0, HIDDEN_BIAS)
 
-    for chunk in range(4):
-        bias[chunk] = hide(chunk * 8, 256, False)
-    bias_far[...] = hide(index, ROWS, True)
     half = q[...].reshape(128, Q_DIM)
     owners = [(yl + 4 - k) & 3 for k in range(4)]
-    out[:, :, Q_DIM:] = jnp.zeros((4, ROWS, 128), F32)
-    for g in range(KV_HEADS):
+
+    def stacked_heads(g):
         heads = [
             half[:, (g * GROUP + h) * HEAD : (g * GROUP + h + 1) * HEAD] for h in range(GROUP)
         ]
-        stacked = jnp.concatenate(heads, axis=0)
-        denominator = None
-        numerator = None
-        tail = None
-        for chunk in range(5):
-            if chunk < 4:
-                keys = blocks[chunk * 8 : chunk * 8 + 8, :, g * HEAD : (g + 1) * HEAD]
-                keys = keys.reshape(256, HEAD)
-                values = blocks[chunk * 8 : chunk * 8 + 8, :, 320 + g * HEAD : 320 + (g + 1) * HEAD]
-                values = values.reshape(256, HEAD)
-                shade = bias[chunk]
-            else:
-                keys = far[:, g * HEAD : (g + 1) * HEAD]
-                values = far[:, 320 + g * HEAD : 320 + (g + 1) * HEAD]
-                shade = bias_far[...]
-            scores = lax.dot_general(
-                stacked, keys, (((1,), (1,)), ((), ())), preferred_element_type=F32
-            )
-            wide_scores = scores.reshape(GROUP, 128, keys.shape[0]) * EXP2_SCALE + shade[None]
-            weight = jnp.exp2(wide_scores).reshape(GROUP * 128, keys.shape[0])
-            product = jnp.dot(weight.astype(BF), values, preferred_element_type=F32)
-            numerator = product if numerator is None else numerator + product
-            if chunk < 4:
-                folded = weight[:, :128] + weight[:, 128:]
-                denominator = folded if denominator is None else denominator + folded
-            else:
-                tail = jnp.sum(weight, axis=1, keepdims=True)
-        denominator = jnp.sum(denominator, axis=1, keepdims=True) + tail
+        return jnp.concatenate(heads, axis=0)
+
+    def keys_values(g, chunk):
+        key_at = slice(g * HEAD, (g + 1) * HEAD)
+        value_at = slice(320 + g * HEAD, 320 + (g + 1) * HEAD)
+        if chunk == 4:
+            return far[:, key_at], far[:, value_at]
+        keys = blocks[chunk * 8 : chunk * 8 + 8, :, key_at].reshape(256, HEAD)
+        return keys, blocks[chunk * 8 : chunk * 8 + 8, :, value_at].reshape(256, HEAD)
+
+    def weigh(stacked, keys, values, shade):
+        scores = lax.dot_general(
+            stacked, keys, (((1,), (1,)), ((), ())), preferred_element_type=F32
+        )
+        wide_scores = scores.reshape(GROUP, 128, keys.shape[0]) * EXP2_SCALE + shade[None]
+        weight = jnp.exp2(wide_scores).reshape(GROUP * 128, keys.shape[0])
+        return weight, jnp.dot(weight.astype(BF), values, preferred_element_type=F32)
+
+    def put(g, numerator, denominator):
         for h in range(GROUP):
             head = g * GROUP + h
             for k in range(4):
@@ -210,6 +198,66 @@
                 out[to, :, head * HEAD : (head + 1) * HEAD] = numerator[at][None]
                 for lane in (Q_DIM + head, Q_DIM + HEAD + head):
                     out[to, :, lane : lane + 1] = denominator[at][None]
+
+    first = jnp.int32(0)
+    end = jnp.int32(0)
+    for s in range(3):
+        end = end + lengths[s]
+        first = jnp.where(wide * TOK_DEV >= end, end, first)
+    first = first >> 8
+    needed = []
+    for chunk in range(4):
+        low, high = chunk * 8, chunk * 8 + 7
+        near = (low <= index) & (yh * 32 + jnp.minimum(high, index) >= first)
+        needed.append(near | ((yh == 1) & (high > index) & (high >= first)))
+    far_needed = (yh == 1) & (index >= first)
+    every = needed[0] & needed[1] & needed[2] & needed[3]
+    out[:, :, Q_DIM:] = jnp.zeros((4, ROWS, 128), F32)
+
+    @pl.when(every)
+    def _():
+        for chunk in range(4):
+            bias[chunk] = hide(chunk * 8, 256, False)
+        bias_far[...] = hide(index, ROWS, True)
+        for g in range(KV_HEADS):
+            stacked = stacked_heads(g)
+            numerator, denominator = None, None
+            for chunk in range(4):
+                weight, product = weigh(stacked, *keys_values(g, chunk), bias[chunk])
+                numerator = product if numerator is None else numerator + product
+                folded = weight[:, :128] + weight[:, 128:]
+                denominator = folded if denominator is None else denominator + folded
+            weight, product = weigh(stacked, *keys_values(g, 4), bias_far[...])
+            denominator = jnp.sum(denominator, axis=1, keepdims=True)
+            denominator = denominator + jnp.sum(weight, axis=1, keepdims=True)
+            put(g, numerator + product, denominator)
+
+    @pl.when(jnp.logical_not(every))
+    def _():
+        tops[...] = jnp.zeros_like(tops)
+        unders[...] = jnp.zeros_like(unders)
+        for chunk in range(4):
+
+            @pl.when(needed[chunk])
+            def _(chunk=chunk):
+                bias[chunk] = hide(chunk * 8, 256, False)
+                for g in range(KV_HEADS):
+                    weight, product = weigh(
+                        stacked_heads(g), *keys_values(g, chunk), bias[chunk]
+                    )
+                    tops[g] += product
+                    unders[g] += weight[:, :128] + weight[:, 128:]
+
+        @pl.when(far_needed)
+        def _():
+            bias_far[...] = hide(index, ROWS, True)
+            for g in range(KV_HEADS):
+                weight, product = weigh(stacked_heads(g), *keys_values(g, 4), bias_far[...])
+                tops[g] += product
+                unders[g, :, :ROWS] += weight
+
+        for g in range(KV_HEADS):
+            put(g, tops[g], jnp.sum(unders[g], axis=1, keepdims=True))
 
 
 def pack_body(here, there, out):
@@ -340,7 +388,12 @@
             jax.ShapeDtypeStruct((4, ROWS, SUMS), F32),
             [SM, SM] + [VM] * 3,
             f"attend{flip}",
-            [pltpu.VMEM((4, 128, 256), F32), pltpu.VMEM((128, ROWS), F32)],
+            [
+                pltpu.VMEM((4, 128, 256), F32),
+                pltpu.VMEM((128, ROWS), F32),
+                pltpu.VMEM((KV_HEADS, GROUP * 128, HEAD), F32),
+                pltpu.VMEM((KV_HEADS, GROUP * 128, 128), F32),
+            ],
         )(place, lengths, given if flip else kept, blocks, far)
 
     sent = attend(1)

time: 167 us -> 163 us (0.976)
  Pallas kernels: 17.3 us -> 13.6 us
    pallas_call x2, Pallas kernels: 8.69 us -> 4.99 us  [attend(): call(functools.partial(attend_body, flip), jax.ShapeDtypeStruct((4, ROWS,...]
  transfers between devices with their start and end apart: 16 -> 16, of which waited for: 12 -> 12; matrix products, arithmetic and copies ran while one was open for 1% -> 1% of each run, Pallas kernels for 4% -> 3%
where the time goes in v11:
time: 163 us; the launch traced here: 162 us
  starting transfers between devices  76.1 us (47%)
  waiting for transfers between devices  51.1 us (31%)
  blocking collectives  16.2 us (10%)
  Pallas kernels  13.6 us (8%)
  other arithmetic  2.54 us (2%)
    ppermute x8, waiting for transfers between devices, shift(): lax.ppermute(value, axis, [(i, (i + step) % count) for i in range(count)])  31.3 us
    ppermute x8, starting transfers between devices, shift(): lax.ppermute(value, axis, [(i, (i + step) % count) for i in range(count)])  26.6 us
    all_to_all x1, starting transfers between devices, spread(): lax.all_to_all(jnp.broadcast_to(x[None], (count,) + x.shape), axes, 0, 0)  16.2 us
    all_gather x1, blocking collectives, on_device(): attended = lax.all_gather(attended, ('yl', 'c'), axis=0, tiled=True)  16.2 us
    all_to_all x1, waiting for transfers between devices, on_device(): parts = lax.all_to_all(packed, 'yl', 0, 0)  10.1 us
    ppermute x2, starting transfers between devices, on_device(): arrived = lax.ppermute(sent, 'c', swap)  8.3 us
    all_to_all x1, starting transfers between devices, on_device(): parts = lax.all_to_all(partial, ('x', 'yl'), 0, 0)  7.5 us
    ppermute x1, starting transfers between devices, on_device(): given = lax.ppermute(kept, 'c', swap)  6.77 us
  transfers between devices with their start and end apart: 16, of which 12 were waited for; matrix products, arithmetic and copies ran while one was open for 1% of the time, Pallas kernels for 3%

profile of v11, /device:TPU:1, one launch (start us, length us, event | category | flops | bytes accessed | tf_op | source)
XLA Modules:
  0.0 161.8 jit_solution(1870506985633441876)
XLA Ops:
  2.2 16.2 %all-to-all-start = ((bf16[16,56,256]{2,1,0:T(8,128)(2,1)}), bf16[16,56,256]{2,1,0:T(8,128)(2,1)S(1)}, u32[]{:S(2)}, u32[]{:S(2)}) async-start(bf16[16,56,256]{2,1,0:T(8,128)(2,1)} %broadcast_in_dim.50), calls=%async_computation | async-start | bytes 917504 | tf_op jit(solution)/shard_map/all_to_all | solution.py:309
  18.5 3.1 %collective-permute-start = (bf16[256,256]{1,0:T(8,128)(2,1)S(1)}, bf16[256,256]{1,0:T(8,128)(2,1)S(1)}, u32[]{:S(2)}, u32[]{:S(2)}) collective-permute-start(bf16[256,256]{1,0:T(8,128)(2,1)S(1)} %copy-done), channel_id=1, source_target_pairs={{0,8},{8,16},{16,24},{24,0},{1,9},{9,17},{17,25},{25,1},{2,10},{10... | collective-permute-start | bytes 393224 | tf_op jit(solution)/shard_map/ppermute | solution.py:322
  21.6 4.4 %collective-permute-start.1 = (bf16[256,256]{1,0:T(8,128)(2,1)S(1)}, bf16[256,256]{1,0:T(8,128)(2,1)S(1)}, u32[]{:S(2)}, u32[]{:S(2)}) collective-permute-start(bf16[256,256]{1,0:T(8,128)(2,1)S(1)} %copy-done), channel_id=1, source_target_pairs={{0,16},{8,24},{16,0},{24,8},{1,17},{9,25},{17,1},{25,9},{2,18},{10... | collective-permute-start | bytes 393224 | tf_op jit(solution)/shard_map/ppermute | solution.py:322
  26.0 3.1 %collective-permute-start.2 = (bf16[256,256]{1,0:T(8,128)(2,1)S(1)}, bf16[256,256]{1,0:T(8,128)(2,1)S(1)}, u32[]{:S(2)}, u32[]{:S(2)}) collective-permute-start(bf16[256,256]{1,0:T(8,128)(2,1)S(1)} %copy-done), channel_id=1, source_target_pairs={{0,24},{8,0},{16,8},{24,16},{1,25},{9,1},{17,9},{25,17},{2,26},{10... | collective-permute-start | bytes 393224 | tf_op jit(solution)/shard_map/ppermute | solution.py:322
  29.5 2.5 %collective-permute-done.2 = bf16[256,256]{1,0:T(8,128)(2,1)S(1)} collective-permute-done((bf16[256,256]{1,0:T(8,128)(2,1)S(1)}, bf16[256,256]{1,0:T(8,128)(2,1)S(1)}, u32[]{:S(2)}, u32[]{:S(2)}) %collective-permute-start.2) | collective-permute-done | bytes 131104 | tf_op jit(solution)/shard_map/ppermute | solution.py:322
  32.0 1.4 all-to-all-done.weight
  34.4 4.4 %collective-permute-start.3 = (f32[4,128,512]{2,1,0:T(8,128)S(1)}, f32[4,128,512]{2,1,0:T(8,128)S(1)}, u32[]{:S(2)}, u32[]{:S(2)}) collective-permute-start(f32[4,128,512]{2,1,0:T(8,128)S(1)} %project1.1), channel_id=1, source_target_pairs={{0,1},{1,0},{2,3},{3,2},{4,5},{5,4},{6,7},{7,6},{8,9},{9,8},{10,11... | collective-permute-start | bytes 3145736 | tf_op jit(solution)/shard_map/ppermute | solution.py:344
  42.3 7.5 %all-to-all-start.1 = ((bf16[16,32,768]{2,1,0:T(8,128)(2,1)}), bf16[16,32,768]{2,1,0:T(8,128)(2,1)S(1)}, u32[]{:S(2)}, u32[]{:S(2)}) async-start(bf16[16,32,768]{2,1,0:T(8,128)(2,1)} %bitcast.12), calls=%async_computation.1 | async-start | bytes 1572864 | tf_op jit(solution)/shard_map/all_to_all | solution.py:349
  50.3 3.3 %collective-permute-start.4 = (bf16[16,24,256]{2,1,0:T(8,128)(2,1)S(1)}, bf16[16,24,256]{2,1,0:T(8,128)(2,1)S(1)}, u32[]{:S(2)}, u32[]{:S(2)}) collective-permute-start(bf16[16,24,256]{2,1,0:T(8,128)(2,1)S(1)} %slice.4.own), channel_id=1, source_target_pairs={{0,8},{8,16},{16,24},{24,0},{1,9},{9,17},{17,25},{25,1},{2,10},{10... | collective-permute-start | bytes 589832 | tf_op jit(solution)/shard_map/ppermute | solution.py:322
  53.6 4.3 %collective-permute-start.5 = (bf16[16,24,256]{2,1,0:T(8,128)(2,1)S(1)}, bf16[16,24,256]{2,1,0:T(8,128)(2,1)S(1)}, u32[]{:S(2)}, u32[]{:S(2)}) collective-permute-start(bf16[16,24,256]{2,1,0:T(8,128)(2,1)S(1)} %slice.4.own), channel_id=1, source_target_pairs={{0,16},{8,24},{16,0},{24,8},{1,17},{9,25},{17,1},{25,9},{2,18},{10... | collective-permute-start | bytes 589832 | tf_op jit(solution)/shard_map/ppermute | solution.py:322
  58.0 7.4 %collective-permute-done.4.one = bf16[16,24,256]{2,1,0:T(8,128)(2,1)S(1)} collective-permute-done((bf16[16,24,256]{2,1,0:T(8,128)(2,1)S(1)}, bf16[16,24,256]{2,1,0:T(8,128)(2,1)S(1)}, u32[]{:S(2)}, u32[]{:S(2)}) %collective-permute-start.4) | collective-permute-done | bytes 196640 | tf_op jit(solution)/shard_map/ppermute | solution.py:322
  65.5 3.9 %collective-permute-done.5.two = bf16[16,24,256]{2,1,0:T(8,128)(2,1)S(1)} collective-permute-done((bf16[16,24,256]{2,1,0:T(8,128)(2,1)S(1)}, bf16[16,24,256]{2,1,0:T(8,128)(2,1)S(1)}, u32[]{:S(2)}, u32[]{:S(2)}) %collective-permute-start.5) | collective-permute-done | bytes 196640 | tf_op jit(solution)/shard_map/ppermute | solution.py:322
  69.3 1.9 %all-to-all-done.1.parts = bf16[16,32,768]{2,1,0:T(8,128)(2,1)S(1)} async-done(((bf16[16,32,768]{2,1,0:T(8,128)(2,1)}), bf16[16,32,768]{2,1,0:T(8,128)(2,1)S(1)}, u32[]{:S(2)}, u32[]{:S(2)}) %all-to-all-start.1) | async-done | bytes 786464 | tf_op jit(solution)/shard_map/all_to_all | solution.py:349
  71.2 1.5 rotate_keys.1
  72.8 2.6 %collective-permute-start.6 = (bf16[32,640]{1,0:T(8,128)(2,1)S(1)}, bf16[32,640]{1,0:T(8,128)(2,1)S(1)}, u32[]{:S(2)}, u32[]{:S(2)}) collective-permute-start(bf16[32,640]{1,0:T(8,128)(2,1)S(1)} %get-tuple-element.22), channel_id=1, source_target_pairs={{0,256},{256,0},{1,257},{257,1},{2,258},{258,2},{3,259},{259,3},{4... | collective-permute-start | bytes 122888 | tf_op jit(solution)/shard_map/ppermute | solution.py:372
  75.5 1.2 rotate_queries.1
  76.7 5.1 %collective-permute-done.6.far = bf16[32,640]{1,0:T(8,128)(2,1)S(1)} collective-permute-done((bf16[32,640]{1,0:T(8,128)(2,1)S(1)}, bf16[32,640]{1,0:T(8,128)(2,1)S(1)}, u32[]{:S(2)}, u32[]{:S(2)}) %collective-permute-start.6) | collective-permute-done | bytes 40992 | tf_op jit(solution)/shard_map/ppermute | solution.py:372
  81.9 1.3 broadcast_select_fusion
  83.1 4.6 %all-to-all-start.2 = ((bf16[32,32,640]{2,1,0:T(8,128)(2,1)}), bf16[32,32,640]{2,1,0:T(8,128)(2,1)S(1)}, u32[]{:S(2)}, u32[]{:S(2)}) async-start(bf16[32,32,640]{2,1,0:T(8,128)(2,1)} %broadcast_select_fusion), calls=%async_computation.2 | async-start | bytes 2621440 | tf_op jit(solution)/shard_map/all_to_all | solution.py:381
  87.7 1.9 %collective-permute-start.8 = (bf16[1,32,1280]{2,1,0:T(8,128)(2,1)S(1)}, bf16[1,32,1280]{2,1,0:T(8,128)(2,1)S(1)}, u32[]{:S(2)}, u32[]{:S(2)}) collective-permute-start(bf16[1,32,1280]{2,1,0:T(8,128)(2,1)S(1)} %bitcast.21), channel_id=1, source_target_pairs={{0,2},{2,4},{4,6},{6,0},{1,3},{3,5},{5,7},{7,1},{8,10},{10,12},{12... | collective-permute-start | bytes 245768 | tf_op jit(solution)/shard_map/ppermute | solution.py:322
  89.7 5.1 %collective-permute-done.8 = bf16[1,32,1280]{2,1,0:T(8,128)(2,1)S(1)} collective-permute-done((bf16[1,32,1280]{2,1,0:T(8,128)(2,1)S(1)}, bf16[1,32,1280]{2,1,0:T(8,128)(2,1)S(1)}, u32[]{:S(2)}, u32[]{:S(2)}) %collective-permute-start.8) | collective-permute-done | bytes 81952 | tf_op jit(solution)/shard_map/ppermute | solution.py:322
  94.7 1.9 %collective-permute-start.9 = (bf16[2,32,1280]{2,1,0:T(8,128)(2,1)S(1)}, bf16[2,32,1280]{2,1,0:T(8,128)(2,1)S(1)}, u32[]{:S(2)}, u32[]{:S(2)}) collective-permute-start(bf16[2,32,1280]{2,1,0:T(8,128)(2,1)S(1)} %pad_maximum_fusion.1), channel_id=1, source_target_pairs={{0,4},{2,6},{4,0},{6,2},{1,5},{3,7},{5,1},{7,3},{8,12},{10,14},{12... | collective-permute-start | bytes 491528 | tf_op jit(solution)/shard_map/ppermute | solution.py:322
  96.7 5.3 %collective-permute-done.9 = bf16[2,32,1280]{2,1,0:T(8,128)(2,1)S(1)} collective-permute-done((bf16[2,32,1280]{2,1,0:T(8,128)(2,1)S(1)}, bf16[2,32,1280]{2,1,0:T(8,128)(2,1)S(1)}, u32[]{:S(2)}, u32[]{:S(2)}) %collective-permute-start.9) | collective-permute-done | bytes 163872 | tf_op jit(solution)/shard_map/ppermute | solution.py:322
  102.0 6.8 %collective-permute-start.10 = (bf16[4,32,1280]{2,1,0:T(8,128)(2,1)S(1)}, bf16[4,32,1280]{2,1,0:T(8,128)(2,1)S(1)}, u32[]{:S(2)}, u32[]{:S(2)}) collective-permute-start(bf16[4,32,1280]{2,1,0:T(8,128)(2,1)S(1)} %pad_maximum_fusion.q), channel_id=1, source_target_pairs={{0,1},{1,0},{2,3},{3,2},{4,5},{5,4},{6,7},{7,6},{8,9},{9,8},{10,11... | collective-permute-start | bytes 983048 | tf_op jit(solution)/shard_map/ppermute | solution.py:379
  108.8 4.6 %collective-permute-start.7 = (bf16[16,24,256]{2,1,0:T(8,128)(2,1)S(1)}, bf16[16,24,256]{2,1,0:T(8,128)(2,1)S(1)}, u32[]{:S(2)}, u32[]{:S(2)}) collective-permute-start(bf16[16,24,256]{2,1,0:T(8,128)(2,1)S(1)} %slice.4.own), channel_id=1, source_target_pairs={{0,24},{8,0},{16,8},{24,16},{1,25},{9,1},{17,9},{25,17},{2,26},{10... | collective-permute-start | bytes 589832 | tf_op jit(solution)/shard_map/ppermute | solution.py:322
  113.4 6.8 %collective-permute-done.7.three = bf16[16,24,256]{2,1,0:T(8,128)(2,1)S(1)} collective-permute-done((bf16[16,24,256]{2,1,0:T(8,128)(2,1)S(1)}, bf16[16,24,256]{2,1,0:T(8,128)(2,1)S(1)}, u32[]{:S(2)}, u32[]{:S(2)}) %collective-permute-start.7) | collective-permute-done | bytes 196640 | tf_op jit(solution)/shard_map/ppermute | solution.py:322
  120.3 2.6 %attend1.1 = f32[4,32,1408]{2,1,0:T(8,128)S(1)} custom-call(s32[7]{0:T(128)S(1)} %stack.31.place, s32[4]{0:T(128)S(1)} %copy-done.1, bf16[4,32,1280]{2,1,0:T(8,128)(2,1)S(1)} %collective-permute-done.10.q, bf16[32,32,640]{2,1,0:T(8,128)(2,1)S(1)} %all-to-all-done.2.blocks, bf16[32,640]{1,0:T(8,128)(2,1)S(1)} %collective-permute-done.6.far), custom_call_target="tpu_custom_call" | custom-call | tf_op jit(solution)/shard_map/attend1/pallas_call | solution.py:386
  122.9 3.9 %collective-permute-start.11 = (f32[4,32,1408]{2,1,0:T(8,128)S(1)}, f32[4,32,1408]{2,1,0:T(8,128)S(1)}, u32[]{:S(2)}, u32[]{:S(2)}) collective-permute-start(f32[4,32,1408]{2,1,0:T(8,128)S(1)} %attend1.1), channel_id=1, source_target_pairs={{0,1},{1,0},{2,3},{3,2},{4,5},{5,4},{6,7},{7,6},{8,9},{9,8},{10,11... | collective-permute-start | bytes 2162696 | tf_op jit(solution)/shard_map/ppermute | solution.py:400
  126.8 2.4 %attend0.1.here = f32[4,32,1408]{2,1,0:T(8,128)S(1)} custom-call(s32[7]{0:T(128)S(1)} %stack.31.place, s32[4]{0:T(128)S(1)} %copy-done.1, bf16[4,32,1280]{2,1,0:T(8,128)(2,1)S(1)} %pad_maximum_fusion.q, bf16[32,32,640]{2,1,0:T(8,128)(2,1)S(1)} %all-to-all-done.2.blocks, bf16[32,640]{1,0:T(8,128)(2,1)S(1)} %collective-permute-done.6.far), custom_call_target="tpu_custom_call" | custom-call | tf_op jit(solution)/shard_map/attend0/pallas_call | solution.py:386
  130.0 3.6 %all-to-all-start.3 = ((bf16[4,32,1408]{2,1,0:T(8,128)(2,1)}), bf16[4,32,1408]{2,1,0:T(8,128)(2,1)S(1)}, u32[]{:S(2)}, u32[]{:S(2)}) async-start(bf16[4,32,1408]{2,1,0:T(8,128)(2,1)} %pack.1), calls=%async_computation.3 | async-start | bytes 720896 | tf_op jit(solution)/shard_map/all_to_all | solution.py:405
  134.3 10.1 %all-to-all-done.3.parts = bf16[4,32,1408]{2,1,0:T(8,128)(2,1)S(1)} async-done(((bf16[4,32,1408]{2,1,0:T(8,128)(2,1)}), bf16[4,32,1408]{2,1,0:T(8,128)(2,1)S(1)}, u32[]{:S(2)}, u32[]{:S(2)}) %all-to-all-start.3) | async-done | bytes 360480 | tf_op jit(solution)/shard_map/all_to_all | solution.py:405
  144.6 16.2 %all_gather.3.attended = bf16[256,1280]{1,0:T(8,128)(2,1)S(1)} all-gather(bf16[32,1280]{1,0:T(8,128)(2,1)S(1)} %divide.1), channel_id=1, replica_groups=mesh['yh'=2,'z'=8,'x'=4,'yl'=4,'c'=2] {'yl','c'}, dimensions={0}, use_global_device_ids=true | all-gather | bytes 737280 | tf_op jit(solution)/shard_map/all_gather | solution.py:410
  (46 shorter events, 10.0 us)
Async XLA Ops:
  0.6 17.8 %copy-start = (bf16[256,256]{1,0:T(8,128)(2,1)S(1)}, bf16[256,256]{1,0:T(8,128)(2,1)}, u32[]{:S(2)}) copy-start(bf16[256,256]{1,0:T(8,128)(2,1)} %param.8) | copy-start | bytes 393220
  0.6 28.4 %copy-start.3 = (bf16[256]{0:T(256)(128)(2,1)S(1)}, bf16[256]{0:T(256)(128)(2,1)}, u32[]{:S(2)}) copy-start(bf16[256]{0:T(256)(128)(2,1)} %param.9) | copy-start | bytes 1540
  2.2 31.2 %all-to-all-start = ((bf16[16,56,256]{2,1,0:T(8,128)(2,1)}), bf16[16,56,256]{2,1,0:T(8,128)(2,1)S(1)}, u32[]{:S(2)}, u32[]{:S(2)}) async-start(bf16[16,56,256]{2,1,0:T(8,128)(2,1)} %broadcast_in_dim.50), calls=%async_computation | async-start | bytes 917504 | tf_op jit(solution)/shard_map/all_to_all | solution.py:309
  18.5 10.7 %collective-permute-start = (bf16[256,256]{1,0:T(8,128)(2,1)S(1)}, bf16[256,256]{1,0:T(8,128)(2,1)S(1)}, u32[]{:S(2)}, u32[]{:S(2)}) collective-permute-start(bf16[256,256]{1,0:T(8,128)(2,1)S(1)} %copy-done), channel_id=1, source_target_pairs={{0,8},{8,16},{16,24},{24,0},{1,9},{9,17},{17,25},{25,1},{2,10},{10... | collective-permute-start | bytes 393224 | tf_op jit(solution)/shard_map/ppermute | solution.py:322
  21.6 7.9 %collective-permute-start.1 = (bf16[256,256]{1,0:T(8,128)(2,1)S(1)}, bf16[256,256]{1,0:T(8,128)(2,1)S(1)}, u32[]{:S(2)}, u32[]{:S(2)}) collective-permute-start(bf16[256,256]{1,0:T(8,128)(2,1)S(1)} %copy-done), channel_id=1, source_target_pairs={{0,16},{8,24},{16,0},{24,8},{1,17},{9,25},{17,1},{25,9},{2,18},{10... | collective-permute-start | bytes 393224 | tf_op jit(solution)/shard_map/ppermute | solution.py:322
  26.0 6.0 %collective-permute-start.2 = (bf16[256,256]{1,0:T(8,128)(2,1)S(1)}, bf16[256,256]{1,0:T(8,128)(2,1)S(1)}, u32[]{:S(2)}, u32[]{:S(2)}) collective-permute-start(bf16[256,256]{1,0:T(8,128)(2,1)S(1)} %copy-done), channel_id=1, source_target_pairs={{0,24},{8,0},{16,8},{24,16},{1,25},{9,1},{17,9},{25,17},{2,26},{10... | collective-permute-start | bytes 393224 | tf_op jit(solution)/shard_map/ppermute | solution.py:322
  34.4 6.7 %collective-permute-start.3 = (f32[4,128,512]{2,1,0:T(8,128)S(1)}, f32[4,128,512]{2,1,0:T(8,128)S(1)}, u32[]{:S(2)}, u32[]{:S(2)}) collective-permute-start(f32[4,128,512]{2,1,0:T(8,128)S(1)} %project1.1), channel_id=1, source_target_pairs={{0,1},{1,0},{2,3},{3,2},{4,5},{5,4},{6,7},{7,6},{8,9},{9,8},{10,11... | collective-permute-start | bytes 3145736 | tf_op jit(solution)/shard_map/ppermute | solution.py:344
  42.3 7.6 %copy-start.4 = (bf16[64]{0:T(256)(128)(2,1)S(1)}, bf16[64]{0:T(256)(128)(2,1)}, u32[]{:S(2)}) copy-start(bf16[64]{0:T(256)(128)(2,1)} %param.12) | copy-start | bytes 388
  42.3 7.7 %copy-start.1 = (s32[4]{0:T(128)S(1)}, s32[4]{0:T(128)}, u32[]{:S(2)}) copy-start(s32[4]{0:T(128)} %lengths.3) | copy-start | bytes 52
  42.3 28.9 %copy-start.2 = (s32[4]{0:T(128)S(1)}, s32[4]{0:T(128)}, u32[]{:S(2)}) copy-start(s32[4]{0:T(128)} %table.1) | copy-start | bytes 52
  42.3 33.1 %copy-start.5 = (bf16[64]{0:T(256)(128)(2,1)S(1)}, bf16[64]{0:T(256)(128)(2,1)}, u32[]{:S(2)}) copy-start(bf16[64]{0:T(256)(128)(2,1)} %param.11) | copy-start | bytes 388
  42.3 28.9 %all-to-all-start.1 = ((bf16[16,32,768]{2,1,0:T(8,128)(2,1)}), bf16[16,32,768]{2,1,0:T(8,128)(2,1)S(1)}, u32[]{:S(2)}, u32[]{:S(2)}) async-start(bf16[16,32,768]{2,1,0:T(8,128)(2,1)} %bitcast.12), calls=%async_computation.1 | async-start | bytes 1572864 | tf_op jit(solution)/shard_map/all_to_all | solution.py:349
  50.3 15.2 %collective-permute-start.4 = (bf16[16,24,256]{2,1,0:T(8,128)(2,1)S(1)}, bf16[16,24,256]{2,1,0:T(8,128)(2,1)S(1)}, u32[]{:S(2)}, u32[]{:S(2)}) collective-permute-start(bf16[16,24,256]{2,1,0:T(8,128)(2,1)S(1)} %slice.4.own), channel_id=1, source_target_pairs={{0,8},{8,16},{16,24},{24,0},{1,9},{9,17},{17,25},{25,1},{2,10},{10... | collective-permute-start | bytes 589832 | tf_op jit(solution)/shard_map/ppermute | solution.py:322
  53.6 15.7 %collective-permute-start.5 = (bf16[16,24,256]{2,1,0:T(8,128)(2,1)S(1)}, bf16[16,24,256]{2,1,0:T(8,128)(2,1)S(1)}, u32[]{:S(2)}, u32[]{:S(2)}) collective-permute-start(bf16[16,24,256]{2,1,0:T(8,128)(2,1)S(1)} %slice.4.own), channel_id=1, source_target_pairs={{0,16},{8,24},{16,0},{24,8},{1,17},{9,25},{17,1},{25,9},{2,18},{10... | collective-permute-start | bytes 589832 | tf_op jit(solution)/shard_map/ppermute | solution.py:322
  72.8 9.1 %collective-permute-start.6 = (bf16[32,640]{1,0:T(8,128)(2,1)S(1)}, bf16[32,640]{1,0:T(8,128)(2,1)S(1)}, u32[]{:S(2)}, u32[]{:S(2)}) collective-permute-start(bf16[32,640]{1,0:T(8,128)(2,1)S(1)} %get-tuple-element.22), channel_id=1, source_target_pairs={{0,256},{256,0},{1,257},{257,1},{2,258},{258,2},{3,259},{259,3},{4... | collective-permute-start | bytes 122888 | tf_op jit(solution)/shard_map/ppermute | solution.py:372
  83.1 37.1 %all-to-all-start.2 = ((bf16[32,32,640]{2,1,0:T(8,128)(2,1)}), bf16[32,32,640]{2,1,0:T(8,128)(2,1)S(1)}, u32[]{:S(2)}, u32[]{:S(2)}) async-start(bf16[32,32,640]{2,1,0:T(8,128)(2,1)} %broadcast_select_fusion), calls=%async_computation.2 | async-start | bytes 2621440 | tf_op jit(solution)/shard_map/all_to_all | solution.py:381
  87.7 7.0 %collective-permute-start.8 = (bf16[1,32,1280]{2,1,0:T(8,128)(2,1)S(1)}, bf16[1,32,1280]{2,1,0:T(8,128)(2,1)S(1)}, u32[]{:S(2)}, u32[]{:S(2)}) collective-permute-start(bf16[1,32,1280]{2,1,0:T(8,128)(2,1)S(1)} %bitcast.21), channel_id=1, source_target_pairs={{0,2},{2,4},{4,6},{6,0},{1,3},{3,5},{5,7},{7,1},{8,10},{10,12},{12... | collective-permute-start | bytes 245768 | tf_op jit(solution)/shard_map/ppermute | solution.py:322
  94.7 7.3 %collective-permute-start.9 = (bf16[2,32,1280]{2,1,0:T(8,128)(2,1)S(1)}, bf16[2,32,1280]{2,1,0:T(8,128)(2,1)S(1)}, u32[]{:S(2)}, u32[]{:S(2)}) collective-permute-start(bf16[2,32,1280]{2,1,0:T(8,128)(2,1)S(1)} %pad_maximum_fusion.1), channel_id=1, source_target_pairs={{0,4},{2,6},{4,0},{6,2},{1,5},{3,7},{5,1},{7,3},{8,12},{10,14},{12... | collective-permute-start | bytes 491528 | tf_op jit(solution)/shard_map/ppermute | solution.py:322
  102.0 18.3 %collective-permute-start.10 = (bf16[4,32,1280]{2,1,0:T(8,128)(2,1)S(1)}, bf16[4,32,1280]{2,1,0:T(8,128)(2,1)S(1)}, u32[]{:S(2)}, u32[]{:S(2)}) collective-permute-start(bf16[4,32,1280]{2,1,0:T(8,128)(2,1)S(1)} %pad_maximum_fusion.q), channel_id=1, source_target_pairs={{0,1},{1,0},{2,3},{3,2},{4,5},{5,4},{6,7},{7,6},{8,9},{9,8},{10,11... | collective-permute-start | bytes 983048 | tf_op jit(solution)/shard_map/ppermute | solution.py:379
  108.8 11.5 %collective-permute-start.7 = (bf16[16,24,256]{2,1,0:T(8,128)(2,1)S(1)}, bf16[16,24,256]{2,1,0:T(8,128)(2,1)S(1)}, u32[]{:S(2)}, u32[]{:S(2)}) collective-permute-start(bf16[16,24,256]{2,1,0:T(8,128)(2,1)S(1)} %slice.4.own), channel_id=1, source_target_pairs={{0,24},{8,0},{16,8},{24,16},{1,25},{9,1},{17,9},{25,17},{2,26},{10... | collective-permute-start | bytes 589832 | tf_op jit(solution)/shard_map/ppermute | solution.py:322
  122.9 6.3 %collective-permute-start.11 = (f32[4,32,1408]{2,1,0:T(8,128)S(1)}, f32[4,32,1408]{2,1,0:T(8,128)S(1)}, u32[]{:S(2)}, u32[]{:S(2)}) collective-permute-start(f32[4,32,1408]{2,1,0:T(8,128)S(1)} %attend1.1), channel_id=1, source_target_pairs={{0,1},{1,0},{2,3},{3,2},{4,5},{5,4},{6,7},{7,6},{8,9},{9,8},{10,11... | collective-permute-start | bytes 2162696 | tf_op jit(solution)/shard_map/ppermute | solution.py:400
  130.0 14.4 %all-to-all-start.3 = ((bf16[4,32,1408]{2,1,0:T(8,128)(2,1)}), bf16[4,32,1408]{2,1,0:T(8,128)(2,1)S(1)}, u32[]{:S(2)}, u32[]{:S(2)}) async-start(bf16[4,32,1408]{2,1,0:T(8,128)(2,1)} %pack.1), calls=%async_computation.3 | async-start | bytes 720896 | tf_op jit(solution)/shard_map/all_to_all | solution.py:405

commit v12 on v11

--- a/solution.py
+++ b/solution.py
@@ -347,8 +347,8 @@
     ).reshape(16, ROWS, 768)
     mixing, partial = lax.optimization_barrier((weight[:, 32:], partial))
     parts = lax.all_to_all(partial, ("x", "yl"), 0, 0)
-    after, across = shift(mixing, "x", 4, 1), shift(mixing, "x", 4, 2)
-    mixing, after, across, parts = lax.optimization_barrier((mixing, after, across, parts))
+    after, before = shift(mixing, "x", 4, 1), shift(mixing, "x", 4, 3)
+    mixing, after, before, parts = lax.optimization_barrier((mixing, after, before, parts))
 
     row = jnp.arange(ROWS, dtype=jnp.int32)
     own = wide * TOK_DEV + row // 8 * PAGE + narrow * 8 + row % 8
@@ -375,12 +375,12 @@
     )(parts, *tables, gains[0])
     far, queries = lax.optimization_barrier((far, queries))
     kept = gather(queries[None], "yl", 4, 4)
-    before = shift(mixing, "x", 4, 3)
+    across = shift(mixing, "x", 4, 2)
     given = lax.ppermute(kept, "c", swap)
     target = jnp.arange(32, dtype=jnp.int32)[:, None, None]
     blocks = lax.all_to_all(jnp.where(target >= index, kv[None], far[None]), ("z", "x"), 0, 0)
 
-    blocks, before, kept, given = lax.optimization_barrier((blocks, before, kept, given))
+    blocks, across, kept, given = lax.optimization_barrier((blocks, across, kept, given))
 
     def attend(flip):
         return call(

time: 163 us -> 164 us (level)
  waiting for transfers between devices: 51.1 us -> 53.1 us
    all_to_all x1, waiting for transfers between devices: 1.91 us -> 5.94 us  [on_device(): parts = lax.all_to_all(partial, ('x', 'yl'), 0, 0)]
    ppermute x8, waiting for transfers between devices: 31.3 us -> 29.5 us  [shift(): lax.ppermute(value, axis, [(i, (i + step) % count) for i in range(count)])]
  transfers between devices with their start and end apart: 16 -> 16, of which waited for: 12 -> 11; matrix products, arithmetic and copies ran while one was open for 1% -> 1% of each run, Pallas kernels for 3% -> 3%
where the time goes in v12:
time: 164 us; the launch traced here: 162 us
  starting transfers between devices  74.6 us (45%)
  waiting for transfers between devices  53.1 us (32%)
  blocking collectives  16 us (10%)
  Pallas kernels  13.6 us (8%)
  other arithmetic  2.54 us (2%)
    ppermute x8, waiting for transfers between devices, shift(): lax.ppermute(value, axis, [(i, (i + step) % count) for i in range(count)])  29.5 us
    ppermute x8, starting transfers between devices, shift(): lax.ppermute(value, axis, [(i, (i + step) % count) for i in range(count)])  25.8 us
    all_to_all x1, starting transfers between devices, spread(): lax.all_to_all(jnp.broadcast_to(x[None], (count,) + x.shape), axes, 0, 0)  16.2 us
    all_gather x1, blocking collectives, on_device(): attended = lax.all_gather(attended, ('yl', 'c'), axis=0, tiled=True)  16 us
    all_to_all x1, waiting for transfers between devices, on_device(): parts = lax.all_to_all(packed, 'yl', 0, 0)  10.3 us
    all_to_all x1, starting transfers between devices, on_device(): parts = lax.all_to_all(partial, ('x', 'yl'), 0, 0)  7.5 us
    ppermute x2, starting transfers between devices, on_device(): arrived = lax.ppermute(sent, 'c', swap)  7.24 us
    ppermute x1, starting transfers between devices, on_device(): given = lax.ppermute(kept, 'c', swap)  6.83 us
  transfers between devices with their start and end apart: 16, of which 11 were waited for; matrix products, arithmetic and copies ran while one was open for 1% of the time, Pallas kernels for 3%

profile of v12, /device:TPU:1, one launch (start us, length us, event | category | flops | bytes accessed | tf_op | source)
XLA Modules:
  0.0 162.2 jit_solution(1511228454151449805)
XLA Ops:
  2.2 16.2 %all-to-all-start = ((bf16[16,56,256]{2,1,0:T(8,128)(2,1)}), bf16[16,56,256]{2,1,0:T(8,128)(2,1)S(1)}, u32[]{:S(2)}, u32[]{:S(2)}) async-start(bf16[16,56,256]{2,1,0:T(8,128)(2,1)} %broadcast_in_dim.50), calls=%async_computation | async-start | bytes 917504 | tf_op jit(solution)/shard_map/all_to_all | solution.py:309
  18.5 3.1 %collective-permute-start = (bf16[256,256]{1,0:T(8,128)(2,1)S(1)}, bf16[256,256]{1,0:T(8,128)(2,1)S(1)}, u32[]{:S(2)}, u32[]{:S(2)}) collective-permute-start(bf16[256,256]{1,0:T(8,128)(2,1)S(1)} %copy-done), channel_id=1, source_target_pairs={{0,8},{8,16},{16,24},{24,0},{1,9},{9,17},{17,25},{25,1},{2,10},{10... | collective-permute-start | bytes 393224 | tf_op jit(solution)/shard_map/ppermute | solution.py:322
  21.6 4.4 %collective-permute-start.1 = (bf16[256,256]{1,0:T(8,128)(2,1)S(1)}, bf16[256,256]{1,0:T(8,128)(2,1)S(1)}, u32[]{:S(2)}, u32[]{:S(2)}) collective-permute-start(bf16[256,256]{1,0:T(8,128)(2,1)S(1)} %copy-done), channel_id=1, source_target_pairs={{0,16},{8,24},{16,0},{24,8},{1,17},{9,25},{17,1},{25,9},{2,18},{10... | collective-permute-start | bytes 393224 | tf_op jit(solution)/shard_map/ppermute | solution.py:322
  26.0 3.1 %collective-permute-start.2 = (bf16[256,256]{1,0:T(8,128)(2,1)S(1)}, bf16[256,256]{1,0:T(8,128)(2,1)S(1)}, u32[]{:S(2)}, u32[]{:S(2)}) collective-permute-start(bf16[256,256]{1,0:T(8,128)(2,1)S(1)} %copy-done), channel_id=1, source_target_pairs={{0,24},{8,0},{16,8},{24,16},{1,25},{9,1},{17,9},{25,17},{2,26},{10... | collective-permute-start | bytes 393224 | tf_op jit(solution)/shard_map/ppermute | solution.py:322
  29.5 2.5 %collective-permute-done.2 = bf16[256,256]{1,0:T(8,128)(2,1)S(1)} collective-permute-done((bf16[256,256]{1,0:T(8,128)(2,1)S(1)}, bf16[256,256]{1,0:T(8,128)(2,1)S(1)}, u32[]{:S(2)}, u32[]{:S(2)}) %collective-permute-start.2) | collective-permute-done | bytes 131104 | tf_op jit(solution)/shard_map/ppermute | solution.py:322
  32.0 1.4 all-to-all-done.weight
  34.4 4.4 %collective-permute-start.3 = (f32[4,128,512]{2,1,0:T(8,128)S(1)}, f32[4,128,512]{2,1,0:T(8,128)S(1)}, u32[]{:S(2)}, u32[]{:S(2)}) collective-permute-start(f32[4,128,512]{2,1,0:T(8,128)S(1)} %project1.1), channel_id=1, source_target_pairs={{0,1},{1,0},{2,3},{3,2},{4,5},{5,4},{6,7},{7,6},{8,9},{9,8},{10,11... | collective-permute-start | bytes 3145736 | tf_op jit(solution)/shard_map/ppermute | solution.py:344
  39.9 1.2 collective-permute-done.3.there
  42.3 7.5 %all-to-all-start.1 = ((bf16[16,32,768]{2,1,0:T(8,128)(2,1)}), bf16[16,32,768]{2,1,0:T(8,128)(2,1)S(1)}, u32[]{:S(2)}, u32[]{:S(2)}) async-start(bf16[16,32,768]{2,1,0:T(8,128)(2,1)} %bitcast.12), calls=%async_computation.1 | async-start | bytes 1572864 | tf_op jit(solution)/shard_map/all_to_all | solution.py:349
  50.3 3.3 %collective-permute-start.4 = (bf16[16,24,256]{2,1,0:T(8,128)(2,1)S(1)}, bf16[16,24,256]{2,1,0:T(8,128)(2,1)S(1)}, u32[]{:S(2)}, u32[]{:S(2)}) collective-permute-start(bf16[16,24,256]{2,1,0:T(8,128)(2,1)S(1)} %slice.4.own), channel_id=1, source_target_pairs={{0,8},{8,16},{16,24},{24,0},{1,9},{9,17},{17,25},{25,1},{2,10},{10... | collective-permute-start | bytes 589832 | tf_op jit(solution)/shard_map/ppermute | solution.py:322
  53.6 3.2 %collective-permute-start.5 = (bf16[16,24,256]{2,1,0:T(8,128)(2,1)S(1)}, bf16[16,24,256]{2,1,0:T(8,128)(2,1)S(1)}, u32[]{:S(2)}, u32[]{:S(2)}) collective-permute-start(bf16[16,24,256]{2,1,0:T(8,128)(2,1)S(1)} %slice.4.own), channel_id=1, source_target_pairs={{0,24},{8,0},{16,8},{24,16},{1,25},{9,1},{17,9},{25,17},{2,26},{10... | collective-permute-start | bytes 589832 | tf_op jit(solution)/shard_map/ppermute | solution.py:322
  57.0 8.3 %collective-permute-done.4.one = bf16[16,24,256]{2,1,0:T(8,128)(2,1)S(1)} collective-permute-done((bf16[16,24,256]{2,1,0:T(8,128)(2,1)S(1)}, bf16[16,24,256]{2,1,0:T(8,128)(2,1)S(1)}, u32[]{:S(2)}, u32[]{:S(2)}) %collective-permute-start.4) | collective-permute-done | bytes 196640 | tf_op jit(solution)/shard_map/ppermute | solution.py:322
  65.3 5.9 %all-to-all-done.1.parts = bf16[16,32,768]{2,1,0:T(8,128)(2,1)S(1)} async-done(((bf16[16,32,768]{2,1,0:T(8,128)(2,1)}), bf16[16,32,768]{2,1,0:T(8,128)(2,1)S(1)}, u32[]{:S(2)}, u32[]{:S(2)}) %all-to-all-start.1) | async-done | bytes 786464 | tf_op jit(solution)/shard_map/all_to_all | solution.py:349
  71.2 1.5 rotate_keys.1
  72.8 2.6 %collective-permute-start.6 = (bf16[32,640]{1,0:T(8,128)(2,1)S(1)}, bf16[32,640]{1,0:T(8,128)(2,1)S(1)}, u32[]{:S(2)}, u32[]{:S(2)}) collective-permute-start(bf16[32,640]{1,0:T(8,128)(2,1)S(1)} %get-tuple-element.22), channel_id=1, source_target_pairs={{0,256},{256,0},{1,257},{257,1},{2,258},{258,2},{3,259},{259,3},{4... | collective-permute-start | bytes 122888 | tf_op jit(solution)/shard_map/ppermute | solution.py:372
  75.5 1.2 rotate_queries.1
  76.7 4.7 %collective-permute-done.6.far = bf16[32,640]{1,0:T(8,128)(2,1)S(1)} collective-permute-done((bf16[32,640]{1,0:T(8,128)(2,1)S(1)}, bf16[32,640]{1,0:T(8,128)(2,1)S(1)}, u32[]{:S(2)}, u32[]{:S(2)}) %collective-permute-start.6) | collective-permute-done | bytes 40992 | tf_op jit(solution)/shard_map/ppermute | solution.py:372
  81.4 1.3 broadcast_select_fusion
  82.7 5.0 %all-to-all-start.2 = ((bf16[32,32,640]{2,1,0:T(8,128)(2,1)}), bf16[32,32,640]{2,1,0:T(8,128)(2,1)S(1)}, u32[]{:S(2)}, u32[]{:S(2)}) async-start(bf16[32,32,640]{2,1,0:T(8,128)(2,1)} %broadcast_select_fusion), calls=%async_computation.2 | async-start | bytes 2621440 | tf_op jit(solution)/shard_map/all_to_all | solution.py:381
  87.7 1.9 %collective-permute-start.8 = (bf16[1,32,1280]{2,1,0:T(8,128)(2,1)S(1)}, bf16[1,32,1280]{2,1,0:T(8,128)(2,1)S(1)}, u32[]{:S(2)}, u32[]{:S(2)}) collective-permute-start(bf16[1,32,1280]{2,1,0:T(8,128)(2,1)S(1)} %bitcast.21), channel_id=1, source_target_pairs={{0,2},{2,4},{4,6},{6,0},{1,3},{3,5},{5,7},{7,1},{8,10},{10,12},{12... | collective-permute-start | bytes 245768 | tf_op jit(solution)/shard_map/ppermute | solution.py:322
  89.6 5.1 %collective-permute-done.8 = bf16[1,32,1280]{2,1,0:T(8,128)(2,1)S(1)} collective-permute-done((bf16[1,32,1280]{2,1,0:T(8,128)(2,1)S(1)}, bf16[1,32,1280]{2,1,0:T(8,128)(2,1)S(1)}, u32[]{:S(2)}, u32[]{:S(2)}) %collective-permute-start.8) | collective-permute-done | bytes 81952 | tf_op jit(solution)/shard_map/ppermute | solution.py:322
  94.7 1.9 %collective-permute-start.9 = (bf16[2,32,1280]{2,1,0:T(8,128)(2,1)S(1)}, bf16[2,32,1280]{2,1,0:T(8,128)(2,1)S(1)}, u32[]{:S(2)}, u32[]{:S(2)}) collective-permute-start(bf16[2,32,1280]{2,1,0:T(8,128)(2,1)S(1)} %pad_maximum_fusion.1), channel_id=1, source_target_pairs={{0,4},{2,6},{4,0},{6,2},{1,5},{3,7},{5,1},{7,3},{8,12},{10,14},{12... | collective-permute-start | bytes 491528 | tf_op jit(solution)/shard_map/ppermute | solution.py:322
  96.6 5.3 %collective-permute-done.9 = bf16[2,32,1280]{2,1,0:T(8,128)(2,1)S(1)} collective-permute-done((bf16[2,32,1280]{2,1,0:T(8,128)(2,1)S(1)}, bf16[2,32,1280]{2,1,0:T(8,128)(2,1)S(1)}, u32[]{:S(2)}, u32[]{:S(2)}) %collective-permute-start.9) | collective-permute-done | bytes 163872 | tf_op jit(solution)/shard_map/ppermute | solution.py:322
  102.0 6.8 %collective-permute-start.10 = (bf16[4,32,1280]{2,1,0:T(8,128)(2,1)S(1)}, bf16[4,32,1280]{2,1,0:T(8,128)(2,1)S(1)}, u32[]{:S(2)}, u32[]{:S(2)}) collective-permute-start(bf16[4,32,1280]{2,1,0:T(8,128)(2,1)S(1)} %pad_maximum_fusion.q), channel_id=1, source_target_pairs={{0,1},{1,0},{2,3},{3,2},{4,5},{5,4},{6,7},{7,6},{8,9},{9,8},{10,11... | collective-permute-start | bytes 983048 | tf_op jit(solution)/shard_map/ppermute | solution.py:379
  108.8 4.9 %collective-permute-start.7 = (bf16[16,24,256]{2,1,0:T(8,128)(2,1)S(1)}, bf16[16,24,256]{2,1,0:T(8,128)(2,1)S(1)}, u32[]{:S(2)}, u32[]{:S(2)}) collective-permute-start(bf16[16,24,256]{2,1,0:T(8,128)(2,1)S(1)} %slice.4.own), channel_id=1, source_target_pairs={{0,16},{8,24},{16,0},{24,8},{1,17},{9,25},{17,1},{25,9},{2,18},{10... | collective-permute-start | bytes 589832 | tf_op jit(solution)/shard_map/ppermute | solution.py:322
  113.7 8.0 %collective-permute-done.7.two = bf16[16,24,256]{2,1,0:T(8,128)(2,1)S(1)} collective-permute-done((bf16[16,24,256]{2,1,0:T(8,128)(2,1)S(1)}, bf16[16,24,256]{2,1,0:T(8,128)(2,1)S(1)}, u32[]{:S(2)}, u32[]{:S(2)}) %collective-permute-start.7) | collective-permute-done | bytes 196640 | tf_op jit(solution)/shard_map/ppermute | solution.py:322
  121.7 2.6 %attend1.1 = f32[4,32,1408]{2,1,0:T(8,128)S(1)} custom-call(s32[7]{0:T(128)S(1)} %stack.31.place, s32[4]{0:T(128)S(1)} %copy-done.1, bf16[4,32,1280]{2,1,0:T(8,128)(2,1)S(1)} %collective-permute-done.10.q, bf16[32,32,640]{2,1,0:T(8,128)(2,1)S(1)} %all-to-all-done.2.blocks, bf16[32,640]{1,0:T(8,128)(2,1)S(1)} %collective-permute-done.6.far), custom_call_target="tpu_custom_call" | custom-call | tf_op jit(solution)/shard_map/attend1/pallas_call | solution.py:386
  124.3 2.8 %collective-permute-start.11 = (f32[4,32,1408]{2,1,0:T(8,128)S(1)}, f32[4,32,1408]{2,1,0:T(8,128)S(1)}, u32[]{:S(2)}, u32[]{:S(2)}) collective-permute-start(f32[4,32,1408]{2,1,0:T(8,128)S(1)} %attend1.1), channel_id=1, source_target_pairs={{0,1},{1,0},{2,3},{3,2},{4,5},{5,4},{6,7},{7,6},{8,9},{9,8},{10,11... | collective-permute-start | bytes 2162696 | tf_op jit(solution)/shard_map/ppermute | solution.py:400
  127.1 2.4 %attend0.1.here = f32[4,32,1408]{2,1,0:T(8,128)S(1)} custom-call(s32[7]{0:T(128)S(1)} %stack.31.place, s32[4]{0:T(128)S(1)} %copy-done.1, bf16[4,32,1280]{2,1,0:T(8,128)(2,1)S(1)} %pad_maximum_fusion.q, bf16[32,32,640]{2,1,0:T(8,128)(2,1)S(1)} %all-to-all-done.2.blocks, bf16[32,640]{1,0:T(8,128)(2,1)S(1)} %collective-permute-done.6.far), custom_call_target="tpu_custom_call" | custom-call | tf_op jit(solution)/shard_map/attend0/pallas_call | solution.py:386
  130.4 3.5 %all-to-all-start.3 = ((bf16[4,32,1408]{2,1,0:T(8,128)(2,1)}), bf16[4,32,1408]{2,1,0:T(8,128)(2,1)S(1)}, u32[]{:S(2)}, u32[]{:S(2)}) async-start(bf16[4,32,1408]{2,1,0:T(8,128)(2,1)} %pack.1), calls=%async_computation.3 | async-start | bytes 720896 | tf_op jit(solution)/shard_map/all_to_all | solution.py:405
  134.6 10.3 %all-to-all-done.3.parts = bf16[4,32,1408]{2,1,0:T(8,128)(2,1)S(1)} async-done(((bf16[4,32,1408]{2,1,0:T(8,128)(2,1)}), bf16[4,32,1408]{2,1,0:T(8,128)(2,1)S(1)}, u32[]{:S(2)}, u32[]{:S(2)}) %all-to-all-start.3) | async-done | bytes 360480 | tf_op jit(solution)/shard_map/all_to_all | solution.py:405
  145.2 16.0 %all_gather.3.attended = bf16[256,1280]{1,0:T(8,128)(2,1)S(1)} all-gather(bf16[32,1280]{1,0:T(8,128)(2,1)S(1)} %divide.1), channel_id=1, replica_groups=mesh['yh'=2,'z'=8,'x'=4,'yl'=4,'c'=2] {'yl','c'}, dimensions={0}, use_global_device_ids=true | all-gather | bytes 737280 | tf_op jit(solution)/shard_map/all_gather | solution.py:410
  (46 shorter events, 8.8 us)
Async XLA Ops:
  0.6 17.8 %copy-start = (bf16[256,256]{1,0:T(8,128)(2,1)S(1)}, bf16[256,256]{1,0:T(8,128)(2,1)}, u32[]{:S(2)}) copy-start(bf16[256,256]{1,0:T(8,128)(2,1)} %param.8) | copy-start | bytes 393220
  0.6 28.4 %copy-start.3 = (bf16[256]{0:T(256)(128)(2,1)S(1)}, bf16[256]{0:T(256)(128)(2,1)}, u32[]{:S(2)}) copy-start(bf16[256]{0:T(256)(128)(2,1)} %param.9) | copy-start | bytes 1540
  2.2 31.2 %all-to-all-start = ((bf16[16,56,256]{2,1,0:T(8,128)(2,1)}), bf16[16,56,256]{2,1,0:T(8,128)(2,1)S(1)}, u32[]{:S(2)}, u32[]{:S(2)}) async-start(bf16[16,56,256]{2,1,0:T(8,128)(2,1)} %broadcast_in_dim.50), calls=%async_computation | async-start | bytes 917504 | tf_op jit(solution)/shard_map/all_to_all | solution.py:309
  18.5 10.7 %collective-permute-start = (bf16[256,256]{1,0:T(8,128)(2,1)S(1)}, bf16[256,256]{1,0:T(8,128)(2,1)S(1)}, u32[]{:S(2)}, u32[]{:S(2)}) collective-permute-start(bf16[256,256]{1,0:T(8,128)(2,1)S(1)} %copy-done), channel_id=1, source_target_pairs={{0,8},{8,16},{16,24},{24,0},{1,9},{9,17},{17,25},{25,1},{2,10},{10... | collective-permute-start | bytes 393224 | tf_op jit(solution)/shard_map/ppermute | solution.py:322
  21.6 7.9 %collective-permute-start.1 = (bf16[256,256]{1,0:T(8,128)(2,1)S(1)}, bf16[256,256]{1,0:T(8,128)(2,1)S(1)}, u32[]{:S(2)}, u32[]{:S(2)}) collective-permute-start(bf16[256,256]{1,0:T(8,128)(2,1)S(1)} %copy-done), channel_id=1, source_target_pairs={{0,16},{8,24},{16,0},{24,8},{1,17},{9,25},{17,1},{25,9},{2,18},{10... | collective-permute-start | bytes 393224 | tf_op jit(solution)/shard_map/ppermute | solution.py:322
  26.0 6.0 %collective-permute-start.2 = (bf16[256,256]{1,0:T(8,128)(2,1)S(1)}, bf16[256,256]{1,0:T(8,128)(2,1)S(1)}, u32[]{:S(2)}, u32[]{:S(2)}) collective-permute-start(bf16[256,256]{1,0:T(8,128)(2,1)S(1)} %copy-done), channel_id=1, source_target_pairs={{0,24},{8,0},{16,8},{24,16},{1,25},{9,1},{17,9},{25,17},{2,26},{10... | collective-permute-start | bytes 393224 | tf_op jit(solution)/shard_map/ppermute | solution.py:322
  34.4 6.7 %collective-permute-start.3 = (f32[4,128,512]{2,1,0:T(8,128)S(1)}, f32[4,128,512]{2,1,0:T(8,128)S(1)}, u32[]{:S(2)}, u32[]{:S(2)}) collective-permute-start(f32[4,128,512]{2,1,0:T(8,128)S(1)} %project1.1), channel_id=1, source_target_pairs={{0,1},{1,0},{2,3},{3,2},{4,5},{5,4},{6,7},{7,6},{8,9},{9,8},{10,11... | collective-permute-start | bytes 3145736 | tf_op jit(solution)/shard_map/ppermute | solution.py:344
  42.3 7.6 %copy-start.4 = (bf16[64]{0:T(256)(128)(2,1)S(1)}, bf16[64]{0:T(256)(128)(2,1)}, u32[]{:S(2)}) copy-start(bf16[64]{0:T(256)(128)(2,1)} %param.12) | copy-start | bytes 388
  42.3 7.7 %copy-start.1 = (s32[4]{0:T(128)S(1)}, s32[4]{0:T(128)}, u32[]{:S(2)}) copy-start(s32[4]{0:T(128)} %lengths.3) | copy-start | bytes 52
  42.3 28.9 %copy-start.2 = (s32[4]{0:T(128)S(1)}, s32[4]{0:T(128)}, u32[]{:S(2)}) copy-start(s32[4]{0:T(128)} %table.1) | copy-start | bytes 52
  42.3 33.1 %copy-start.5 = (bf16[64]{0:T(256)(128)(2,1)S(1)}, bf16[64]{0:T(256)(128)(2,1)}, u32[]{:S(2)}) copy-start(bf16[64]{0:T(256)(128)(2,1)} %param.11) | copy-start | bytes 388
  42.3 28.9 %all-to-all-start.1 = ((bf16[16,32,768]{2,1,0:T(8,128)(2,1)}), bf16[16,32,768]{2,1,0:T(8,128)(2,1)S(1)}, u32[]{:S(2)}, u32[]{:S(2)}) async-start(bf16[16,32,768]{2,1,0:T(8,128)(2,1)} %bitcast.12), calls=%async_computation.1 | async-start | bytes 1572864 | tf_op jit(solution)/shard_map/all_to_all | solution.py:349
  50.3 15.0 %collective-permute-start.4 = (bf16[16,24,256]{2,1,0:T(8,128)(2,1)S(1)}, bf16[16,24,256]{2,1,0:T(8,128)(2,1)S(1)}, u32[]{:S(2)}, u32[]{:S(2)}) collective-permute-start(bf16[16,24,256]{2,1,0:T(8,128)(2,1)S(1)} %slice.4.own), channel_id=1, source_target_pairs={{0,8},{8,16},{16,24},{24,0},{1,9},{9,17},{17,25},{25,1},{2,10},{10... | collective-permute-start | bytes 589832 | tf_op jit(solution)/shard_map/ppermute | solution.py:322
  53.6 11.7 %collective-permute-start.5 = (bf16[16,24,256]{2,1,0:T(8,128)(2,1)S(1)}, bf16[16,24,256]{2,1,0:T(8,128)(2,1)S(1)}, u32[]{:S(2)}, u32[]{:S(2)}) collective-permute-start(bf16[16,24,256]{2,1,0:T(8,128)(2,1)S(1)} %slice.4.own), channel_id=1, source_target_pairs={{0,24},{8,0},{16,8},{24,16},{1,25},{9,1},{17,9},{25,17},{2,26},{10... | collective-permute-start | bytes 589832 | tf_op jit(solution)/shard_map/ppermute | solution.py:322
  72.8 8.6 %collective-permute-start.6 = (bf16[32,640]{1,0:T(8,128)(2,1)S(1)}, bf16[32,640]{1,0:T(8,128)(2,1)S(1)}, u32[]{:S(2)}, u32[]{:S(2)}) collective-permute-start(bf16[32,640]{1,0:T(8,128)(2,1)S(1)} %get-tuple-element.22), channel_id=1, source_target_pairs={{0,256},{256,0},{1,257},{257,1},{2,258},{258,2},{3,259},{259,3},{4... | collective-permute-start | bytes 122888 | tf_op jit(solution)/shard_map/ppermute | solution.py:372
  82.7 39.0 %all-to-all-start.2 = ((bf16[32,32,640]{2,1,0:T(8,128)(2,1)}), bf16[32,32,640]{2,1,0:T(8,128)(2,1)S(1)}, u32[]{:S(2)}, u32[]{:S(2)}) async-start(bf16[32,32,640]{2,1,0:T(8,128)(2,1)} %broadcast_select_fusion), calls=%async_computation.2 | async-start | bytes 2621440 | tf_op jit(solution)/shard_map/all_to_all | solution.py:381
  87.7 7.0 %collective-permute-start.8 = (bf16[1,32,1280]{2,1,0:T(8,128)(2,1)S(1)}, bf16[1,32,1280]{2,1,0:T(8,128)(2,1)S(1)}, u32[]{:S(2)}, u32[]{:S(2)}) collective-permute-start(bf16[1,32,1280]{2,1,0:T(8,128)(2,1)S(1)} %bitcast.21), channel_id=1, source_target_pairs={{0,2},{2,4},{4,6},{6,0},{1,3},{3,5},{5,7},{7,1},{8,10},{10,12},{12... | collective-permute-start | bytes 245768 | tf_op jit(solution)/shard_map/ppermute | solution.py:322
  94.7 7.3 %collective-permute-start.9 = (bf16[2,32,1280]{2,1,0:T(8,128)(2,1)S(1)}, bf16[2,32,1280]{2,1,0:T(8,128)(2,1)S(1)}, u32[]{:S(2)}, u32[]{:S(2)}) collective-permute-start(bf16[2,32,1280]{2,1,0:T(8,128)(2,1)S(1)} %pad_maximum_fusion.1), channel_id=1, source_target_pairs={{0,4},{2,6},{4,0},{6,2},{1,5},{3,7},{5,1},{7,3},{8,12},{10,14},{12... | collective-permute-start | bytes 491528 | tf_op jit(solution)/shard_map/ppermute | solution.py:322
  102.0 19.8 %collective-permute-start.10 = (bf16[4,32,1280]{2,1,0:T(8,128)(2,1)S(1)}, bf16[4,32,1280]{2,1,0:T(8,128)(2,1)S(1)}, u32[]{:S(2)}, u32[]{:S(2)}) collective-permute-start(bf16[4,32,1280]{2,1,0:T(8,128)(2,1)S(1)} %pad_maximum_fusion.q), channel_id=1, source_target_pairs={{0,1},{1,0},{2,3},{3,2},{4,5},{5,4},{6,7},{7,6},{8,9},{9,8},{10,11... | collective-permute-start | bytes 983048 | tf_op jit(solution)/shard_map/ppermute | solution.py:379
  108.8 12.9 %collective-permute-start.7 = (bf16[16,24,256]{2,1,0:T(8,128)(2,1)S(1)}, bf16[16,24,256]{2,1,0:T(8,128)(2,1)S(1)}, u32[]{:S(2)}, u32[]{:S(2)}) collective-permute-start(bf16[16,24,256]{2,1,0:T(8,128)(2,1)S(1)} %slice.4.own), channel_id=1, source_target_pairs={{0,16},{8,24},{16,0},{24,8},{1,17},{9,25},{17,1},{25,9},{2,18},{10... | collective-permute-start | bytes 589832 | tf_op jit(solution)/shard_map/ppermute | solution.py:322
  124.3 5.2 %collective-permute-start.11 = (f32[4,32,1408]{2,1,0:T(8,128)S(1)}, f32[4,32,1408]{2,1,0:T(8,128)S(1)}, u32[]{:S(2)}, u32[]{:S(2)}) collective-permute-start(f32[4,32,1408]{2,1,0:T(8,128)S(1)} %attend1.1), channel_id=1, source_target_pairs={{0,1},{1,0},{2,3},{3,2},{4,5},{5,4},{6,7},{7,6},{8,9},{9,8},{10,11... | collective-permute-start | bytes 2162696 | tf_op jit(solution)/shard_map/ppermute | solution.py:400
  130.4 14.5 %all-to-all-start.3 = ((bf16[4,32,1408]{2,1,0:T(8,128)(2,1)}), bf16[4,32,1408]{2,1,0:T(8,128)(2,1)S(1)}, u32[]{:S(2)}, u32[]{:S(2)}) async-start(bf16[4,32,1408]{2,1,0:T(8,128)(2,1)} %pack.1), calls=%async_computation.3 | async-start | bytes 720896 | tf_op jit(solution)/shard_map/all_to_all | solution.py:405
